TPU v7x, 256 devices: a whole 4x4x8 slice. The times are simulated.
256 devices in a mesh: lat: 16 (over y, x), kpt: 16 (over z, core).
Axes of the slice: x: 4, y: 4, z: 8, core: 2. Of those that a mesh axis runs over, the one named last changes fastest.
Arguments:
- coarse: bfloat16 [2, 16, 256, 12288], P(None, 'lat', 'kpt'), may hold values from -0.1875 to 0.1875
- rp_vectors: int32 [16, 3], P('lat'), may hold values from -4 to 4
- rp_weights: int32 [16], P('lat'), may hold values from 1 to 3
- re_vectors: int32 [256, 3], replicated, may hold values from -4 to 4
- re_weights: int32 [256], replicated, may hold values from 1 to 3
- q_points: float32 [2, 3], replicated, may hold values from 0 to 1
- k_points: float32 [1024, 3], P('kpt'), may hold values from 0 to 1
- modes_rot: bfloat16 [2, 2, 48, 48], replicated, may hold values from -0.625 to 0.625
- u_k: bfloat16 [2, 1024, 16, 16], P(None, 'kpt'), may hold values from -1 to 1
- u_kq: bfloat16 [2, 2, 1024, 16, 16], P(None, None, 'kpt'), may hold values from -1 to 1
- mask_k: int32 [1024, 16], P('kpt'), may hold values 0 or 1
- mask_kq: int32 [2, 1024, 16], P(None, 'kpt'), may hold values 0 or 1
Outputs:
- coupling: bfloat16 [2, 1024, 2, 12288], P(None, 'kpt', None, 'lat')
All inputs are finite; a program needn't handle non-finite values. No bound on the sum of `mask_k` or of `mask_kq` on one device may be relied on, other than what follows from the above.
Results may differ from a plain program's by a relative error of at most 0.017.
Values may be sent and summed in bfloat16 or wider, within the bound.
No kernel may reach another device: no remote copies, remote signals or barrier semaphores. Data moves between devices by JAX's collectives and lax.ppermute only.
A program may use at most 64 MiB of HBM per device.

v0:
```python
import jax
import jax.numpy as jnp
from jax import lax
from jax.sharding import PartitionSpec as P

two_pi = 6.283185307179586


def phases(points, vectors, weights):
    cells = vectors.astype(jnp.float32)
    argument = two_pi * (
        points[:, 0:1] * cells[None, :, 0]
        + points[:, 1:2] * cells[None, :, 1]
        + points[:, 2:3] * cells[None, :, 2]
    )
    inverse = 1.0 / weights.astype(jnp.float32)
    return (
        (jnp.cos(argument) * inverse).astype(jnp.bfloat16),
        (jnp.sin(argument) * inverse).astype(jnp.bfloat16),
    )


def rotate_modes(values, modes_rot):
    shape = values.shape
    mode_count = modes_rot.shape[2]
    split = values.reshape(shape[0], shape[1], shape[2], mode_count, shape[3] // mode_count)
    br = jnp.einsum(
        "qmn,qrmx->qrnx", modes_rot[0], split[0], preferred_element_type=jnp.float32
    ) - jnp.einsum("qmn,qrmx->qrnx", modes_rot[1], split[1], preferred_element_type=jnp.float32)
    bi = jnp.einsum(
        "qmn,qrmx->qrnx", modes_rot[0], split[1], preferred_element_type=jnp.float32
    ) + jnp.einsum("qmn,qrmx->qrnx", modes_rot[1], split[0], preferred_element_type=jnp.float32)
    return jnp.stack([br, bi]).reshape(shape).astype(jnp.bfloat16)


def phonon_sum(block, vectors, weights, q_points):
    phase_real, phase_imag = phases(q_points, vectors, weights)
    rows = block.shape[1]
    cells = block.shape[2]
    lanes = block.shape[3]
    flat_real = block[0].reshape(rows, cells * lanes)
    flat_imag = block[1].reshape(rows, cells * lanes)
    part_real = jnp.dot(phase_real, flat_real, preferred_element_type=jnp.float32) - jnp.dot(
        phase_imag, flat_imag, preferred_element_type=jnp.float32
    )
    part_imag = jnp.dot(phase_real, flat_imag, preferred_element_type=jnp.float32) + jnp.dot(
        phase_imag, flat_real, preferred_element_type=jnp.float32
    )
    return jnp.stack([part_real, part_imag]).reshape(2, q_points.shape[0], cells, lanes)


def per_device(
    coarse,
    rp_vectors,
    rp_weights,
    re_vectors,
    re_weights,
    q_points,
    k_points,
    modes_rot,
    u_k,
    u_kq,
    mask_k,
    mask_kq,
):
    q_count = q_points.shape[0]
    k_count = k_points.shape[0]
    band_count = u_k.shape[2]
    partial_value = phonon_sum(coarse, rp_vectors, rp_weights, q_points)
    summed = lax.psum_scatter(partial_value, "lat", scatter_dimension=2, tiled=True).astype(
        jnp.bfloat16
    )
    rotated = rotate_modes(summed, modes_rot)
    shared = lax.all_to_all(rotated, "lat", split_axis=3, concat_axis=2, tiled=True)
    lane_local = shared.shape[3]
    portion = lax.all_gather(shared, "kpt", axis=2, tiled=True)
    kreal, kimag = phases(k_points, re_vectors, re_weights)
    er = jnp.einsum(
        "kr,qrx->kqx", kreal, portion[0], preferred_element_type=jnp.float32
    ) - jnp.einsum("kr,qrx->kqx", kimag, portion[1], preferred_element_type=jnp.float32)
    ei = jnp.einsum(
        "kr,qrx->kqx", kreal, portion[1], preferred_element_type=jnp.float32
    ) + jnp.einsum("kr,qrx->kqx", kimag, portion[0], preferred_element_type=jnp.float32)
    totals = jnp.stack([er, ei])
    mode_local = lane_local // (band_count * band_count)
    field = totals.astype(jnp.bfloat16).reshape(
        2, k_count, q_count, mode_local, band_count, band_count
    )
    tr = jnp.einsum(
        "kqmab,kbn->kqman", field[0], u_k[0], preferred_element_type=jnp.float32
    ) - jnp.einsum("kqmab,kbn->kqman", field[1], u_k[1], preferred_element_type=jnp.float32)
    ti = jnp.einsum(
        "kqmab,kbn->kqman", field[0], u_k[1], preferred_element_type=jnp.float32
    ) + jnp.einsum("kqmab,kbn->kqman", field[1], u_k[0], preferred_element_type=jnp.float32)
    tr = tr.astype(jnp.bfloat16)
    ti = ti.astype(jnp.bfloat16)
    outr = jnp.einsum(
        "qkac,kqman->kqmcn", u_kq[0], tr, preferred_element_type=jnp.float32
    ) + jnp.einsum("qkac,kqman->kqmcn", u_kq[1], ti, preferred_element_type=jnp.float32)
    outi = jnp.einsum(
        "qkac,kqman->kqmcn", u_kq[0], ti, preferred_element_type=jnp.float32
    ) - jnp.einsum("qkac,kqman->kqmcn", u_kq[1], tr, preferred_element_type=jnp.float32)
    window = (
        jnp.transpose(mask_kq.astype(jnp.float32), (1, 0, 2))[:, :, None, :, None]
        * mask_k.astype(jnp.float32)[:, None, None, None, :]
    )
    result = jnp.stack([outr * window, outi * window])
    return result.reshape(2, k_count, q_count, lane_local).astype(jnp.bfloat16)


def solution(mesh):
    placed = (
        P(None, "lat", "kpt", None),
        P("lat", None),
        P("lat"),
        P(),
        P(),
        P(),
        P("kpt", None),
        P(),
        P(None, "kpt", None, None),
        P(None, None, "kpt", None, None),
        P("kpt", None),
        P(None, "kpt", None),
    )
    return jax.shard_map(
        per_device,
        mesh=mesh,
        in_specs=placed,
        out_specs=P(None, "kpt", None, "lat"),
        check_vma=False,
    )
```

profile of v0, /device:TPU:1, one launch (start us, length us, event | category | flops | bytes accessed | tf_op | source)
XLA Modules:
  0.0 256.3 jit_solution(5092199044945277099)
XLA Ops:
  6.5 0.0 all-gather.2.cloned.1.call-start
  7.2 0.7 convert_element_type.53
  7.8 0.6 fusion.56
  8.5 1.2 convert_bitcast_fusion.1
  9.7 0.0 copy-start.10
  9.7 0.2 copy.137
  9.9 0.2 copy.138
  10.1 0.3 copy-done.10
  10.4 2.1 convert_reduce_fusion.1
  12.4 1.5 multiply_subtract_fusion
  13.9 1.4 pad_maximum_fusion
  15.3 0.0 copy-start.15
  15.4 0.0 copy-start.7
  15.4 86.5 %all-reduce.2 = bf16[2,2,16,12288]{3,1,2,0:T(2,128)(2,1)} all-reduce(f32[2,2,16,12288]{3,1,2,0:T(2,128)S(1)} %pad_maximum_fusion), channel_id=2, replica_groups=mesh['lat'=16,'kpt'=16] {'lat'}, use_global_device_ids=true, to_apply=%region_0.0.clone | all-reduce | flops 786432 | bytes 4718592
  101.9 0.0 copy-done.15
  101.9 0.6 dynamic-slice
  102.5 1.6 dynamic-slice_convert_fusion
  104.1 0.1 fusion.54
  104.2 0.0 copy-done.7
  104.2 0.2 fusion.25
  104.4 0.2 fusion.27
  104.6 0.2 fusion.4
  104.8 0.2 fusion.5
  105.0 0.1 pad_maximum_fusion.2
  105.1 10.0 %copy.99 = bf16[2,2,1,12288]{1,0,2,3:T(2,128)(2,1)} copy(bf16[2,2,1,12288]{3,1,2,0:T(2,128)(2,1)S(1)} %pad_maximum_fusion.2) | data formatting | bytes 196608 | tf_op jit(solution)/shard_map/stack | solution.py:33
  115.1 13.7 %reshape.158 = bf16[16,2,1536]{2,1,0:T(2,128)(2,1)S(1)} reshape(bf16[12288,1,2,2]{3,2,1,0:T(2,128)(2,1)} %bitcast.147) | data formatting | bytes 196608
  128.8 9.2 %all_to_all.12 = bf16[16,2,1536]{2,1,0:T(2,128)(2,1)S(1)} all-to-all(bf16[16,2,1536]{2,1,0:T(2,128)(2,1)S(1)} %reshape.158), channel_id=1, replica_groups=mesh['lat'=16,'kpt'=16] {'lat'}, dimensions={0} | all-to-all | bytes 196608 | tf_op jit(solution)/shard_map/all_to_all | solution.py:74
  138.0 14.7 %reshape.159 = bf16[12288,1,2,2]{3,2,1,0:T(2,128)(2,1)} reshape(bf16[16,2,1536]{2,1,0:T(2,128)(2,1)S(1)} %all_to_all.12) | data formatting | bytes 196608
  152.8 9.9 %copy.128 = bf16[2,2,16,768]{3,2,1,0:T(8,128)(2,1)} copy(bf16[2,2,16,768]{1,0,3,2:T(2,128)(2,1)} %bitcast.148) | data formatting | bytes 196608 | tf_op jit(solution)/shard_map/all_to_all | solution.py:74
  162.7 0.0 all-gather.2.cloned.1.call-update
  162.7 0.0 copy-done.12
  162.7 0.0 copy-done.11
  162.7 0.0 copy-done.8
  162.8 0.3 copy.133
  163.0 1.0 copy.134
  164.0 1.5 copy.136
  165.5 1.5 copy.135
  167.1 0.7 broadcast_multiply_fusion
  167.8 45.9 %all-gather.2.cloned.1.call-done = bf16[2,2,256,768]{3,2,1,0:T(8,128)(2,1)} async-done(((bf16[2,2,16,768]{3,2,1,0:T(8,128)(2,1)}), bf16[2,2,256,768]{3,2,1,0:T(8,128)(2,1)}) %all-gather.2.cloned.1.call-update) | async-done | bytes 1572880 | tf_op jit(solution)/shard_map/all_gather | solution.py:76
  213.8 1.7 fusion.9
  215.5 1.6 fusion.1
  217.1 0.9 copy.104
  218.1 0.5 fusion.8
  218.6 0.5 fusion
  219.1 0.2 copy.101
  219.3 1.3 copy.103
  220.6 2.2 copy.106
  222.8 1.5 fusion.21
  224.3 0.5 fusion.19
  224.8 0.5 add_convert_fusion
  225.4 0.4 copy-done.4
  225.8 0.6 subtract_convert_fusion
  226.3 0.5 copy-done.2
  226.8 2.4 fusion.10
  229.2 0.6 fusion.16
  229.8 2.3 fusion.14
  232.1 2.3 fusion.12
  234.4 3.4 %copy.118 = f32[64,2,3,16,16]{0,3,4,2,1:T(8,128)} copy(f32[64,2,3,16,16]{4,3,2,1,0:T(8,128)} %fusion.10) | data formatting | bytes 786432 | tf_op jit(solution)/shard_map/qkac,kqman->kqmcn/dot_general | solution.py:102
  237.9 2.3 copy.113
  240.1 3.6 %copy.117 = f32[64,2,3,16,16]{0,3,4,2,1:T(8,128)} copy(f32[64,2,3,16,16]{4,3,2,1,0:T(8,128)} %fusion.14) | data formatting | bytes 786432 | tf_op jit(solution)/shard_map/qkac,kqman->kqmcn/dot_general | solution.py:100
  243.8 2.3 copy.114
  246.1 2.1 fusion.7
  248.1 0.2 pad_maximum_fusion.1
  248.3 1.1 copy.119
  (31 shorter events, 0.1 us)
Async XLA Ops:
  6.5 207.2 %all-gather.2.cloned.1.call-start = ((), (), s32[]{:S(2)}) async-start(), calls=%async_computation.1 | async-start | bytes 1671168 | tf_op jit(solution)/shard_map/all_gather | solution.py:76
  9.7 0.7 copy-start.10
  15.3 86.6 %copy-start.15 = (u32[256]{0:T(256)S(1)}, u32[256]{0:T(256)}, u32[]{:S(2)}) copy-start(u32[256]{0:T(256)} %constant.12) | copy-start | bytes 3076
  15.4 88.8 %copy-start.7 = (bf16[2,2,48,48]{3,2,1,0:T(8,128)(2,1)S(1)}, bf16[2,2,48,48]{3,2,1,0:T(8,128)(2,1)}, u32[]{:S(2)}) copy-start(bf16[2,2,48,48]{3,2,1,0:T(8,128)(2,1)} %param.19) | copy-start | bytes 55300
  152.7 9.9 %copy-start.12 = (s32[256,3]{0,1:T(4,128)S(1)}, s32[256,3]{0,1:T(4,128)}, u32[]{:S(2)}) copy-start(s32[256,3]{0,1:T(4,128)} %param.15) | copy-start | bytes 9220
  152.7 10.0 %copy-start.11 = (s32[64,16]{0,1:T(8,128)S(1)}, s32[64,16]{0,1:T(8,128)}, u32[]{:S(2)}) copy-start(s32[64,16]{0,1:T(8,128)} %param.22) | copy-start | bytes 12292
  152.8 10.0 %copy-start.8 = (bf16[2,64,16,16]{1,3,2,0:T(8,128)(2,1)S(1)}, bf16[2,64,16,16]{1,3,2,0:T(8,128)(2,1)}, u32[]{:S(2)}) copy-start(bf16[2,64,16,16]{1,3,2,0:T(8,128)(2,1)} %param.20) | copy-start | bytes 196612
  152.8 11.2 %copy-start.6 = (bf16[2,2,64,16,16]{2,4,3,1,0:T(8,128)(2,1)S(1)}, bf16[2,2,64,16,16]{2,4,3,1,0:T(8,128)(2,1)}, u32[]{:S(2)}) copy-start(bf16[2,2,64,16,16]{2,4,3,1,0:T(8,128)(2,1)} %param.21) | copy-start | bytes 393220
  162.6 4.4 %copy-start.14 = (s32[256]{0:T(256)S(1)}, s32[256]{0:T(256)}, u32[]{:S(2)}) copy-start(s32[256]{0:T(256)} %param.16) | copy-start | bytes 3076
  162.7 4.4 %copy-start.13 = (f32[64,3]{0,1:T(4,128)S(1)}, f32[64,3]{0,1:T(4,128)}, u32[]{:S(2)}) copy-start(f32[64,3]{0,1:T(4,128)} %param.18) | copy-start | bytes 2308
  162.7 4.5 %copy-start.9 = (s32[2,64,16]{1,2,0:T(8,128)S(1)}, s32[2,64,16]{1,2,0:T(8,128)}, u32[]{:S(2)}) copy-start(s32[2,64,16]{1,2,0:T(8,128)} %param.23) | copy-start | bytes 24580
  213.7 4.3 %copy-start.1 = (bf16[2,2,256,768]{3,2,1,0:T(8,128)(2,1)S(1)}, bf16[2,2,256,768]{3,2,1,0:T(8,128)(2,1)}, u32[]{:S(2)}) copy-start(bf16[2,2,256,768]{3,2,1,0:T(8,128)(2,1)} %all-gather.2.cloned.1.call-done) | copy-start | bytes 4718596
  224.8 1.0 copy-start.4
  225.8 1.0 copy-start.2
  226.8 2.4 copy-start.3
  240.1 3.6 %copy-start = (f32[64,2,3,16,16]{4,3,2,1,0:T(8,128)S(1)}, f32[64,2,3,16,16]{4,3,2,1,0:T(8,128)}, u32[]{:S(2)}) copy-start(f32[64,2,3,16,16]{4,3,2,1,0:T(8,128)} %fusion.12) | copy-start | bytes 1179652
  243.8 2.3 copy-start.5
Sparse Core Ops, SparseCore 0:
  162.8 50.9 all-gather.1
where the time goes:
time: 257 us; the launch traced here: 256 us
  blocking collectives  95.8 us (37%)
  local copies, waits for them, and re-layouts  74.4 us (29%)
  waiting for transfers between devices  45.9 us (18%)
  matrix products  15.8 us (6%)
  between operations  14.4 us (6%)
  other arithmetic  9.95 us (4%)
    unnamed x1, blocking collectives  86.5 us
    all_gather x1, waiting for transfers between devices, per_device(): portion = lax.all_gather(shared, 'kpt', axis=2, tiled=True)  45.9 us
    unnamed x41, local copies, waits for them, and re-layouts  34.8 us
    another operation x3, local copies, waits for them, and re-layouts, rotate_modes(): return jnp.stack([br, bi]).reshape(shape).astype(jnp.bfloat16)  10 us
    all_to_all x1, local copies, waits for them, and re-layouts, per_device(): lax.all_to_all(rotated, 'lat', split_axis=3, concat_axis=2, tiled=True)  9.89 us
    all_to_all x1, blocking collectives, per_device(): lax.all_to_all(rotated, 'lat', split_axis=3, concat_axis=2, tiled=True)  9.25 us
  transfers between devices with their start and end apart: 1, of which 1 were waited for; matrix products, arithmetic and copies ran while one was open for 2% of the time, Pallas kernels for 0%

commit v1 on v0

v1 whole, which is shorter than its diff:
```python
import jax
import jax.numpy as jnp
from jax import lax
from jax.experimental import pallas as pl
from jax.experimental.pallas import tpu as pltpu
from jax.sharding import PartitionSpec as P

two_pi = 6.283185307179586
f32 = jnp.float32
bf16 = jnp.bfloat16

MODES = 48
BANDS = 16
CELLS = 16
LAT = 16
NQ = 2
KPTS = 64
PER = MODES // LAT
LANES = PER * BANDS * BANDS
STRIDE_S = 2 * MODES
ROWS = NQ * 2 * CELLS


def rotate_body(qp_ref, rv_ref, rw_ref, rot_ref, coarse_ref, out_ref, mat_ref, s_ref, o_ref):
    weight = 1.0 / jnp.full((8, 128), rw_ref[0], jnp.int32).astype(f32)
    for q in range(NQ):
        arg = two_pi * (
            qp_ref[q, 0] * rv_ref[0, 0].astype(f32)
            + qp_ref[q, 1] * rv_ref[0, 1].astype(f32)
            + qp_ref[q, 2] * rv_ref[0, 2].astype(f32)
        )
        angle = jnp.full((8, 128), arg, f32)
        pr = (jnp.cos(angle) * weight).astype(bf16).astype(f32)[0:1, 0:1]
        pi = (jnp.sin(angle) * weight).astype(bf16).astype(f32)[0:1, 0:1]
        rr = rot_ref[0, q].astype(f32)
        ri = rot_ref[1, q].astype(f32)
        cr = rr * pr - ri * pi
        ci = rr * pi + ri * pr
        top = jnp.concatenate([cr, -ci], axis=0)
        low = jnp.concatenate([ci, cr], axis=0)
        mat_ref[q * 96:q * 96 + 48, 0:96] = top.T
        mat_ref[q * 96 + 48:q * 96 + 96, 0:96] = low.T
    rows = []
    for g in range(2 * NQ):
        for j in range(PER):
            rows.append(mat_ref[pl.ds(g * 48 + j, LAT, stride=PER), :])
    mat = jnp.concatenate(rows, axis=0)[:, 0:96].astype(bf16)
    for part in range(2):
        for m in range(MODES):
            for h in range(2):
                at = (2 * m + h) * 128
                tile = coarse_ref[part, 0, :, at:at + 128].astype(f32)
                s_ref[h, pl.ds(part * MODES + m, CELLS, stride=STRIDE_S), :] = tile
    for e in range(CELLS):
        for h in range(2):
            block = s_ref[h, e * STRIDE_S:e * STRIDE_S + 96, :].astype(bf16)
            res = jnp.dot(mat, block, preferred_element_type=f32)
            for g in range(2 * NQ):
                for j in range(PER):
                    at = (g * PER + j) * LAT
                    o_ref[2 * j + h, pl.ds(g * CELLS + e, LAT, stride=ROWS), :] = res[at:at + LAT]
    for l in range(LAT):
        for t in range(2 * PER):
            out_ref[l, :, t * 128:(t + 1) * 128] = o_ref[t, l * ROWS:(l + 1) * ROWS, :].astype(bf16)


def sum_body(x_ref, out_ref):
    for r in range(0, ROWS, 16):
        acc = x_ref[0, r:r + 16, :].astype(f32)
        for p in range(1, LAT):
            acc = acc + x_ref[p, r:r + 16, :].astype(f32)
        out_ref[r:r + 16, :] = acc.astype(bf16)


def prep_body(at_ref, kp_ref, rv_ref, u_ref, uq_ref, mk_ref, mq_ref, ph_ref, uo_ref, lo_ref):
    z = at_ref[0]
    c = at_ref[1]
    lane = lax.broadcasted_iota(jnp.int32, (256, 512), 1)
    src = lax.broadcasted_iota(jnp.int32, (256, 512), 0)
    block = lane >> 5
    home = (((z - block) & 7) << 1) + (c ^ (block >> 3))
    cell = (home << 4) + (lane & 15)
    pick = jnp.where(src == cell, 1.0, 0.0).astype(bf16)
    vec = jnp.dot(rv_ref[...].astype(f32).astype(bf16), pick, preferred_element_type=f32)
    kp = kp_ref[...]
    arg = two_pi * (
        kp[:, 0:1] * vec[0:1, :] + kp[:, 1:2] * vec[1:2, :] + kp[:, 2:3] * vec[2:3, :]
    )
    inverse = 1.0 / vec[3:4, :]
    co = jnp.cos(arg) * inverse
    si = jnp.sin(arg) * inverse
    first = (lax.broadcasted_iota(jnp.int32, (KPTS, 512), 1) & 16) == 0
    ph_ref[0:KPTS, :] = jnp.where(first, co, -si).astype(bf16)
    ph_ref[KPTS:2 * KPTS, :] = jnp.where(first, si, co).astype(bf16)
    row = lax.broadcasted_iota(jnp.int32, (KPTS, 128), 0)
    col = lax.broadcasted_iota(jnp.int32, (KPTS, 128), 1)
    spread = jnp.where((col >> 1) == row, 1.0, 0.0).astype(bf16)
    row2 = lax.broadcasted_iota(jnp.int32, (128, 128), 0)
    col2 = lax.broadcasted_iota(jnp.int32, (128, 128), 1)
    place = jnp.where((((col2 & 1) << 6) + (col2 >> 1)) == row2, 1.0, 0.0).astype(bf16)
    dims = (((0,), (0,)), ((), ()))
    mk = lax.dot_general(mk_ref[...].astype(f32).astype(bf16), spread, dims, preferred_element_type=f32)
    mq = lax.dot_general(mq_ref[...].astype(f32).astype(bf16), place, dims, preferred_element_type=f32)
    for part in range(2):
        ut = lax.dot_general(u_ref[part], spread, dims, preferred_element_type=f32)
        lt = lax.dot_general(uq_ref[part], place, dims, preferred_element_type=f32)
        for b in range(BANDS):
            uo_ref[part, b] = ut[b * 16:(b + 1) * 16] * mk
            lo_ref[part, b] = lt[b * 16:(b + 1) * 16] * mq


def couple_body(*refs):
    xs = refs[:16]
    ph_ref, u_ref, l_ref, out_ref, y_ref, bl_ref, h_ref, r_ref = refs[16:]
    ph = ph_ref[...]
    for q in range(NQ):
        x = jnp.concatenate([r[q * 32:(q + 1) * 32, :] for r in xs], axis=0)
        t = jnp.dot(ph, x, preferred_element_type=f32)
        for part in range(2):
            for v in range(2 * PER):
                y_ref[part, v, pl.ds(q, KPTS, stride=2), :] = t[
                    part * KPTS:(part + 1) * KPTS, v * 128:(v + 1) * 128
                ]
    for part in range(2):
        for v in range(2 * PER):
            bl_ref[part, v * 128:(v + 1) * 128, :] = y_ref[part, v].T.astype(bf16).astype(f32)

    group = 4

    def first(i, _):
        base = i * group * BANDS
        accr = [jnp.zeros((16, 128), f32) for _ in range(group)]
        acci = [jnp.zeros((16, 128), f32) for _ in range(group)]
        for b in range(BANDS):
            ur = u_ref[0, b]
            ui = u_ref[1, b]
            for s in range(group):
                xr = bl_ref[0, pl.ds(base + s * BANDS + b, 1), :]
                xi = bl_ref[1, pl.ds(base + s * BANDS + b, 1), :]
                accr[s] = accr[s] + (xr * ur - xi * ui)
                acci[s] = acci[s] + (xr * ui + xi * ur)
        for s in range(group):
            h_ref[0, i * group + s] = accr[s].astype(bf16).astype(f32)
            h_ref[1, i * group + s] = acci[s].astype(bf16).astype(f32)
        return 0

    lax.fori_loop(0, PER * BANDS // group, first, 0)

    per = BANDS // group

    def second(i, _):
        n = i // per
        c0 = (i - n * per) * group
        accr = [jnp.zeros((16, 128), f32) for _ in range(group)]
        acci = [jnp.zeros((16, 128), f32) for _ in range(group)]
        for a in range(BANDS):
            hr = h_ref[0, n * BANDS + a]
            hi = h_ref[1, n * BANDS + a]
            for s in range(group):
                lr = l_ref[0, a, pl.ds(c0 + s, 1), :]
                li = l_ref[1, a, pl.ds(c0 + s, 1), :]
                accr[s] = accr[s] + (lr * hr + li * hi)
                acci[s] = acci[s] + (lr * hi - li * hr)
        for s in range(group):
            r_ref[0, i * group + s] = accr[s]
            r_ref[1, i * group + s] = acci[s]
        return 0

    lax.fori_loop(0, PER * per, second, 0)
    for part in range(2):
        for v in range(2 * PER):
            tile = r_ref[part, v * 8:(v + 1) * 8].reshape(128, 128).T
            out_ref[part, :, v * 128:(v + 1) * 128] = tile.astype(bf16)


def vmem():
    return pl.BlockSpec(memory_space=pltpu.VMEM)


def smem():
    return pl.BlockSpec(memory_space=pltpu.SMEM)


def params():
    return pltpu.CompilerParams(vmem_limit_bytes=40 << 20)


def per_device(
    coarse,
    rp_vectors,
    rp_weights,
    re_vectors,
    re_weights,
    q_points,
    k_points,
    modes_rot,
    u_k,
    u_kq,
    mask_k,
    mask_kq,
):
    rotated = pl.pallas_call(
        rotate_body,
        out_shape=jax.ShapeDtypeStruct((LAT, ROWS, LANES), bf16),
        in_specs=[smem(), smem(), smem(), vmem(), vmem()],
        out_specs=vmem(),
        scratch_shapes=[
            pltpu.VMEM((192, 128), f32),
            pltpu.VMEM((2, CELLS * STRIDE_S, 128), f32),
            pltpu.VMEM((2 * PER, LAT * ROWS, 128), f32),
        ],
        compiler_params=params(),
        name="rotate",
    )(q_points, rp_vectors, rp_weights, modes_rot, coarse)
    parts = lax.all_to_all(rotated, "lat", 0, 0, tiled=True)

    index = lax.axis_index("kpt")
    at = jnp.stack([index // 2, index % 2]).astype(jnp.int32)
    lattice = jnp.concatenate(
        [re_vectors.T, re_weights[None, :], jnp.zeros((4, re_weights.shape[0]), jnp.int32)], axis=0
    )
    phase, right, left = pl.pallas_call(
        prep_body,
        out_shape=(
            jax.ShapeDtypeStruct((2 * KPTS, 512), bf16),
            jax.ShapeDtypeStruct((2, BANDS, BANDS, 128), f32),
            jax.ShapeDtypeStruct((2, BANDS, BANDS, 128), f32),
        ),
        in_specs=[smem()] + [vmem()] * 6,
        out_specs=(vmem(),) * 3,
        compiler_params=params(),
        name="prep",
    )(
        at,
        k_points,
        lattice,
        u_k.reshape(2, KPTS, BANDS * BANDS),
        u_kq.reshape(2, NQ * KPTS, BANDS * BANDS),
        mask_k,
        mask_kq.reshape(NQ * KPTS, BANDS),
    )

    own = pl.pallas_call(
        sum_body,
        out_shape=jax.ShapeDtypeStruct((ROWS, LANES), bf16),
        in_specs=[vmem()],
        out_specs=vmem(),
        compiler_params=params(),
        name="add_up",
    )(parts)

    def shift(x, step):
        return lax.ppermute(x, "kpt", [(i, (i + 2 * step) % 16) for i in range(16)])

    def swap(x):
        return lax.ppermute(x, "kpt", [(i, i ^ 1) for i in range(16)])

    up = shift(own, 3)
    down = shift(own, -3)
    blocks = {0: own, 3: up, 5: down}
    blocks[1] = shift(own, 1)
    blocks[7] = shift(own, -1)
    blocks[4] = shift(up, 1)
    blocks[2] = shift(up, -1)
    blocks[6] = shift(down, 1)
    near = [blocks[i] for i in range(8)]
    far = [swap(x) for x in near]

    result = pl.pallas_call(
        couple_body,
        out_shape=jax.ShapeDtypeStruct((2, 2 * KPTS, LANES), bf16),
        in_specs=[vmem()] * 19,
        out_specs=vmem(),
        scratch_shapes=[
            pltpu.VMEM((2, 2 * PER, 128, 128), f32),
            pltpu.VMEM((2, LANES, 128), f32),
            pltpu.VMEM((2, PER * BANDS, BANDS, 128), f32),
            pltpu.VMEM((2, PER * BANDS, BANDS, 128), f32),
        ],
        compiler_params=params(),
        name="couple",
    )(*near, *far, phase, right, left)
    return result.reshape(2, KPTS, NQ, LANES)


def solution(mesh):
    placed = (
        P(None, "lat", "kpt", None),
        P("lat", None),
        P("lat"),
        P(),
        P(),
        P(),
        P("kpt", None),
        P(),
        P(None, "kpt", None, None),
        P(None, None, "kpt", None, None),
        P("kpt", None),
        P(None, "kpt", None),
    )
    return jax.shard_map(
        per_device,
        mesh=mesh,
        in_specs=placed,
        out_specs=P(None, "kpt", None, "lat"),
        check_vma=False,
    )
```

time: 257 us -> 72.1 us (0.28)
  local copies, waits for them, and re-layouts: 74.4 us -> 5.15 us
  blocking collectives: 95.8 us -> 29.1 us
  waiting for transfers between devices: 45.9 us -> 2.34 us
  starting transfers between devices: 0.01 us -> 23.5 us
  matrix products: 15.8 us -> 0 us
  between operations: 14.4 us -> 0.83 us
  Pallas kernels: 0 us -> 10.9 us
  other arithmetic: 9.95 us -> 0.15 us
    unnamed x1 -> x0, blocking collectives: 86.5 us -> none
    all_gather x1 -> x0, waiting for transfers between devices: 45.9 us -> none  [per_device(): portion = lax.all_gather(shared, 'kpt', axis=2, tiled=True)]
    unnamed x41 -> x26, local copies, waits for them, and re-layouts: 34.8 us -> 3.82 us
    ppermute x0 -> x15, starting transfers between devices: none -> 23.5 us  [the longest x7 13.4 us: shift(): return lax.ppermute(x, 'kpt', [(i, (i + 2 * step) % 16) for i in range(16)])]
    all_to_all x1, blocking collectives: 9.25 us -> 29.1 us  [per_device(): parts = lax.all_to_all(rotated, 'lat', 0, 0, tiled=True)]
    dot_general x16 -> x0, matrix products: 15.8 us -> none  [the longest x1 2.35 us: per_device(): jnp.einsum('qkac,kqman->kqmcn', u_kq[1], tr, preferred_element_type=jnp.f...]
    another operation x6 -> x0, local copies, waits for them, and re-layouts: 12.3 us -> none  [the longest x3 10 us: rotate_modes(): return jnp.stack([br, bi]).reshape(shape).astype(jnp.bfloat16)]
    dot_general x4 -> x0, local copies, waits for them, and re-layouts: 11.6 us -> none  [the longest x1 3.62 us: per_device(): jnp.einsum('qkac,kqman->kqmcn', u_kq[0], ti, preferred_element_type=jnp.f...]
  transfers between devices with their start and end apart: 1 -> 15, of which waited for: 1 -> 1; matrix products, arithmetic and copies ran while one was open for 2% -> 2% of each run, Pallas kernels for 0% -> 2%
where the time goes in v1:
time: 72.1 us; the launch traced here: 71.9 us
  blocking collectives  29.1 us (40%)
  starting transfers between devices  23.5 us (33%)
  Pallas kernels  10.9 us (15%)
  local copies, waits for them, and re-layouts  5.15 us (7%)
  waiting for transfers between devices  2.34 us (3%)
  between operations  0.83 us (1%)
    all_to_all x1, blocking collectives, per_device(): parts = lax.all_to_all(rotated, 'lat', 0, 0, tiled=True)  29.1 us
    ppermute x7, starting transfers between devices, shift(): return lax.ppermute(x, 'kpt', [(i, (i + 2 * step) % 16) for i in range(16)])  13.4 us
    ppermute x8, starting transfers between devices, swap(): return lax.ppermute(x, 'kpt', [(i, i ^ 1) for i in range(16)])  10.1 us
    pallas_call x1, Pallas kernels, per_device(): pl.pallas_call(rotate_body, out_shape=jax.ShapeDtypeStruct((LAT, ROWS, LA...  4.86 us
    pallas_call x1, Pallas kernels, per_device(): pl.pallas_call(couple_body, out_shape=jax.ShapeDtypeStruct((2, 2 * KPTS,...  4.54 us
    unnamed x26, local copies, waits for them, and re-layouts  3.82 us
    ppermute x7, waiting for transfers between devices, shift(): return lax.ppermute(x, 'kpt', [(i, (i + 2 * step) % 16) for i in range(16)])  2.32 us
  transfers between devices with their start and end apart: 15, of which 1 were waited for; matrix products, arithmetic and copies ran while one was open for 2% of the time, Pallas kernels for 2%

profile of v1, /device:TPU:1, one launch (start us, length us, event | category | flops | bytes accessed | tf_op | source)
XLA Modules:
  0.0 71.9 jit_solution(8832314046161636647)
XLA Ops:
  0.7 0.0 copy-start
  0.7 1.1 %copy-done = bf16[2,1,16,12288]{3,2,1,0:T(8,128)(2,1)S(1)} copy-done((bf16[2,1,16,12288]{3,2,1,0:T(8,128)(2,1)S(1)}, bf16[2,1,16,12288]{3,2,1,0:T(8,128)(2,1)}, u32[]{:S(2)}) %copy-start) | copy-done | bytes 786456
  1.8 0.0 copy-start.1
  1.8 0.8 %copy-done.1 = bf16[2,2,48,48]{3,2,1,0:T(8,128)(2,1)S(1)} copy-done((bf16[2,2,48,48]{3,2,1,0:T(8,128)(2,1)S(1)}, bf16[2,2,48,48]{3,2,1,0:T(8,128)(2,1)}, u32[]{:S(2)}) %copy-start.1) | copy-done | bytes 18456
  2.6 0.0 copy-start.2
  2.6 0.7 copy-done.2
  3.3 0.0 copy-start.3
  3.3 0.7 copy-done.3
  3.9 4.9 %rotate.1 = bf16[16,64,768]{2,1,0:T(8,128)(2,1)S(1)} custom-call(f32[2,3]{1,0:T(2,128)S(1)} %copy-done.2, s32[1,3]{1,0:T(1,128)S(1)} %copy-done.3, s32[1]{0:T(128)S(6)} %copy.24.rw_ref, bf16[2,2,48,48]{3,2,1,0:T(8,128)(2,1)S(1)} %copy-done.1, bf16[2,1,16,12288]{3,2,1,0:T(8,128)(2,1)S(1)} %copy-done), custom_call_target="tpu_custom_call" | custom-call | tf_op jit(solution)/shard_map/rotate/pallas_call | solution.py:202
  8.8 29.1 %all_to_all.5.x_ref = bf16[16,64,768]{2,1,0:T(8,128)(2,1)S(1)} all-to-all(bf16[16,64,768]{2,1,0:T(8,128)(2,1)S(1)} %rotate.1), channel_id=1, replica_groups=mesh['lat'=16,'kpt'=16] {'lat'}, dimensions={0} | all-to-all | bytes 3145728 | tf_op jit(solution)/shard_map/all_to_all | solution.py:215
  37.9 0.0 copy-start.4
  37.9 0.0 copy-start.7
  38.0 0.0 copy-start.6
  38.0 0.2 add_up.1.refs_0_
  38.2 4.4 %collective-permute-start.1 = (bf16[64,768]{1,0:T(8,128)(2,1)S(1)}, bf16[64,768]{1,0:T(8,128)(2,1)S(1)}, u32[]{:S(2)}, u32[]{:S(2)}) collective-permute-start(bf16[64,768]{1,0:T(8,128)(2,1)S(1)} %add_up.1.refs_0_), channel_id=1, source_target_pairs={{0,6},{1,7},{2,8},{3,9},{4,10},{5,11},{6,12},{7,13},{8,14},{9,15},... | collective-permute-start | bytes 294920 | tf_op jit(solution)/shard_map/ppermute | solution.py:253
  42.6 2.9 %collective-permute-start = (bf16[64,768]{1,0:T(8,128)(2,1)S(1)}, bf16[64,768]{1,0:T(8,128)(2,1)S(1)}, u32[]{:S(2)}, u32[]{:S(2)}) collective-permute-start(bf16[64,768]{1,0:T(8,128)(2,1)S(1)} %add_up.1.refs_0_), channel_id=1, source_target_pairs={{0,2},{1,3},{2,4},{3,5},{4,6},{5,7},{6,8},{7,9},{8,10},{9,11},{10,... | collective-permute-start | bytes 294920 | tf_op jit(solution)/shard_map/ppermute | solution.py:253
  45.5 0.1 collective-permute-start.4
  45.6 1.5 %collective-permute-start.6 = (bf16[64,768]{1,0:T(8,128)(2,1)S(1)}, bf16[64,768]{1,0:T(8,128)(2,1)S(1)}, u32[]{:S(2)}, u32[]{:S(2)}) collective-permute-start(bf16[64,768]{1,0:T(8,128)(2,1)S(1)} %add_up.1.refs_0_), channel_id=1, source_target_pairs={{0,14},{1,15},{2,0},{3,1},{4,2},{5,3},{6,4},{7,5},{8,6},{9,7},{10,... | collective-permute-start | bytes 294920 | tf_op jit(solution)/shard_map/ppermute | solution.py:253
  47.1 2.8 %collective-permute-start.7 = (bf16[64,768]{1,0:T(8,128)(2,1)S(1)}, bf16[64,768]{1,0:T(8,128)(2,1)S(1)}, u32[]{:S(2)}, u32[]{:S(2)}) collective-permute-start(bf16[64,768]{1,0:T(8,128)(2,1)S(1)} %add_up.1.refs_0_), channel_id=1, source_target_pairs={{0,1},{1,0},{2,3},{3,2},{4,5},{5,4},{6,7},{7,6},{8,9},{9,8},{10,11... | collective-permute-start | bytes 294920 | tf_op jit(solution)/shard_map/ppermute | solution.py:256
  49.9 0.1 pad.2.clone
  50.0 0.0 collective-permute-done.1.refs_3_
  50.0 3.0 %collective-permute-start.2 = (bf16[64,768]{1,0:T(8,128)(2,1)S(1)}, bf16[64,768]{1,0:T(8,128)(2,1)S(1)}, u32[]{:S(2)}, u32[]{:S(2)}) collective-permute-start(bf16[64,768]{1,0:T(8,128)(2,1)S(1)} %collective-permute-done.1.refs_3_), channel_id=1, source_target_pairs={{0,14},{1,15},{2,0},{3,1},{4,2},{5,3},{6,4},{7,5},{8,6},{9,7},{10,... | collective-permute-start | bytes 294920 | tf_op jit(solution)/shard_map/ppermute | solution.py:253
  53.0 0.0 collective-permute-done.refs_1_
  53.0 0.1 collective-permute-start.3
  53.0 0.0 collective-permute-done.4.refs_5_
  53.0 5.1 %collective-permute-start.10 = (bf16[64,768]{1,0:T(8,128)(2,1)S(1)}, bf16[64,768]{1,0:T(8,128)(2,1)S(1)}, u32[]{:S(2)}, u32[]{:S(2)}) collective-permute-start(bf16[64,768]{1,0:T(8,128)(2,1)S(1)} %collective-permute-done.1.refs_3_), channel_id=1, source_target_pairs={{0,1},{1,0},{2,3},{3,2},{4,5},{5,4},{6,7},{7,6},{8,9},{9,8},{10,11... | collective-permute-start | bytes 294920 | tf_op jit(solution)/shard_map/ppermute | solution.py:256
  58.1 0.0 collective-permute-done.6.refs_7_
  58.1 1.4 %collective-permute-start.5 = (bf16[64,768]{1,0:T(8,128)(2,1)S(1)}, bf16[64,768]{1,0:T(8,128)(2,1)S(1)}, u32[]{:S(2)}, u32[]{:S(2)}) collective-permute-start(bf16[64,768]{1,0:T(8,128)(2,1)S(1)} %collective-permute-done.4.refs_5_), channel_id=1, source_target_pairs={{0,2},{1,3},{2,4},{3,5},{4,6},{5,7},{6,8},{7,9},{8,10},{9,11},{10,... | collective-permute-start | bytes 294920 | tf_op jit(solution)/shard_map/ppermute | solution.py:253
  59.5 0.0 collective-permute-done.7.refs_8_
  59.5 0.3 collective-permute-start.8
  59.8 0.0 copy-done.8
  59.8 0.0 copy-done.10
  59.8 0.1 add_add_fusion.rv_ref
  59.9 0.0 copy-done.9
  59.9 0.1 copy.20.kp_ref
  60.0 0.0 copy-done.5
  60.0 0.1 copy.21.u_ref
  60.1 0.0 copy-done.4
  60.1 0.3 copy.18
  60.4 0.1 reshape.13
  60.6 0.1 copy.22.uq_ref
  60.7 0.0 copy-done.7
  60.7 0.1 copy.23.mk_ref
  60.8 0.0 copy-done.6
  60.8 0.1 copy.19
  60.9 0.0 collective-permute-done.2.refs_2_
  60.9 0.3 collective-permute-start.12
  61.2 0.0 collective-permute-done.3.refs_4_
  61.2 0.3 collective-permute-start.14
  61.5 2.3 %collective-permute-done.5.refs_6_ = bf16[64,768]{1,0:T(8,128)(2,1)S(1)} collective-permute-done((bf16[64,768]{1,0:T(8,128)(2,1)S(1)}, bf16[64,768]{1,0:T(8,128)(2,1)S(1)}, u32[]{:S(2)}, u32[]{:S(2)}) %collective-permute-start.5) | collective-permute-done | bytes 98336 | tf_op jit(solution)/shard_map/ppermute | solution.py:253
  63.8 0.8 %collective-permute-start.9 = (bf16[64,768]{1,0:T(8,128)(2,1)S(1)}, bf16[64,768]{1,0:T(8,128)(2,1)S(1)}, u32[]{:S(2)}, u32[]{:S(2)}) collective-permute-start(bf16[64,768]{1,0:T(8,128)(2,1)S(1)} %collective-permute-done.2.refs_2_), channel_id=1, source_target_pairs={{0,1},{1,0},{2,3},{3,2},{4,5},{5,4},{6,7},{7,6},{8,9},{9,8},{10,11... | collective-permute-start | bytes 294920 | tf_op jit(solution)/shard_map/ppermute | solution.py:256
  64.6 0.0 collective-permute-done.8.refs_9_
  64.6 0.0 collective-permute-start.11
  64.6 0.0 collective-permute-done.10.refs_11_
  64.6 0.5 collective-permute-start.13
  65.1 0.1 pad_add_fusion.at_ref
  65.1 1.3 %prep.1 = (bf16[128,512]{1,0:T(8,128)(2,1)S(1)}, f32[2,16,16,128]{3,2,1,0:T(8,128)S(1)}, f32[2,16,16,128]{3,2,1,0:T(8,128)S(1)}) custom-call(s32[2]{0:T(128)S(1)} %pad_add_fusion.at_ref, f32[64,3]{1,0:T(8,128)S(1)} %copy.20.kp_ref, s32[8,256]{1,0:T(8,128)S(1)} %add_add_fusion.rv_ref, bf16[2,64,256]{2,1,0:T(8,128)(2,1)S(1)} %copy.21.u_ref, ...), custom_call_target="tpu_custom_call" | custom-call | tf_op jit(solution)/shard_map/prep/pallas_call | solution.py:222
  66.4 0.0 collective-permute-done.12.refs_13_
  66.4 0.0 collective-permute-done.14.refs_15_
  66.4 0.0 collective-permute-done.9.refs_10_
  66.4 0.0 collective-permute-done.11.refs_12_
  66.5 0.0 collective-permute-done.13.refs_14_
  66.5 4.5 %couple.1 = bf16[2,128,768]{2,1,0:T(8,128)(2,1)S(1)} custom-call(bf16[64,768]{1,0:T(8,128)(2,1)S(1)} %add_up.1.refs_0_, bf16[64,768]{1,0:T(8,128)(2,1)S(1)} %collective-permute-done.refs_1_, bf16[64,768]{1,0:T(8,128)(2,1)S(1)} %collective-permute-done.2.refs_2_, bf16[64,768]{1,0:T(8,128)(2,1)S(1)} %collective-permute-done.1.refs_3_, ...), custom_call_target="tpu_custom_call" | custom-call | tf_op jit(solution)/shard_map/couple/pallas_call | solution.py:269
  71.0 0.9 %reshape.15 = bf16[2,64,2,768]{3,2,1,0:T(2,128)(2,1)} reshape(bf16[2,128,768]{2,1,0:T(8,128)(2,1)S(1)} %couple.1) | data formatting | bytes 786432 | tf_op jit(solution)/shard_map/reshape | solution.py:283
  (5 shorter events, 0.0 us)
Async XLA Ops:
  0.7 1.1 %copy-start = (bf16[2,1,16,12288]{3,2,1,0:T(8,128)(2,1)S(1)}, bf16[2,1,16,12288]{3,2,1,0:T(8,128)(2,1)}, u32[]{:S(2)}) copy-start(bf16[2,1,16,12288]{3,2,1,0:T(8,128)(2,1)} %coarse_ref.1) | copy-start | bytes 2359300
  1.8 0.8 %copy-start.1 = (bf16[2,2,48,48]{3,2,1,0:T(8,128)(2,1)S(1)}, bf16[2,2,48,48]{3,2,1,0:T(8,128)(2,1)}, u32[]{:S(2)}) copy-start(bf16[2,2,48,48]{3,2,1,0:T(8,128)(2,1)} %rot_ref.1) | copy-start | bytes 55300
  2.6 0.7 copy-start.2
  3.3 0.7 copy-start.3
  37.9 21.9 %copy-start.8 = (s32[256,3]{0,1:T(4,128)S(1)}, s32[256,3]{0,1:T(4,128)}, u32[]{:S(2)}) copy-start(s32[256,3]{0,1:T(4,128)} %param.15) | copy-start | bytes 9220
  37.9 21.9 %copy-start.10 = (s32[256]{0:T(256)S(1)}, s32[256]{0:T(256)}, u32[]{:S(2)}) copy-start(s32[256]{0:T(256)} %param.16) | copy-start | bytes 3076
  37.9 22.0 %copy-start.9 = (f32[64,3]{0,1:T(4,128)S(1)}, f32[64,3]{0,1:T(4,128)}, u32[]{:S(2)}) copy-start(f32[64,3]{0,1:T(4,128)} %param.18) | copy-start | bytes 2308
  37.9 22.1 %copy-start.5 = (bf16[2,64,16,16]{1,3,2,0:T(8,128)(2,1)S(1)}, bf16[2,64,16,16]{1,3,2,0:T(8,128)(2,1)}, u32[]{:S(2)}) copy-start(bf16[2,64,16,16]{1,3,2,0:T(8,128)(2,1)} %param.20) | copy-start | bytes 196612
  37.9 22.2 %copy-start.4 = (bf16[2,2,64,16,16]{2,4,3,1,0:T(8,128)(2,1)S(1)}, bf16[2,2,64,16,16]{2,4,3,1,0:T(8,128)(2,1)}, u32[]{:S(2)}) copy-start(bf16[2,2,64,16,16]{2,4,3,1,0:T(8,128)(2,1)} %param.21) | copy-start | bytes 393220
  37.9 22.7 %copy-start.7 = (s32[64,16]{0,1:T(8,128)S(1)}, s32[64,16]{0,1:T(8,128)}, u32[]{:S(2)}) copy-start(s32[64,16]{0,1:T(8,128)} %param.22) | copy-start | bytes 12292
  38.0 22.8 %copy-start.6 = (s32[2,64,16]{1,2,0:T(8,128)S(1)}, s32[2,64,16]{1,2,0:T(8,128)}, u32[]{:S(2)}) copy-start(s32[2,64,16]{1,2,0:T(8,128)} %param.23) | copy-start | bytes 24580
  38.2 11.8 %collective-permute-start.1 = (bf16[64,768]{1,0:T(8,128)(2,1)S(1)}, bf16[64,768]{1,0:T(8,128)(2,1)S(1)}, u32[]{:S(2)}, u32[]{:S(2)}) collective-permute-start(bf16[64,768]{1,0:T(8,128)(2,1)S(1)} %add_up.1.refs_0_), channel_id=1, source_target_pairs={{0,6},{1,7},{2,8},{3,9},{4,10},{5,11},{6,12},{7,13},{8,14},{9,15},... | collective-permute-start | bytes 294920 | tf_op jit(solution)/shard_map/ppermute | solution.py:253
  42.6 10.4 %collective-permute-start = (bf16[64,768]{1,0:T(8,128)(2,1)S(1)}, bf16[64,768]{1,0:T(8,128)(2,1)S(1)}, u32[]{:S(2)}, u32[]{:S(2)}) collective-permute-start(bf16[64,768]{1,0:T(8,128)(2,1)S(1)} %add_up.1.refs_0_), channel_id=1, source_target_pairs={{0,2},{1,3},{2,4},{3,5},{4,6},{5,7},{6,8},{7,9},{8,10},{9,11},{10,... | collective-permute-start | bytes 294920 | tf_op jit(solution)/shard_map/ppermute | solution.py:253
  45.5 7.6 %collective-permute-start.4 = (bf16[64,768]{1,0:T(8,128)(2,1)S(1)}, bf16[64,768]{1,0:T(8,128)(2,1)S(1)}, u32[]{:S(2)}, u32[]{:S(2)}) collective-permute-start(bf16[64,768]{1,0:T(8,128)(2,1)S(1)} %add_up.1.refs_0_), channel_id=1, source_target_pairs={{0,10},{1,11},{2,12},{3,13},{4,14},{5,15},{6,0},{7,1},{8,2},{9,3},... | collective-permute-start | bytes 294920 | tf_op jit(solution)/shard_map/ppermute | solution.py:253
  45.6 12.6 %collective-permute-start.6 = (bf16[64,768]{1,0:T(8,128)(2,1)S(1)}, bf16[64,768]{1,0:T(8,128)(2,1)S(1)}, u32[]{:S(2)}, u32[]{:S(2)}) collective-permute-start(bf16[64,768]{1,0:T(8,128)(2,1)S(1)} %add_up.1.refs_0_), channel_id=1, source_target_pairs={{0,14},{1,15},{2,0},{3,1},{4,2},{5,3},{6,4},{7,5},{8,6},{9,7},{10,... | collective-permute-start | bytes 294920 | tf_op jit(solution)/shard_map/ppermute | solution.py:253
  47.1 12.4 %collective-permute-start.7 = (bf16[64,768]{1,0:T(8,128)(2,1)S(1)}, bf16[64,768]{1,0:T(8,128)(2,1)S(1)}, u32[]{:S(2)}, u32[]{:S(2)}) collective-permute-start(bf16[64,768]{1,0:T(8,128)(2,1)S(1)} %add_up.1.refs_0_), channel_id=1, source_target_pairs={{0,1},{1,0},{2,3},{3,2},{4,5},{5,4},{6,7},{7,6},{8,9},{9,8},{10,11... | collective-permute-start | bytes 294920 | tf_op jit(solution)/shard_map/ppermute | solution.py:256
  50.0 10.9 %collective-permute-start.2 = (bf16[64,768]{1,0:T(8,128)(2,1)S(1)}, bf16[64,768]{1,0:T(8,128)(2,1)S(1)}, u32[]{:S(2)}, u32[]{:S(2)}) collective-permute-start(bf16[64,768]{1,0:T(8,128)(2,1)S(1)} %collective-permute-done.1.refs_3_), channel_id=1, source_target_pairs={{0,14},{1,15},{2,0},{3,1},{4,2},{5,3},{6,4},{7,5},{8,6},{9,7},{10,... | collective-permute-start | bytes 294920 | tf_op jit(solution)/shard_map/ppermute | solution.py:253
  53.0 8.2 %collective-permute-start.3 = (bf16[64,768]{1,0:T(8,128)(2,1)S(1)}, bf16[64,768]{1,0:T(8,128)(2,1)S(1)}, u32[]{:S(2)}, u32[]{:S(2)}) collective-permute-start(bf16[64,768]{1,0:T(8,128)(2,1)S(1)} %collective-permute-done.1.refs_3_), channel_id=1, source_target_pairs={{0,2},{1,3},{2,4},{3,5},{4,6},{5,7},{6,8},{7,9},{8,10},{9,11},{10,... | collective-permute-start | bytes 294920 | tf_op jit(solution)/shard_map/ppermute | solution.py:253
  53.0 11.5 %collective-permute-start.10 = (bf16[64,768]{1,0:T(8,128)(2,1)S(1)}, bf16[64,768]{1,0:T(8,128)(2,1)S(1)}, u32[]{:S(2)}, u32[]{:S(2)}) collective-permute-start(bf16[64,768]{1,0:T(8,128)(2,1)S(1)} %collective-permute-done.1.refs_3_), channel_id=1, source_target_pairs={{0,1},{1,0},{2,3},{3,2},{4,5},{5,4},{6,7},{7,6},{8,9},{9,8},{10,11... | collective-permute-start | bytes 294920 | tf_op jit(solution)/shard_map/ppermute | solution.py:256
  58.1 5.6 %collective-permute-start.5 = (bf16[64,768]{1,0:T(8,128)(2,1)S(1)}, bf16[64,768]{1,0:T(8,128)(2,1)S(1)}, u32[]{:S(2)}, u32[]{:S(2)}) collective-permute-start(bf16[64,768]{1,0:T(8,128)(2,1)S(1)} %collective-permute-done.4.refs_5_), channel_id=1, source_target_pairs={{0,2},{1,3},{2,4},{3,5},{4,6},{5,7},{6,8},{7,9},{8,10},{9,11},{10,... | collective-permute-start | bytes 294920 | tf_op jit(solution)/shard_map/ppermute | solution.py:253
  59.5 5.0 %collective-permute-start.8 = (bf16[64,768]{1,0:T(8,128)(2,1)S(1)}, bf16[64,768]{1,0:T(8,128)(2,1)S(1)}, u32[]{:S(2)}, u32[]{:S(2)}) collective-permute-start(bf16[64,768]{1,0:T(8,128)(2,1)S(1)} %collective-permute-done.refs_1_), channel_id=1, source_target_pairs={{0,1},{1,0},{2,3},{3,2},{4,5},{5,4},{6,7},{7,6},{8,9},{9,8},{10,11... | collective-permute-start | bytes 294920 | tf_op jit(solution)/shard_map/ppermute | solution.py:256
  60.9 5.5 %collective-permute-start.12 = (bf16[64,768]{1,0:T(8,128)(2,1)S(1)}, bf16[64,768]{1,0:T(8,128)(2,1)S(1)}, u32[]{:S(2)}, u32[]{:S(2)}) collective-permute-start(bf16[64,768]{1,0:T(8,128)(2,1)S(1)} %collective-permute-done.4.refs_5_), channel_id=1, source_target_pairs={{0,1},{1,0},{2,3},{3,2},{4,5},{5,4},{6,7},{7,6},{8,9},{9,8},{10,11... | collective-permute-start | bytes 294920 | tf_op jit(solution)/shard_map/ppermute | solution.py:256
  61.2 5.2 %collective-permute-start.14 = (bf16[64,768]{1,0:T(8,128)(2,1)S(1)}, bf16[64,768]{1,0:T(8,128)(2,1)S(1)}, u32[]{:S(2)}, u32[]{:S(2)}) collective-permute-start(bf16[64,768]{1,0:T(8,128)(2,1)S(1)} %collective-permute-done.6.refs_7_), channel_id=1, source_target_pairs={{0,1},{1,0},{2,3},{3,2},{4,5},{5,4},{6,7},{7,6},{8,9},{9,8},{10,11... | collective-permute-start | bytes 294920 | tf_op jit(solution)/shard_map/ppermute | solution.py:256
  63.8 2.7 %collective-permute-start.9 = (bf16[64,768]{1,0:T(8,128)(2,1)S(1)}, bf16[64,768]{1,0:T(8,128)(2,1)S(1)}, u32[]{:S(2)}, u32[]{:S(2)}) collective-permute-start(bf16[64,768]{1,0:T(8,128)(2,1)S(1)} %collective-permute-done.2.refs_2_), channel_id=1, source_target_pairs={{0,1},{1,0},{2,3},{3,2},{4,5},{5,4},{6,7},{7,6},{8,9},{9,8},{10,11... | collective-permute-start | bytes 294920 | tf_op jit(solution)/shard_map/ppermute | solution.py:256
  64.6 1.9 %collective-permute-start.11 = (bf16[64,768]{1,0:T(8,128)(2,1)S(1)}, bf16[64,768]{1,0:T(8,128)(2,1)S(1)}, u32[]{:S(2)}, u32[]{:S(2)}) collective-permute-start(bf16[64,768]{1,0:T(8,128)(2,1)S(1)} %collective-permute-done.3.refs_4_), channel_id=1, source_target_pairs={{0,1},{1,0},{2,3},{3,2},{4,5},{5,4},{6,7},{7,6},{8,9},{9,8},{10,11... | collective-permute-start | bytes 294920 | tf_op jit(solution)/shard_map/ppermute | solution.py:256
  64.6 1.9 %collective-permute-start.13 = (bf16[64,768]{1,0:T(8,128)(2,1)S(1)}, bf16[64,768]{1,0:T(8,128)(2,1)S(1)}, u32[]{:S(2)}, u32[]{:S(2)}) collective-permute-start(bf16[64,768]{1,0:T(8,128)(2,1)S(1)} %collective-permute-done.5.refs_6_), channel_id=1, source_target_pairs={{0,1},{1,0},{2,3},{3,2},{4,5},{5,4},{6,7},{7,6},{8,9},{9,8},{10,11... | collective-permute-start | bytes 294920 | tf_op jit(solution)/shard_map/ppermute | solution.py:256

commit v2 on v1

--- a/solution.py
+++ b/solution.py
@@ -19,10 +19,36 @@
 LANES = PER * BANDS * BANDS
 STRIDE_S = 2 * MODES
 ROWS = NQ * 2 * CELLS
-
-
-def rotate_body(qp_ref, rv_ref, rw_ref, rot_ref, coarse_ref, out_ref, mat_ref, s_ref, o_ref):
-    weight = 1.0 / jnp.full((8, 128), rw_ref[0], jnp.int32).astype(f32)
+CHUNKS = 4
+CHUNK = MODES * BANDS * BANDS // CHUNKS
+
+
+def rotate_body(
+    qp_hbm, rv_hbm, rw_hbm, rot_hbm, coarse_hbm, out_ref,
+    qp_ref, rv_ref, rw_ref, rot_ref, coarse_ref, mat_ref, s_ref, o_ref, sems,
+):
+    small = [
+        pltpu.make_async_copy(src, dst, sems.at[i])
+        for i, (src, dst) in enumerate(
+            [(qp_hbm, qp_ref), (rv_hbm, rv_ref), (rw_hbm, rw_ref), (rot_hbm, rot_ref)]
+        )
+    ]
+    large = []
+    for part in range(2):
+        for i in range(CHUNKS):
+            lanes = pl.ds(i * CHUNK, CHUNK)
+            large.append(
+                pltpu.make_async_copy(
+                    coarse_hbm.at[part, 0, :, lanes],
+                    coarse_ref.at[part, :, lanes],
+                    sems.at[4 + part * CHUNKS + i],
+                )
+            )
+    for copy in small + large:
+        copy.start()
+    for copy in small:
+        copy.wait()
+    weight = 1.0 / jnp.full((8, 128), rw_ref[0, 0], jnp.int32).astype(f32)
     for q in range(NQ):
         arg = two_pi * (
             qp_ref[q, 0] * rv_ref[0, 0].astype(f32)
@@ -47,9 +73,11 @@
     mat = jnp.concatenate(rows, axis=0)[:, 0:96].astype(bf16)
     for part in range(2):
         for m in range(MODES):
+            if m * 256 % CHUNK == 0:
+                large[part * CHUNKS + m * 256 // CHUNK].wait()
             for h in range(2):
                 at = (2 * m + h) * 128
-                tile = coarse_ref[part, 0, :, at:at + 128].astype(f32)
+                tile = coarse_ref[part, :, at:at + 128].astype(f32)
                 s_ref[h, pl.ds(part * MODES + m, CELLS, stride=STRIDE_S), :] = tile
     for e in range(CELLS):
         for h in range(2):
@@ -109,12 +137,29 @@
             lo_ref[part, b] = lt[b * 16:(b + 1) * 16] * mq
 
 
+def pack_body(own_ref, up_ref, down_ref, order_ref, three_ref, two_ref):
+    for i, ref in enumerate((own_ref, up_ref, down_ref)):
+        value = ref[...]
+        three_ref[i * ROWS:(i + 1) * ROWS, :] = value
+        if i < 2:
+            two_ref[i * ROWS:(i + 1) * ROWS, :] = value
+
+
+PLACE = ((0, 0), (1, 0), (2, 1), (0, 1), (1, 1), (0, 2), (1, 2), (2, 0))
+
+
 def couple_body(*refs):
-    xs = refs[:16]
-    ph_ref, u_ref, l_ref, out_ref, y_ref, bl_ref, h_ref, r_ref = refs[16:]
+    ph_ref, u_ref, l_ref, out_ref, y_ref, bl_ref, h_ref, r_ref = refs[6:]
     ph = ph_ref[...]
     for q in range(NQ):
-        x = jnp.concatenate([r[q * 32:(q + 1) * 32, :] for r in xs], axis=0)
+        x = jnp.concatenate(
+            [
+                refs[side * 3 + i][j * ROWS + q * 32:j * ROWS + (q + 1) * 32, :]
+                for side in range(2)
+                for i, j in PLACE
+            ],
+            axis=0,
+        )
         t = jnp.dot(ph, x, preferred_element_type=f32)
         for part in range(2):
             for v in range(2 * PER):
@@ -177,6 +222,10 @@
     return pl.BlockSpec(memory_space=pltpu.VMEM)
 
 
+def hbm():
+    return pl.BlockSpec(memory_space=pltpu.HBM)
+
+
 def smem():
     return pl.BlockSpec(memory_space=pltpu.SMEM)
 
@@ -202,16 +251,22 @@
     rotated = pl.pallas_call(
         rotate_body,
         out_shape=jax.ShapeDtypeStruct((LAT, ROWS, LANES), bf16),
-        in_specs=[smem(), smem(), smem(), vmem(), vmem()],
+        in_specs=[hbm()] * 5,
         out_specs=vmem(),
         scratch_shapes=[
+            pltpu.SMEM((NQ, 3), f32),
+            pltpu.SMEM((1, 3), jnp.int32),
+            pltpu.SMEM((1, 1), jnp.int32),
+            pltpu.VMEM((2, NQ, MODES, MODES), bf16),
+            pltpu.VMEM((2, CELLS, MODES * BANDS * BANDS), bf16),
             pltpu.VMEM((192, 128), f32),
             pltpu.VMEM((2, CELLS * STRIDE_S, 128), f32),
             pltpu.VMEM((2 * PER, LAT * ROWS, 128), f32),
+            pltpu.SemaphoreType.DMA((4 + 2 * CHUNKS,)),
         ],
-        compiler_params=params(),
+        compiler_params=pltpu.CompilerParams(vmem_limit_bytes=63 << 20),
         name="rotate",
-    )(q_points, rp_vectors, rp_weights, modes_rot, coarse)
+    )(q_points, rp_vectors, rp_weights[None, :], modes_rot, coarse)
     parts = lax.all_to_all(rotated, "lat", 0, 0, tiled=True)
 
     index = lax.axis_index("kpt")
@@ -257,19 +312,26 @@
 
     up = shift(own, 3)
     down = shift(own, -3)
-    blocks = {0: own, 3: up, 5: down}
-    blocks[1] = shift(own, 1)
-    blocks[7] = shift(own, -1)
-    blocks[4] = shift(up, 1)
-    blocks[2] = shift(up, -1)
-    blocks[6] = shift(down, 1)
-    near = [blocks[i] for i in range(8)]
+    packed, pair = pl.pallas_call(
+        pack_body,
+        out_shape=(
+            jax.ShapeDtypeStruct((3 * ROWS, LANES), bf16),
+            jax.ShapeDtypeStruct((2 * ROWS, LANES), bf16),
+        ),
+        in_specs=[vmem()] * 3 + [pl.BlockSpec(memory_space=pl.ANY)],
+        out_specs=(vmem(), vmem()),
+        compiler_params=params(),
+        name="pack",
+    )(own, up, down, phase)
+    plus = shift(packed, 1)
+    minus = shift(pair, -1)
+    near = [packed, plus, minus]
     far = [swap(x) for x in near]
 
     result = pl.pallas_call(
         couple_body,
         out_shape=jax.ShapeDtypeStruct((2, 2 * KPTS, LANES), bf16),
-        in_specs=[vmem()] * 19,
+        in_specs=[vmem()] * 9,
         out_specs=vmem(),
         scratch_shapes=[
             pltpu.VMEM((2, 2 * PER, 128, 128), f32),

time: 72.1 us -> 70.6 us (0.979)
  blocking collectives: 29.1 us -> 0 us
  waiting for transfers between devices: 2.34 us -> 25.3 us
  starting transfers between devices: 23.5 us -> 29.3 us
  local copies, waits for them, and re-layouts: 5.15 us -> 1.91 us
  Pallas kernels: 10.9 us -> 13 us
    all_to_all x1 -> x0, blocking collectives: 29.1 us -> none  [per_device(): parts = lax.all_to_all(rotated, 'lat', 0, 0, tiled=True)]
    all_to_all x0 -> x1, waiting for transfers between devices: none -> 21.7 us  [per_device(): parts = lax.all_to_all(rotated, 'lat', 0, 0, tiled=True)]
    all_to_all x0 -> x1, starting transfers between devices: none -> 7.72 us  [per_device(): parts = lax.all_to_all(rotated, 'lat', 0, 0, tiled=True)]
    unnamed x26 -> x18, local copies, waits for them, and re-layouts: 3.82 us -> 0.58 us
    pallas_call x1, Pallas kernels: 4.86 us -> 6.95 us  [per_device(): pl.pallas_call(rotate_body, out_shape=jax.ShapeDtypeStruct((LAT, ROWS, LA...]
    ppermute x7 -> x4, starting transfers between devices: 13.4 us -> 11.8 us  [shift(): return lax.ppermute(x, 'kpt', [(i, (i + 2 * step) % 16) for i in range(16)])]
    ppermute x8 -> x3, waiting for transfers between devices: 0.02 us -> 1.07 us  [swap(): return lax.ppermute(x, 'kpt', [(i, i ^ 1) for i in range(16)])]
    ppermute x8 -> x3, starting transfers between devices: 10.1 us -> 9.75 us  [swap(): return lax.ppermute(x, 'kpt', [(i, i ^ 1) for i in range(16)])]
  transfers between devices with their start and end apart: 15 -> 8, of which waited for: 1 -> 4; matrix products, arithmetic and copies ran while one was open for 2% -> 2% of each run, Pallas kernels for 2% -> 2%
where the time goes in v2:
time: 70.6 us; the launch traced here: 70.4 us
  starting transfers between devices  29.3 us (42%)
  waiting for transfers between devices  25.3 us (36%)
  Pallas kernels  13 us (18%)
  local copies, waits for them, and re-layouts  1.91 us (3%)
  between operations  0.83 us (1%)
    all_to_all x1, waiting for transfers between devices, per_device(): parts = lax.all_to_all(rotated, 'lat', 0, 0, tiled=True)  21.7 us
    ppermute x4, starting transfers between devices, shift(): return lax.ppermute(x, 'kpt', [(i, (i + 2 * step) % 16) for i in range(16)])  11.8 us
    ppermute x3, starting transfers between devices, swap(): return lax.ppermute(x, 'kpt', [(i, i ^ 1) for i in range(16)])  9.75 us
    all_to_all x1, starting transfers between devices, per_device(): parts = lax.all_to_all(rotated, 'lat', 0, 0, tiled=True)  7.72 us
    pallas_call x1, Pallas kernels, per_device(): pl.pallas_call(rotate_body, out_shape=jax.ShapeDtypeStruct((LAT, ROWS, LA...  6.95 us
    pallas_call x1, Pallas kernels, per_device(): pl.pallas_call(couple_body, out_shape=jax.ShapeDtypeStruct((2, 2 * KPTS,...  4.51 us
    ppermute x4, waiting for transfers between devices, shift(): return lax.ppermute(x, 'kpt', [(i, (i + 2 * step) % 16) for i in range(16)])  2.49 us
  transfers between devices with their start and end apart: 8, of which 4 were waited for; matrix products, arithmetic and copies ran while one was open for 2% of the time, Pallas kernels for 2%

profile of v2, /device:TPU:1, one launch (start us, length us, event | category | flops | bytes accessed | tf_op | source)
XLA Modules:
  0.0 70.4 jit_solution(13861924763021526853)
XLA Ops:
  0.7 6.9 %rotate.1 = bf16[16,64,768]{2,1,0:T(8,128)(2,1)} custom-call(f32[2,3]{1,0:T(2,128)} %qp_hbm.1, s32[1,3]{1,0:T(1,128)} %rv_hbm.1, s32[1,1]{1,0:T(1,128)} %bitcast.9.rw_hbm, bf16[2,2,48,48]{3,2,1,0:T(8,128)(2,1)} %rot_hbm.1, bf16[2,1,16,12288]{3,2,1,0:T(8,128)(2,1)} %coarse_hbm.1), custom_call_target="tpu_custom_call" | custom-call | tf_op jit(solution)/shard_map/rotate/pallas_call | solution.py:251
  7.6 0.0 copy-start.5
  7.6 0.0 copy-start.1
  7.6 0.0 copy-start
  7.6 0.0 copy-start.3
  7.7 0.0 copy-start.2
  7.7 7.7 %all-to-all-start = ((bf16[16,64,768]{2,1,0:T(8,128)(2,1)}), bf16[16,64,768]{2,1,0:T(8,128)(2,1)S(1)}, u32[]{:S(2)}, u32[]{:S(2)}) async-start(bf16[16,64,768]{2,1,0:T(8,128)(2,1)} %rotate.1), calls=%async_computation | async-start | bytes 3145728 | tf_op jit(solution)/shard_map/all_to_all | solution.py:270
  15.4 0.0 copy-start.4
  15.4 0.0 copy-start.6
  15.4 0.0 copy-done.5
  15.4 0.1 copy.20.kp_ref
  15.5 0.1 pad.2.clone
  15.6 0.0 copy-done.1
  15.6 0.1 copy.21.u_ref
  15.7 0.0 copy-done
  15.7 0.3 copy.18
  16.0 0.1 reshape.13
  16.2 0.1 copy.22.uq_ref
  16.3 0.0 copy-done.3
  16.3 0.1 copy.23.mk_ref
  16.4 0.0 copy-done.2
  16.4 0.1 copy.19
  16.5 0.0 copy-done.4
  16.5 0.0 copy-done.6
  16.5 0.1 add_add_fusion.rv_ref
  16.6 21.7 %all-to-all-done.x_ref = bf16[16,64,768]{2,1,0:T(8,128)(2,1)S(1)} async-done(((bf16[16,64,768]{2,1,0:T(8,128)(2,1)}), bf16[16,64,768]{2,1,0:T(8,128)(2,1)S(1)}, u32[]{:S(2)}, u32[]{:S(2)}) %all-to-all-start) | async-done | bytes 1572896 | tf_op jit(solution)/shard_map/all_to_all | solution.py:270
  38.3 0.2 add_up.1.own_ref
  38.5 4.4 %collective-permute-start = (bf16[64,768]{1,0:T(8,128)(2,1)S(1)}, bf16[64,768]{1,0:T(8,128)(2,1)S(1)}, u32[]{:S(2)}, u32[]{:S(2)}) collective-permute-start(bf16[64,768]{1,0:T(8,128)(2,1)S(1)} %add_up.1.own_ref), channel_id=1, source_target_pairs={{0,6},{1,7},{2,8},{3,9},{4,10},{5,11},{6,12},{7,13},{8,14},{9,15},... | collective-permute-start | bytes 294920 | tf_op jit(solution)/shard_map/ppermute | solution.py:308
  42.9 2.2 %collective-permute-start.1 = (bf16[64,768]{1,0:T(8,128)(2,1)S(1)}, bf16[64,768]{1,0:T(8,128)(2,1)S(1)}, u32[]{:S(2)}, u32[]{:S(2)}) collective-permute-start(bf16[64,768]{1,0:T(8,128)(2,1)S(1)} %add_up.1.own_ref), channel_id=1, source_target_pairs={{0,10},{1,11},{2,12},{3,13},{4,14},{5,15},{6,0},{7,1},{8,2},{9,3},... | collective-permute-start | bytes 294920 | tf_op jit(solution)/shard_map/ppermute | solution.py:308
  45.1 0.1 pad_add_fusion.at_ref
  45.2 1.3 %prep.1 = (bf16[128,512]{1,0:T(8,128)(2,1)S(1)}, f32[2,16,16,128]{3,2,1,0:T(8,128)S(1)}, f32[2,16,16,128]{3,2,1,0:T(8,128)S(1)}) custom-call(s32[2]{0:T(128)S(1)} %pad_add_fusion.at_ref, f32[64,3]{1,0:T(8,128)S(1)} %copy.20.kp_ref, s32[8,256]{1,0:T(8,128)S(1)} %add_add_fusion.rv_ref, bf16[2,64,256]{2,1,0:T(8,128)(2,1)S(1)} %copy.21.u_ref, ...), custom_call_target="tpu_custom_call" | custom-call | tf_op jit(solution)/shard_map/prep/pallas_call | solution.py:277
  46.4 0.8 %collective-permute-done.up_ref = bf16[64,768]{1,0:T(8,128)(2,1)S(1)} collective-permute-done((bf16[64,768]{1,0:T(8,128)(2,1)S(1)}, bf16[64,768]{1,0:T(8,128)(2,1)S(1)}, u32[]{:S(2)}, u32[]{:S(2)}) %collective-permute-start) | collective-permute-done | bytes 98336 | tf_op jit(solution)/shard_map/ppermute | solution.py:308
  47.2 1.7 %collective-permute-done.1.down_ref = bf16[64,768]{1,0:T(8,128)(2,1)S(1)} collective-permute-done((bf16[64,768]{1,0:T(8,128)(2,1)S(1)}, bf16[64,768]{1,0:T(8,128)(2,1)S(1)}, u32[]{:S(2)}, u32[]{:S(2)}) %collective-permute-start.1) | collective-permute-done | bytes 98336 | tf_op jit(solution)/shard_map/ppermute | solution.py:308
  49.0 5.2 %collective-permute-start.2 = (bf16[192,768]{1,0:T(8,128)(2,1)S(1)}, bf16[192,768]{1,0:T(8,128)(2,1)S(1)}, u32[]{:S(2)}, u32[]{:S(2)}) collective-permute-start(bf16[192,768]{1,0:T(8,128)(2,1)S(1)} %get-tuple-element.11.refs_0_), channel_id=1, source_target_pairs={{0,2},{1,3},{2,4},{3,5},{4,6},{5,7},{6,8},{7,9},{8,10},{9,11},{10,... | collective-permute-start | bytes 884744 | tf_op jit(solution)/shard_map/ppermute | solution.py:308
  54.1 0.0 collective-permute-start.3
  54.1 4.1 %collective-permute-start.4 = (bf16[192,768]{1,0:T(8,128)(2,1)S(1)}, bf16[192,768]{1,0:T(8,128)(2,1)S(1)}, u32[]{:S(2)}, u32[]{:S(2)}) collective-permute-start(bf16[192,768]{1,0:T(8,128)(2,1)S(1)} %get-tuple-element.11.refs_0_), channel_id=1, source_target_pairs={{0,1},{1,0},{2,3},{3,2},{4,5},{5,4},{6,7},{7,6},{8,9},{9,8},{10,11... | collective-permute-start | bytes 884744 | tf_op jit(solution)/shard_map/ppermute | solution.py:311
  58.2 0.0 collective-permute-done.2.refs_1_
  58.2 4.2 %collective-permute-start.5 = (bf16[192,768]{1,0:T(8,128)(2,1)S(1)}, bf16[192,768]{1,0:T(8,128)(2,1)S(1)}, u32[]{:S(2)}, u32[]{:S(2)}) collective-permute-start(bf16[192,768]{1,0:T(8,128)(2,1)S(1)} %collective-permute-done.2.refs_1_), channel_id=1, source_target_pairs={{0,1},{1,0},{2,3},{3,2},{4,5},{5,4},{6,7},{7,6},{8,9},{9,8},{10,11... | collective-permute-start | bytes 884744 | tf_op jit(solution)/shard_map/ppermute | solution.py:311
  62.5 0.0 collective-permute-done.3.refs_2_
  62.5 1.4 %collective-permute-start.6 = (bf16[128,768]{1,0:T(8,128)(2,1)S(1)}, bf16[128,768]{1,0:T(8,128)(2,1)S(1)}, u32[]{:S(2)}, u32[]{:S(2)}) collective-permute-start(bf16[128,768]{1,0:T(8,128)(2,1)S(1)} %collective-permute-done.3.refs_2_), channel_id=1, source_target_pairs={{0,1},{1,0},{2,3},{3,2},{4,5},{5,4},{6,7},{7,6},{8,9},{9,8},{10,11... | collective-permute-start | bytes 589832 | tf_op jit(solution)/shard_map/ppermute | solution.py:311
  63.9 0.0 collective-permute-done.4.refs_3_
  63.9 1.1 %collective-permute-done.6.refs_5_ = bf16[128,768]{1,0:T(8,128)(2,1)S(1)} collective-permute-done((bf16[128,768]{1,0:T(8,128)(2,1)S(1)}, bf16[128,768]{1,0:T(8,128)(2,1)S(1)}, u32[]{:S(2)}, u32[]{:S(2)}) %collective-permute-start.6) | collective-permute-done | bytes 196640 | tf_op jit(solution)/shard_map/ppermute | solution.py:311
  65.0 0.0 collective-permute-done.5.refs_4_
  65.0 4.5 %couple.1 = bf16[2,128,768]{2,1,0:T(8,128)(2,1)S(1)} custom-call(bf16[192,768]{1,0:T(8,128)(2,1)S(1)} %get-tuple-element.11.refs_0_, bf16[192,768]{1,0:T(8,128)(2,1)S(1)} %collective-permute-done.2.refs_1_, bf16[128,768]{1,0:T(8,128)(2,1)S(1)} %collective-permute-done.3.refs_2_, bf16[192,768]{1,0:T(8,128)(2,1)S(1)} %collective-permute-done.4.refs_3_, ...), custom_call_target="tpu_custom_call" | custom-call | tf_op jit(solution)/shard_map/couple/pallas_call | solution.py:331
  69.5 0.9 %reshape.15 = bf16[2,64,2,768]{3,2,1,0:T(2,128)(2,1)} reshape(bf16[2,128,768]{2,1,0:T(8,128)(2,1)S(1)} %couple.1) | data formatting | bytes 786432 | tf_op jit(solution)/shard_map/reshape | solution.py:345
  (2 shorter events, 0.0 us)
Async XLA Ops:
  7.6 7.8 %copy-start.5 = (f32[64,3]{0,1:T(4,128)S(1)}, f32[64,3]{0,1:T(4,128)}, u32[]{:S(2)}) copy-start(f32[64,3]{0,1:T(4,128)} %param.18) | copy-start | bytes 2308
  7.6 8.0 %copy-start.1 = (bf16[2,64,16,16]{1,3,2,0:T(8,128)(2,1)S(1)}, bf16[2,64,16,16]{1,3,2,0:T(8,128)(2,1)}, u32[]{:S(2)}) copy-start(bf16[2,64,16,16]{1,3,2,0:T(8,128)(2,1)} %param.20) | copy-start | bytes 196612
  7.6 8.1 %copy-start = (bf16[2,2,64,16,16]{2,4,3,1,0:T(8,128)(2,1)S(1)}, bf16[2,2,64,16,16]{2,4,3,1,0:T(8,128)(2,1)}, u32[]{:S(2)}) copy-start(bf16[2,2,64,16,16]{2,4,3,1,0:T(8,128)(2,1)} %param.21) | copy-start | bytes 393220
  7.6 8.7 %copy-start.3 = (s32[64,16]{0,1:T(8,128)S(1)}, s32[64,16]{0,1:T(8,128)}, u32[]{:S(2)}) copy-start(s32[64,16]{0,1:T(8,128)} %param.22) | copy-start | bytes 12292
  7.7 8.7 %copy-start.2 = (s32[2,64,16]{1,2,0:T(8,128)S(1)}, s32[2,64,16]{1,2,0:T(8,128)}, u32[]{:S(2)}) copy-start(s32[2,64,16]{1,2,0:T(8,128)} %param.23) | copy-start | bytes 24580
  7.7 30.6 %all-to-all-start = ((bf16[16,64,768]{2,1,0:T(8,128)(2,1)}), bf16[16,64,768]{2,1,0:T(8,128)(2,1)S(1)}, u32[]{:S(2)}, u32[]{:S(2)}) async-start(bf16[16,64,768]{2,1,0:T(8,128)(2,1)} %rotate.1), calls=%async_computation | async-start | bytes 3145728 | tf_op jit(solution)/shard_map/all_to_all | solution.py:270
  15.4 1.1 %copy-start.4 = (s32[256,3]{0,1:T(4,128)S(1)}, s32[256,3]{0,1:T(4,128)}, u32[]{:S(2)}) copy-start(s32[256,3]{0,1:T(4,128)} %param.15) | copy-start | bytes 9220
  15.4 1.1 %copy-start.6 = (s32[256]{0:T(256)S(1)}, s32[256]{0:T(256)}, u32[]{:S(2)}) copy-start(s32[256]{0:T(256)} %param.16) | copy-start | bytes 3076
  38.5 8.8 %collective-permute-start = (bf16[64,768]{1,0:T(8,128)(2,1)S(1)}, bf16[64,768]{1,0:T(8,128)(2,1)S(1)}, u32[]{:S(2)}, u32[]{:S(2)}) collective-permute-start(bf16[64,768]{1,0:T(8,128)(2,1)S(1)} %add_up.1.own_ref), channel_id=1, source_target_pairs={{0,6},{1,7},{2,8},{3,9},{4,10},{5,11},{6,12},{7,13},{8,14},{9,15},... | collective-permute-start | bytes 294920 | tf_op jit(solution)/shard_map/ppermute | solution.py:308
  42.9 6.0 %collective-permute-start.1 = (bf16[64,768]{1,0:T(8,128)(2,1)S(1)}, bf16[64,768]{1,0:T(8,128)(2,1)S(1)}, u32[]{:S(2)}, u32[]{:S(2)}) collective-permute-start(bf16[64,768]{1,0:T(8,128)(2,1)S(1)} %add_up.1.own_ref), channel_id=1, source_target_pairs={{0,10},{1,11},{2,12},{3,13},{4,14},{5,15},{6,0},{7,1},{8,2},{9,3},... | collective-permute-start | bytes 294920 | tf_op jit(solution)/shard_map/ppermute | solution.py:308
  49.0 9.3 %collective-permute-start.2 = (bf16[192,768]{1,0:T(8,128)(2,1)S(1)}, bf16[192,768]{1,0:T(8,128)(2,1)S(1)}, u32[]{:S(2)}, u32[]{:S(2)}) collective-permute-start(bf16[192,768]{1,0:T(8,128)(2,1)S(1)} %get-tuple-element.11.refs_0_), channel_id=1, source_target_pairs={{0,2},{1,3},{2,4},{3,5},{4,6},{5,7},{6,8},{7,9},{8,10},{9,11},{10,... | collective-permute-start | bytes 884744 | tf_op jit(solution)/shard_map/ppermute | solution.py:308
  54.1 8.3 %collective-permute-start.3 = (bf16[128,768]{1,0:T(8,128)(2,1)S(1)}, bf16[128,768]{1,0:T(8,128)(2,1)S(1)}, u32[]{:S(2)}, u32[]{:S(2)}) collective-permute-start(bf16[128,768]{1,0:T(8,128)(2,1)S(1)} %get-tuple-element.12), channel_id=1, source_target_pairs={{0,14},{1,15},{2,0},{3,1},{4,2},{5,3},{6,4},{7,5},{8,6},{9,7},{10,... | collective-permute-start | bytes 589832 | tf_op jit(solution)/shard_map/ppermute | solution.py:308
  54.1 9.8 %collective-permute-start.4 = (bf16[192,768]{1,0:T(8,128)(2,1)S(1)}, bf16[192,768]{1,0:T(8,128)(2,1)S(1)}, u32[]{:S(2)}, u32[]{:S(2)}) collective-permute-start(bf16[192,768]{1,0:T(8,128)(2,1)S(1)} %get-tuple-element.11.refs_0_), channel_id=1, source_target_pairs={{0,1},{1,0},{2,3},{3,2},{4,5},{5,4},{6,7},{7,6},{8,9},{9,8},{10,11... | collective-permute-start | bytes 884744 | tf_op jit(solution)/shard_map/ppermute | solution.py:311
  58.2 6.7 %collective-permute-start.5 = (bf16[192,768]{1,0:T(8,128)(2,1)S(1)}, bf16[192,768]{1,0:T(8,128)(2,1)S(1)}, u32[]{:S(2)}, u32[]{:S(2)}) collective-permute-start(bf16[192,768]{1,0:T(8,128)(2,1)S(1)} %collective-permute-done.2.refs_1_), channel_id=1, source_target_pairs={{0,1},{1,0},{2,3},{3,2},{4,5},{5,4},{6,7},{7,6},{8,9},{9,8},{10,11... | collective-permute-start | bytes 884744 | tf_op jit(solution)/shard_map/ppermute | solution.py:311
  62.5 2.5 %collective-permute-start.6 = (bf16[128,768]{1,0:T(8,128)(2,1)S(1)}, bf16[128,768]{1,0:T(8,128)(2,1)S(1)}, u32[]{:S(2)}, u32[]{:S(2)}) collective-permute-start(bf16[128,768]{1,0:T(8,128)(2,1)S(1)} %collective-permute-done.3.refs_2_), channel_id=1, source_target_pairs={{0,1},{1,0},{2,3},{3,2},{4,5},{5,4},{6,7},{7,6},{8,9},{9,8},{10,11... | collective-permute-start | bytes 589832 | tf_op jit(solution)/shard_map/ppermute | solution.py:311

commit v3 on v2

--- a/solution.py
+++ b/solution.py
@@ -1,3 +1,5 @@
+import functools
+
 import jax
 import jax.numpy as jnp
 from jax import lax
@@ -18,14 +20,14 @@
 PER = MODES // LAT
 LANES = PER * BANDS * BANDS
 STRIDE_S = 2 * MODES
-ROWS = NQ * 2 * CELLS
+ROWS = 2 * CELLS
 CHUNKS = 4
 CHUNK = MODES * BANDS * BANDS // CHUNKS
 
 
 def rotate_body(
-    qp_hbm, rv_hbm, rw_hbm, rot_hbm, coarse_hbm, out_ref,
-    qp_ref, rv_ref, rw_ref, rot_ref, coarse_ref, mat_ref, s_ref, o_ref, sems,
+    qp_hbm, rv_hbm, rw_hbm, rot_hbm, coarse_hbm, order_ref, out_ref,
+    qp_ref, rv_ref, rw_ref, rot_ref, coarse_ref, mat_ref, s_ref, o_ref, sems, *, q,
 ):
     small = [
         pltpu.make_async_copy(src, dst, sems.at[i])
@@ -49,25 +51,22 @@
     for copy in small:
         copy.wait()
     weight = 1.0 / jnp.full((8, 128), rw_ref[0, 0], jnp.int32).astype(f32)
-    for q in range(NQ):
-        arg = two_pi * (
-            qp_ref[q, 0] * rv_ref[0, 0].astype(f32)
-            + qp_ref[q, 1] * rv_ref[0, 1].astype(f32)
-            + qp_ref[q, 2] * rv_ref[0, 2].astype(f32)
-        )
-        angle = jnp.full((8, 128), arg, f32)
-        pr = (jnp.cos(angle) * weight).astype(bf16).astype(f32)[0:1, 0:1]
-        pi = (jnp.sin(angle) * weight).astype(bf16).astype(f32)[0:1, 0:1]
-        rr = rot_ref[0, q].astype(f32)
-        ri = rot_ref[1, q].astype(f32)
-        cr = rr * pr - ri * pi
-        ci = rr * pi + ri * pr
-        top = jnp.concatenate([cr, -ci], axis=0)
-        low = jnp.concatenate([ci, cr], axis=0)
-        mat_ref[q * 96:q * 96 + 48, 0:96] = top.T
-        mat_ref[q * 96 + 48:q * 96 + 96, 0:96] = low.T
+    arg = two_pi * (
+        qp_ref[q, 0] * rv_ref[0, 0].astype(f32)
+        + qp_ref[q, 1] * rv_ref[0, 1].astype(f32)
+        + qp_ref[q, 2] * rv_ref[0, 2].astype(f32)
+    )
+    angle = jnp.full((8, 128), arg, f32)
+    pr = (jnp.cos(angle) * weight).astype(bf16).astype(f32)[0:1, 0:1]
+    pi = (jnp.sin(angle) * weight).astype(bf16).astype(f32)[0:1, 0:1]
+    rr = rot_ref[0, q].astype(f32)
+    ri = rot_ref[1, q].astype(f32)
+    cr = rr * pr - ri * pi
+    ci = rr * pi + ri * pr
+    mat_ref[0:48, 0:96] = jnp.concatenate([cr, -ci], axis=0).T
+    mat_ref[48:96, 0:96] = jnp.concatenate([ci, cr], axis=0).T
     rows = []
-    for g in range(2 * NQ):
+    for g in range(2):
         for j in range(PER):
             rows.append(mat_ref[pl.ds(g * 48 + j, LAT, stride=PER), :])
     mat = jnp.concatenate(rows, axis=0)[:, 0:96].astype(bf16)
@@ -83,7 +82,7 @@
         for h in range(2):
             block = s_ref[h, e * STRIDE_S:e * STRIDE_S + 96, :].astype(bf16)
             res = jnp.dot(mat, block, preferred_element_type=f32)
-            for g in range(2 * NQ):
+            for g in range(2):
                 for j in range(PER):
                     at = (g * PER + j) * LAT
                     o_ref[2 * j + h, pl.ds(g * CELLS + e, LAT, stride=ROWS), :] = res[at:at + LAT]
@@ -92,7 +91,8 @@
             out_ref[l, :, t * 128:(t + 1) * 128] = o_ref[t, l * ROWS:(l + 1) * ROWS, :].astype(bf16)
 
 
-def sum_body(x_ref, out_ref):
+def sum_body(x_ref, *refs):
+    out_ref = refs[-1]
     for r in range(0, ROWS, 16):
         acc = x_ref[0, r:r + 16, :].astype(f32)
         for p in range(1, LAT):
@@ -149,12 +149,12 @@
 
 
 def couple_body(*refs):
-    ph_ref, u_ref, l_ref, out_ref, y_ref, bl_ref, h_ref, r_ref = refs[6:]
+    ph_ref, u_ref, l_ref, out_ref, y_ref, bl_ref, h_ref, r_ref = refs[12:]
     ph = ph_ref[...]
     for q in range(NQ):
         x = jnp.concatenate(
             [
-                refs[side * 3 + i][j * ROWS + q * 32:j * ROWS + (q + 1) * 32, :]
+                refs[q * 6 + side * 3 + i][j * ROWS:(j + 1) * ROWS, :]
                 for side in range(2)
                 for i, j in PLACE
             ],
@@ -234,6 +234,63 @@
     return pltpu.CompilerParams(vmem_limit_bytes=40 << 20)
 
 
+def rotate(q, *args):
+    return pl.pallas_call(
+        functools.partial(rotate_body, q=q),
+        out_shape=jax.ShapeDtypeStruct((LAT, ROWS, LANES), bf16),
+        in_specs=[hbm()] * 5 + [pl.BlockSpec(memory_space=pl.ANY)],
+        out_specs=vmem(),
+        scratch_shapes=[
+            pltpu.SMEM((NQ, 3), f32),
+            pltpu.SMEM((1, 3), jnp.int32),
+            pltpu.SMEM((1, 1), jnp.int32),
+            pltpu.VMEM((2, NQ, MODES, MODES), bf16),
+            pltpu.VMEM((2, CELLS, MODES * BANDS * BANDS), bf16),
+            pltpu.VMEM((96, 128), f32),
+            pltpu.VMEM((2, CELLS * STRIDE_S, 128), f32),
+            pltpu.VMEM((2 * PER, LAT * ROWS, 128), f32),
+            pltpu.SemaphoreType.DMA((4 + 2 * CHUNKS,)),
+        ],
+        compiler_params=pltpu.CompilerParams(vmem_limit_bytes=(63 if q == 0 else 40) << 20),
+        name=f"rotate{q}",
+    )(*args)
+
+
+def add_up(parts, order):
+    return pl.pallas_call(
+        sum_body,
+        out_shape=jax.ShapeDtypeStruct((ROWS, LANES), bf16),
+        in_specs=[vmem()] + [pl.BlockSpec(memory_space=pl.ANY)] * len(order),
+        out_specs=vmem(),
+        compiler_params=params(),
+        name="add_up",
+    )(parts, *order)
+
+
+def shift(x, step):
+    return lax.ppermute(x, "kpt", [(i, (i + 2 * step) % 16) for i in range(16)])
+
+
+def swap(x):
+    return lax.ppermute(x, "kpt", [(i, i ^ 1) for i in range(16)])
+
+
+def gather(own, order):
+    packed, pair = pl.pallas_call(
+        pack_body,
+        out_shape=(
+            jax.ShapeDtypeStruct((3 * ROWS, LANES), bf16),
+            jax.ShapeDtypeStruct((2 * ROWS, LANES), bf16),
+        ),
+        in_specs=[vmem()] * 3 + [pl.BlockSpec(memory_space=pl.ANY)],
+        out_specs=(vmem(), vmem()),
+        compiler_params=params(),
+        name="pack",
+    )(own, shift(own, 3), shift(own, -3), order)
+    near = [packed, shift(packed, 1), shift(pair, -1)]
+    return near + [swap(x) for x in near]
+
+
 def per_device(
     coarse,
     rp_vectors,
@@ -248,26 +305,12 @@
     mask_k,
     mask_kq,
 ):
-    rotated = pl.pallas_call(
-        rotate_body,
-        out_shape=jax.ShapeDtypeStruct((LAT, ROWS, LANES), bf16),
-        in_specs=[hbm()] * 5,
-        out_specs=vmem(),
-        scratch_shapes=[
-            pltpu.SMEM((NQ, 3), f32),
-            pltpu.SMEM((1, 3), jnp.int32),
-            pltpu.SMEM((1, 1), jnp.int32),
-            pltpu.VMEM((2, NQ, MODES, MODES), bf16),
-            pltpu.VMEM((2, CELLS, MODES * BANDS * BANDS), bf16),
-            pltpu.VMEM((192, 128), f32),
-            pltpu.VMEM((2, CELLS * STRIDE_S, 128), f32),
-            pltpu.VMEM((2 * PER, LAT * ROWS, 128), f32),
-            pltpu.SemaphoreType.DMA((4 + 2 * CHUNKS,)),
-        ],
-        compiler_params=pltpu.CompilerParams(vmem_limit_bytes=63 << 20),
-        name="rotate",
-    )(q_points, rp_vectors, rp_weights[None, :], modes_rot, coarse)
-    parts = lax.all_to_all(rotated, "lat", 0, 0, tiled=True)
+    small = (q_points, rp_vectors, rp_weights[None, :], modes_rot)
+    parts = []
+    order = q_points
+    for q in range(NQ):
+        order = rotate(q, *small, coarse, order)
+        parts.append(lax.all_to_all(order, "lat", 0, 0, tiled=True))
 
     index = lax.axis_index("kpt")
     at = jnp.stack([index // 2, index % 2]).astype(jnp.int32)
@@ -295,43 +338,14 @@
         mask_kq.reshape(NQ * KPTS, BANDS),
     )
 
-    own = pl.pallas_call(
-        sum_body,
-        out_shape=jax.ShapeDtypeStruct((ROWS, LANES), bf16),
-        in_specs=[vmem()],
-        out_specs=vmem(),
-        compiler_params=params(),
-        name="add_up",
-    )(parts)
-
-    def shift(x, step):
-        return lax.ppermute(x, "kpt", [(i, (i + 2 * step) % 16) for i in range(16)])
-
-    def swap(x):
-        return lax.ppermute(x, "kpt", [(i, i ^ 1) for i in range(16)])
-
-    up = shift(own, 3)
-    down = shift(own, -3)
-    packed, pair = pl.pallas_call(
-        pack_body,
-        out_shape=(
-            jax.ShapeDtypeStruct((3 * ROWS, LANES), bf16),
-            jax.ShapeDtypeStruct((2 * ROWS, LANES), bf16),
-        ),
-        in_specs=[vmem()] * 3 + [pl.BlockSpec(memory_space=pl.ANY)],
-        out_specs=(vmem(), vmem()),
-        compiler_params=params(),
-        name="pack",
-    )(own, up, down, phase)
-    plus = shift(packed, 1)
-    minus = shift(pair, -1)
-    near = [packed, plus, minus]
-    far = [swap(x) for x in near]
+    spread = []
+    for q in range(NQ):
+        spread += gather(add_up(parts[q], spread), phase)
 
     result = pl.pallas_call(
         couple_body,
         out_shape=jax.ShapeDtypeStruct((2, 2 * KPTS, LANES), bf16),
-        in_specs=[vmem()] * 9,
+        in_specs=[vmem()] * 15,
         out_specs=vmem(),
         scratch_shapes=[
             pltpu.VMEM((2, 2 * PER, 128, 128), f32),
@@ -341,7 +355,7 @@
         ],
         compiler_params=params(),
         name="couple",
-    )(*near, *far, phase, right, left)
+    )(*spread, phase, right, left)
     return result.reshape(2, KPTS, NQ, LANES)
 
 

time: 70.6 us -> 79.1 us (1.12)
  starting transfers between devices: 29.3 us -> 40.1 us
  waiting for transfers between devices: 25.3 us -> 17.7 us
  Pallas kernels: 13 us -> 16 us
  local copies, waits for them, and re-layouts: 1.91 us -> 3.83 us
    all_to_all x1 -> x2, waiting for transfers between devices: 21.7 us -> 7.64 us  [per_device(): parts.append(lax.all_to_all(order, 'lat', 0, 0, tiled=True))]
    ppermute x4 -> x8, waiting for transfers between devices: 2.49 us -> 7.82 us  [shift(): return lax.ppermute(x, 'kpt', [(i, (i + 2 * step) % 16) for i in range(16)])]
    ppermute x4 -> x8, starting transfers between devices: 11.8 us -> 15.7 us  [shift(): return lax.ppermute(x, 'kpt', [(i, (i + 2 * step) % 16) for i in range(16)])]
    all_to_all x1 -> x2, starting transfers between devices: 7.72 us -> 11.5 us  [per_device(): parts.append(lax.all_to_all(order, 'lat', 0, 0, tiled=True))]
    ppermute x3 -> x6, starting transfers between devices: 9.75 us -> 12.9 us  [swap(): return lax.ppermute(x, 'kpt', [(i, i ^ 1) for i in range(16)])]
    pallas_call x3 -> x6, Pallas kernels: 7.19 us -> 10.2 us  [the longest x2 9.99 us: rotate(): pl.pallas_call(functools.partial(rotate_body, q=q), out_shape=jax.ShapeDt...]
    unnamed x18 -> x28, local copies, waits for them, and re-layouts: 0.58 us -> 2.5 us
    ppermute x3 -> x6, waiting for transfers between devices: 1.07 us -> 2.23 us  [swap(): return lax.ppermute(x, 'kpt', [(i, i ^ 1) for i in range(16)])]
  transfers between devices with their start and end apart: 8 -> 16, of which waited for: 4 -> 6; matrix products, arithmetic and copies ran while one was open for 2% -> 1% of each run, Pallas kernels for 2% -> 8%
where the time goes in v3:
time: 79.1 us; the launch traced here: 78.7 us
  starting transfers between devices  40.1 us (51%)
  waiting for transfers between devices  17.7 us (22%)
  Pallas kernels  16 us (20%)
  local copies, waits for them, and re-layouts  3.83 us (5%)
  between operations  0.89 us (1%)
    ppermute x8, starting transfers between devices, shift(): return lax.ppermute(x, 'kpt', [(i, (i + 2 * step) % 16) for i in range(16)])  15.7 us
    ppermute x6, starting transfers between devices, swap(): return lax.ppermute(x, 'kpt', [(i, i ^ 1) for i in range(16)])  12.9 us
    all_to_all x2, starting transfers between devices, per_device(): parts.append(lax.all_to_all(order, 'lat', 0, 0, tiled=True))  11.5 us
    pallas_call x2, Pallas kernels, rotate(): pl.pallas_call(functools.partial(rotate_body, q=q), out_shape=jax.ShapeDt...  9.99 us
    ppermute x8, waiting for transfers between devices, shift(): return lax.ppermute(x, 'kpt', [(i, (i + 2 * step) % 16) for i in range(16)])  7.82 us
    all_to_all x2, waiting for transfers between devices, per_device(): parts.append(lax.all_to_all(order, 'lat', 0, 0, tiled=True))  7.64 us
    pallas_call x1, Pallas kernels, per_device(): pl.pallas_call(couple_body, out_shape=jax.ShapeDtypeStruct((2, 2 * KPTS,...  4.51 us
    unnamed x28, local copies, waits for them, and re-layouts  2.5 us
  transfers between devices with their start and end apart: 16, of which 6 were waited for; matrix products, arithmetic and copies ran while one was open for 1% of the time, Pallas kernels for 8%

profile of v3, /device:TPU:1, one launch (start us, length us, event | category | flops | bytes accessed | tf_op | source)
XLA Modules:
  0.0 78.7 jit_solution(862510617767203511)
XLA Ops:
  0.7 0.0 copy-start.2
  0.7 5.1 %rotate0.1.order_ref = bf16[16,32,768]{2,1,0:T(8,128)(2,1)} custom-call(f32[2,3]{1,0:T(2,128)} %qp_hbm.3, s32[1,3]{1,0:T(1,128)} %rv_hbm.3, s32[1,1]{1,0:T(1,128)} %bitcast.9.rw_hbm, bf16[2,2,48,48]{3,2,1,0:T(8,128)(2,1)} %rot_hbm.3, bf16[2,1,16,12288]{3,2,1,0:T(8,128)(2,1)} %coarse_hbm.3, f32[2,3]{1,0:T(2,128)} %qp_hbm.3), custom_call_target="tpu_custom_call" | custom-call | tf_op jit(solution)/shard_map/rotate0/pallas_call | solution.py:238
  5.8 0.0 copy-start
  5.8 0.0 copy-start.1
  5.8 7.7 %all-to-all-start = ((bf16[16,32,768]{2,1,0:T(8,128)(2,1)}), bf16[16,32,768]{2,1,0:T(8,128)(2,1)S(1)}, u32[]{:S(2)}, u32[]{:S(2)}) async-start(bf16[16,32,768]{2,1,0:T(8,128)(2,1)} %rotate0.1.order_ref), calls=%async_computation | async-start | bytes 1572864 | tf_op jit(solution)/shard_map/all_to_all | solution.py:313
  13.6 0.0 copy-start.3
  13.6 0.0 copy-start.4
  13.6 0.0 copy-done.2
  13.6 0.6 copy-done.3
  14.3 4.8 %rotate1.1 = bf16[16,32,768]{2,1,0:T(8,128)(2,1)} custom-call(f32[2,3]{1,0:T(2,128)S(1)} %copy-done.3, s32[1,3]{1,0:T(1,128)S(1)} %copy-done.4, s32[1,1]{1,0:T(1,128)} %bitcast.10.rw_hbm, bf16[2,2,48,48]{3,2,1,0:T(8,128)(2,1)S(1)} %copy-done.2, bf16[2,1,16,12288]{3,2,1,0:T(8,128)(2,1)S(1)} %copy-done.1, bf16[16,32,768]{2,1,0:T(8,128)(2,1)S(1)} %copy-done), custom_call_target="tpu_custom_call" | custom-call | tf_op jit(solution)/shard_map/rotate1/pallas_call | solution.py:238
  19.1 7.6 %all-to-all-done.x_ref = bf16[16,32,768]{2,1,0:T(8,128)(2,1)S(1)} async-done(((bf16[16,32,768]{2,1,0:T(8,128)(2,1)}), bf16[16,32,768]{2,1,0:T(8,128)(2,1)S(1)}, u32[]{:S(2)}, u32[]{:S(2)}) %all-to-all-start) | async-done | bytes 786464 | tf_op jit(solution)/shard_map/all_to_all | solution.py:313
  26.8 3.8 %all-to-all-start.1 = ((bf16[16,32,768]{2,1,0:T(8,128)(2,1)}), bf16[16,32,768]{2,1,0:T(8,128)(2,1)S(1)}, u32[]{:S(2)}, u32[]{:S(2)}) async-start(bf16[16,32,768]{2,1,0:T(8,128)(2,1)} %rotate1.1), calls=%async_computation.1 | async-start | bytes 1572864 | tf_op jit(solution)/shard_map/all_to_all | solution.py:313
  30.6 0.1 pad.2.clone
  30.7 0.7 copy-done.9
  31.4 0.0 copy-done.11
  31.4 0.1 add_add_fusion.rv_ref
  31.4 0.1 add_up.2.own_ref
  31.6 0.0 copy-start.5
  31.6 6.5 %collective-permute-start.1 = (bf16[32,768]{1,0:T(8,128)(2,1)S(1)}, bf16[32,768]{1,0:T(8,128)(2,1)S(1)}, u32[]{:S(2)}, u32[]{:S(2)}) collective-permute-start(bf16[32,768]{1,0:T(8,128)(2,1)S(1)} %add_up.2.own_ref), channel_id=1, source_target_pairs={{0,10},{1,11},{2,12},{3,13},{4,14},{5,15},{6,0},{7,1},{8,2},{9,3},... | collective-permute-start | bytes 147464 | tf_op jit(solution)/shard_map/ppermute | solution.py:271
  38.1 0.0 collective-permute-start
  38.1 0.1 pad_add_fusion.at_ref
  38.2 0.0 copy-done.10
  38.2 0.1 copy.20.kp_ref
  38.3 0.0 copy-done.8
  38.3 0.1 copy.23.mk_ref
  38.4 0.0 copy-done.6
  38.4 0.0 copy-start.7
  38.4 0.1 copy.21.u_ref
  38.5 0.6 copy-done.7
  39.1 0.1 copy.19
  39.2 0.3 copy.18
  39.5 0.1 reshape.13
  39.6 0.1 copy.22.uq_ref
  39.7 1.3 %prep.1 = (bf16[128,512]{1,0:T(8,128)(2,1)S(1)}, f32[2,16,16,128]{3,2,1,0:T(8,128)S(1)}, f32[2,16,16,128]{3,2,1,0:T(8,128)S(1)}) custom-call(s32[2]{0:T(128)S(1)} %pad_add_fusion.at_ref, f32[64,3]{1,0:T(8,128)S(1)} %copy.20.kp_ref, s32[8,256]{1,0:T(8,128)S(1)} %add_add_fusion.rv_ref, bf16[2,64,256]{2,1,0:T(8,128)(2,1)S(1)} %copy.21.u_ref, ...), custom_call_target="tpu_custom_call" | custom-call | tf_op jit(solution)/shard_map/prep/pallas_call | solution.py:320
  41.0 0.0 collective-permute-done.1.down_ref
  41.0 3.1 %collective-permute-done.up_ref = bf16[32,768]{1,0:T(8,128)(2,1)S(1)} collective-permute-done((bf16[32,768]{1,0:T(8,128)(2,1)S(1)}, bf16[32,768]{1,0:T(8,128)(2,1)S(1)}, u32[]{:S(2)}, u32[]{:S(2)}) %collective-permute-start) | collective-permute-done | bytes 49184 | tf_op jit(solution)/shard_map/ppermute | solution.py:271
  44.1 1.5 %collective-permute-start.2 = (bf16[96,768]{1,0:T(8,128)(2,1)S(1)}, bf16[96,768]{1,0:T(8,128)(2,1)S(1)}, u32[]{:S(2)}, u32[]{:S(2)}) collective-permute-start(bf16[96,768]{1,0:T(8,128)(2,1)S(1)} %get-tuple-element.13.refs_0_), channel_id=1, source_target_pairs={{0,2},{1,3},{2,4},{3,5},{4,6},{5,7},{6,8},{7,9},{8,10},{9,11},{10,... | collective-permute-start | bytes 442376 | tf_op jit(solution)/shard_map/ppermute | solution.py:271
  45.6 1.3 %collective-permute-start.3 = (bf16[64,768]{1,0:T(8,128)(2,1)S(1)}, bf16[64,768]{1,0:T(8,128)(2,1)S(1)}, u32[]{:S(2)}, u32[]{:S(2)}) collective-permute-start(bf16[64,768]{1,0:T(8,128)(2,1)S(1)} %get-tuple-element.14), channel_id=1, source_target_pairs={{0,14},{1,15},{2,0},{3,1},{4,2},{5,3},{6,4},{7,5},{8,6},{9,7},{10,... | collective-permute-start | bytes 294920 | tf_op jit(solution)/shard_map/ppermute | solution.py:271
  46.9 4.8 %collective-permute-start.4 = (bf16[96,768]{1,0:T(8,128)(2,1)S(1)}, bf16[96,768]{1,0:T(8,128)(2,1)S(1)}, u32[]{:S(2)}, u32[]{:S(2)}) collective-permute-start(bf16[96,768]{1,0:T(8,128)(2,1)S(1)} %get-tuple-element.13.refs_0_), channel_id=1, source_target_pairs={{0,1},{1,0},{2,3},{3,2},{4,5},{5,4},{6,7},{7,6},{8,9},{9,8},{10,11... | collective-permute-start | bytes 442376 | tf_op jit(solution)/shard_map/ppermute | solution.py:275
  51.7 0.0 collective-permute-done.2.refs_1_
  51.7 3.1 %collective-permute-start.5 = (bf16[96,768]{1,0:T(8,128)(2,1)S(1)}, bf16[96,768]{1,0:T(8,128)(2,1)S(1)}, u32[]{:S(2)}, u32[]{:S(2)}) collective-permute-start(bf16[96,768]{1,0:T(8,128)(2,1)S(1)} %collective-permute-done.2.refs_1_), channel_id=1, source_target_pairs={{0,1},{1,0},{2,3},{3,2},{4,5},{5,4},{6,7},{7,6},{8,9},{9,8},{10,11... | collective-permute-start | bytes 442376 | tf_op jit(solution)/shard_map/ppermute | solution.py:275
  54.8 0.0 collective-permute-done.3.refs_2_
  54.8 0.0 collective-permute-start.6
  54.8 0.0 all-to-all-done.1.x_ref
  54.8 0.0 collective-permute-done.4.refs_3_
  54.8 1.3 %collective-permute-done.6.refs_5_ = bf16[64,768]{1,0:T(8,128)(2,1)S(1)} collective-permute-done((bf16[64,768]{1,0:T(8,128)(2,1)S(1)}, bf16[64,768]{1,0:T(8,128)(2,1)S(1)}, u32[]{:S(2)}, u32[]{:S(2)}) %collective-permute-start.6) | collective-permute-done | bytes 98336 | tf_op jit(solution)/shard_map/ppermute | solution.py:275
  56.1 0.0 collective-permute-done.5.refs_4_
  56.1 0.1 add_up.3.own_ref
  56.2 0.1 collective-permute-start.8
  56.3 3.3 %collective-permute-start.7 = (bf16[32,768]{1,0:T(8,128)(2,1)S(1)}, bf16[32,768]{1,0:T(8,128)(2,1)S(1)}, u32[]{:S(2)}, u32[]{:S(2)}) collective-permute-start(bf16[32,768]{1,0:T(8,128)(2,1)S(1)} %add_up.3.own_ref), channel_id=1, source_target_pairs={{0,6},{1,7},{2,8},{3,9},{4,10},{5,11},{6,12},{7,13},{8,14},{9,15},... | collective-permute-start | bytes 147464 | tf_op jit(solution)/shard_map/ppermute | solution.py:271
  59.5 4.1 %collective-permute-done.8.down_ref = bf16[32,768]{1,0:T(8,128)(2,1)S(1)} collective-permute-done((bf16[32,768]{1,0:T(8,128)(2,1)S(1)}, bf16[32,768]{1,0:T(8,128)(2,1)S(1)}, u32[]{:S(2)}, u32[]{:S(2)}) %collective-permute-start.8) | collective-permute-done | bytes 49184 | tf_op jit(solution)/shard_map/ppermute | solution.py:271
  63.7 0.0 collective-permute-done.7.up_ref
  63.7 2.9 %collective-permute-start.9 = (bf16[96,768]{1,0:T(8,128)(2,1)S(1)}, bf16[96,768]{1,0:T(8,128)(2,1)S(1)}, u32[]{:S(2)}, u32[]{:S(2)}) collective-permute-start(bf16[96,768]{1,0:T(8,128)(2,1)S(1)} %get-tuple-element.15.refs_6_), channel_id=1, source_target_pairs={{0,2},{1,3},{2,4},{3,5},{4,6},{5,7},{6,8},{7,9},{8,10},{9,11},{10,... | collective-permute-start | bytes 442376 | tf_op jit(solution)/shard_map/ppermute | solution.py:271
  66.6 0.2 collective-permute-start.10
  66.8 2.0 %collective-permute-start.11 = (bf16[96,768]{1,0:T(8,128)(2,1)S(1)}, bf16[96,768]{1,0:T(8,128)(2,1)S(1)}, u32[]{:S(2)}, u32[]{:S(2)}) collective-permute-start(bf16[96,768]{1,0:T(8,128)(2,1)S(1)} %get-tuple-element.15.refs_6_), channel_id=1, source_target_pairs={{0,1},{1,0},{2,3},{3,2},{4,5},{5,4},{6,7},{7,6},{8,9},{9,8},{10,11... | collective-permute-start | bytes 442376 | tf_op jit(solution)/shard_map/ppermute | solution.py:275
  68.7 0.6 collective-permute-done.9.refs_7_
  69.3 2.6 %collective-permute-start.12 = (bf16[96,768]{1,0:T(8,128)(2,1)S(1)}, bf16[96,768]{1,0:T(8,128)(2,1)S(1)}, u32[]{:S(2)}, u32[]{:S(2)}) collective-permute-start(bf16[96,768]{1,0:T(8,128)(2,1)S(1)} %collective-permute-done.9.refs_7_), channel_id=1, source_target_pairs={{0,1},{1,0},{2,3},{3,2},{4,5},{5,4},{6,7},{7,6},{8,9},{9,8},{10,11... | collective-permute-start | bytes 442376 | tf_op jit(solution)/shard_map/ppermute | solution.py:275
  71.9 0.0 collective-permute-done.10.refs_8_
  71.9 0.5 collective-permute-start.13
  72.3 0.0 collective-permute-done.11.refs_9_
  72.3 0.9 %collective-permute-done.13.refs_11_ = bf16[64,768]{1,0:T(8,128)(2,1)S(1)} collective-permute-done((bf16[64,768]{1,0:T(8,128)(2,1)S(1)}, bf16[64,768]{1,0:T(8,128)(2,1)S(1)}, u32[]{:S(2)}, u32[]{:S(2)}) %collective-permute-start.13) | collective-permute-done | bytes 98336 | tf_op jit(solution)/shard_map/ppermute | solution.py:275
  73.3 0.0 collective-permute-done.12.refs_10_
  73.3 4.5 %couple.1 = bf16[2,128,768]{2,1,0:T(8,128)(2,1)S(1)} custom-call(bf16[96,768]{1,0:T(8,128)(2,1)S(1)} %get-tuple-element.13.refs_0_, bf16[96,768]{1,0:T(8,128)(2,1)S(1)} %collective-permute-done.2.refs_1_, bf16[64,768]{1,0:T(8,128)(2,1)S(1)} %collective-permute-done.3.refs_2_, bf16[96,768]{1,0:T(8,128)(2,1)S(1)} %collective-permute-done.4.refs_3_, ...), custom_call_target="tpu_custom_call" | custom-call | tf_op jit(solution)/shard_map/couple/pallas_call | solution.py:345
  77.8 0.9 %reshape.15 = bf16[2,64,2,768]{3,2,1,0:T(2,128)(2,1)} reshape(bf16[2,128,768]{2,1,0:T(8,128)(2,1)S(1)} %couple.1) | data formatting | bytes 786432 | tf_op jit(solution)/shard_map/reshape | solution.py:359
  (12 shorter events, 0.1 us)
Async XLA Ops:
  0.7 12.9 %copy-start.2 = (bf16[2,2,48,48]{3,2,1,0:T(8,128)(2,1)S(1)}, bf16[2,2,48,48]{3,2,1,0:T(8,128)(2,1)}, u32[]{:S(2)}) copy-start(bf16[2,2,48,48]{3,2,1,0:T(8,128)(2,1)} %rot_hbm.3) | copy-start | bytes 55300
  5.8 7.8 %copy-start = (bf16[16,32,768]{2,1,0:T(8,128)(2,1)S(1)}, bf16[16,32,768]{2,1,0:T(8,128)(2,1)}, u32[]{:S(2)}) copy-start(bf16[16,32,768]{2,1,0:T(8,128)(2,1)} %rotate0.1.order_ref) | copy-start | bytes 2359300
  5.8 7.8 %copy-start.1 = (bf16[2,1,16,12288]{3,2,1,0:T(8,128)(2,1)S(1)}, bf16[2,1,16,12288]{3,2,1,0:T(8,128)(2,1)}, u32[]{:S(2)}) copy-start(bf16[2,1,16,12288]{3,2,1,0:T(8,128)(2,1)} %coarse_hbm.3) | copy-start | bytes 2359300
  5.8 20.9 %all-to-all-start = ((bf16[16,32,768]{2,1,0:T(8,128)(2,1)}), bf16[16,32,768]{2,1,0:T(8,128)(2,1)S(1)}, u32[]{:S(2)}, u32[]{:S(2)}) async-start(bf16[16,32,768]{2,1,0:T(8,128)(2,1)} %rotate0.1.order_ref), calls=%async_computation | async-start | bytes 1572864 | tf_op jit(solution)/shard_map/all_to_all | solution.py:313
  13.6 0.7 copy-start.3
  13.6 0.7 copy-start.4
  26.8 28.0 %all-to-all-start.1 = ((bf16[16,32,768]{2,1,0:T(8,128)(2,1)}), bf16[16,32,768]{2,1,0:T(8,128)(2,1)S(1)}, u32[]{:S(2)}, u32[]{:S(2)}) async-start(bf16[16,32,768]{2,1,0:T(8,128)(2,1)} %rotate1.1), calls=%async_computation.1 | async-start | bytes 1572864 | tf_op jit(solution)/shard_map/all_to_all | solution.py:313
  30.7 0.7 copy-start.9
  30.7 0.7 copy-start.11
  31.4 6.7 %copy-start.10 = (f32[64,3]{0,1:T(4,128)S(1)}, f32[64,3]{0,1:T(4,128)}, u32[]{:S(2)}) copy-start(f32[64,3]{0,1:T(4,128)} %param.18) | copy-start | bytes 2308
  31.4 6.8 %copy-start.8 = (s32[64,16]{0,1:T(8,128)S(1)}, s32[64,16]{0,1:T(8,128)}, u32[]{:S(2)}) copy-start(s32[64,16]{0,1:T(8,128)} %param.22) | copy-start | bytes 12292
  31.4 6.9 %copy-start.6 = (bf16[2,64,16,16]{1,3,2,0:T(8,128)(2,1)S(1)}, bf16[2,64,16,16]{1,3,2,0:T(8,128)(2,1)}, u32[]{:S(2)}) copy-start(bf16[2,64,16,16]{1,3,2,0:T(8,128)(2,1)} %param.20) | copy-start | bytes 196612
  31.6 7.6 %copy-start.5 = (bf16[2,2,64,16,16]{2,4,3,1,0:T(8,128)(2,1)S(1)}, bf16[2,2,64,16,16]{2,4,3,1,0:T(8,128)(2,1)}, u32[]{:S(2)}) copy-start(bf16[2,2,64,16,16]{2,4,3,1,0:T(8,128)(2,1)} %param.21) | copy-start | bytes 393220
  31.6 9.4 %collective-permute-start.1 = (bf16[32,768]{1,0:T(8,128)(2,1)S(1)}, bf16[32,768]{1,0:T(8,128)(2,1)S(1)}, u32[]{:S(2)}, u32[]{:S(2)}) collective-permute-start(bf16[32,768]{1,0:T(8,128)(2,1)S(1)} %add_up.2.own_ref), channel_id=1, source_target_pairs={{0,10},{1,11},{2,12},{3,13},{4,14},{5,15},{6,0},{7,1},{8,2},{9,3},... | collective-permute-start | bytes 147464 | tf_op jit(solution)/shard_map/ppermute | solution.py:271
  38.1 6.0 %collective-permute-start = (bf16[32,768]{1,0:T(8,128)(2,1)S(1)}, bf16[32,768]{1,0:T(8,128)(2,1)S(1)}, u32[]{:S(2)}, u32[]{:S(2)}) collective-permute-start(bf16[32,768]{1,0:T(8,128)(2,1)S(1)} %add_up.2.own_ref), channel_id=1, source_target_pairs={{0,6},{1,7},{2,8},{3,9},{4,10},{5,11},{6,12},{7,13},{8,14},{9,15},... | collective-permute-start | bytes 147464 | tf_op jit(solution)/shard_map/ppermute | solution.py:271
  38.4 0.7 copy-start.7
  44.1 7.5 %collective-permute-start.2 = (bf16[96,768]{1,0:T(8,128)(2,1)S(1)}, bf16[96,768]{1,0:T(8,128)(2,1)S(1)}, u32[]{:S(2)}, u32[]{:S(2)}) collective-permute-start(bf16[96,768]{1,0:T(8,128)(2,1)S(1)} %get-tuple-element.13.refs_0_), channel_id=1, source_target_pairs={{0,2},{1,3},{2,4},{3,5},{4,6},{5,7},{6,8},{7,9},{8,10},{9,11},{10,... | collective-permute-start | bytes 442376 | tf_op jit(solution)/shard_map/ppermute | solution.py:271
  45.6 9.2 %collective-permute-start.3 = (bf16[64,768]{1,0:T(8,128)(2,1)S(1)}, bf16[64,768]{1,0:T(8,128)(2,1)S(1)}, u32[]{:S(2)}, u32[]{:S(2)}) collective-permute-start(bf16[64,768]{1,0:T(8,128)(2,1)S(1)} %get-tuple-element.14), channel_id=1, source_target_pairs={{0,14},{1,15},{2,0},{3,1},{4,2},{5,3},{6,4},{7,5},{8,6},{9,7},{10,... | collective-permute-start | bytes 294920 | tf_op jit(solution)/shard_map/ppermute | solution.py:271
  46.9 7.9 %collective-permute-start.4 = (bf16[96,768]{1,0:T(8,128)(2,1)S(1)}, bf16[96,768]{1,0:T(8,128)(2,1)S(1)}, u32[]{:S(2)}, u32[]{:S(2)}) collective-permute-start(bf16[96,768]{1,0:T(8,128)(2,1)S(1)} %get-tuple-element.13.refs_0_), channel_id=1, source_target_pairs={{0,1},{1,0},{2,3},{3,2},{4,5},{5,4},{6,7},{7,6},{8,9},{9,8},{10,11... | collective-permute-start | bytes 442376 | tf_op jit(solution)/shard_map/ppermute | solution.py:275
  51.7 4.4 %collective-permute-start.5 = (bf16[96,768]{1,0:T(8,128)(2,1)S(1)}, bf16[96,768]{1,0:T(8,128)(2,1)S(1)}, u32[]{:S(2)}, u32[]{:S(2)}) collective-permute-start(bf16[96,768]{1,0:T(8,128)(2,1)S(1)} %collective-permute-done.2.refs_1_), channel_id=1, source_target_pairs={{0,1},{1,0},{2,3},{3,2},{4,5},{5,4},{6,7},{7,6},{8,9},{9,8},{10,11... | collective-permute-start | bytes 442376 | tf_op jit(solution)/shard_map/ppermute | solution.py:275
  54.8 1.3 %collective-permute-start.6 = (bf16[64,768]{1,0:T(8,128)(2,1)S(1)}, bf16[64,768]{1,0:T(8,128)(2,1)S(1)}, u32[]{:S(2)}, u32[]{:S(2)}) collective-permute-start(bf16[64,768]{1,0:T(8,128)(2,1)S(1)} %collective-permute-done.3.refs_2_), channel_id=1, source_target_pairs={{0,1},{1,0},{2,3},{3,2},{4,5},{5,4},{6,7},{7,6},{8,9},{9,8},{10,11... | collective-permute-start | bytes 294920 | tf_op jit(solution)/shard_map/ppermute | solution.py:275
  56.2 7.5 %collective-permute-start.8 = (bf16[32,768]{1,0:T(8,128)(2,1)S(1)}, bf16[32,768]{1,0:T(8,128)(2,1)S(1)}, u32[]{:S(2)}, u32[]{:S(2)}) collective-permute-start(bf16[32,768]{1,0:T(8,128)(2,1)S(1)} %add_up.3.own_ref), channel_id=1, source_target_pairs={{0,10},{1,11},{2,12},{3,13},{4,14},{5,15},{6,0},{7,1},{8,2},{9,3},... | collective-permute-start | bytes 147464 | tf_op jit(solution)/shard_map/ppermute | solution.py:271
  56.3 7.4 %collective-permute-start.7 = (bf16[32,768]{1,0:T(8,128)(2,1)S(1)}, bf16[32,768]{1,0:T(8,128)(2,1)S(1)}, u32[]{:S(2)}, u32[]{:S(2)}) collective-permute-start(bf16[32,768]{1,0:T(8,128)(2,1)S(1)} %add_up.3.own_ref), channel_id=1, source_target_pairs={{0,6},{1,7},{2,8},{3,9},{4,10},{5,11},{6,12},{7,13},{8,14},{9,15},... | collective-permute-start | bytes 147464 | tf_op jit(solution)/shard_map/ppermute | solution.py:271
  63.7 5.6 %collective-permute-start.9 = (bf16[96,768]{1,0:T(8,128)(2,1)S(1)}, bf16[96,768]{1,0:T(8,128)(2,1)S(1)}, u32[]{:S(2)}, u32[]{:S(2)}) collective-permute-start(bf16[96,768]{1,0:T(8,128)(2,1)S(1)} %get-tuple-element.15.refs_6_), channel_id=1, source_target_pairs={{0,2},{1,3},{2,4},{3,5},{4,6},{5,7},{6,8},{7,9},{8,10},{9,11},{10,... | collective-permute-start | bytes 442376 | tf_op jit(solution)/shard_map/ppermute | solution.py:271
  66.6 5.3 %collective-permute-start.10 = (bf16[64,768]{1,0:T(8,128)(2,1)S(1)}, bf16[64,768]{1,0:T(8,128)(2,1)S(1)}, u32[]{:S(2)}, u32[]{:S(2)}) collective-permute-start(bf16[64,768]{1,0:T(8,128)(2,1)S(1)} %get-tuple-element.16), channel_id=1, source_target_pairs={{0,14},{1,15},{2,0},{3,1},{4,2},{5,3},{6,4},{7,5},{8,6},{9,7},{10,... | collective-permute-start | bytes 294920 | tf_op jit(solution)/shard_map/ppermute | solution.py:271
  66.8 5.6 %collective-permute-start.11 = (bf16[96,768]{1,0:T(8,128)(2,1)S(1)}, bf16[96,768]{1,0:T(8,128)(2,1)S(1)}, u32[]{:S(2)}, u32[]{:S(2)}) collective-permute-start(bf16[96,768]{1,0:T(8,128)(2,1)S(1)} %get-tuple-element.15.refs_6_), channel_id=1, source_target_pairs={{0,1},{1,0},{2,3},{3,2},{4,5},{5,4},{6,7},{7,6},{8,9},{9,8},{10,11... | collective-permute-start | bytes 442376 | tf_op jit(solution)/shard_map/ppermute | solution.py:275
  69.3 4.0 %collective-permute-start.12 = (bf16[96,768]{1,0:T(8,128)(2,1)S(1)}, bf16[96,768]{1,0:T(8,128)(2,1)S(1)}, u32[]{:S(2)}, u32[]{:S(2)}) collective-permute-start(bf16[96,768]{1,0:T(8,128)(2,1)S(1)} %collective-permute-done.9.refs_7_), channel_id=1, source_target_pairs={{0,1},{1,0},{2,3},{3,2},{4,5},{5,4},{6,7},{7,6},{8,9},{9,8},{10,11... | collective-permute-start | bytes 442376 | tf_op jit(solution)/shard_map/ppermute | solution.py:275
  71.9 1.4 %collective-permute-start.13 = (bf16[64,768]{1,0:T(8,128)(2,1)S(1)}, bf16[64,768]{1,0:T(8,128)(2,1)S(1)}, u32[]{:S(2)}, u32[]{:S(2)}) collective-permute-start(bf16[64,768]{1,0:T(8,128)(2,1)S(1)} %collective-permute-done.10.refs_8_), channel_id=1, source_target_pairs={{0,1},{1,0},{2,3},{3,2},{4,5},{5,4},{6,7},{7,6},{8,9},{9,8},{10,11... | collective-permute-start | bytes 294920 | tf_op jit(solution)/shard_map/ppermute | solution.py:275

commit v4 on v1

v4 whole, which is shorter than its diff:
```python
import jax
import jax.numpy as jnp
from jax import lax
from jax.experimental import pallas as pl
from jax.experimental.pallas import tpu as pltpu
from jax.sharding import PartitionSpec as P

two_pi = 6.283185307179586
f32 = jnp.float32
bf16 = jnp.bfloat16

MODES = 48
BANDS = 16
CELLS = 16
LAT = 16
ZED = 8
NQ = 2
KPTS = 64
PER = MODES // LAT
LANES = PER * BANDS * BANDS
STRIDE_S = 2 * MODES
SENT = 2 * MODES + 8
CHUNKS = 4
CHUNK = MODES * BANDS * BANDS // CHUNKS
SOURCES = ZED * LAT
WIDTH = PER * 128


def split_body(
    qp_hbm, rv_hbm, rw_hbm, coarse_hbm, out_ref, qp_ref, rv_ref, rw_ref, coarse_ref, s_ref, sems
):
    small = [
        pltpu.make_async_copy(src, dst, sems.at[i])
        for i, (src, dst) in enumerate([(qp_hbm, qp_ref), (rv_hbm, rv_ref), (rw_hbm, rw_ref)])
    ]
    large = []
    for part in range(2):
        for i in range(CHUNKS):
            lanes = pl.ds(i * CHUNK, CHUNK)
            large.append(
                pltpu.make_async_copy(
                    coarse_hbm.at[part, 0, :, lanes],
                    coarse_ref.at[part, :, lanes],
                    sems.at[3 + part * CHUNKS + i],
                )
            )
    for copy in large + small:
        copy.start()
    for part in range(2):
        for m in range(MODES):
            if m * 256 % CHUNK == 0:
                large[part * CHUNKS + m * 256 // CHUNK].wait()
            for h in range(2):
                at = (2 * m + h) * 128
                tile = coarse_ref[part, :, at:at + 128].astype(f32)
                s_ref[h, pl.ds(part * MODES + m, CELLS, stride=STRIDE_S), :] = tile
    for copy in small:
        copy.wait()
    weight = 1.0 / jnp.full((8, 128), rw_ref[0, 0], jnp.int32).astype(f32)
    rows = []
    for q in range(NQ):
        arg = two_pi * (
            qp_ref[q, 0] * rv_ref[0, 0].astype(f32)
            + qp_ref[q, 1] * rv_ref[0, 1].astype(f32)
            + qp_ref[q, 2] * rv_ref[0, 2].astype(f32)
        )
        angle = jnp.full((8, 128), arg, f32)
        rows += [jnp.cos(angle) * weight, jnp.sin(angle) * weight]
    line = lax.broadcasted_iota(jnp.int32, (8, 128), 0)
    phase = rows[3]
    for i in range(3):
        phase = jnp.where(line == i, rows[i], phase)
    phase = phase.astype(bf16)
    for e in range(CELLS):
        for h in range(2):
            lanes = slice(h * 128, (h + 1) * 128)
            out_ref[e, 0:96, lanes] = s_ref[h, e * STRIDE_S:e * STRIDE_S + 96, :].astype(bf16)
            out_ref[e, 96:SENT, lanes] = phase


def turn_body(rot_ref, mat_ref, t_ref):
    for q in range(NQ):
        rr = rot_ref[0, q].astype(f32)
        ri = rot_ref[1, q].astype(f32)
        t_ref[0:48, 0:96] = jnp.concatenate([rr, -ri], axis=0).T
        t_ref[48:96, 0:96] = jnp.concatenate([ri, rr], axis=0).T
        rows = []
        for g in range(2):
            for j in range(PER):
                rows.append(t_ref[pl.ds(g * 48 + j, LAT, stride=PER), :])
        mat_ref[q] = jnp.concatenate(rows, axis=0)[:, 0:96].astype(bf16)


def branch_body(x_ref, mat_ref, order_ref, out_ref, o_ref):
    for h in range(2):
        lanes = slice(h * 128, (h + 1) * 128)
        sums = [jnp.zeros((MODES, 128), f32) for _ in range(2 * NQ)]
        for p in range(LAT):
            xr = x_ref[p, 0:MODES, lanes].astype(f32)
            xi = x_ref[p, MODES:2 * MODES, lanes].astype(f32)
            phase = x_ref[p, 96:SENT, lanes].astype(f32)
            for q in range(NQ):
                pr = phase[2 * q:2 * q + 1]
                pi = phase[2 * q + 1:2 * q + 2]
                sums[2 * q] = sums[2 * q] + (pr * xr - pi * xi)
                sums[2 * q + 1] = sums[2 * q + 1] + (pr * xi + pi * xr)
        for q in range(NQ):
            on_q = jnp.concatenate([sums[2 * q], sums[2 * q + 1]], axis=0).astype(bf16)
            res = jnp.dot(mat_ref[q], on_q, preferred_element_type=f32)
            for g in range(2):
                for j in range(PER):
                    at = (g * PER + j) * LAT
                    o_ref[j, pl.ds(q * 4 + g * 2 + h, LAT, stride=8), :] = res[at:at + LAT]
    for j in range(PER):
        value = o_ref[j].reshape(LAT, 8, 128).astype(bf16)
        for z in range(ZED):
            out_ref[z * LAT:(z + 1) * LAT, :, j * 128:(j + 1) * 128] = value


def prep_body(core_ref, kp_ref, rv_ref, u_ref, uq_ref, mk_ref, mq_ref, ph_ref, uo_ref, lo_ref):
    c = core_ref[0]
    lane = lax.broadcasted_iota(jnp.int32, (256, 256), 1)
    src = lax.broadcasted_iota(jnp.int32, (256, 256), 0)
    home = (((lane >> 4) & 7) << 1) + (c ^ (lane >> 7))
    cell = (home << 4) + (lane & 15)
    pick = jnp.where(src == cell, 1.0, 0.0).astype(bf16)
    vec = jnp.dot(rv_ref[...].astype(f32).astype(bf16), pick, preferred_element_type=f32)
    kp = kp_ref[...]
    arg = two_pi * (
        kp[:, 0:1] * vec[0:1, :] + kp[:, 1:2] * vec[1:2, :] + kp[:, 2:3] * vec[2:3, :]
    )
    inverse = 1.0 / vec[3:4, :]
    both = jnp.concatenate([jnp.cos(arg) * inverse, jnp.sin(arg) * inverse], axis=0).astype(bf16)
    for piece in range(4):
        wide = lax.broadcasted_iota(jnp.int32, (256, 512), 1) + piece * 512
        deep = lax.broadcasted_iota(jnp.int32, (256, 512), 0)
        spread8 = jnp.where((wide >> 3) == deep, 1.0, 0.0).astype(bf16)
        grown = jnp.dot(both, spread8, preferred_element_type=f32)
        co = grown[0:KPTS]
        si = grown[KPTS:2 * KPTS]
        kind = lax.broadcasted_iota(jnp.int32, (KPTS, 512), 1) & 7
        real = (kind & 2) == 0
        values = (jnp.where(real, co, -si), jnp.where(real, si, co))
        for q in range(NQ):
            for h in range(2):
                mine = (kind & 5) == q * 4 + h
                for part in range(2):
                    at = ((q * 2 + h) * 2 + part) * KPTS
                    ph_ref[at:at + KPTS, piece * 512:(piece + 1) * 512] = jnp.where(
                        mine, values[part], 0.0
                    ).astype(bf16)
    row = lax.broadcasted_iota(jnp.int32, (KPTS, 128), 0)
    col = lax.broadcasted_iota(jnp.int32, (KPTS, 128), 1)
    spread = jnp.where((col >> 1) == row, 1.0, 0.0).astype(bf16)
    row2 = lax.broadcasted_iota(jnp.int32, (128, 128), 0)
    col2 = lax.broadcasted_iota(jnp.int32, (128, 128), 1)
    place = jnp.where((((col2 & 1) << 6) + (col2 >> 1)) == row2, 1.0, 0.0).astype(bf16)
    dims = (((0,), (0,)), ((), ()))
    mk = lax.dot_general(mk_ref[...].astype(f32).astype(bf16), spread, dims, preferred_element_type=f32)
    mq = lax.dot_general(mq_ref[...].astype(f32).astype(bf16), place, dims, preferred_element_type=f32)
    for part in range(2):
        ut = lax.dot_general(u_ref[part], spread, dims, preferred_element_type=f32)
        lt = lax.dot_general(uq_ref[part], place, dims, preferred_element_type=f32)
        for b in range(BANDS):
            uo_ref[part, b] = ut[b * 16:(b + 1) * 16] * mk
            lo_ref[part, b] = lt[b * 16:(b + 1) * 16] * mq


def couple_body(near_ref, far_ref, ph_ref, u_ref, l_ref, out_ref, y_ref, bl_ref, h_ref, r_ref):
    half = SOURCES * 8
    t = jnp.dot(
        ph_ref[:, 0:half], near_ref[...].reshape(half, WIDTH), preferred_element_type=f32
    ) + jnp.dot(
        ph_ref[:, half:2 * half], far_ref[...].reshape(half, WIDTH), preferred_element_type=f32
    )
    for q in range(NQ):
        for h in range(2):
            for part in range(2):
                at = ((q * 2 + h) * 2 + part) * KPTS
                for j in range(PER):
                    y_ref[part, 2 * j + h, pl.ds(q, KPTS, stride=2), :] = t[
                        at:at + KPTS, j * 128:(j + 1) * 128
                    ]
    for part in range(2):
        for v in range(2 * PER):
            bl_ref[part, v * 128:(v + 1) * 128, :] = y_ref[part, v].T.astype(bf16).astype(f32)

    group = 4

    def first(i, _):
        base = i * group * BANDS
        accr = [jnp.zeros((16, 128), f32) for _ in range(group)]
        acci = [jnp.zeros((16, 128), f32) for _ in range(group)]
        for b in range(BANDS):
            ur = u_ref[0, b]
            ui = u_ref[1, b]
            for s in range(group):
                xr = bl_ref[0, pl.ds(base + s * BANDS + b, 1), :]
                xi = bl_ref[1, pl.ds(base + s * BANDS + b, 1), :]
                accr[s] = accr[s] + (xr * ur - xi * ui)
                acci[s] = acci[s] + (xr * ui + xi * ur)
        for s in range(group):
            h_ref[0, i * group + s] = accr[s].astype(bf16).astype(f32)
            h_ref[1, i * group + s] = acci[s].astype(bf16).astype(f32)
        return 0

    lax.fori_loop(0, PER * BANDS // group, first, 0)

    per = BANDS // group

    def second(i, _):
        n = i // per
        c0 = (i - n * per) * group
        accr = [jnp.zeros((16, 128), f32) for _ in range(group)]
        acci = [jnp.zeros((16, 128), f32) for _ in range(group)]
        for a in range(BANDS):
            hr = h_ref[0, n * BANDS + a]
            hi = h_ref[1, n * BANDS + a]
            for s in range(group):
                lr = l_ref[0, a, pl.ds(c0 + s, 1), :]
                li = l_ref[1, a, pl.ds(c0 + s, 1), :]
                accr[s] = accr[s] + (lr * hr + li * hi)
                acci[s] = acci[s] + (lr * hi - li * hr)
        for s in range(group):
            r_ref[0, i * group + s] = accr[s]
            r_ref[1, i * group + s] = acci[s]
        return 0

    lax.fori_loop(0, PER * per, second, 0)
    for part in range(2):
        for v in range(2 * PER):
            tile = r_ref[part, v * 8:(v + 1) * 8].reshape(128, 128).T
            out_ref[part, :, v * 128:(v + 1) * 128] = tile.astype(bf16)


def vmem():
    return pl.BlockSpec(memory_space=pltpu.VMEM)


def hbm():
    return pl.BlockSpec(memory_space=pltpu.HBM)


def smem():
    return pl.BlockSpec(memory_space=pltpu.SMEM)


def params(mib=40):
    return pltpu.CompilerParams(vmem_limit_bytes=mib << 20)


def per_device(
    coarse,
    rp_vectors,
    rp_weights,
    re_vectors,
    re_weights,
    q_points,
    k_points,
    modes_rot,
    u_k,
    u_kq,
    mask_k,
    mask_kq,
):
    cells = pl.pallas_call(
        split_body,
        out_shape=jax.ShapeDtypeStruct((CELLS, SENT, 256), bf16),
        in_specs=[hbm()] * 4,
        out_specs=vmem(),
        scratch_shapes=[
            pltpu.SMEM((NQ, 3), f32),
            pltpu.SMEM((1, 3), jnp.int32),
            pltpu.SMEM((1, 1), jnp.int32),
            pltpu.VMEM((2, CELLS, MODES * BANDS * BANDS), bf16),
            pltpu.VMEM((2, CELLS * STRIDE_S, 128), f32),
            pltpu.SemaphoreType.DMA((3 + 2 * CHUNKS,)),
        ],
        compiler_params=params(63),
        name="split",
    )(q_points, rp_vectors, rp_weights[None, :], coarse)
    parts = lax.all_to_all(cells, "lat", 0, 0, tiled=True)

    turn = pl.pallas_call(
        turn_body,
        out_shape=jax.ShapeDtypeStruct((NQ, 2 * MODES, 2 * MODES), bf16),
        in_specs=[vmem()],
        out_specs=vmem(),
        scratch_shapes=[pltpu.VMEM((2 * MODES, 128), f32)],
        compiler_params=params(),
        name="turn",
    )(modes_rot)
    core = (lax.axis_index("kpt") & 1).astype(jnp.int32).reshape(1)
    lattice = jnp.concatenate(
        [re_vectors.T, re_weights[None, :], jnp.zeros((4, re_weights.shape[0]), jnp.int32)], axis=0
    )
    phase, right, left = pl.pallas_call(
        prep_body,
        out_shape=(
            jax.ShapeDtypeStruct((8 * KPTS, 2 * SOURCES * 8), bf16),
            jax.ShapeDtypeStruct((2, BANDS, BANDS, 128), f32),
            jax.ShapeDtypeStruct((2, BANDS, BANDS, 128), f32),
        ),
        in_specs=[smem()] + [vmem()] * 6,
        out_specs=(vmem(),) * 3,
        compiler_params=params(),
        name="prep",
    )(
        core,
        k_points,
        lattice,
        u_k.reshape(2, KPTS, BANDS * BANDS),
        u_kq.reshape(2, NQ * KPTS, BANDS * BANDS),
        mask_k,
        mask_kq.reshape(NQ * KPTS, BANDS),
    )

    branch = pl.pallas_call(
        branch_body,
        out_shape=jax.ShapeDtypeStruct((SOURCES, 8, WIDTH), bf16),
        in_specs=[vmem()] * 2 + [pl.BlockSpec(memory_space=pl.ANY)],
        out_specs=vmem(),
        scratch_shapes=[pltpu.VMEM((PER, LAT * 8, 128), f32)],
        compiler_params=params(),
        name="branch",
    )(parts, turn, phase)
    same_core = [[l * 16 + 2 * z + c for z in range(ZED) for l in range(LAT)] for c in range(2)]
    near = lax.all_to_all(
        branch, ("lat", "kpt"), 0, 0, tiled=True, axis_index_groups=same_core
    )
    far = lax.ppermute(near, "kpt", [(i, i ^ 1) for i in range(16)])

    result = pl.pallas_call(
        couple_body,
        out_shape=jax.ShapeDtypeStruct((2, 2 * KPTS, LANES), bf16),
        in_specs=[vmem()] * 5,
        out_specs=vmem(),
        scratch_shapes=[
            pltpu.VMEM((2, 2 * PER, 128, 128), f32),
            pltpu.VMEM((2, LANES, 128), f32),
            pltpu.VMEM((2, PER * BANDS, BANDS, 128), f32),
            pltpu.VMEM((2, PER * BANDS, BANDS, 128), f32),
        ],
        compiler_params=params(),
        name="couple",
    )(near, far, phase, right, left)
    return result.reshape(2, KPTS, NQ, LANES)


def solution(mesh):
    placed = (
        P(None, "lat", "kpt", None),
        P("lat", None),
        P("lat"),
        P(),
        P(),
        P(),
        P("kpt", None),
        P(),
        P(None, "kpt", None, None),
        P(None, None, "kpt", None, None),
        P("kpt", None),
        P(None, "kpt", None),
    )
    return jax.shard_map(
        per_device,
        mesh=mesh,
        in_specs=placed,
        out_specs=P(None, "kpt", None, "lat"),
        check_vma=False,
    )
```

time: 72.1 us -> 74.5 us (1.033)
  starting transfers between devices: 23.5 us -> 11.7 us
  waiting for transfers between devices: 2.34 us -> 11.3 us
  blocking collectives: 29.1 us -> 35.3 us
  local copies, waits for them, and re-layouts: 5.15 us -> 3.96 us
    ppermute x15 -> x1, starting transfers between devices: 23.5 us -> 4.07 us  [per_device(): far = lax.ppermute(near, 'kpt', [(i, i ^ 1) for i in range(16)])]
    all_to_all x0 -> x1, waiting for transfers between devices: none -> 9.43 us  [per_device(): parts = lax.all_to_all(cells, 'lat', 0, 0, tiled=True)]
    all_to_all x0 -> x1, starting transfers between devices: none -> 7.6 us  [per_device(): parts = lax.all_to_all(cells, 'lat', 0, 0, tiled=True)]
    all_to_all x1, blocking collectives: 29.1 us -> 35.3 us  [per_device(): lax.all_to_all(branch, ('lat', 'kpt'), 0, 0, tiled=True, axis_index_group...]
    unnamed x26, local copies, waits for them, and re-layouts: 3.82 us -> 2.64 us
    pallas_call x1, Pallas kernels: 4.54 us -> 5.41 us  [per_device(): pl.pallas_call(couple_body, out_shape=jax.ShapeDtypeStruct((2, 2 * KPTS,...]
    pallas_call x3 -> x4, Pallas kernels: 6.32 us -> 5.49 us  [the longest x1 3.54 us: per_device(): pl.pallas_call(split_body, out_shape=jax.ShapeDtypeStruct((CELLS, SENT, 2...]
    ppermute x15 -> x1, waiting for transfers between devices: 2.34 us -> 1.91 us  [per_device(): far = lax.ppermute(near, 'kpt', [(i, i ^ 1) for i in range(16)])]
  transfers between devices with their start and end apart: 15 -> 2, of which waited for: 1 -> 2; matrix products, arithmetic and copies ran while one was open for 2% -> 2% of each run, Pallas kernels for 2% -> 2%
where the time goes in v4:
time: 74.5 us; the launch traced here: 74.1 us
  blocking collectives  35.3 us (47%)
  starting transfers between devices  11.7 us (16%)
  waiting for transfers between devices  11.3 us (15%)
  Pallas kernels  10.9 us (15%)
  local copies, waits for them, and re-layouts  3.96 us (5%)
  between operations  0.88 us (1%)
    all_to_all x1, blocking collectives, per_device(): lax.all_to_all(branch, ('lat', 'kpt'), 0, 0, tiled=True, axis_index_group...  35.3 us
    all_to_all x1, waiting for transfers between devices, per_device(): parts = lax.all_to_all(cells, 'lat', 0, 0, tiled=True)  9.43 us
    all_to_all x1, starting transfers between devices, per_device(): parts = lax.all_to_all(cells, 'lat', 0, 0, tiled=True)  7.6 us
    pallas_call x1, Pallas kernels, per_device(): pl.pallas_call(couple_body, out_shape=jax.ShapeDtypeStruct((2, 2 * KPTS,...  5.41 us
    ppermute x1, starting transfers between devices, per_device(): far = lax.ppermute(near, 'kpt', [(i, i ^ 1) for i in range(16)])  4.07 us
    pallas_call x1, Pallas kernels, per_device(): pl.pallas_call(split_body, out_shape=jax.ShapeDtypeStruct((CELLS, SENT, 2...  3.54 us
    unnamed x26, local copies, waits for them, and re-layouts  2.64 us
    ppermute x1, waiting for transfers between devices, per_device(): far = lax.ppermute(near, 'kpt', [(i, i ^ 1) for i in range(16)])  1.91 us
  transfers between devices with their start and end apart: 2, of which 2 were waited for; matrix products, arithmetic and copies ran while one was open for 2% of the time, Pallas kernels for 2%

profile of v4, /device:TPU:1, one launch (start us, length us, event | category | flops | bytes accessed | tf_op | source)
XLA Modules:
  0.0 74.1 jit_solution(11341346875942322359)
XLA Ops:
  0.0 0.0 copy-start.9
  0.0 0.0 copy-start.7
  0.0 0.0 copy-start.3
  0.0 0.0 copy-start.5
  0.0 0.0 copy-start.6
  0.0 0.0 copy-start.4
  0.7 0.0 copy-start.8
  0.8 0.0 copy-start.10
  0.8 3.5 %split.1 = bf16[16,104,256]{2,1,0:T(8,128)(2,1)} custom-call(f32[2,3]{1,0:T(2,128)} %qp_hbm.1, s32[1,3]{1,0:T(1,128)} %rv_hbm.1, s32[1,1]{1,0:T(1,128)} %bitcast.8.rw_hbm, bf16[2,1,16,12288]{3,2,1,0:T(8,128)(2,1)} %coarse_hbm.1), custom_call_target="tpu_custom_call" | custom-call | tf_op jit(solution)/shard_map/split/pallas_call | solution.py:266
  4.3 7.6 %all-to-all-start = ((bf16[16,104,256]{2,1,0:T(8,128)(2,1)}), bf16[16,104,256]{2,1,0:T(8,128)(2,1)S(1)}, u32[]{:S(2)}, u32[]{:S(2)}) async-start(bf16[16,104,256]{2,1,0:T(8,128)(2,1)} %split.1), calls=%async_computation | async-start | bytes 1703936 | tf_op jit(solution)/shard_map/all_to_all | solution.py:282
  11.9 0.1 pad.2.clone
  12.0 0.0 copy-done.9
  12.0 0.7 copy.20.kp_ref
  12.7 0.0 copy-done.7
  12.7 0.1 copy.23.mk_ref
  12.8 0.0 copy-done.3
  12.8 0.1 turn.1.mat_ref
  12.9 0.0 copy-done.5
  12.9 0.1 copy.21.u_ref
  13.0 0.0 copy-done.6
  13.1 0.1 copy.19
  13.1 0.0 copy-done.4
  13.1 0.3 copy.18
  13.4 0.1 reshape.17
  13.6 0.1 copy.22.uq_ref
  13.7 0.0 copy-done.8
  13.7 0.0 copy-done.10
  13.7 0.1 add_add_fusion.rv_ref
  13.8 0.0 copy-start.2
  13.8 0.8 %copy-done.2 = f32[64,3]{1,0:T(8,128)S(1)} copy-done((f32[64,3]{1,0:T(8,128)S(1)}, f32[64,3]{1,0:T(8,128)}, u32[]{:S(2)}) %copy-start.2) | copy-done | bytes 792
  14.5 1.1 %prep.1 = (bf16[512,2048]{1,0:T(8,128)(2,1)S(1)}, f32[2,16,16,128]{3,2,1,0:T(8,128)S(1)}, f32[2,16,16,128]{3,2,1,0:T(8,128)S(1)}) custom-call(s32[1]{0:T(128)} %bitcast.1.core_ref, f32[64,3]{1,0:T(8,128)S(1)} %copy-done.2, s32[8,256]{1,0:T(8,128)S(1)} %add_add_fusion.rv_ref, bf16[2,64,256]{2,1,0:T(8,128)(2,1)S(1)} %copy.21.u_ref, ...), custom_call_target="tpu_custom_call" | custom-call | tf_op jit(solution)/shard_map/prep/pallas_call | solution.py:297
  15.7 0.0 copy-start
  15.7 0.7 copy-done
  16.4 9.4 %all-to-all-done.x_ref = bf16[16,104,256]{2,1,0:T(8,128)(2,1)S(1)} async-done(((bf16[16,104,256]{2,1,0:T(8,128)(2,1)}), bf16[16,104,256]{2,1,0:T(8,128)(2,1)S(1)}, u32[]{:S(2)}, u32[]{:S(2)}) %all-to-all-start) | async-done | bytes 852000 | tf_op jit(solution)/shard_map/all_to_all | solution.py:282
  25.8 0.0 copy-start.1
  25.8 0.7 branch.1
  26.5 35.3 %all_to_all.10.near_ref = bf16[128,8,384]{2,1,0:T(8,128)(2,1)S(1)} all-to-all(bf16[128,8,384]{2,1,0:T(8,128)(2,1)S(1)} %branch.1), channel_id=1, replica_groups={{0,16,32,48,64,80,96,112,128,144,160,176,192,208,224,240,2,18,34,50,66,..., dimensions={0} | all-to-all | bytes 1572864 | tf_op jit(solution)/shard_map/all_to_all | solution.py:328
  61.9 4.1 %collective-permute-start = (bf16[128,8,384]{2,1,0:T(8,128)(2,1)S(1)}, bf16[128,8,384]{2,1,0:T(8,128)(2,1)S(1)}, u32[]{:S(2)}, u32[]{:S(2)}) collective-permute-start(bf16[128,8,384]{2,1,0:T(8,128)(2,1)S(1)} %all_to_all.10.near_ref), channel_id=1, source_target_pairs={{0,1},{1,0},{2,3},{3,2},{4,5},{5,4},{6,7},{7,6},{8,9},{9,8},{10,11... | collective-permute-start | bytes 2359304 | tf_op jit(solution)/shard_map/ppermute | solution.py:331
  65.9 1.9 %collective-permute-done.far_ref = bf16[128,8,384]{2,1,0:T(8,128)(2,1)S(1)} collective-permute-done((bf16[128,8,384]{2,1,0:T(8,128)(2,1)S(1)}, bf16[128,8,384]{2,1,0:T(8,128)(2,1)S(1)}, u32[]{:S(2)}, u32[]{:S(2)}) %collective-permute-start) | collective-permute-done | bytes 786464 | tf_op jit(solution)/shard_map/ppermute | solution.py:331
  67.8 0.0 copy-done.1
  67.8 5.4 %couple.1 = bf16[2,128,768]{2,1,0:T(8,128)(2,1)S(1)} custom-call(bf16[128,8,384]{2,1,0:T(8,128)(2,1)S(1)} %all_to_all.10.near_ref, bf16[128,8,384]{2,1,0:T(8,128)(2,1)S(1)} %collective-permute-done.far_ref, bf16[512,2048]{1,0:T(8,128)(2,1)S(1)} %get-tuple-element.8.order_ref.ph_ref, f32[2,16,16,128]{3,2,1,0:T(8,128)S(1)} %get-tuple-element.9.u_ref, ...), custom_call_target="tpu_custom_call" | custom-call | tf_op jit(solution)/shard_map/couple/pallas_call | solution.py:333
  73.3 0.9 %reshape.19 = bf16[2,64,2,768]{3,2,1,0:T(2,128)(2,1)} reshape(bf16[2,128,768]{2,1,0:T(8,128)(2,1)S(1)} %couple.1) | data formatting | bytes 786432 | tf_op jit(solution)/shard_map/reshape | solution.py:347
  (1 shorter events, 0.0 us)
Async XLA Ops:
  0.0 12.0 %copy-start.9 = (f32[64,3]{0,1:T(4,128)S(1)}, f32[64,3]{0,1:T(4,128)}, u32[]{:S(2)}) copy-start(f32[64,3]{0,1:T(4,128)} %param.18) | copy-start | bytes 2308
  0.0 12.7 %copy-start.7 = (s32[64,16]{0,1:T(8,128)S(1)}, s32[64,16]{0,1:T(8,128)}, u32[]{:S(2)}) copy-start(s32[64,16]{0,1:T(8,128)} %param.22) | copy-start | bytes 12292
  0.0 12.8 %copy-start.3 = (bf16[2,2,48,48]{3,2,1,0:T(8,128)(2,1)S(1)}, bf16[2,2,48,48]{3,2,1,0:T(8,128)(2,1)}, u32[]{:S(2)}) copy-start(bf16[2,2,48,48]{3,2,1,0:T(8,128)(2,1)} %rot_ref.1) | copy-start | bytes 55300
  0.0 12.9 %copy-start.5 = (bf16[2,64,16,16]{1,3,2,0:T(8,128)(2,1)S(1)}, bf16[2,64,16,16]{1,3,2,0:T(8,128)(2,1)}, u32[]{:S(2)}) copy-start(bf16[2,64,16,16]{1,3,2,0:T(8,128)(2,1)} %param.20) | copy-start | bytes 196612
  0.0 13.0 %copy-start.6 = (s32[2,64,16]{1,2,0:T(8,128)S(1)}, s32[2,64,16]{1,2,0:T(8,128)}, u32[]{:S(2)}) copy-start(s32[2,64,16]{1,2,0:T(8,128)} %param.23) | copy-start | bytes 24580
  0.0 13.1 %copy-start.4 = (bf16[2,2,64,16,16]{2,4,3,1,0:T(8,128)(2,1)S(1)}, bf16[2,2,64,16,16]{2,4,3,1,0:T(8,128)(2,1)}, u32[]{:S(2)}) copy-start(bf16[2,2,64,16,16]{2,4,3,1,0:T(8,128)(2,1)} %param.21) | copy-start | bytes 393220
  0.7 12.9 %copy-start.8 = (s32[256,3]{0,1:T(4,128)S(1)}, s32[256,3]{0,1:T(4,128)}, u32[]{:S(2)}) copy-start(s32[256,3]{0,1:T(4,128)} %param.15) | copy-start | bytes 9220
  0.8 12.9 %copy-start.10 = (s32[256]{0:T(256)S(1)}, s32[256]{0:T(256)}, u32[]{:S(2)}) copy-start(s32[256]{0:T(256)} %param.16) | copy-start | bytes 3076
  4.3 21.5 %all-to-all-start = ((bf16[16,104,256]{2,1,0:T(8,128)(2,1)}), bf16[16,104,256]{2,1,0:T(8,128)(2,1)S(1)}, u32[]{:S(2)}, u32[]{:S(2)}) async-start(bf16[16,104,256]{2,1,0:T(8,128)(2,1)} %split.1), calls=%async_computation | async-start | bytes 1703936 | tf_op jit(solution)/shard_map/all_to_all | solution.py:282
  13.8 0.8 %copy-start.2 = (f32[64,3]{1,0:T(8,128)S(1)}, f32[64,3]{1,0:T(8,128)}, u32[]{:S(2)}) copy-start(f32[64,3]{1,0:T(8,128)} %copy.20.kp_ref) | copy-start | bytes 2308
  15.7 0.7 copy-start
  25.8 42.0 %copy-start.1 = (f32[2,16,16,128]{3,2,1,0:T(8,128)S(1)}, f32[2,16,16,128]{3,2,1,0:T(8,128)}, u32[]{:S(2)}) copy-start(f32[2,16,16,128]{3,2,1,0:T(8,128)} %copy-done) | copy-start | bytes 786436
  61.9 6.0 %collective-permute-start = (bf16[128,8,384]{2,1,0:T(8,128)(2,1)S(1)}, bf16[128,8,384]{2,1,0:T(8,128)(2,1)S(1)}, u32[]{:S(2)}, u32[]{:S(2)}) collective-permute-start(bf16[128,8,384]{2,1,0:T(8,128)(2,1)S(1)} %all_to_all.10.near_ref), channel_id=1, source_target_pairs={{0,1},{1,0},{2,3},{3,2},{4,5},{5,4},{6,7},{7,6},{8,9},{9,8},{10,11... | collective-permute-start | bytes 2359304 | tf_op jit(solution)/shard_map/ppermute | solution.py:331

commit v5 on v2

--- a/solution.py
+++ b/solution.py
@@ -17,8 +17,9 @@
 KPTS = 64
 PER = MODES // LAT
 LANES = PER * BANDS * BANDS
-STRIDE_S = 2 * MODES
+STRIDE_S = 2 * MODES + 1
 ROWS = NQ * 2 * CELLS
+STRIDE_O = ROWS + 1
 CHUNKS = 4
 CHUNK = MODES * BANDS * BANDS // CHUNKS
 
@@ -80,16 +81,19 @@
                 tile = coarse_ref[part, :, at:at + 128].astype(f32)
                 s_ref[h, pl.ds(part * MODES + m, CELLS, stride=STRIDE_S), :] = tile
     for e in range(CELLS):
+        block = jnp.concatenate(
+            [s_ref[h, e * STRIDE_S:e * STRIDE_S + 96, :].astype(bf16) for h in range(2)], axis=1
+        )
+        both = jnp.dot(mat, block, preferred_element_type=f32)
         for h in range(2):
-            block = s_ref[h, e * STRIDE_S:e * STRIDE_S + 96, :].astype(bf16)
-            res = jnp.dot(mat, block, preferred_element_type=f32)
+            res = both[:, h * 128:(h + 1) * 128]
             for g in range(2 * NQ):
                 for j in range(PER):
                     at = (g * PER + j) * LAT
-                    o_ref[2 * j + h, pl.ds(g * CELLS + e, LAT, stride=ROWS), :] = res[at:at + LAT]
+                    o_ref[2 * j + h, pl.ds(g * CELLS + e, LAT, stride=STRIDE_O), :] = res[at:at + LAT]
     for l in range(LAT):
         for t in range(2 * PER):
-            out_ref[l, :, t * 128:(t + 1) * 128] = o_ref[t, l * ROWS:(l + 1) * ROWS, :].astype(bf16)
+            out_ref[l, :, t * 128:(t + 1) * 128] = o_ref[t, l * STRIDE_O:l * STRIDE_O + ROWS, :].astype(bf16)
 
 
 def sum_body(x_ref, out_ref):
@@ -215,7 +219,7 @@
     for part in range(2):
         for v in range(2 * PER):
             tile = r_ref[part, v * 8:(v + 1) * 8].reshape(128, 128).T
-            out_ref[part, :, v * 128:(v + 1) * 128] = tile.astype(bf16)
+            out_ref[part, :, :, v * 128:(v + 1) * 128] = tile.reshape(KPTS, NQ, 128).astype(bf16)
 
 
 def vmem():
@@ -261,7 +265,7 @@
             pltpu.VMEM((2, CELLS, MODES * BANDS * BANDS), bf16),
             pltpu.VMEM((192, 128), f32),
             pltpu.VMEM((2, CELLS * STRIDE_S, 128), f32),
-            pltpu.VMEM((2 * PER, LAT * ROWS, 128), f32),
+            pltpu.VMEM((2 * PER, LAT * STRIDE_O, 128), f32),
             pltpu.SemaphoreType.DMA((4 + 2 * CHUNKS,)),
         ],
         compiler_params=pltpu.CompilerParams(vmem_limit_bytes=63 << 20),
@@ -330,7 +334,7 @@
 
     result = pl.pallas_call(
         couple_body,
-        out_shape=jax.ShapeDtypeStruct((2, 2 * KPTS, LANES), bf16),
+        out_shape=jax.ShapeDtypeStruct((2, KPTS, NQ, LANES), bf16),
         in_specs=[vmem()] * 9,
         out_specs=vmem(),
         scratch_shapes=[
@@ -342,7 +346,7 @@
         compiler_params=params(),
         name="couple",
     )(*near, *far, phase, right, left)
-    return result.reshape(2, KPTS, NQ, LANES)
+    return result
 
 
 def solution(mesh):

time: 70.6 us -> 66.8 us (0.946)
  Pallas kernels: 13 us -> 10.2 us
  local copies, waits for them, and re-layouts: 1.91 us -> 1.01 us
    pallas_call x1, Pallas kernels: 6.95 us -> 3.29 us  [per_device(): pl.pallas_call(rotate_body, out_shape=jax.ShapeDtypeStruct((LAT, ROWS, LA...]
    pallas_call x1, Pallas kernels: 4.51 us -> 5.43 us  [per_device(): pl.pallas_call(couple_body, out_shape=jax.ShapeDtypeStruct((2, KPTS, NQ,...]
    reshape x1 -> x0, local copies, waits for them, and re-layouts: 0.89 us -> none  [per_device(): return result.reshape(2, KPTS, NQ, LANES)]
where the time goes in v5:
time: 66.8 us; the launch traced here: 66.6 us
  starting transfers between devices  29.2 us (44%)
  waiting for transfers between devices  25.3 us (38%)
  Pallas kernels  10.2 us (15%)
  local copies, waits for them, and re-layouts  1.01 us (2%)
  between operations  0.83 us (1%)
    all_to_all x1, waiting for transfers between devices, per_device(): parts = lax.all_to_all(rotated, 'lat', 0, 0, tiled=True)  21.7 us
    ppermute x4, starting transfers between devices, shift(): return lax.ppermute(x, 'kpt', [(i, (i + 2 * step) % 16) for i in range(16)])  11.8 us
    ppermute x3, starting transfers between devices, swap(): return lax.ppermute(x, 'kpt', [(i, i ^ 1) for i in range(16)])  9.67 us
    all_to_all x1, starting transfers between devices, per_device(): parts = lax.all_to_all(rotated, 'lat', 0, 0, tiled=True)  7.73 us
    pallas_call x1, Pallas kernels, per_device(): pl.pallas_call(couple_body, out_shape=jax.ShapeDtypeStruct((2, KPTS, NQ,...  5.43 us
    pallas_call x1, Pallas kernels, per_device(): pl.pallas_call(rotate_body, out_shape=jax.ShapeDtypeStruct((LAT, ROWS, LA...  3.29 us
    ppermute x4, waiting for transfers between devices, shift(): return lax.ppermute(x, 'kpt', [(i, (i + 2 * step) % 16) for i in range(16)])  2.48 us
  transfers between devices with their start and end apart: 8, of which 4 were waited for; matrix products, arithmetic and copies ran while one was open for 2% of the time, Pallas kernels for 2%

profile of v5, /device:TPU:1, one launch (start us, length us, event | category | flops | bytes accessed | tf_op | source)
XLA Modules:
  0.0 66.6 jit_solution(3590852400314641593)
XLA Ops:
  0.7 3.3 %rotate.1 = bf16[16,64,768]{2,1,0:T(8,128)(2,1)} custom-call(f32[2,3]{1,0:T(2,128)} %qp_hbm.1, s32[1,3]{1,0:T(1,128)} %rv_hbm.1, s32[1,1]{1,0:T(1,128)} %bitcast.9.rw_hbm, bf16[2,2,48,48]{3,2,1,0:T(8,128)(2,1)} %rot_hbm.1, bf16[2,1,16,12288]{3,2,1,0:T(8,128)(2,1)} %coarse_hbm.1), custom_call_target="tpu_custom_call" | custom-call | tf_op jit(solution)/shard_map/rotate/pallas_call | solution.py:255
  3.9 0.0 copy-start.5
  4.0 0.0 copy-start.1
  4.0 0.0 copy-start
  4.0 0.0 copy-start.3
  4.0 0.0 copy-start.2
  4.0 7.7 %all-to-all-start = ((bf16[16,64,768]{2,1,0:T(8,128)(2,1)}), bf16[16,64,768]{2,1,0:T(8,128)(2,1)S(1)}, u32[]{:S(2)}, u32[]{:S(2)}) async-start(bf16[16,64,768]{2,1,0:T(8,128)(2,1)} %rotate.1), calls=%async_computation | async-start | bytes 3145728 | tf_op jit(solution)/shard_map/all_to_all | solution.py:274
  11.7 0.0 copy-start.4
  11.8 0.0 copy-start.6
  11.8 0.0 copy-done.5
  11.8 0.1 copy.20.kp_ref
  11.9 0.1 pad.2.clone
  12.0 0.0 copy-done.1
  12.0 0.1 copy.21.u_ref
  12.1 0.0 copy-done
  12.1 0.3 copy.18
  12.4 0.1 reshape.10
  12.5 0.1 copy.22.uq_ref
  12.6 0.0 copy-done.3
  12.6 0.1 copy.23.mk_ref
  12.7 0.0 copy-done.2
  12.7 0.1 copy.19
  12.8 0.0 copy-done.4
  12.8 0.0 copy-done.6
  12.8 0.1 add_add_fusion.rv_ref
  12.9 21.7 %all-to-all-done.x_ref = bf16[16,64,768]{2,1,0:T(8,128)(2,1)S(1)} async-done(((bf16[16,64,768]{2,1,0:T(8,128)(2,1)}), bf16[16,64,768]{2,1,0:T(8,128)(2,1)S(1)}, u32[]{:S(2)}, u32[]{:S(2)}) %all-to-all-start) | async-done | bytes 1572896 | tf_op jit(solution)/shard_map/all_to_all | solution.py:274
  34.6 0.2 add_up.1.own_ref
  34.8 4.4 %collective-permute-start = (bf16[64,768]{1,0:T(8,128)(2,1)S(1)}, bf16[64,768]{1,0:T(8,128)(2,1)S(1)}, u32[]{:S(2)}, u32[]{:S(2)}) collective-permute-start(bf16[64,768]{1,0:T(8,128)(2,1)S(1)} %add_up.1.own_ref), channel_id=1, source_target_pairs={{0,6},{1,7},{2,8},{3,9},{4,10},{5,11},{6,12},{7,13},{8,14},{9,15},... | collective-permute-start | bytes 294920 | tf_op jit(solution)/shard_map/ppermute | solution.py:312
  39.2 2.2 %collective-permute-start.1 = (bf16[64,768]{1,0:T(8,128)(2,1)S(1)}, bf16[64,768]{1,0:T(8,128)(2,1)S(1)}, u32[]{:S(2)}, u32[]{:S(2)}) collective-permute-start(bf16[64,768]{1,0:T(8,128)(2,1)S(1)} %add_up.1.own_ref), channel_id=1, source_target_pairs={{0,10},{1,11},{2,12},{3,13},{4,14},{5,15},{6,0},{7,1},{8,2},{9,3},... | collective-permute-start | bytes 294920 | tf_op jit(solution)/shard_map/ppermute | solution.py:312
  41.5 0.1 pad_add_fusion.at_ref
  41.5 1.3 %prep.1 = (bf16[128,512]{1,0:T(8,128)(2,1)S(1)}, f32[2,16,16,128]{3,2,1,0:T(8,128)S(1)}, f32[2,16,16,128]{3,2,1,0:T(8,128)S(1)}) custom-call(s32[2]{0:T(128)S(1)} %pad_add_fusion.at_ref, f32[64,3]{1,0:T(8,128)S(1)} %copy.20.kp_ref, s32[8,256]{1,0:T(8,128)S(1)} %add_add_fusion.rv_ref, bf16[2,64,256]{2,1,0:T(8,128)(2,1)S(1)} %copy.21.u_ref, ...), custom_call_target="tpu_custom_call" | custom-call | tf_op jit(solution)/shard_map/prep/pallas_call | solution.py:281
  42.8 0.8 %collective-permute-done.up_ref = bf16[64,768]{1,0:T(8,128)(2,1)S(1)} collective-permute-done((bf16[64,768]{1,0:T(8,128)(2,1)S(1)}, bf16[64,768]{1,0:T(8,128)(2,1)S(1)}, u32[]{:S(2)}, u32[]{:S(2)}) %collective-permute-start) | collective-permute-done | bytes 98336 | tf_op jit(solution)/shard_map/ppermute | solution.py:312
  43.6 1.7 %collective-permute-done.1.down_ref = bf16[64,768]{1,0:T(8,128)(2,1)S(1)} collective-permute-done((bf16[64,768]{1,0:T(8,128)(2,1)S(1)}, bf16[64,768]{1,0:T(8,128)(2,1)S(1)}, u32[]{:S(2)}, u32[]{:S(2)}) %collective-permute-start.1) | collective-permute-done | bytes 98336 | tf_op jit(solution)/shard_map/ppermute | solution.py:312
  45.3 5.1 %collective-permute-start.2 = (bf16[192,768]{1,0:T(8,128)(2,1)S(1)}, bf16[192,768]{1,0:T(8,128)(2,1)S(1)}, u32[]{:S(2)}, u32[]{:S(2)}) collective-permute-start(bf16[192,768]{1,0:T(8,128)(2,1)S(1)} %get-tuple-element.11.refs_0_), channel_id=1, source_target_pairs={{0,2},{1,3},{2,4},{3,5},{4,6},{5,7},{6,8},{7,9},{8,10},{9,11},{10,... | collective-permute-start | bytes 884744 | tf_op jit(solution)/shard_map/ppermute | solution.py:312
  50.4 0.0 collective-permute-start.3
  50.4 4.0 %collective-permute-start.4 = (bf16[192,768]{1,0:T(8,128)(2,1)S(1)}, bf16[192,768]{1,0:T(8,128)(2,1)S(1)}, u32[]{:S(2)}, u32[]{:S(2)}) collective-permute-start(bf16[192,768]{1,0:T(8,128)(2,1)S(1)} %get-tuple-element.11.refs_0_), channel_id=1, source_target_pairs={{0,1},{1,0},{2,3},{3,2},{4,5},{5,4},{6,7},{7,6},{8,9},{9,8},{10,11... | collective-permute-start | bytes 884744 | tf_op jit(solution)/shard_map/ppermute | solution.py:315
  54.4 0.0 collective-permute-done.2.refs_1_
  54.4 4.4 %collective-permute-start.5 = (bf16[192,768]{1,0:T(8,128)(2,1)S(1)}, bf16[192,768]{1,0:T(8,128)(2,1)S(1)}, u32[]{:S(2)}, u32[]{:S(2)}) collective-permute-start(bf16[192,768]{1,0:T(8,128)(2,1)S(1)} %collective-permute-done.2.refs_1_), channel_id=1, source_target_pairs={{0,1},{1,0},{2,3},{3,2},{4,5},{5,4},{6,7},{7,6},{8,9},{9,8},{10,11... | collective-permute-start | bytes 884744 | tf_op jit(solution)/shard_map/ppermute | solution.py:315
  58.8 0.0 collective-permute-done.3.refs_2_
  58.8 1.3 %collective-permute-start.6 = (bf16[128,768]{1,0:T(8,128)(2,1)S(1)}, bf16[128,768]{1,0:T(8,128)(2,1)S(1)}, u32[]{:S(2)}, u32[]{:S(2)}) collective-permute-start(bf16[128,768]{1,0:T(8,128)(2,1)S(1)} %collective-permute-done.3.refs_2_), channel_id=1, source_target_pairs={{0,1},{1,0},{2,3},{3,2},{4,5},{5,4},{6,7},{7,6},{8,9},{9,8},{10,11... | collective-permute-start | bytes 589832 | tf_op jit(solution)/shard_map/ppermute | solution.py:315
  60.1 0.0 collective-permute-done.4.refs_3_
  60.1 1.1 %collective-permute-done.6.refs_5_ = bf16[128,768]{1,0:T(8,128)(2,1)S(1)} collective-permute-done((bf16[128,768]{1,0:T(8,128)(2,1)S(1)}, bf16[128,768]{1,0:T(8,128)(2,1)S(1)}, u32[]{:S(2)}, u32[]{:S(2)}) %collective-permute-start.6) | collective-permute-done | bytes 196640 | tf_op jit(solution)/shard_map/ppermute | solution.py:315
  61.2 0.0 collective-permute-done.5.refs_4_
  61.2 5.4 %couple.1 = bf16[2,64,2,768]{3,2,1,0:T(2,128)(2,1)} custom-call(bf16[192,768]{1,0:T(8,128)(2,1)S(1)} %get-tuple-element.11.refs_0_, bf16[192,768]{1,0:T(8,128)(2,1)S(1)} %collective-permute-done.2.refs_1_, bf16[128,768]{1,0:T(8,128)(2,1)S(1)} %collective-permute-done.3.refs_2_, bf16[192,768]{1,0:T(8,128)(2,1)S(1)} %collective-permute-done.4.refs_3_, ...), custom_call_target="tpu_custom_call" | custom-call | tf_op jit(solution)/shard_map/couple/pallas_call | solution.py:335
  (2 shorter events, 0.0 us)
Async XLA Ops:
  3.9 7.8 %copy-start.5 = (f32[64,3]{0,1:T(4,128)S(1)}, f32[64,3]{0,1:T(4,128)}, u32[]{:S(2)}) copy-start(f32[64,3]{0,1:T(4,128)} %param.18) | copy-start | bytes 2308
  4.0 8.0 %copy-start.1 = (bf16[2,64,16,16]{1,3,2,0:T(8,128)(2,1)S(1)}, bf16[2,64,16,16]{1,3,2,0:T(8,128)(2,1)}, u32[]{:S(2)}) copy-start(bf16[2,64,16,16]{1,3,2,0:T(8,128)(2,1)} %param.20) | copy-start | bytes 196612
  4.0 8.1 %copy-start = (bf16[2,2,64,16,16]{2,4,3,1,0:T(8,128)(2,1)S(1)}, bf16[2,2,64,16,16]{2,4,3,1,0:T(8,128)(2,1)}, u32[]{:S(2)}) copy-start(bf16[2,2,64,16,16]{2,4,3,1,0:T(8,128)(2,1)} %param.21) | copy-start | bytes 393220
  4.0 8.7 %copy-start.3 = (s32[64,16]{0,1:T(8,128)S(1)}, s32[64,16]{0,1:T(8,128)}, u32[]{:S(2)}) copy-start(s32[64,16]{0,1:T(8,128)} %param.22) | copy-start | bytes 12292
  4.0 8.7 %copy-start.2 = (s32[2,64,16]{1,2,0:T(8,128)S(1)}, s32[2,64,16]{1,2,0:T(8,128)}, u32[]{:S(2)}) copy-start(s32[2,64,16]{1,2,0:T(8,128)} %param.23) | copy-start | bytes 24580
  4.0 30.6 %all-to-all-start = ((bf16[16,64,768]{2,1,0:T(8,128)(2,1)}), bf16[16,64,768]{2,1,0:T(8,128)(2,1)S(1)}, u32[]{:S(2)}, u32[]{:S(2)}) async-start(bf16[16,64,768]{2,1,0:T(8,128)(2,1)} %rotate.1), calls=%async_computation | async-start | bytes 3145728 | tf_op jit(solution)/shard_map/all_to_all | solution.py:274
  11.7 1.1 %copy-start.4 = (s32[256,3]{0,1:T(4,128)S(1)}, s32[256,3]{0,1:T(4,128)}, u32[]{:S(2)}) copy-start(s32[256,3]{0,1:T(4,128)} %param.15) | copy-start | bytes 9220
  11.8 1.1 %copy-start.6 = (s32[256]{0:T(256)S(1)}, s32[256]{0:T(256)}, u32[]{:S(2)}) copy-start(s32[256]{0:T(256)} %param.16) | copy-start | bytes 3076
  34.8 8.8 %collective-permute-start = (bf16[64,768]{1,0:T(8,128)(2,1)S(1)}, bf16[64,768]{1,0:T(8,128)(2,1)S(1)}, u32[]{:S(2)}, u32[]{:S(2)}) collective-permute-start(bf16[64,768]{1,0:T(8,128)(2,1)S(1)} %add_up.1.own_ref), channel_id=1, source_target_pairs={{0,6},{1,7},{2,8},{3,9},{4,10},{5,11},{6,12},{7,13},{8,14},{9,15},... | collective-permute-start | bytes 294920 | tf_op jit(solution)/shard_map/ppermute | solution.py:312
  39.2 6.0 %collective-permute-start.1 = (bf16[64,768]{1,0:T(8,128)(2,1)S(1)}, bf16[64,768]{1,0:T(8,128)(2,1)S(1)}, u32[]{:S(2)}, u32[]{:S(2)}) collective-permute-start(bf16[64,768]{1,0:T(8,128)(2,1)S(1)} %add_up.1.own_ref), channel_id=1, source_target_pairs={{0,10},{1,11},{2,12},{3,13},{4,14},{5,15},{6,0},{7,1},{8,2},{9,3},... | collective-permute-start | bytes 294920 | tf_op jit(solution)/shard_map/ppermute | solution.py:312
  45.3 9.1 %collective-permute-start.2 = (bf16[192,768]{1,0:T(8,128)(2,1)S(1)}, bf16[192,768]{1,0:T(8,128)(2,1)S(1)}, u32[]{:S(2)}, u32[]{:S(2)}) collective-permute-start(bf16[192,768]{1,0:T(8,128)(2,1)S(1)} %get-tuple-element.11.refs_0_), channel_id=1, source_target_pairs={{0,2},{1,3},{2,4},{3,5},{4,6},{5,7},{6,8},{7,9},{8,10},{9,11},{10,... | collective-permute-start | bytes 884744 | tf_op jit(solution)/shard_map/ppermute | solution.py:312
  50.4 8.4 %collective-permute-start.3 = (bf16[128,768]{1,0:T(8,128)(2,1)S(1)}, bf16[128,768]{1,0:T(8,128)(2,1)S(1)}, u32[]{:S(2)}, u32[]{:S(2)}) collective-permute-start(bf16[128,768]{1,0:T(8,128)(2,1)S(1)} %get-tuple-element.12), channel_id=1, source_target_pairs={{0,14},{1,15},{2,0},{3,1},{4,2},{5,3},{6,4},{7,5},{8,6},{9,7},{10,... | collective-permute-start | bytes 589832 | tf_op jit(solution)/shard_map/ppermute | solution.py:312
  50.4 9.7 %collective-permute-start.4 = (bf16[192,768]{1,0:T(8,128)(2,1)S(1)}, bf16[192,768]{1,0:T(8,128)(2,1)S(1)}, u32[]{:S(2)}, u32[]{:S(2)}) collective-permute-start(bf16[192,768]{1,0:T(8,128)(2,1)S(1)} %get-tuple-element.11.refs_0_), channel_id=1, source_target_pairs={{0,1},{1,0},{2,3},{3,2},{4,5},{5,4},{6,7},{7,6},{8,9},{9,8},{10,11... | collective-permute-start | bytes 884744 | tf_op jit(solution)/shard_map/ppermute | solution.py:315
  54.4 6.7 %collective-permute-start.5 = (bf16[192,768]{1,0:T(8,128)(2,1)S(1)}, bf16[192,768]{1,0:T(8,128)(2,1)S(1)}, u32[]{:S(2)}, u32[]{:S(2)}) collective-permute-start(bf16[192,768]{1,0:T(8,128)(2,1)S(1)} %collective-permute-done.2.refs_1_), channel_id=1, source_target_pairs={{0,1},{1,0},{2,3},{3,2},{4,5},{5,4},{6,7},{7,6},{8,9},{9,8},{10,11... | collective-permute-start | bytes 884744 | tf_op jit(solution)/shard_map/ppermute | solution.py:315
  58.8 2.3 %collective-permute-start.6 = (bf16[128,768]{1,0:T(8,128)(2,1)S(1)}, bf16[128,768]{1,0:T(8,128)(2,1)S(1)}, u32[]{:S(2)}, u32[]{:S(2)}) collective-permute-start(bf16[128,768]{1,0:T(8,128)(2,1)S(1)} %collective-permute-done.3.refs_2_), channel_id=1, source_target_pairs={{0,1},{1,0},{2,3},{3,2},{4,5},{5,4},{6,7},{7,6},{8,9},{9,8},{10,11... | collective-permute-start | bytes 589832 | tf_op jit(solution)/shard_map/ppermute | solution.py:315

commit v6 on v5

--- a/solution.py
+++ b/solution.py
@@ -133,32 +133,33 @@
     dims = (((0,), (0,)), ((), ()))
     mk = lax.dot_general(mk_ref[...].astype(f32).astype(bf16), spread, dims, preferred_element_type=f32)
     mq = lax.dot_general(mq_ref[...].astype(f32).astype(bf16), place, dims, preferred_element_type=f32)
-    for part in range(2):
-        ut = lax.dot_general(u_ref[part], spread, dims, preferred_element_type=f32)
-        lt = lax.dot_general(uq_ref[part], place, dims, preferred_element_type=f32)
+    ur, ui = (
+        lax.dot_general(u_ref[part], spread, dims, preferred_element_type=f32) for part in range(2)
+    )
+    lr, li = (
+        lax.dot_general(uq_ref[part], place, dims, preferred_element_type=f32) for part in range(2)
+    )
+    for i, (u, left) in enumerate(((ur, lr), (ui - ur, -(li + lr)), (ur + ui, lr - li))):
         for b in range(BANDS):
-            uo_ref[part, b] = ut[b * 16:(b + 1) * 16] * mk
-            lo_ref[part, b] = lt[b * 16:(b + 1) * 16] * mq
-
-
-def pack_body(own_ref, up_ref, down_ref, order_ref, three_ref, two_ref):
-    for i, ref in enumerate((own_ref, up_ref, down_ref)):
-        value = ref[...]
-        three_ref[i * ROWS:(i + 1) * ROWS, :] = value
-        if i < 2:
-            two_ref[i * ROWS:(i + 1) * ROWS, :] = value
-
-
-PLACE = ((0, 0), (1, 0), (2, 1), (0, 1), (1, 1), (0, 2), (1, 2), (2, 0))
+            uo_ref[i, b] = u[b * 16:(b + 1) * 16] * mk
+            lo_ref[i, b] = left[b * 16:(b + 1) * 16] * mq
+
+
+def pack_body(own_ref, across_ref, order_ref, out_ref):
+    out_ref[0:ROWS, :] = own_ref[...]
+    out_ref[ROWS:2 * ROWS, :] = across_ref[...]
+
+
+PLACE = ((0, 0), (3, 0), (1, 0), (4, 1), (0, 1), (3, 1), (2, 0), (4, 0))
 
 
 def couple_body(*refs):
-    ph_ref, u_ref, l_ref, out_ref, y_ref, bl_ref, h_ref, r_ref = refs[6:]
+    ph_ref, u_ref, l_ref, out_ref, y_ref, bl_ref, h_ref, r_ref = refs[10:]
     ph = ph_ref[...]
     for q in range(NQ):
         x = jnp.concatenate(
             [
-                refs[side * 3 + i][j * ROWS + q * 32:j * ROWS + (q + 1) * 32, :]
+                refs[side * 5 + i][j * ROWS + q * 32:j * ROWS + (q + 1) * 32, :]
                 for side in range(2)
                 for i, j in PLACE
             ],
@@ -170,27 +171,29 @@
                 y_ref[part, v, pl.ds(q, KPTS, stride=2), :] = t[
                     part * KPTS:(part + 1) * KPTS, v * 128:(v + 1) * 128
                 ]
-    for part in range(2):
-        for v in range(2 * PER):
-            bl_ref[part, v * 128:(v + 1) * 128, :] = y_ref[part, v].T.astype(bf16).astype(f32)
+    for v in range(2 * PER):
+        rows = slice(v * 128, (v + 1) * 128)
+        xr, xi = (y_ref[part, v].T.astype(bf16).astype(f32) for part in range(2))
+        bl_ref[0, rows, :] = xr + xi
+        bl_ref[1, rows, :] = xr
+        bl_ref[2, rows, :] = xi
 
     group = 4
 
     def first(i, _):
         base = i * group * BANDS
-        accr = [jnp.zeros((16, 128), f32) for _ in range(group)]
-        acci = [jnp.zeros((16, 128), f32) for _ in range(group)]
+        acc = [[jnp.zeros((16, 128), f32) for _ in range(3)] for _ in range(group)]
         for b in range(BANDS):
-            ur = u_ref[0, b]
-            ui = u_ref[1, b]
+            us = [u_ref[t, b] for t in range(3)]
             for s in range(group):
-                xr = bl_ref[0, pl.ds(base + s * BANDS + b, 1), :]
-                xi = bl_ref[1, pl.ds(base + s * BANDS + b, 1), :]
-                accr[s] = accr[s] + (xr * ur - xi * ui)
-                acci[s] = acci[s] + (xr * ui + xi * ur)
+                for t in range(3):
+                    acc[s][t] = acc[s][t] + bl_ref[t, pl.ds(base + s * BANDS + b, 1), :] * us[t]
         for s in range(group):
-            h_ref[0, i * group + s] = accr[s].astype(bf16).astype(f32)
-            h_ref[1, i * group + s] = acci[s].astype(bf16).astype(f32)
+            hr = (acc[s][0] - acc[s][2]).astype(bf16).astype(f32)
+            hi = (acc[s][0] + acc[s][1]).astype(bf16).astype(f32)
+            h_ref[0, i * group + s] = hr + hi
+            h_ref[1, i * group + s] = hr
+            h_ref[2, i * group + s] = hi
         return 0
 
     lax.fori_loop(0, PER * BANDS // group, first, 0)
@@ -200,19 +203,15 @@
     def second(i, _):
         n = i // per
         c0 = (i - n * per) * group
-        accr = [jnp.zeros((16, 128), f32) for _ in range(group)]
-        acci = [jnp.zeros((16, 128), f32) for _ in range(group)]
+        acc = [[jnp.zeros((16, 128), f32) for _ in range(3)] for _ in range(group)]
         for a in range(BANDS):
-            hr = h_ref[0, n * BANDS + a]
-            hi = h_ref[1, n * BANDS + a]
+            hs = [h_ref[t, n * BANDS + a] for t in range(3)]
             for s in range(group):
-                lr = l_ref[0, a, pl.ds(c0 + s, 1), :]
-                li = l_ref[1, a, pl.ds(c0 + s, 1), :]
-                accr[s] = accr[s] + (lr * hr + li * hi)
-                acci[s] = acci[s] + (lr * hi - li * hr)
+                for t in range(3):
+                    acc[s][t] = acc[s][t] + l_ref[t, a, pl.ds(c0 + s, 1), :] * hs[t]
         for s in range(group):
-            r_ref[0, i * group + s] = accr[s]
-            r_ref[1, i * group + s] = acci[s]
+            r_ref[0, i * group + s] = acc[s][0] - acc[s][2]
+            r_ref[1, i * group + s] = acc[s][0] + acc[s][1]
         return 0
 
     lax.fori_loop(0, PER * per, second, 0)
@@ -282,8 +281,8 @@
         prep_body,
         out_shape=(
             jax.ShapeDtypeStruct((2 * KPTS, 512), bf16),
-            jax.ShapeDtypeStruct((2, BANDS, BANDS, 128), f32),
-            jax.ShapeDtypeStruct((2, BANDS, BANDS, 128), f32),
+            jax.ShapeDtypeStruct((3, BANDS, BANDS, 128), f32),
+            jax.ShapeDtypeStruct((3, BANDS, BANDS, 128), f32),
         ),
         in_specs=[smem()] + [vmem()] * 6,
         out_specs=(vmem(),) * 3,
@@ -314,33 +313,27 @@
     def swap(x):
         return lax.ppermute(x, "kpt", [(i, i ^ 1) for i in range(16)])
 
-    up = shift(own, 3)
-    down = shift(own, -3)
-    packed, pair = pl.pallas_call(
+    across = shift(own, 4)
+    packed = pl.pallas_call(
         pack_body,
-        out_shape=(
-            jax.ShapeDtypeStruct((3 * ROWS, LANES), bf16),
-            jax.ShapeDtypeStruct((2 * ROWS, LANES), bf16),
-        ),
-        in_specs=[vmem()] * 3 + [pl.BlockSpec(memory_space=pl.ANY)],
-        out_specs=(vmem(), vmem()),
+        out_shape=jax.ShapeDtypeStruct((2 * ROWS, LANES), bf16),
+        in_specs=[vmem()] * 2 + [pl.BlockSpec(memory_space=pl.ANY)],
+        out_specs=vmem(),
         compiler_params=params(),
         name="pack",
-    )(own, up, down, phase)
-    plus = shift(packed, 1)
-    minus = shift(pair, -1)
-    near = [packed, plus, minus]
+    )(own, across, phase)
+    near = [packed, shift(own, 2), shift(own, -2), shift(packed, 1), shift(packed, -1)]
     far = [swap(x) for x in near]
 
     result = pl.pallas_call(
         couple_body,
         out_shape=jax.ShapeDtypeStruct((2, KPTS, NQ, LANES), bf16),
-        in_specs=[vmem()] * 9,
+        in_specs=[vmem()] * 13,
         out_specs=vmem(),
         scratch_shapes=[
             pltpu.VMEM((2, 2 * PER, 128, 128), f32),
-            pltpu.VMEM((2, LANES, 128), f32),
-            pltpu.VMEM((2, PER * BANDS, BANDS, 128), f32),
+            pltpu.VMEM((3, LANES, 128), f32),
+            pltpu.VMEM((3, PER * BANDS, BANDS, 128), f32),
             pltpu.VMEM((2, PER * BANDS, BANDS, 128), f32),
         ],
         compiler_params=params(),

time: 66.8 us -> 68.3 us (1.022)
  starting transfers between devices: 29.2 us -> 33 us
  waiting for transfers between devices: 25.3 us -> 23.4 us
    ppermute x4 -> x5, starting transfers between devices: 11.8 us -> 14.7 us  [shift(): return lax.ppermute(x, 'kpt', [(i, (i + 2 * step) % 16) for i in range(16)])]
    ppermute x4 -> x5, waiting for transfers between devices: 2.48 us -> 0.76 us  [shift(): return lax.ppermute(x, 'kpt', [(i, (i + 2 * step) % 16) for i in range(16)])]
    ppermute x3 -> x5, starting transfers between devices: 9.67 us -> 10.6 us  [swap(): return lax.ppermute(x, 'kpt', [(i, i ^ 1) for i in range(16)])]
  transfers between devices with their start and end apart: 8 -> 11, of which waited for: 4 -> 3; matrix products, arithmetic and copies ran while one was open for 2% -> 2% of each run, Pallas kernels for 2% -> 2%
where the time goes in v6:
time: 68.3 us; the launch traced here: 68.1 us
  starting transfers between devices  33 us (48%)
  waiting for transfers between devices  23.4 us (34%)
  Pallas kernels  9.68 us (14%)
  local copies, waits for them, and re-layouts  1.01 us (1%)
  between operations  0.83 us (1%)
    all_to_all x1, waiting for transfers between devices, per_device(): parts = lax.all_to_all(rotated, 'lat', 0, 0, tiled=True)  21.7 us
    ppermute x5, starting transfers between devices, shift(): return lax.ppermute(x, 'kpt', [(i, (i + 2 * step) % 16) for i in range(16)])  14.7 us
    ppermute x5, starting transfers between devices, swap(): return lax.ppermute(x, 'kpt', [(i, i ^ 1) for i in range(16)])  10.6 us
    all_to_all x1, starting transfers between devices, per_device(): parts = lax.all_to_all(rotated, 'lat', 0, 0, tiled=True)  7.73 us
    pallas_call x1, Pallas kernels, per_device(): pl.pallas_call(couple_body, out_shape=jax.ShapeDtypeStruct((2, KPTS, NQ,...  4.89 us
    pallas_call x1, Pallas kernels, per_device(): pl.pallas_call(rotate_body, out_shape=jax.ShapeDtypeStruct((LAT, ROWS, LA...  3.29 us
  transfers between devices with their start and end apart: 11, of which 3 were waited for; matrix products, arithmetic and copies ran while one was open for 2% of the time, Pallas kernels for 2%

profile of v6, /device:TPU:1, one launch (start us, length us, event | category | flops | bytes accessed | tf_op | source)
XLA Modules:
  0.0 68.1 jit_solution(4271168652913470642)
XLA Ops:
  0.7 3.3 %rotate.1 = bf16[16,64,768]{2,1,0:T(8,128)(2,1)} custom-call(f32[2,3]{1,0:T(2,128)} %qp_hbm.1, s32[1,3]{1,0:T(1,128)} %rv_hbm.1, s32[1,1]{1,0:T(1,128)} %bitcast.9.rw_hbm, bf16[2,2,48,48]{3,2,1,0:T(8,128)(2,1)} %rot_hbm.1, bf16[2,1,16,12288]{3,2,1,0:T(8,128)(2,1)} %coarse_hbm.1), custom_call_target="tpu_custom_call" | custom-call | tf_op jit(solution)/shard_map/rotate/pallas_call | solution.py:254
  4.0 0.0 copy-start.5
  4.0 0.0 copy-start.1
  4.0 0.0 copy-start
  4.0 0.0 copy-start.3
  4.0 0.0 copy-start.2
  4.0 7.7 %all-to-all-start = ((bf16[16,64,768]{2,1,0:T(8,128)(2,1)}), bf16[16,64,768]{2,1,0:T(8,128)(2,1)S(1)}, u32[]{:S(2)}, u32[]{:S(2)}) async-start(bf16[16,64,768]{2,1,0:T(8,128)(2,1)} %rotate.1), calls=%async_computation | async-start | bytes 3145728 | tf_op jit(solution)/shard_map/all_to_all | solution.py:273
  11.7 0.0 copy-start.4
  11.8 0.0 copy-start.6
  11.8 0.0 copy-done.5
  11.8 0.1 copy.20.kp_ref
  11.9 0.1 pad.2.clone
  12.0 0.0 copy-done.1
  12.0 0.1 copy.21.u_ref
  12.1 0.0 copy-done
  12.1 0.3 copy.18
  12.4 0.1 reshape.10
  12.5 0.1 copy.22.uq_ref
  12.6 0.0 copy-done.3
  12.7 0.1 copy.23.mk_ref
  12.7 0.0 copy-done.2
  12.7 0.1 copy.19
  12.8 0.0 copy-done.4
  12.8 0.0 copy-done.6
  12.8 0.1 add_add_fusion.rv_ref
  12.9 21.7 %all-to-all-done.x_ref = bf16[16,64,768]{2,1,0:T(8,128)(2,1)S(1)} async-done(((bf16[16,64,768]{2,1,0:T(8,128)(2,1)}), bf16[16,64,768]{2,1,0:T(8,128)(2,1)S(1)}, u32[]{:S(2)}, u32[]{:S(2)}) %all-to-all-start) | async-done | bytes 1572896 | tf_op jit(solution)/shard_map/all_to_all | solution.py:273
  34.6 0.2 add_up.1.own_ref
  34.8 7.0 %collective-permute-start = (bf16[64,768]{1,0:T(8,128)(2,1)S(1)}, bf16[64,768]{1,0:T(8,128)(2,1)S(1)}, u32[]{:S(2)}, u32[]{:S(2)}) collective-permute-start(bf16[64,768]{1,0:T(8,128)(2,1)S(1)} %add_up.1.own_ref), channel_id=1, source_target_pairs={{0,8},{1,9},{2,10},{3,11},{4,12},{5,13},{6,14},{7,15},{8,0},{9,1},... | collective-permute-start | bytes 294920 | tf_op jit(solution)/shard_map/ppermute | solution.py:311
  41.9 0.1 pad_add_fusion.at_ref
  41.9 1.3 %prep.1 = (bf16[128,512]{1,0:T(8,128)(2,1)S(1)}, f32[3,16,16,128]{3,2,1,0:T(8,128)S(1)}, f32[3,16,16,128]{3,2,1,0:T(8,128)S(1)}) custom-call(s32[2]{0:T(128)S(1)} %pad_add_fusion.at_ref, f32[64,3]{1,0:T(8,128)S(1)} %copy.20.kp_ref, s32[8,256]{1,0:T(8,128)S(1)} %add_add_fusion.rv_ref, bf16[2,64,256]{2,1,0:T(8,128)(2,1)S(1)} %copy.21.u_ref, ...), custom_call_target="tpu_custom_call" | custom-call | tf_op jit(solution)/shard_map/prep/pallas_call | solution.py:280
  43.2 0.8 %collective-permute-done.across_ref = bf16[64,768]{1,0:T(8,128)(2,1)S(1)} collective-permute-done((bf16[64,768]{1,0:T(8,128)(2,1)S(1)}, bf16[64,768]{1,0:T(8,128)(2,1)S(1)}, u32[]{:S(2)}, u32[]{:S(2)}) %collective-permute-start) | collective-permute-done | bytes 98336 | tf_op jit(solution)/shard_map/ppermute | solution.py:311
  44.0 0.7 %collective-permute-start.3 = (bf16[128,768]{1,0:T(8,128)(2,1)S(1)}, bf16[128,768]{1,0:T(8,128)(2,1)S(1)}, u32[]{:S(2)}, u32[]{:S(2)}) collective-permute-start(bf16[128,768]{1,0:T(8,128)(2,1)S(1)} %pack.1.refs_0_), channel_id=1, source_target_pairs={{0,2},{1,3},{2,4},{3,5},{4,6},{5,7},{6,8},{7,9},{8,10},{9,11},{10,... | collective-permute-start | bytes 589832 | tf_op jit(solution)/shard_map/ppermute | solution.py:311
  44.7 3.5 %collective-permute-start.4 = (bf16[128,768]{1,0:T(8,128)(2,1)S(1)}, bf16[128,768]{1,0:T(8,128)(2,1)S(1)}, u32[]{:S(2)}, u32[]{:S(2)}) collective-permute-start(bf16[128,768]{1,0:T(8,128)(2,1)S(1)} %pack.1.refs_0_), channel_id=1, source_target_pairs={{0,14},{1,15},{2,0},{3,1},{4,2},{5,3},{6,4},{7,5},{8,6},{9,7},{10,... | collective-permute-start | bytes 589832 | tf_op jit(solution)/shard_map/ppermute | solution.py:311
  48.1 0.0 collective-permute-start.1
  48.1 3.6 %collective-permute-start.2 = (bf16[64,768]{1,0:T(8,128)(2,1)S(1)}, bf16[64,768]{1,0:T(8,128)(2,1)S(1)}, u32[]{:S(2)}, u32[]{:S(2)}) collective-permute-start(bf16[64,768]{1,0:T(8,128)(2,1)S(1)} %add_up.1.own_ref), channel_id=1, source_target_pairs={{0,12},{1,13},{2,14},{3,15},{4,0},{5,1},{6,2},{7,3},{8,4},{9,5},{1... | collective-permute-start | bytes 294920 | tf_op jit(solution)/shard_map/ppermute | solution.py:311
  51.7 4.5 %collective-permute-start.5 = (bf16[128,768]{1,0:T(8,128)(2,1)S(1)}, bf16[128,768]{1,0:T(8,128)(2,1)S(1)}, u32[]{:S(2)}, u32[]{:S(2)}) collective-permute-start(bf16[128,768]{1,0:T(8,128)(2,1)S(1)} %pack.1.refs_0_), channel_id=1, source_target_pairs={{0,1},{1,0},{2,3},{3,2},{4,5},{5,4},{6,7},{7,6},{8,9},{9,8},{10,11... | collective-permute-start | bytes 589832 | tf_op jit(solution)/shard_map/ppermute | solution.py:314
  56.3 0.0 collective-permute-done.3.refs_3_
  56.3 0.2 collective-permute-start.8
  56.5 0.0 collective-permute-done.4.refs_4_
  56.5 0.3 collective-permute-start.9
  56.8 0.0 collective-permute-done.1.refs_1_
  56.8 3.1 %collective-permute-start.6 = (bf16[64,768]{1,0:T(8,128)(2,1)S(1)}, bf16[64,768]{1,0:T(8,128)(2,1)S(1)}, u32[]{:S(2)}, u32[]{:S(2)}) collective-permute-start(bf16[64,768]{1,0:T(8,128)(2,1)S(1)} %collective-permute-done.1.refs_1_), channel_id=1, source_target_pairs={{0,1},{1,0},{2,3},{3,2},{4,5},{5,4},{6,7},{7,6},{8,9},{9,8},{10,11... | collective-permute-start | bytes 294920 | tf_op jit(solution)/shard_map/ppermute | solution.py:314
  59.9 0.0 collective-permute-done.2.refs_2_
  59.9 2.4 %collective-permute-start.7 = (bf16[64,768]{1,0:T(8,128)(2,1)S(1)}, bf16[64,768]{1,0:T(8,128)(2,1)S(1)}, u32[]{:S(2)}, u32[]{:S(2)}) collective-permute-start(bf16[64,768]{1,0:T(8,128)(2,1)S(1)} %collective-permute-done.2.refs_2_), channel_id=1, source_target_pairs={{0,1},{1,0},{2,3},{3,2},{4,5},{5,4},{6,7},{7,6},{8,9},{9,8},{10,11... | collective-permute-start | bytes 294920 | tf_op jit(solution)/shard_map/ppermute | solution.py:314
  62.3 0.0 collective-permute-done.6.refs_6_
  62.3 0.9 %collective-permute-done.7.refs_7_ = bf16[64,768]{1,0:T(8,128)(2,1)S(1)} collective-permute-done((bf16[64,768]{1,0:T(8,128)(2,1)S(1)}, bf16[64,768]{1,0:T(8,128)(2,1)S(1)}, u32[]{:S(2)}, u32[]{:S(2)}) %collective-permute-start.7) | collective-permute-done | bytes 98336 | tf_op jit(solution)/shard_map/ppermute | solution.py:314
  63.2 0.0 collective-permute-done.5.refs_5_
  63.2 0.0 collective-permute-done.8.refs_8_
  63.2 0.0 collective-permute-done.9.refs_9_
  63.3 4.9 %couple.1 = bf16[2,64,2,768]{3,2,1,0:T(2,128)(2,1)} custom-call(bf16[128,768]{1,0:T(8,128)(2,1)S(1)} %pack.1.refs_0_, bf16[64,768]{1,0:T(8,128)(2,1)S(1)} %collective-permute-done.1.refs_1_, bf16[64,768]{1,0:T(8,128)(2,1)S(1)} %collective-permute-done.2.refs_2_, bf16[128,768]{1,0:T(8,128)(2,1)S(1)} %collective-permute-done.3.refs_3_, ...), custom_call_target="tpu_custom_call" | custom-call | tf_op jit(solution)/shard_map/couple/pallas_call | solution.py:328
  (2 shorter events, 0.0 us)
Async XLA Ops:
  4.0 7.8 %copy-start.5 = (f32[64,3]{0,1:T(4,128)S(1)}, f32[64,3]{0,1:T(4,128)}, u32[]{:S(2)}) copy-start(f32[64,3]{0,1:T(4,128)} %param.18) | copy-start | bytes 2308
  4.0 8.0 %copy-start.1 = (bf16[2,64,16,16]{1,3,2,0:T(8,128)(2,1)S(1)}, bf16[2,64,16,16]{1,3,2,0:T(8,128)(2,1)}, u32[]{:S(2)}) copy-start(bf16[2,64,16,16]{1,3,2,0:T(8,128)(2,1)} %param.20) | copy-start | bytes 196612
  4.0 8.1 %copy-start = (bf16[2,2,64,16,16]{2,4,3,1,0:T(8,128)(2,1)S(1)}, bf16[2,2,64,16,16]{2,4,3,1,0:T(8,128)(2,1)}, u32[]{:S(2)}) copy-start(bf16[2,2,64,16,16]{2,4,3,1,0:T(8,128)(2,1)} %param.21) | copy-start | bytes 393220
  4.0 8.7 %copy-start.3 = (s32[64,16]{0,1:T(8,128)S(1)}, s32[64,16]{0,1:T(8,128)}, u32[]{:S(2)}) copy-start(s32[64,16]{0,1:T(8,128)} %param.22) | copy-start | bytes 12292
  4.0 8.7 %copy-start.2 = (s32[2,64,16]{1,2,0:T(8,128)S(1)}, s32[2,64,16]{1,2,0:T(8,128)}, u32[]{:S(2)}) copy-start(s32[2,64,16]{1,2,0:T(8,128)} %param.23) | copy-start | bytes 24580
  4.0 30.6 %all-to-all-start = ((bf16[16,64,768]{2,1,0:T(8,128)(2,1)}), bf16[16,64,768]{2,1,0:T(8,128)(2,1)S(1)}, u32[]{:S(2)}, u32[]{:S(2)}) async-start(bf16[16,64,768]{2,1,0:T(8,128)(2,1)} %rotate.1), calls=%async_computation | async-start | bytes 3145728 | tf_op jit(solution)/shard_map/all_to_all | solution.py:273
  11.7 1.1 %copy-start.4 = (s32[256,3]{0,1:T(4,128)S(1)}, s32[256,3]{0,1:T(4,128)}, u32[]{:S(2)}) copy-start(s32[256,3]{0,1:T(4,128)} %param.15) | copy-start | bytes 9220
  11.8 1.1 %copy-start.6 = (s32[256]{0:T(256)S(1)}, s32[256]{0:T(256)}, u32[]{:S(2)}) copy-start(s32[256]{0:T(256)} %param.16) | copy-start | bytes 3076
  34.8 9.1 %collective-permute-start = (bf16[64,768]{1,0:T(8,128)(2,1)S(1)}, bf16[64,768]{1,0:T(8,128)(2,1)S(1)}, u32[]{:S(2)}, u32[]{:S(2)}) collective-permute-start(bf16[64,768]{1,0:T(8,128)(2,1)S(1)} %add_up.1.own_ref), channel_id=1, source_target_pairs={{0,8},{1,9},{2,10},{3,11},{4,12},{5,13},{6,14},{7,15},{8,0},{9,1},... | collective-permute-start | bytes 294920 | tf_op jit(solution)/shard_map/ppermute | solution.py:311
  44.0 12.3 %collective-permute-start.3 = (bf16[128,768]{1,0:T(8,128)(2,1)S(1)}, bf16[128,768]{1,0:T(8,128)(2,1)S(1)}, u32[]{:S(2)}, u32[]{:S(2)}) collective-permute-start(bf16[128,768]{1,0:T(8,128)(2,1)S(1)} %pack.1.refs_0_), channel_id=1, source_target_pairs={{0,2},{1,3},{2,4},{3,5},{4,6},{5,7},{6,8},{7,9},{8,10},{9,11},{10,... | collective-permute-start | bytes 589832 | tf_op jit(solution)/shard_map/ppermute | solution.py:311
  44.7 11.8 %collective-permute-start.4 = (bf16[128,768]{1,0:T(8,128)(2,1)S(1)}, bf16[128,768]{1,0:T(8,128)(2,1)S(1)}, u32[]{:S(2)}, u32[]{:S(2)}) collective-permute-start(bf16[128,768]{1,0:T(8,128)(2,1)S(1)} %pack.1.refs_0_), channel_id=1, source_target_pairs={{0,14},{1,15},{2,0},{3,1},{4,2},{5,3},{6,4},{7,5},{8,6},{9,7},{10,... | collective-permute-start | bytes 589832 | tf_op jit(solution)/shard_map/ppermute | solution.py:311
  48.1 8.6 %collective-permute-start.1 = (bf16[64,768]{1,0:T(8,128)(2,1)S(1)}, bf16[64,768]{1,0:T(8,128)(2,1)S(1)}, u32[]{:S(2)}, u32[]{:S(2)}) collective-permute-start(bf16[64,768]{1,0:T(8,128)(2,1)S(1)} %add_up.1.own_ref), channel_id=1, source_target_pairs={{0,4},{1,5},{2,6},{3,7},{4,8},{5,9},{6,10},{7,11},{8,12},{9,13},{1... | collective-permute-start | bytes 294920 | tf_op jit(solution)/shard_map/ppermute | solution.py:311
  48.1 11.8 %collective-permute-start.2 = (bf16[64,768]{1,0:T(8,128)(2,1)S(1)}, bf16[64,768]{1,0:T(8,128)(2,1)S(1)}, u32[]{:S(2)}, u32[]{:S(2)}) collective-permute-start(bf16[64,768]{1,0:T(8,128)(2,1)S(1)} %add_up.1.own_ref), channel_id=1, source_target_pairs={{0,12},{1,13},{2,14},{3,15},{4,0},{5,1},{6,2},{7,3},{8,4},{9,5},{1... | collective-permute-start | bytes 294920 | tf_op jit(solution)/shard_map/ppermute | solution.py:311
  51.7 11.5 %collective-permute-start.5 = (bf16[128,768]{1,0:T(8,128)(2,1)S(1)}, bf16[128,768]{1,0:T(8,128)(2,1)S(1)}, u32[]{:S(2)}, u32[]{:S(2)}) collective-permute-start(bf16[128,768]{1,0:T(8,128)(2,1)S(1)} %pack.1.refs_0_), channel_id=1, source_target_pairs={{0,1},{1,0},{2,3},{3,2},{4,5},{5,4},{6,7},{7,6},{8,9},{9,8},{10,11... | collective-permute-start | bytes 589832 | tf_op jit(solution)/shard_map/ppermute | solution.py:314
  56.3 7.0 %collective-permute-start.8 = (bf16[128,768]{1,0:T(8,128)(2,1)S(1)}, bf16[128,768]{1,0:T(8,128)(2,1)S(1)}, u32[]{:S(2)}, u32[]{:S(2)}) collective-permute-start(bf16[128,768]{1,0:T(8,128)(2,1)S(1)} %collective-permute-done.3.refs_3_), channel_id=1, source_target_pairs={{0,1},{1,0},{2,3},{3,2},{4,5},{5,4},{6,7},{7,6},{8,9},{9,8},{10,11... | collective-permute-start | bytes 589832 | tf_op jit(solution)/shard_map/ppermute | solution.py:314
  56.5 6.7 %collective-permute-start.9 = (bf16[128,768]{1,0:T(8,128)(2,1)S(1)}, bf16[128,768]{1,0:T(8,128)(2,1)S(1)}, u32[]{:S(2)}, u32[]{:S(2)}) collective-permute-start(bf16[128,768]{1,0:T(8,128)(2,1)S(1)} %collective-permute-done.4.refs_4_), channel_id=1, source_target_pairs={{0,1},{1,0},{2,3},{3,2},{4,5},{5,4},{6,7},{7,6},{8,9},{9,8},{10,11... | collective-permute-start | bytes 589832 | tf_op jit(solution)/shard_map/ppermute | solution.py:314
  56.8 5.5 %collective-permute-start.6 = (bf16[64,768]{1,0:T(8,128)(2,1)S(1)}, bf16[64,768]{1,0:T(8,128)(2,1)S(1)}, u32[]{:S(2)}, u32[]{:S(2)}) collective-permute-start(bf16[64,768]{1,0:T(8,128)(2,1)S(1)} %collective-permute-done.1.refs_1_), channel_id=1, source_target_pairs={{0,1},{1,0},{2,3},{3,2},{4,5},{5,4},{6,7},{7,6},{8,9},{9,8},{10,11... | collective-permute-start | bytes 294920 | tf_op jit(solution)/shard_map/ppermute | solution.py:314
  59.9 3.3 %collective-permute-start.7 = (bf16[64,768]{1,0:T(8,128)(2,1)S(1)}, bf16[64,768]{1,0:T(8,128)(2,1)S(1)}, u32[]{:S(2)}, u32[]{:S(2)}) collective-permute-start(bf16[64,768]{1,0:T(8,128)(2,1)S(1)} %collective-permute-done.2.refs_2_), channel_id=1, source_target_pairs={{0,1},{1,0},{2,3},{3,2},{4,5},{5,4},{6,7},{7,6},{8,9},{9,8},{10,11... | collective-permute-start | bytes 294920 | tf_op jit(solution)/shard_map/ppermute | solution.py:314

commit v7 on v6

--- a/solution.py
+++ b/solution.py
@@ -21,12 +21,13 @@
 ROWS = NQ * 2 * CELLS
 STRIDE_O = ROWS + 1
 CHUNKS = 4
+SENDS = 4
 CHUNK = MODES * BANDS * BANDS // CHUNKS
 
 
 def rotate_body(
-    qp_hbm, rv_hbm, rw_hbm, rot_hbm, coarse_hbm, out_ref,
-    qp_ref, rv_ref, rw_ref, rot_ref, coarse_ref, mat_ref, s_ref, o_ref, sems,
+    qp_hbm, rv_hbm, rw_hbm, rot_hbm, coarse_hbm, out_hbm,
+    qp_ref, rv_ref, rw_ref, rot_ref, coarse_ref, mat_ref, s_ref, o_ref, send_ref, sems,
 ):
     small = [
         pltpu.make_async_copy(src, dst, sems.at[i])
@@ -45,8 +46,16 @@
                     sems.at[4 + part * CHUNKS + i],
                 )
             )
-    for copy in small + large:
+    for copy in large + small:
         copy.start()
+    for part in range(2):
+        for m in range(MODES):
+            if m * 256 % CHUNK == 0:
+                large[part * CHUNKS + m * 256 // CHUNK].wait()
+            for h in range(2):
+                at = (2 * m + h) * 128
+                tile = coarse_ref[part, :, at:at + 128].astype(f32)
+                s_ref[h, pl.ds(part * MODES + m, CELLS, stride=STRIDE_S), :] = tile
     for copy in small:
         copy.wait()
     weight = 1.0 / jnp.full((8, 128), rw_ref[0, 0], jnp.int32).astype(f32)
@@ -72,14 +81,6 @@
         for j in range(PER):
             rows.append(mat_ref[pl.ds(g * 48 + j, LAT, stride=PER), :])
     mat = jnp.concatenate(rows, axis=0)[:, 0:96].astype(bf16)
-    for part in range(2):
-        for m in range(MODES):
-            if m * 256 % CHUNK == 0:
-                large[part * CHUNKS + m * 256 // CHUNK].wait()
-            for h in range(2):
-                at = (2 * m + h) * 128
-                tile = coarse_ref[part, :, at:at + 128].astype(f32)
-                s_ref[h, pl.ds(part * MODES + m, CELLS, stride=STRIDE_S), :] = tile
     for e in range(CELLS):
         block = jnp.concatenate(
             [s_ref[h, e * STRIDE_S:e * STRIDE_S + 96, :].astype(bf16) for h in range(2)], axis=1
@@ -91,9 +92,22 @@
                 for j in range(PER):
                     at = (g * PER + j) * LAT
                     o_ref[2 * j + h, pl.ds(g * CELLS + e, LAT, stride=STRIDE_O), :] = res[at:at + LAT]
+    sends = []
     for l in range(LAT):
         for t in range(2 * PER):
-            out_ref[l, :, t * 128:(t + 1) * 128] = o_ref[t, l * STRIDE_O:l * STRIDE_O + ROWS, :].astype(bf16)
+            send_ref[l, :, t * 128:(t + 1) * 128] = o_ref[
+                t, l * STRIDE_O:l * STRIDE_O + ROWS, :
+            ].astype(bf16)
+        if l % SENDS == SENDS - 1:
+            part = pl.ds(l + 1 - SENDS, SENDS)
+            sends.append(
+                pltpu.make_async_copy(
+                    send_ref.at[part], out_hbm.at[part], sems.at[4 + 2 * CHUNKS + l // SENDS]
+                )
+            )
+            sends[-1].start()
+    for copy in sends:
+        copy.wait()
 
 
 def sum_body(x_ref, out_ref):
@@ -145,21 +159,24 @@
             lo_ref[i, b] = left[b * 16:(b + 1) * 16] * mq
 
 
-def pack_body(own_ref, across_ref, order_ref, out_ref):
-    out_ref[0:ROWS, :] = own_ref[...]
-    out_ref[ROWS:2 * ROWS, :] = across_ref[...]
-
-
-PLACE = ((0, 0), (3, 0), (1, 0), (4, 1), (0, 1), (3, 1), (2, 0), (4, 0))
+def pack_body(own_ref, up_ref, down_ref, order_ref, three_ref, two_ref):
+    for i, ref in enumerate((own_ref, up_ref, down_ref)):
+        value = ref[...]
+        three_ref[i * ROWS:(i + 1) * ROWS, :] = value
+        if i < 2:
+            two_ref[i * ROWS:(i + 1) * ROWS, :] = value
+
+
+PLACE = ((0, 0), (1, 0), (2, 1), (0, 1), (1, 1), (0, 2), (1, 2), (2, 0))
 
 
 def couple_body(*refs):
-    ph_ref, u_ref, l_ref, out_ref, y_ref, bl_ref, h_ref, r_ref = refs[10:]
+    ph_ref, u_ref, l_ref, out_hbm, y_ref, bl_ref, h_ref, r_ref, out_ref, sems = refs[6:]
     ph = ph_ref[...]
     for q in range(NQ):
         x = jnp.concatenate(
             [
-                refs[side * 5 + i][j * ROWS + q * 32:j * ROWS + (q + 1) * 32, :]
+                refs[side * 3 + i][j * ROWS + q * 32:j * ROWS + (q + 1) * 32, :]
                 for side in range(2)
                 for i, j in PLACE
             ],
@@ -198,27 +215,37 @@
 
     lax.fori_loop(0, PER * BANDS // group, first, 0)
 
-    per = BANDS // group
-
-    def second(i, _):
-        n = i // per
-        c0 = (i - n * per) * group
-        acc = [[jnp.zeros((16, 128), f32) for _ in range(3)] for _ in range(group)]
-        for a in range(BANDS):
-            hs = [h_ref[t, n * BANDS + a] for t in range(3)]
+    copies = []
+    for n in range(PER):
+
+        def second(i, _):
+            acc = [[jnp.zeros((16, 128), f32) for _ in range(3)] for _ in range(group)]
+            for a in range(BANDS):
+                hs = [h_ref[t, n * BANDS + a] for t in range(3)]
+                for s in range(group):
+                    for t in range(3):
+                        row = l_ref[t, a, pl.ds(i * group + s, 1), :]
+                        acc[s][t] = acc[s][t] + row * hs[t]
             for s in range(group):
-                for t in range(3):
-                    acc[s][t] = acc[s][t] + l_ref[t, a, pl.ds(c0 + s, 1), :] * hs[t]
-        for s in range(group):
-            r_ref[0, i * group + s] = acc[s][0] - acc[s][2]
-            r_ref[1, i * group + s] = acc[s][0] + acc[s][1]
-        return 0
-
-    lax.fori_loop(0, PER * per, second, 0)
-    for part in range(2):
-        for v in range(2 * PER):
-            tile = r_ref[part, v * 8:(v + 1) * 8].reshape(128, 128).T
-            out_ref[part, :, :, v * 128:(v + 1) * 128] = tile.reshape(KPTS, NQ, 128).astype(bf16)
+                r_ref[0, i * group + s] = acc[s][0] - acc[s][2]
+                r_ref[1, i * group + s] = acc[s][0] + acc[s][1]
+            return 0
+
+        lax.fori_loop(0, BANDS // group, second, 0)
+        for part in range(2):
+            for h in range(2):
+                tile = r_ref[part, h * 8:(h + 1) * 8].reshape(128, 128).T
+                at = (2 * n + h) * 128
+                out_ref[part, :, :, at:at + 128] = tile.reshape(KPTS, NQ, 128).astype(bf16)
+        lanes = pl.ds(n * 256, 256)
+        copies.append(
+            pltpu.make_async_copy(
+                out_ref.at[:, :, :, lanes], out_hbm.at[:, :, :, lanes], sems.at[n]
+            )
+        )
+        copies[-1].start()
+    for copy in copies:
+        copy.wait()
 
 
 def vmem():
@@ -255,7 +282,7 @@
         rotate_body,
         out_shape=jax.ShapeDtypeStruct((LAT, ROWS, LANES), bf16),
         in_specs=[hbm()] * 5,
-        out_specs=vmem(),
+        out_specs=hbm(),
         scratch_shapes=[
             pltpu.SMEM((NQ, 3), f32),
             pltpu.SMEM((1, 3), jnp.int32),
@@ -265,7 +292,8 @@
             pltpu.VMEM((192, 128), f32),
             pltpu.VMEM((2, CELLS * STRIDE_S, 128), f32),
             pltpu.VMEM((2 * PER, LAT * STRIDE_O, 128), f32),
-            pltpu.SemaphoreType.DMA((4 + 2 * CHUNKS,)),
+            pltpu.VMEM((LAT, ROWS, LANES), bf16),
+            pltpu.SemaphoreType.DMA((4 + 2 * CHUNKS + LAT // SENDS,)),
         ],
         compiler_params=pltpu.CompilerParams(vmem_limit_bytes=63 << 20),
         name="rotate",
@@ -313,28 +341,36 @@
     def swap(x):
         return lax.ppermute(x, "kpt", [(i, i ^ 1) for i in range(16)])
 
-    across = shift(own, 4)
-    packed = pl.pallas_call(
+    up = shift(own, 3)
+    down = shift(own, -3)
+    packed, pair = pl.pallas_call(
         pack_body,
-        out_shape=jax.ShapeDtypeStruct((2 * ROWS, LANES), bf16),
-        in_specs=[vmem()] * 2 + [pl.BlockSpec(memory_space=pl.ANY)],
-        out_specs=vmem(),
+        out_shape=(
+            jax.ShapeDtypeStruct((3 * ROWS, LANES), bf16),
+            jax.ShapeDtypeStruct((2 * ROWS, LANES), bf16),
+        ),
+        in_specs=[vmem()] * 3 + [pl.BlockSpec(memory_space=pl.ANY)],
+        out_specs=(vmem(), vmem()),
         compiler_params=params(),
         name="pack",
-    )(own, across, phase)
-    near = [packed, shift(own, 2), shift(own, -2), shift(packed, 1), shift(packed, -1)]
+    )(own, up, down, phase)
+    plus = shift(packed, 1)
+    minus = shift(pair, -1)
+    near = [packed, plus, minus]
     far = [swap(x) for x in near]
 
     result = pl.pallas_call(
         couple_body,
         out_shape=jax.ShapeDtypeStruct((2, KPTS, NQ, LANES), bf16),
-        in_specs=[vmem()] * 13,
-        out_specs=vmem(),
+        in_specs=[vmem()] * 9,
+        out_specs=hbm(),
         scratch_shapes=[
             pltpu.VMEM((2, 2 * PER, 128, 128), f32),
             pltpu.VMEM((3, LANES, 128), f32),
             pltpu.VMEM((3, PER * BANDS, BANDS, 128), f32),
-            pltpu.VMEM((2, PER * BANDS, BANDS, 128), f32),
+            pltpu.VMEM((2, BANDS, BANDS, 128), f32),
+            pltpu.VMEM((2, KPTS, NQ, LANES), bf16),
+            pltpu.SemaphoreType.DMA((PER,)),
         ],
         compiler_params=params(),
         name="couple",

time: 68.3 us -> 66.6 us (0.975)
  starting transfers between devices: 33 us -> 29.4 us
  waiting for transfers between devices: 23.4 us -> 25.2 us
    ppermute x5 -> x4, starting transfers between devices: 14.7 us -> 11.9 us  [shift(): return lax.ppermute(x, 'kpt', [(i, (i + 2 * step) % 16) for i in range(16)])]
    ppermute x5 -> x4, waiting for transfers between devices: 0.76 us -> 2.42 us  [shift(): return lax.ppermute(x, 'kpt', [(i, (i + 2 * step) % 16) for i in range(16)])]
    ppermute x5 -> x3, starting transfers between devices: 10.6 us -> 9.79 us  [swap(): return lax.ppermute(x, 'kpt', [(i, i ^ 1) for i in range(16)])]
  transfers between devices with their start and end apart: 11 -> 8, of which waited for: 3 -> 4; matrix products, arithmetic and copies ran while one was open for 2% -> 2% of each run, Pallas kernels for 2% -> 2%
where the time goes in v7:
time: 66.6 us; the launch traced here: 66.4 us
  starting transfers between devices  29.4 us (44%)
  waiting for transfers between devices  25.2 us (38%)
  Pallas kernels  9.85 us (15%)
  local copies, waits for them, and re-layouts  1.01 us (2%)
  between operations  0.83 us (1%)
    all_to_all x1, waiting for transfers between devices, per_device(): parts = lax.all_to_all(rotated, 'lat', 0, 0, tiled=True)  21.7 us
    ppermute x4, starting transfers between devices, shift(): return lax.ppermute(x, 'kpt', [(i, (i + 2 * step) % 16) for i in range(16)])  11.9 us
    ppermute x3, starting transfers between devices, swap(): return lax.ppermute(x, 'kpt', [(i, i ^ 1) for i in range(16)])  9.79 us
    all_to_all x1, starting transfers between devices, per_device(): parts = lax.all_to_all(rotated, 'lat', 0, 0, tiled=True)  7.73 us
    pallas_call x1, Pallas kernels, per_device(): pl.pallas_call(couple_body, out_shape=jax.ShapeDtypeStruct((2, KPTS, NQ,...  4.93 us
    pallas_call x1, Pallas kernels, per_device(): pl.pallas_call(rotate_body, out_shape=jax.ShapeDtypeStruct((LAT, ROWS, LA...  3.41 us
    ppermute x4, waiting for transfers between devices, shift(): return lax.ppermute(x, 'kpt', [(i, (i + 2 * step) % 16) for i in range(16)])  2.42 us
  transfers between devices with their start and end apart: 8, of which 4 were waited for; matrix products, arithmetic and copies ran while one was open for 2% of the time, Pallas kernels for 2%

profile of v7, /device:TPU:1, one launch (start us, length us, event | category | flops | bytes accessed | tf_op | source)
XLA Modules:
  0.0 66.4 jit_solution(7674555154064815338)
XLA Ops:
  0.7 3.4 %rotate.1 = bf16[16,64,768]{2,1,0:T(8,128)(2,1)} custom-call(f32[2,3]{1,0:T(2,128)} %qp_hbm.1, s32[1,3]{1,0:T(1,128)} %rv_hbm.1, s32[1,1]{1,0:T(1,128)} %bitcast.9.rw_hbm, bf16[2,2,48,48]{3,2,1,0:T(8,128)(2,1)} %rot_hbm.1, bf16[2,1,16,12288]{3,2,1,0:T(8,128)(2,1)} %coarse_hbm.1), custom_call_target="tpu_custom_call" | custom-call | tf_op jit(solution)/shard_map/rotate/pallas_call | solution.py:281
  4.1 0.0 copy-start.5
  4.1 0.0 copy-start.1
  4.1 0.0 copy-start
  4.1 0.0 copy-start.3
  4.1 0.0 copy-start.2
  4.1 7.7 %all-to-all-start = ((bf16[16,64,768]{2,1,0:T(8,128)(2,1)}), bf16[16,64,768]{2,1,0:T(8,128)(2,1)S(1)}, u32[]{:S(2)}, u32[]{:S(2)}) async-start(bf16[16,64,768]{2,1,0:T(8,128)(2,1)} %rotate.1), calls=%async_computation | async-start | bytes 3145728 | tf_op jit(solution)/shard_map/all_to_all | solution.py:301
  11.9 0.0 copy-start.4
  11.9 0.0 copy-start.6
  11.9 0.0 copy-done.5
  11.9 0.1 copy.20.kp_ref
  12.0 0.1 pad.2.clone
  12.1 0.0 copy-done.1
  12.1 0.1 copy.21.u_ref
  12.2 0.0 copy-done
  12.2 0.3 copy.18
  12.5 0.1 reshape.10
  12.6 0.1 copy.22.uq_ref
  12.8 0.0 copy-done.3
  12.8 0.1 copy.23.mk_ref
  12.9 0.0 copy-done.2
  12.9 0.1 copy.19
  12.9 0.0 copy-done.4
  12.9 0.0 copy-done.6
  13.0 0.1 add_add_fusion.rv_ref
  13.0 21.7 %all-to-all-done.x_ref = bf16[16,64,768]{2,1,0:T(8,128)(2,1)S(1)} async-done(((bf16[16,64,768]{2,1,0:T(8,128)(2,1)}), bf16[16,64,768]{2,1,0:T(8,128)(2,1)S(1)}, u32[]{:S(2)}, u32[]{:S(2)}) %all-to-all-start) | async-done | bytes 1572896 | tf_op jit(solution)/shard_map/all_to_all | solution.py:301
  34.7 0.2 add_up.1.own_ref
  34.9 4.4 %collective-permute-start = (bf16[64,768]{1,0:T(8,128)(2,1)S(1)}, bf16[64,768]{1,0:T(8,128)(2,1)S(1)}, u32[]{:S(2)}, u32[]{:S(2)}) collective-permute-start(bf16[64,768]{1,0:T(8,128)(2,1)S(1)} %add_up.1.own_ref), channel_id=1, source_target_pairs={{0,6},{1,7},{2,8},{3,9},{4,10},{5,11},{6,12},{7,13},{8,14},{9,15},... | collective-permute-start | bytes 294920 | tf_op jit(solution)/shard_map/ppermute | solution.py:339
  39.4 2.2 %collective-permute-start.1 = (bf16[64,768]{1,0:T(8,128)(2,1)S(1)}, bf16[64,768]{1,0:T(8,128)(2,1)S(1)}, u32[]{:S(2)}, u32[]{:S(2)}) collective-permute-start(bf16[64,768]{1,0:T(8,128)(2,1)S(1)} %add_up.1.own_ref), channel_id=1, source_target_pairs={{0,10},{1,11},{2,12},{3,13},{4,14},{5,15},{6,0},{7,1},{8,2},{9,3},... | collective-permute-start | bytes 294920 | tf_op jit(solution)/shard_map/ppermute | solution.py:339
  41.6 0.1 pad_add_fusion.at_ref
  41.7 1.3 %prep.1 = (bf16[128,512]{1,0:T(8,128)(2,1)S(1)}, f32[3,16,16,128]{3,2,1,0:T(8,128)S(1)}, f32[3,16,16,128]{3,2,1,0:T(8,128)S(1)}) custom-call(s32[2]{0:T(128)S(1)} %pad_add_fusion.at_ref, f32[64,3]{1,0:T(8,128)S(1)} %copy.20.kp_ref, s32[8,256]{1,0:T(8,128)S(1)} %add_add_fusion.rv_ref, bf16[2,64,256]{2,1,0:T(8,128)(2,1)S(1)} %copy.21.u_ref, ...), custom_call_target="tpu_custom_call" | custom-call | tf_op jit(solution)/shard_map/prep/pallas_call | solution.py:308
  42.9 0.8 %collective-permute-done.up_ref = bf16[64,768]{1,0:T(8,128)(2,1)S(1)} collective-permute-done((bf16[64,768]{1,0:T(8,128)(2,1)S(1)}, bf16[64,768]{1,0:T(8,128)(2,1)S(1)}, u32[]{:S(2)}, u32[]{:S(2)}) %collective-permute-start) | collective-permute-done | bytes 98336 | tf_op jit(solution)/shard_map/ppermute | solution.py:339
  43.7 1.7 %collective-permute-done.1.down_ref = bf16[64,768]{1,0:T(8,128)(2,1)S(1)} collective-permute-done((bf16[64,768]{1,0:T(8,128)(2,1)S(1)}, bf16[64,768]{1,0:T(8,128)(2,1)S(1)}, u32[]{:S(2)}, u32[]{:S(2)}) %collective-permute-start.1) | collective-permute-done | bytes 98336 | tf_op jit(solution)/shard_map/ppermute | solution.py:339
  45.4 5.2 %collective-permute-start.2 = (bf16[192,768]{1,0:T(8,128)(2,1)S(1)}, bf16[192,768]{1,0:T(8,128)(2,1)S(1)}, u32[]{:S(2)}, u32[]{:S(2)}) collective-permute-start(bf16[192,768]{1,0:T(8,128)(2,1)S(1)} %get-tuple-element.11.refs_0_), channel_id=1, source_target_pairs={{0,2},{1,3},{2,4},{3,5},{4,6},{5,7},{6,8},{7,9},{8,10},{9,11},{10,... | collective-permute-start | bytes 884744 | tf_op jit(solution)/shard_map/ppermute | solution.py:339
  50.6 0.0 collective-permute-start.3
  50.6 4.1 %collective-permute-start.4 = (bf16[192,768]{1,0:T(8,128)(2,1)S(1)}, bf16[192,768]{1,0:T(8,128)(2,1)S(1)}, u32[]{:S(2)}, u32[]{:S(2)}) collective-permute-start(bf16[192,768]{1,0:T(8,128)(2,1)S(1)} %get-tuple-element.11.refs_0_), channel_id=1, source_target_pairs={{0,1},{1,0},{2,3},{3,2},{4,5},{5,4},{6,7},{7,6},{8,9},{9,8},{10,11... | collective-permute-start | bytes 884744 | tf_op jit(solution)/shard_map/ppermute | solution.py:342
  54.8 0.0 collective-permute-done.2.refs_1_
  54.8 4.2 %collective-permute-start.5 = (bf16[192,768]{1,0:T(8,128)(2,1)S(1)}, bf16[192,768]{1,0:T(8,128)(2,1)S(1)}, u32[]{:S(2)}, u32[]{:S(2)}) collective-permute-start(bf16[192,768]{1,0:T(8,128)(2,1)S(1)} %collective-permute-done.2.refs_1_), channel_id=1, source_target_pairs={{0,1},{1,0},{2,3},{3,2},{4,5},{5,4},{6,7},{7,6},{8,9},{9,8},{10,11... | collective-permute-start | bytes 884744 | tf_op jit(solution)/shard_map/ppermute | solution.py:342
  59.0 0.0 collective-permute-done.3.refs_2_
  59.0 1.4 %collective-permute-start.6 = (bf16[128,768]{1,0:T(8,128)(2,1)S(1)}, bf16[128,768]{1,0:T(8,128)(2,1)S(1)}, u32[]{:S(2)}, u32[]{:S(2)}) collective-permute-start(bf16[128,768]{1,0:T(8,128)(2,1)S(1)} %collective-permute-done.3.refs_2_), channel_id=1, source_target_pairs={{0,1},{1,0},{2,3},{3,2},{4,5},{5,4},{6,7},{7,6},{8,9},{9,8},{10,11... | collective-permute-start | bytes 589832 | tf_op jit(solution)/shard_map/ppermute | solution.py:342
  60.4 0.0 collective-permute-done.4.refs_3_
  60.4 1.1 %collective-permute-done.6.refs_5_ = bf16[128,768]{1,0:T(8,128)(2,1)S(1)} collective-permute-done((bf16[128,768]{1,0:T(8,128)(2,1)S(1)}, bf16[128,768]{1,0:T(8,128)(2,1)S(1)}, u32[]{:S(2)}, u32[]{:S(2)}) %collective-permute-start.6) | collective-permute-done | bytes 196640 | tf_op jit(solution)/shard_map/ppermute | solution.py:342
  61.5 0.0 collective-permute-done.5.refs_4_
  61.5 4.9 %couple.1 = bf16[2,64,2,768]{3,2,1,0:T(2,128)(2,1)} custom-call(bf16[192,768]{1,0:T(8,128)(2,1)S(1)} %get-tuple-element.11.refs_0_, bf16[192,768]{1,0:T(8,128)(2,1)S(1)} %collective-permute-done.2.refs_1_, bf16[128,768]{1,0:T(8,128)(2,1)S(1)} %collective-permute-done.3.refs_2_, bf16[192,768]{1,0:T(8,128)(2,1)S(1)} %collective-permute-done.4.refs_3_, ...), custom_call_target="tpu_custom_call" | custom-call | tf_op jit(solution)/shard_map/couple/pallas_call | solution.py:362
  (2 shorter events, 0.0 us)
Async XLA Ops:
  4.1 7.8 %copy-start.5 = (f32[64,3]{0,1:T(4,128)S(1)}, f32[64,3]{0,1:T(4,128)}, u32[]{:S(2)}) copy-start(f32[64,3]{0,1:T(4,128)} %param.18) | copy-start | bytes 2308
  4.1 8.0 %copy-start.1 = (bf16[2,64,16,16]{1,3,2,0:T(8,128)(2,1)S(1)}, bf16[2,64,16,16]{1,3,2,0:T(8,128)(2,1)}, u32[]{:S(2)}) copy-start(bf16[2,64,16,16]{1,3,2,0:T(8,128)(2,1)} %param.20) | copy-start | bytes 196612
  4.1 8.1 %copy-start = (bf16[2,2,64,16,16]{2,4,3,1,0:T(8,128)(2,1)S(1)}, bf16[2,2,64,16,16]{2,4,3,1,0:T(8,128)(2,1)}, u32[]{:S(2)}) copy-start(bf16[2,2,64,16,16]{2,4,3,1,0:T(8,128)(2,1)} %param.21) | copy-start | bytes 393220
  4.1 8.7 %copy-start.3 = (s32[64,16]{0,1:T(8,128)S(1)}, s32[64,16]{0,1:T(8,128)}, u32[]{:S(2)}) copy-start(s32[64,16]{0,1:T(8,128)} %param.22) | copy-start | bytes 12292
  4.1 8.7 %copy-start.2 = (s32[2,64,16]{1,2,0:T(8,128)S(1)}, s32[2,64,16]{1,2,0:T(8,128)}, u32[]{:S(2)}) copy-start(s32[2,64,16]{1,2,0:T(8,128)} %param.23) | copy-start | bytes 24580
  4.1 30.6 %all-to-all-start = ((bf16[16,64,768]{2,1,0:T(8,128)(2,1)}), bf16[16,64,768]{2,1,0:T(8,128)(2,1)S(1)}, u32[]{:S(2)}, u32[]{:S(2)}) async-start(bf16[16,64,768]{2,1,0:T(8,128)(2,1)} %rotate.1), calls=%async_computation | async-start | bytes 3145728 | tf_op jit(solution)/shard_map/all_to_all | solution.py:301
  11.9 1.1 %copy-start.4 = (s32[256,3]{0,1:T(4,128)S(1)}, s32[256,3]{0,1:T(4,128)}, u32[]{:S(2)}) copy-start(s32[256,3]{0,1:T(4,128)} %param.15) | copy-start | bytes 9220
  11.9 1.1 %copy-start.6 = (s32[256]{0:T(256)S(1)}, s32[256]{0:T(256)}, u32[]{:S(2)}) copy-start(s32[256]{0:T(256)} %param.16) | copy-start | bytes 3076
  34.9 8.8 %collective-permute-start = (bf16[64,768]{1,0:T(8,128)(2,1)S(1)}, bf16[64,768]{1,0:T(8,128)(2,1)S(1)}, u32[]{:S(2)}, u32[]{:S(2)}) collective-permute-start(bf16[64,768]{1,0:T(8,128)(2,1)S(1)} %add_up.1.own_ref), channel_id=1, source_target_pairs={{0,6},{1,7},{2,8},{3,9},{4,10},{5,11},{6,12},{7,13},{8,14},{9,15},... | collective-permute-start | bytes 294920 | tf_op jit(solution)/shard_map/ppermute | solution.py:339
  39.4 6.0 %collective-permute-start.1 = (bf16[64,768]{1,0:T(8,128)(2,1)S(1)}, bf16[64,768]{1,0:T(8,128)(2,1)S(1)}, u32[]{:S(2)}, u32[]{:S(2)}) collective-permute-start(bf16[64,768]{1,0:T(8,128)(2,1)S(1)} %add_up.1.own_ref), channel_id=1, source_target_pairs={{0,10},{1,11},{2,12},{3,13},{4,14},{5,15},{6,0},{7,1},{8,2},{9,3},... | collective-permute-start | bytes 294920 | tf_op jit(solution)/shard_map/ppermute | solution.py:339
  45.4 9.4 %collective-permute-start.2 = (bf16[192,768]{1,0:T(8,128)(2,1)S(1)}, bf16[192,768]{1,0:T(8,128)(2,1)S(1)}, u32[]{:S(2)}, u32[]{:S(2)}) collective-permute-start(bf16[192,768]{1,0:T(8,128)(2,1)S(1)} %get-tuple-element.11.refs_0_), channel_id=1, source_target_pairs={{0,2},{1,3},{2,4},{3,5},{4,6},{5,7},{6,8},{7,9},{8,10},{9,11},{10,... | collective-permute-start | bytes 884744 | tf_op jit(solution)/shard_map/ppermute | solution.py:339
  50.6 8.4 %collective-permute-start.3 = (bf16[128,768]{1,0:T(8,128)(2,1)S(1)}, bf16[128,768]{1,0:T(8,128)(2,1)S(1)}, u32[]{:S(2)}, u32[]{:S(2)}) collective-permute-start(bf16[128,768]{1,0:T(8,128)(2,1)S(1)} %get-tuple-element.12), channel_id=1, source_target_pairs={{0,14},{1,15},{2,0},{3,1},{4,2},{5,3},{6,4},{7,5},{8,6},{9,7},{10,... | collective-permute-start | bytes 589832 | tf_op jit(solution)/shard_map/ppermute | solution.py:339
  50.6 9.8 %collective-permute-start.4 = (bf16[192,768]{1,0:T(8,128)(2,1)S(1)}, bf16[192,768]{1,0:T(8,128)(2,1)S(1)}, u32[]{:S(2)}, u32[]{:S(2)}) collective-permute-start(bf16[192,768]{1,0:T(8,128)(2,1)S(1)} %get-tuple-element.11.refs_0_), channel_id=1, source_target_pairs={{0,1},{1,0},{2,3},{3,2},{4,5},{5,4},{6,7},{7,6},{8,9},{9,8},{10,11... | collective-permute-start | bytes 884744 | tf_op jit(solution)/shard_map/ppermute | solution.py:342
  54.8 6.7 %collective-permute-start.5 = (bf16[192,768]{1,0:T(8,128)(2,1)S(1)}, bf16[192,768]{1,0:T(8,128)(2,1)S(1)}, u32[]{:S(2)}, u32[]{:S(2)}) collective-permute-start(bf16[192,768]{1,0:T(8,128)(2,1)S(1)} %collective-permute-done.2.refs_1_), channel_id=1, source_target_pairs={{0,1},{1,0},{2,3},{3,2},{4,5},{5,4},{6,7},{7,6},{8,9},{9,8},{10,11... | collective-permute-start | bytes 884744 | tf_op jit(solution)/shard_map/ppermute | solution.py:342
  59.0 2.5 %collective-permute-start.6 = (bf16[128,768]{1,0:T(8,128)(2,1)S(1)}, bf16[128,768]{1,0:T(8,128)(2,1)S(1)}, u32[]{:S(2)}, u32[]{:S(2)}) collective-permute-start(bf16[128,768]{1,0:T(8,128)(2,1)S(1)} %collective-permute-done.3.refs_2_), channel_id=1, source_target_pairs={{0,1},{1,0},{2,3},{3,2},{4,5},{5,4},{6,7},{7,6},{8,9},{9,8},{10,11... | collective-permute-start | bytes 589832 | tf_op jit(solution)/shard_map/ppermute | solution.py:342

commit v8 on v6

--- a/solution.py
+++ b/solution.py
@@ -145,21 +145,28 @@
             lo_ref[i, b] = left[b * 16:(b + 1) * 16] * mq
 
 
-def pack_body(own_ref, across_ref, order_ref, out_ref):
+def pack_body(own_ref, back_ref, out_ref):
     out_ref[0:ROWS, :] = own_ref[...]
-    out_ref[ROWS:2 * ROWS, :] = across_ref[...]
-
-
-PLACE = ((0, 0), (3, 0), (1, 0), (4, 1), (0, 1), (3, 1), (2, 0), (4, 0))
+    out_ref[ROWS:2 * ROWS, :] = back_ref[...]
+
+
+def pack_all_body(own_ref, back_ref, ahead_ref, across_ref, order_ref, pair_ref, out_ref):
+    pair_ref[0:ROWS, :] = own_ref[...]
+    pair_ref[ROWS:2 * ROWS, :] = ahead_ref[...]
+    for i, ref in enumerate((own_ref, back_ref, ahead_ref, across_ref)):
+        out_ref[i * ROWS:(i + 1) * ROWS, :] = ref[...]
+
+
+PLACE = ((0, 0), (1, 0), (0, 1), (1, 1), (0, 3), (2, 1), (0, 2), (2, 0))
 
 
 def couple_body(*refs):
-    ph_ref, u_ref, l_ref, out_ref, y_ref, bl_ref, h_ref, r_ref = refs[10:]
+    ph_ref, u_ref, l_ref, out_ref, y_ref, bl_ref, h_ref, r_ref = refs[6:]
     ph = ph_ref[...]
     for q in range(NQ):
         x = jnp.concatenate(
             [
-                refs[side * 5 + i][j * ROWS + q * 32:j * ROWS + (q + 1) * 32, :]
+                refs[side * 3 + i][j * ROWS + q * 32:j * ROWS + (q + 1) * 32, :]
                 for side in range(2)
                 for i, j in PLACE
             ],
@@ -313,22 +320,35 @@
     def swap(x):
         return lax.ppermute(x, "kpt", [(i, i ^ 1) for i in range(16)])
 
+    back = shift(own, 2)
+    ahead = shift(own, -2)
     across = shift(own, 4)
-    packed = pl.pallas_call(
+    pair = pl.pallas_call(
         pack_body,
         out_shape=jax.ShapeDtypeStruct((2 * ROWS, LANES), bf16),
-        in_specs=[vmem()] * 2 + [pl.BlockSpec(memory_space=pl.ANY)],
+        in_specs=[vmem()] * 2,
         out_specs=vmem(),
         compiler_params=params(),
         name="pack",
-    )(own, across, phase)
-    near = [packed, shift(own, 2), shift(own, -2), shift(packed, 1), shift(packed, -1)]
+    )(own, back)
+    other, packed = pl.pallas_call(
+        pack_all_body,
+        out_shape=(
+            jax.ShapeDtypeStruct((2 * ROWS, LANES), bf16),
+            jax.ShapeDtypeStruct((4 * ROWS, LANES), bf16),
+        ),
+        in_specs=[vmem()] * 4 + [pl.BlockSpec(memory_space=pl.ANY)],
+        out_specs=(vmem(), vmem()),
+        compiler_params=params(),
+        name="pack_all",
+    )(own, back, ahead, across, phase)
+    near = [packed, shift(pair, 1), shift(other, -1)]
     far = [swap(x) for x in near]
 
     result = pl.pallas_call(
         couple_body,
         out_shape=jax.ShapeDtypeStruct((2, KPTS, NQ, LANES), bf16),
-        in_specs=[vmem()] * 13,
+        in_specs=[vmem()] * 9,
         out_specs=vmem(),
         scratch_shapes=[
             pltpu.VMEM((2, 2 * PER, 128, 128), f32),

time: 68.3 us -> 68.9 us (level)
  waiting for transfers between devices: 23.4 us -> 30.5 us
  starting transfers between devices: 33 us -> 26.5 us
    ppermute x5, waiting for transfers between devices: 0.76 us -> 7.7 us  [shift(): return lax.ppermute(x, 'kpt', [(i, (i + 2 * step) % 16) for i in range(16)])]
    ppermute x5 -> x3, starting transfers between devices: 10.6 us -> 6.84 us  [swap(): return lax.ppermute(x, 'kpt', [(i, i ^ 1) for i in range(16)])]
    ppermute x5, starting transfers between devices: 14.7 us -> 11.9 us  [shift(): return lax.ppermute(x, 'kpt', [(i, (i + 2 * step) % 16) for i in range(16)])]
  transfers between devices with their start and end apart: 11 -> 9, of which waited for: 3 -> 4; matrix products, arithmetic and copies ran while one was open for 2% -> 2% of each run, Pallas kernels for 2% -> 2%
where the time goes in v8:
time: 68.9 us; the launch traced here: 68.7 us
  waiting for transfers between devices  30.5 us (44%)
  starting transfers between devices  26.5 us (38%)
  Pallas kernels  9.71 us (14%)
  local copies, waits for them, and re-layouts  1.01 us (1%)
  between operations  0.84 us (1%)
    all_to_all x1, waiting for transfers between devices, per_device(): parts = lax.all_to_all(rotated, 'lat', 0, 0, tiled=True)  21.7 us
    ppermute x5, starting transfers between devices, shift(): return lax.ppermute(x, 'kpt', [(i, (i + 2 * step) % 16) for i in range(16)])  11.9 us
    all_to_all x1, starting transfers between devices, per_device(): parts = lax.all_to_all(rotated, 'lat', 0, 0, tiled=True)  7.73 us
    ppermute x5, waiting for transfers between devices, shift(): return lax.ppermute(x, 'kpt', [(i, (i + 2 * step) % 16) for i in range(16)])  7.7 us
    ppermute x3, starting transfers between devices, swap(): return lax.ppermute(x, 'kpt', [(i, i ^ 1) for i in range(16)])  6.84 us
    pallas_call x1, Pallas kernels, per_device(): pl.pallas_call(couple_body, out_shape=jax.ShapeDtypeStruct((2, KPTS, NQ,...  4.89 us
    pallas_call x1, Pallas kernels, per_device(): pl.pallas_call(rotate_body, out_shape=jax.ShapeDtypeStruct((LAT, ROWS, LA...  3.28 us
  transfers between devices with their start and end apart: 9, of which 4 were waited for; matrix products, arithmetic and copies ran while one was open for 2% of the time, Pallas kernels for 2%

profile of v8, /device:TPU:1, one launch (start us, length us, event | category | flops | bytes accessed | tf_op | source)
XLA Modules:
  0.0 68.7 jit_solution(4182681813088660506)
XLA Ops:
  0.7 3.3 %rotate.1 = bf16[16,64,768]{2,1,0:T(8,128)(2,1)} custom-call(f32[2,3]{1,0:T(2,128)} %qp_hbm.1, s32[1,3]{1,0:T(1,128)} %rv_hbm.1, s32[1,1]{1,0:T(1,128)} %bitcast.9.rw_hbm, bf16[2,2,48,48]{3,2,1,0:T(8,128)(2,1)} %rot_hbm.1, bf16[2,1,16,12288]{3,2,1,0:T(8,128)(2,1)} %coarse_hbm.1), custom_call_target="tpu_custom_call" | custom-call | tf_op jit(solution)/shard_map/rotate/pallas_call | solution.py:261
  3.9 0.0 copy-start.5
  4.0 0.0 copy-start.1
  4.0 0.0 copy-start
  4.0 0.0 copy-start.3
  4.0 0.0 copy-start.2
  4.0 7.7 %all-to-all-start = ((bf16[16,64,768]{2,1,0:T(8,128)(2,1)}), bf16[16,64,768]{2,1,0:T(8,128)(2,1)S(1)}, u32[]{:S(2)}, u32[]{:S(2)}) async-start(bf16[16,64,768]{2,1,0:T(8,128)(2,1)} %rotate.1), calls=%async_computation | async-start | bytes 3145728 | tf_op jit(solution)/shard_map/all_to_all | solution.py:280
  11.7 0.0 copy-start.4
  11.8 0.0 copy-start.6
  11.8 0.0 copy-done.5
  11.8 0.1 copy.20.kp_ref
  11.9 0.1 pad.2.clone
  12.0 0.0 copy-done.1
  12.0 0.1 copy.21.u_ref
  12.1 0.0 copy-done
  12.1 0.3 copy.18
  12.4 0.1 reshape.10
  12.5 0.1 copy.22.uq_ref
  12.6 0.0 copy-done.3
  12.6 0.1 copy.23.mk_ref
  12.7 0.0 copy-done.2
  12.7 0.1 copy.19
  12.8 0.0 copy-done.4
  12.8 0.0 copy-done.6
  12.8 0.1 add_add_fusion.rv_ref
  12.9 21.7 %all-to-all-done.x_ref = bf16[16,64,768]{2,1,0:T(8,128)(2,1)S(1)} async-done(((bf16[16,64,768]{2,1,0:T(8,128)(2,1)}), bf16[16,64,768]{2,1,0:T(8,128)(2,1)S(1)}, u32[]{:S(2)}, u32[]{:S(2)}) %all-to-all-start) | async-done | bytes 1572896 | tf_op jit(solution)/shard_map/all_to_all | solution.py:280
  34.6 0.2 add_up.1.own_ref
  34.8 3.1 %collective-permute-start = (bf16[64,768]{1,0:T(8,128)(2,1)S(1)}, bf16[64,768]{1,0:T(8,128)(2,1)S(1)}, u32[]{:S(2)}, u32[]{:S(2)}) collective-permute-start(bf16[64,768]{1,0:T(8,128)(2,1)S(1)} %add_up.1.own_ref), channel_id=1, source_target_pairs={{0,4},{1,5},{2,6},{3,7},{4,8},{5,9},{6,10},{7,11},{8,12},{9,13},{1... | collective-permute-start | bytes 294920 | tf_op jit(solution)/shard_map/ppermute | solution.py:318
  37.9 3.1 %collective-permute-start.1 = (bf16[64,768]{1,0:T(8,128)(2,1)S(1)}, bf16[64,768]{1,0:T(8,128)(2,1)S(1)}, u32[]{:S(2)}, u32[]{:S(2)}) collective-permute-start(bf16[64,768]{1,0:T(8,128)(2,1)S(1)} %add_up.1.own_ref), channel_id=1, source_target_pairs={{0,12},{1,13},{2,14},{3,15},{4,0},{5,1},{6,2},{7,3},{8,4},{9,5},{1... | collective-permute-start | bytes 294920 | tf_op jit(solution)/shard_map/ppermute | solution.py:318
  41.0 4.4 %collective-permute-start.2 = (bf16[64,768]{1,0:T(8,128)(2,1)S(1)}, bf16[64,768]{1,0:T(8,128)(2,1)S(1)}, u32[]{:S(2)}, u32[]{:S(2)}) collective-permute-start(bf16[64,768]{1,0:T(8,128)(2,1)S(1)} %add_up.1.own_ref), channel_id=1, source_target_pairs={{0,8},{1,9},{2,10},{3,11},{4,12},{5,13},{6,14},{7,15},{8,0},{9,1},... | collective-permute-start | bytes 294920 | tf_op jit(solution)/shard_map/ppermute | solution.py:318
  45.4 0.1 pad_add_fusion.at_ref
  45.5 1.3 %prep.1 = (bf16[128,512]{1,0:T(8,128)(2,1)S(1)}, f32[3,16,16,128]{3,2,1,0:T(8,128)S(1)}, f32[3,16,16,128]{3,2,1,0:T(8,128)S(1)}) custom-call(s32[2]{0:T(128)S(1)} %pad_add_fusion.at_ref, f32[64,3]{1,0:T(8,128)S(1)} %copy.20.kp_ref, s32[8,256]{1,0:T(8,128)S(1)} %add_add_fusion.rv_ref, bf16[2,64,256]{2,1,0:T(8,128)(2,1)S(1)} %copy.21.u_ref, ...), custom_call_target="tpu_custom_call" | custom-call | tf_op jit(solution)/shard_map/prep/pallas_call | solution.py:287
  46.8 0.0 collective-permute-done.back_ref
  46.8 0.8 %collective-permute-start.3 = (bf16[128,768]{1,0:T(8,128)(2,1)S(1)}, bf16[128,768]{1,0:T(8,128)(2,1)S(1)}, u32[]{:S(2)}, u32[]{:S(2)}) collective-permute-start(bf16[128,768]{1,0:T(8,128)(2,1)S(1)} %pack.1), channel_id=1, source_target_pairs={{0,2},{1,3},{2,4},{3,5},{4,6},{5,7},{6,8},{7,9},{8,10},{9,11},{10,... | collective-permute-start | bytes 589832 | tf_op jit(solution)/shard_map/ppermute | solution.py:318
  47.6 0.0 collective-permute-done.1.ahead_ref
  47.6 3.3 %collective-permute-done.2.across_ref = bf16[64,768]{1,0:T(8,128)(2,1)S(1)} collective-permute-done((bf16[64,768]{1,0:T(8,128)(2,1)S(1)}, bf16[64,768]{1,0:T(8,128)(2,1)S(1)}, u32[]{:S(2)}, u32[]{:S(2)}) %collective-permute-start.2) | collective-permute-done | bytes 98336 | tf_op jit(solution)/shard_map/ppermute | solution.py:318
  50.9 4.5 %collective-permute-start.5 = (bf16[256,768]{1,0:T(8,128)(2,1)S(1)}, bf16[256,768]{1,0:T(8,128)(2,1)S(1)}, u32[]{:S(2)}, u32[]{:S(2)}) collective-permute-start(bf16[256,768]{1,0:T(8,128)(2,1)S(1)} %get-tuple-element.11.refs_0_), channel_id=1, source_target_pairs={{0,1},{1,0},{2,3},{3,2},{4,5},{5,4},{6,7},{7,6},{8,9},{9,8},{10,11... | collective-permute-start | bytes 1179656 | tf_op jit(solution)/shard_map/ppermute | solution.py:321
  55.4 0.5 collective-permute-start.4
  55.9 0.0 collective-permute-done.3.refs_1_
  55.9 1.5 %collective-permute-start.6 = (bf16[128,768]{1,0:T(8,128)(2,1)S(1)}, bf16[128,768]{1,0:T(8,128)(2,1)S(1)}, u32[]{:S(2)}, u32[]{:S(2)}) collective-permute-start(bf16[128,768]{1,0:T(8,128)(2,1)S(1)} %collective-permute-done.3.refs_1_), channel_id=1, source_target_pairs={{0,1},{1,0},{2,3},{3,2},{4,5},{5,4},{6,7},{7,6},{8,9},{9,8},{10,11... | collective-permute-start | bytes 589832 | tf_op jit(solution)/shard_map/ppermute | solution.py:321
  57.4 4.4 %collective-permute-done.4.refs_2_ = bf16[128,768]{1,0:T(8,128)(2,1)S(1)} collective-permute-done((bf16[128,768]{1,0:T(8,128)(2,1)S(1)}, bf16[128,768]{1,0:T(8,128)(2,1)S(1)}, u32[]{:S(2)}, u32[]{:S(2)}) %collective-permute-start.4) | collective-permute-done | bytes 196640 | tf_op jit(solution)/shard_map/ppermute | solution.py:318
  61.9 0.9 %collective-permute-start.7 = (bf16[128,768]{1,0:T(8,128)(2,1)S(1)}, bf16[128,768]{1,0:T(8,128)(2,1)S(1)}, u32[]{:S(2)}, u32[]{:S(2)}) collective-permute-start(bf16[128,768]{1,0:T(8,128)(2,1)S(1)} %collective-permute-done.4.refs_2_), channel_id=1, source_target_pairs={{0,1},{1,0},{2,3},{3,2},{4,5},{5,4},{6,7},{7,6},{8,9},{9,8},{10,11... | collective-permute-start | bytes 589832 | tf_op jit(solution)/shard_map/ppermute | solution.py:321
  62.7 0.0 collective-permute-done.5.refs_3_
  62.7 0.0 collective-permute-done.6.refs_4_
  62.7 1.1 %collective-permute-done.7.refs_5_ = bf16[128,768]{1,0:T(8,128)(2,1)S(1)} collective-permute-done((bf16[128,768]{1,0:T(8,128)(2,1)S(1)}, bf16[128,768]{1,0:T(8,128)(2,1)S(1)}, u32[]{:S(2)}, u32[]{:S(2)}) %collective-permute-start.7) | collective-permute-done | bytes 196640 | tf_op jit(solution)/shard_map/ppermute | solution.py:321
  63.8 4.9 %couple.1 = bf16[2,64,2,768]{3,2,1,0:T(2,128)(2,1)} custom-call(bf16[256,768]{1,0:T(8,128)(2,1)S(1)} %get-tuple-element.11.refs_0_, bf16[128,768]{1,0:T(8,128)(2,1)S(1)} %collective-permute-done.3.refs_1_, bf16[128,768]{1,0:T(8,128)(2,1)S(1)} %collective-permute-done.4.refs_2_, bf16[256,768]{1,0:T(8,128)(2,1)S(1)} %collective-permute-done.5.refs_3_, ...), custom_call_target="tpu_custom_call" | custom-call | tf_op jit(solution)/shard_map/couple/pallas_call | solution.py:348
  (3 shorter events, 0.1 us)
Async XLA Ops:
  3.9 7.8 %copy-start.5 = (f32[64,3]{0,1:T(4,128)S(1)}, f32[64,3]{0,1:T(4,128)}, u32[]{:S(2)}) copy-start(f32[64,3]{0,1:T(4,128)} %param.18) | copy-start | bytes 2308
  4.0 8.0 %copy-start.1 = (bf16[2,64,16,16]{1,3,2,0:T(8,128)(2,1)S(1)}, bf16[2,64,16,16]{1,3,2,0:T(8,128)(2,1)}, u32[]{:S(2)}) copy-start(bf16[2,64,16,16]{1,3,2,0:T(8,128)(2,1)} %param.20) | copy-start | bytes 196612
  4.0 8.1 %copy-start = (bf16[2,2,64,16,16]{2,4,3,1,0:T(8,128)(2,1)S(1)}, bf16[2,2,64,16,16]{2,4,3,1,0:T(8,128)(2,1)}, u32[]{:S(2)}) copy-start(bf16[2,2,64,16,16]{2,4,3,1,0:T(8,128)(2,1)} %param.21) | copy-start | bytes 393220
  4.0 8.7 %copy-start.3 = (s32[64,16]{0,1:T(8,128)S(1)}, s32[64,16]{0,1:T(8,128)}, u32[]{:S(2)}) copy-start(s32[64,16]{0,1:T(8,128)} %param.22) | copy-start | bytes 12292
  4.0 8.7 %copy-start.2 = (s32[2,64,16]{1,2,0:T(8,128)S(1)}, s32[2,64,16]{1,2,0:T(8,128)}, u32[]{:S(2)}) copy-start(s32[2,64,16]{1,2,0:T(8,128)} %param.23) | copy-start | bytes 24580
  4.0 30.6 %all-to-all-start = ((bf16[16,64,768]{2,1,0:T(8,128)(2,1)}), bf16[16,64,768]{2,1,0:T(8,128)(2,1)S(1)}, u32[]{:S(2)}, u32[]{:S(2)}) async-start(bf16[16,64,768]{2,1,0:T(8,128)(2,1)} %rotate.1), calls=%async_computation | async-start | bytes 3145728 | tf_op jit(solution)/shard_map/all_to_all | solution.py:280
  11.7 1.1 %copy-start.4 = (s32[256,3]{0,1:T(4,128)S(1)}, s32[256,3]{0,1:T(4,128)}, u32[]{:S(2)}) copy-start(s32[256,3]{0,1:T(4,128)} %param.15) | copy-start | bytes 9220
  11.8 1.1 %copy-start.6 = (s32[256]{0:T(256)S(1)}, s32[256]{0:T(256)}, u32[]{:S(2)}) copy-start(s32[256]{0:T(256)} %param.16) | copy-start | bytes 3076
  34.8 11.9 %collective-permute-start = (bf16[64,768]{1,0:T(8,128)(2,1)S(1)}, bf16[64,768]{1,0:T(8,128)(2,1)S(1)}, u32[]{:S(2)}, u32[]{:S(2)}) collective-permute-start(bf16[64,768]{1,0:T(8,128)(2,1)S(1)} %add_up.1.own_ref), channel_id=1, source_target_pairs={{0,4},{1,5},{2,6},{3,7},{4,8},{5,9},{6,10},{7,11},{8,12},{9,13},{1... | collective-permute-start | bytes 294920 | tf_op jit(solution)/shard_map/ppermute | solution.py:318
  37.9 9.7 %collective-permute-start.1 = (bf16[64,768]{1,0:T(8,128)(2,1)S(1)}, bf16[64,768]{1,0:T(8,128)(2,1)S(1)}, u32[]{:S(2)}, u32[]{:S(2)}) collective-permute-start(bf16[64,768]{1,0:T(8,128)(2,1)S(1)} %add_up.1.own_ref), channel_id=1, source_target_pairs={{0,12},{1,13},{2,14},{3,15},{4,0},{5,1},{6,2},{7,3},{8,4},{9,5},{1... | collective-permute-start | bytes 294920 | tf_op jit(solution)/shard_map/ppermute | solution.py:318
  41.0 9.8 %collective-permute-start.2 = (bf16[64,768]{1,0:T(8,128)(2,1)S(1)}, bf16[64,768]{1,0:T(8,128)(2,1)S(1)}, u32[]{:S(2)}, u32[]{:S(2)}) collective-permute-start(bf16[64,768]{1,0:T(8,128)(2,1)S(1)} %add_up.1.own_ref), channel_id=1, source_target_pairs={{0,8},{1,9},{2,10},{3,11},{4,12},{5,13},{6,14},{7,15},{8,0},{9,1},... | collective-permute-start | bytes 294920 | tf_op jit(solution)/shard_map/ppermute | solution.py:318
  46.8 9.1 %collective-permute-start.3 = (bf16[128,768]{1,0:T(8,128)(2,1)S(1)}, bf16[128,768]{1,0:T(8,128)(2,1)S(1)}, u32[]{:S(2)}, u32[]{:S(2)}) collective-permute-start(bf16[128,768]{1,0:T(8,128)(2,1)S(1)} %pack.1), channel_id=1, source_target_pairs={{0,2},{1,3},{2,4},{3,5},{4,6},{5,7},{6,8},{7,9},{8,10},{9,11},{10,... | collective-permute-start | bytes 589832 | tf_op jit(solution)/shard_map/ppermute | solution.py:318
  50.9 11.8 %collective-permute-start.5 = (bf16[256,768]{1,0:T(8,128)(2,1)S(1)}, bf16[256,768]{1,0:T(8,128)(2,1)S(1)}, u32[]{:S(2)}, u32[]{:S(2)}) collective-permute-start(bf16[256,768]{1,0:T(8,128)(2,1)S(1)} %get-tuple-element.11.refs_0_), channel_id=1, source_target_pairs={{0,1},{1,0},{2,3},{3,2},{4,5},{5,4},{6,7},{7,6},{8,9},{9,8},{10,11... | collective-permute-start | bytes 1179656 | tf_op jit(solution)/shard_map/ppermute | solution.py:321
  55.4 6.5 %collective-permute-start.4 = (bf16[128,768]{1,0:T(8,128)(2,1)S(1)}, bf16[128,768]{1,0:T(8,128)(2,1)S(1)}, u32[]{:S(2)}, u32[]{:S(2)}) collective-permute-start(bf16[128,768]{1,0:T(8,128)(2,1)S(1)} %get-tuple-element.12), channel_id=1, source_target_pairs={{0,14},{1,15},{2,0},{3,1},{4,2},{5,3},{6,4},{7,5},{8,6},{9,7},{10,... | collective-permute-start | bytes 589832 | tf_op jit(solution)/shard_map/ppermute | solution.py:318
  55.9 6.8 %collective-permute-start.6 = (bf16[128,768]{1,0:T(8,128)(2,1)S(1)}, bf16[128,768]{1,0:T(8,128)(2,1)S(1)}, u32[]{:S(2)}, u32[]{:S(2)}) collective-permute-start(bf16[128,768]{1,0:T(8,128)(2,1)S(1)} %collective-permute-done.3.refs_1_), channel_id=1, source_target_pairs={{0,1},{1,0},{2,3},{3,2},{4,5},{5,4},{6,7},{7,6},{8,9},{9,8},{10,11... | collective-permute-start | bytes 589832 | tf_op jit(solution)/shard_map/ppermute | solution.py:321
  61.9 1.9 %collective-permute-start.7 = (bf16[128,768]{1,0:T(8,128)(2,1)S(1)}, bf16[128,768]{1,0:T(8,128)(2,1)S(1)}, u32[]{:S(2)}, u32[]{:S(2)}) collective-permute-start(bf16[128,768]{1,0:T(8,128)(2,1)S(1)} %collective-permute-done.4.refs_2_), channel_id=1, source_target_pairs={{0,1},{1,0},{2,3},{3,2},{4,5},{5,4},{6,7},{7,6},{8,9},{9,8},{10,11... | collective-permute-start | bytes 589832 | tf_op jit(solution)/shard_map/ppermute | solution.py:321

commit v9 on v6

--- a/solution.py
+++ b/solution.py
@@ -145,21 +145,24 @@
             lo_ref[i, b] = left[b * 16:(b + 1) * 16] * mq
 
 
-def pack_body(own_ref, across_ref, order_ref, out_ref):
-    out_ref[0:ROWS, :] = own_ref[...]
-    out_ref[ROWS:2 * ROWS, :] = across_ref[...]
-
-
-PLACE = ((0, 0), (3, 0), (1, 0), (4, 1), (0, 1), (3, 1), (2, 0), (4, 0))
+def pack_body(own_ref, back_ref, ahead_ref, order_ref, three_ref, two_ref):
+    for i, ref in enumerate((own_ref, back_ref, ahead_ref)):
+        value = ref[...]
+        three_ref[i * ROWS:(i + 1) * ROWS, :] = value
+        if i > 0:
+            two_ref[(i - 1) * ROWS:i * ROWS, :] = value
+
+
+PLACE = ((0, 0), (1, 0), (2, 0), (0, 1), (1, 1), (2, 1), (0, 2), (1, 2))
 
 
 def couple_body(*refs):
-    ph_ref, u_ref, l_ref, out_ref, y_ref, bl_ref, h_ref, r_ref = refs[10:]
+    ph_ref, u_ref, l_ref, out_ref, y_ref, bl_ref, h_ref, r_ref = refs[6:]
     ph = ph_ref[...]
     for q in range(NQ):
         x = jnp.concatenate(
             [
-                refs[side * 5 + i][j * ROWS + q * 32:j * ROWS + (q + 1) * 32, :]
+                refs[side * 3 + i][j * ROWS + q * 32:j * ROWS + (q + 1) * 32, :]
                 for side in range(2)
                 for i, j in PLACE
             ],
@@ -313,22 +316,28 @@
     def swap(x):
         return lax.ppermute(x, "kpt", [(i, i ^ 1) for i in range(16)])
 
-    across = shift(own, 4)
-    packed = pl.pallas_call(
+    back = shift(own, 3)
+    ahead = shift(own, -2)
+    packed, pair = pl.pallas_call(
         pack_body,
-        out_shape=jax.ShapeDtypeStruct((2 * ROWS, LANES), bf16),
-        in_specs=[vmem()] * 2 + [pl.BlockSpec(memory_space=pl.ANY)],
-        out_specs=vmem(),
+        out_shape=(
+            jax.ShapeDtypeStruct((3 * ROWS, LANES), bf16),
+            jax.ShapeDtypeStruct((2 * ROWS, LANES), bf16),
+        ),
+        in_specs=[vmem()] * 3 + [pl.BlockSpec(memory_space=pl.ANY)],
+        out_specs=(vmem(), vmem()),
         compiler_params=params(),
         name="pack",
-    )(own, across, phase)
-    near = [packed, shift(own, 2), shift(own, -2), shift(packed, 1), shift(packed, -1)]
+    )(own, back, ahead, phase)
+    plus = shift(packed, 1)
+    minus = shift(pair, -1)
+    near = [packed, plus, minus]
     far = [swap(x) for x in near]
 
     result = pl.pallas_call(
         couple_body,
         out_shape=jax.ShapeDtypeStruct((2, KPTS, NQ, LANES), bf16),
-        in_specs=[vmem()] * 13,
+        in_specs=[vmem()] * 9,
         out_specs=vmem(),
         scratch_shapes=[
             pltpu.VMEM((2, 2 * PER, 128, 128), f32),

time: 68.3 us -> 64.2 us (0.940)
  starting transfers between devices: 33 us -> 27.1 us
  waiting for transfers between devices: 23.4 us -> 25.3 us
    ppermute x5 -> x4, starting transfers between devices: 14.7 us -> 9.29 us  [shift(): return lax.ppermute(x, 'kpt', [(i, (i + 2 * step) % 16) for i in range(16)])]
    ppermute x5 -> x4, waiting for transfers between devices: 0.76 us -> 2.27 us  [shift(): return lax.ppermute(x, 'kpt', [(i, (i + 2 * step) % 16) for i in range(16)])]
    ppermute x5 -> x3, starting transfers between devices: 10.6 us -> 10.1 us  [swap(): return lax.ppermute(x, 'kpt', [(i, i ^ 1) for i in range(16)])]
  transfers between devices with their start and end apart: 11 -> 8, of which waited for: 3 -> 4; matrix products, arithmetic and copies ran while one was open for 2% -> 2% of each run, Pallas kernels for 2% -> 2%
where the time goes in v9:
time: 64.2 us; the launch traced here: 64 us
  starting transfers between devices  27.1 us (42%)
  waiting for transfers between devices  25.3 us (39%)
  Pallas kernels  9.69 us (15%)
  local copies, waits for them, and re-layouts  1.01 us (2%)
  between operations  0.83 us (1%)
    all_to_all x1, waiting for transfers between devices, per_device(): parts = lax.all_to_all(rotated, 'lat', 0, 0, tiled=True)  21.7 us
    ppermute x3, starting transfers between devices, swap(): return lax.ppermute(x, 'kpt', [(i, i ^ 1) for i in range(16)])  10.1 us
    ppermute x4, starting transfers between devices, shift(): return lax.ppermute(x, 'kpt', [(i, (i + 2 * step) % 16) for i in range(16)])  9.29 us
    all_to_all x1, starting transfers between devices, per_device(): parts = lax.all_to_all(rotated, 'lat', 0, 0, tiled=True)  7.73 us
    pallas_call x1, Pallas kernels, per_device(): pl.pallas_call(couple_body, out_shape=jax.ShapeDtypeStruct((2, KPTS, NQ,...  4.89 us
    pallas_call x1, Pallas kernels, per_device(): pl.pallas_call(rotate_body, out_shape=jax.ShapeDtypeStruct((LAT, ROWS, LA...  3.29 us
    ppermute x4, waiting for transfers between devices, shift(): return lax.ppermute(x, 'kpt', [(i, (i + 2 * step) % 16) for i in range(16)])  2.27 us
  transfers between devices with their start and end apart: 8, of which 4 were waited for; matrix products, arithmetic and copies ran while one was open for 2% of the time, Pallas kernels for 2%

profile of v9, /device:TPU:1, one launch (start us, length us, event | category | flops | bytes accessed | tf_op | source)
XLA Modules:
  0.0 64.0 jit_solution(9600207812210266764)
XLA Ops:
  0.7 3.3 %rotate.1 = bf16[16,64,768]{2,1,0:T(8,128)(2,1)} custom-call(f32[2,3]{1,0:T(2,128)} %qp_hbm.1, s32[1,3]{1,0:T(1,128)} %rv_hbm.1, s32[1,1]{1,0:T(1,128)} %bitcast.9.rw_hbm, bf16[2,2,48,48]{3,2,1,0:T(8,128)(2,1)} %rot_hbm.1, bf16[2,1,16,12288]{3,2,1,0:T(8,128)(2,1)} %coarse_hbm.1), custom_call_target="tpu_custom_call" | custom-call | tf_op jit(solution)/shard_map/rotate/pallas_call | solution.py:257
  3.9 0.0 copy-start.5
  4.0 0.0 copy-start.1
  4.0 0.0 copy-start
  4.0 0.0 copy-start.3
  4.0 0.0 copy-start.2
  4.0 7.7 %all-to-all-start = ((bf16[16,64,768]{2,1,0:T(8,128)(2,1)}), bf16[16,64,768]{2,1,0:T(8,128)(2,1)S(1)}, u32[]{:S(2)}, u32[]{:S(2)}) async-start(bf16[16,64,768]{2,1,0:T(8,128)(2,1)} %rotate.1), calls=%async_computation | async-start | bytes 3145728 | tf_op jit(solution)/shard_map/all_to_all | solution.py:276
  11.7 0.0 copy-start.4
  11.8 0.0 copy-start.6
  11.8 0.0 copy-done.5
  11.8 0.1 copy.20.kp_ref
  11.9 0.1 pad.2.clone
  12.0 0.0 copy-done.1
  12.0 0.1 copy.21.u_ref
  12.1 0.0 copy-done
  12.1 0.3 copy.18
  12.4 0.1 reshape.10
  12.5 0.1 copy.22.uq_ref
  12.6 0.0 copy-done.3
  12.6 0.1 copy.23.mk_ref
  12.7 0.0 copy-done.2
  12.7 0.1 copy.19
  12.8 0.0 copy-done.4
  12.8 0.0 copy-done.6
  12.8 0.1 add_add_fusion.rv_ref
  12.9 21.7 %all-to-all-done.x_ref = bf16[16,64,768]{2,1,0:T(8,128)(2,1)S(1)} async-done(((bf16[16,64,768]{2,1,0:T(8,128)(2,1)}), bf16[16,64,768]{2,1,0:T(8,128)(2,1)S(1)}, u32[]{:S(2)}, u32[]{:S(2)}) %all-to-all-start) | async-done | bytes 1572896 | tf_op jit(solution)/shard_map/all_to_all | solution.py:276
  34.6 0.2 add_up.1.own_ref
  34.8 4.4 %collective-permute-start = (bf16[64,768]{1,0:T(8,128)(2,1)S(1)}, bf16[64,768]{1,0:T(8,128)(2,1)S(1)}, u32[]{:S(2)}, u32[]{:S(2)}) collective-permute-start(bf16[64,768]{1,0:T(8,128)(2,1)S(1)} %add_up.1.own_ref), channel_id=1, source_target_pairs={{0,6},{1,7},{2,8},{3,9},{4,10},{5,11},{6,12},{7,13},{8,14},{9,15},... | collective-permute-start | bytes 294920 | tf_op jit(solution)/shard_map/ppermute | solution.py:314
  39.2 1.8 %collective-permute-start.1 = (bf16[64,768]{1,0:T(8,128)(2,1)S(1)}, bf16[64,768]{1,0:T(8,128)(2,1)S(1)}, u32[]{:S(2)}, u32[]{:S(2)}) collective-permute-start(bf16[64,768]{1,0:T(8,128)(2,1)S(1)} %add_up.1.own_ref), channel_id=1, source_target_pairs={{0,12},{1,13},{2,14},{3,15},{4,0},{5,1},{6,2},{7,3},{8,4},{9,5},{1... | collective-permute-start | bytes 294920 | tf_op jit(solution)/shard_map/ppermute | solution.py:314
  41.0 0.1 pad_add_fusion.at_ref
  41.1 1.3 %prep.1 = (bf16[128,512]{1,0:T(8,128)(2,1)S(1)}, f32[3,16,16,128]{3,2,1,0:T(8,128)S(1)}, f32[3,16,16,128]{3,2,1,0:T(8,128)S(1)}) custom-call(s32[2]{0:T(128)S(1)} %pad_add_fusion.at_ref, f32[64,3]{1,0:T(8,128)S(1)} %copy.20.kp_ref, s32[8,256]{1,0:T(8,128)S(1)} %add_add_fusion.rv_ref, bf16[2,64,256]{2,1,0:T(8,128)(2,1)S(1)} %copy.21.u_ref, ...), custom_call_target="tpu_custom_call" | custom-call | tf_op jit(solution)/shard_map/prep/pallas_call | solution.py:283
  42.4 1.2 %collective-permute-done.back_ref = bf16[64,768]{1,0:T(8,128)(2,1)S(1)} collective-permute-done((bf16[64,768]{1,0:T(8,128)(2,1)S(1)}, bf16[64,768]{1,0:T(8,128)(2,1)S(1)}, u32[]{:S(2)}, u32[]{:S(2)}) %collective-permute-start) | collective-permute-done | bytes 98336 | tf_op jit(solution)/shard_map/ppermute | solution.py:314
  43.6 1.1 %collective-permute-done.1.ahead_ref = bf16[64,768]{1,0:T(8,128)(2,1)S(1)} collective-permute-done((bf16[64,768]{1,0:T(8,128)(2,1)S(1)}, bf16[64,768]{1,0:T(8,128)(2,1)S(1)}, u32[]{:S(2)}, u32[]{:S(2)}) %collective-permute-start.1) | collective-permute-done | bytes 98336 | tf_op jit(solution)/shard_map/ppermute | solution.py:314
  44.7 2.2 %collective-permute-start.2 = (bf16[192,768]{1,0:T(8,128)(2,1)S(1)}, bf16[192,768]{1,0:T(8,128)(2,1)S(1)}, u32[]{:S(2)}, u32[]{:S(2)}) collective-permute-start(bf16[192,768]{1,0:T(8,128)(2,1)S(1)} %get-tuple-element.11.refs_0_), channel_id=1, source_target_pairs={{0,2},{1,3},{2,4},{3,5},{4,6},{5,7},{6,8},{7,9},{8,10},{9,11},{10,... | collective-permute-start | bytes 884744 | tf_op jit(solution)/shard_map/ppermute | solution.py:314
  46.9 0.9 %collective-permute-start.3 = (bf16[128,768]{1,0:T(8,128)(2,1)S(1)}, bf16[128,768]{1,0:T(8,128)(2,1)S(1)}, u32[]{:S(2)}, u32[]{:S(2)}) collective-permute-start(bf16[128,768]{1,0:T(8,128)(2,1)S(1)} %get-tuple-element.12), channel_id=1, source_target_pairs={{0,14},{1,15},{2,0},{3,1},{4,2},{5,3},{6,4},{7,5},{8,6},{9,7},{10,... | collective-permute-start | bytes 589832 | tf_op jit(solution)/shard_map/ppermute | solution.py:314
  47.8 5.3 %collective-permute-start.4 = (bf16[192,768]{1,0:T(8,128)(2,1)S(1)}, bf16[192,768]{1,0:T(8,128)(2,1)S(1)}, u32[]{:S(2)}, u32[]{:S(2)}) collective-permute-start(bf16[192,768]{1,0:T(8,128)(2,1)S(1)} %get-tuple-element.11.refs_0_), channel_id=1, source_target_pairs={{0,1},{1,0},{2,3},{3,2},{4,5},{5,4},{6,7},{7,6},{8,9},{9,8},{10,11... | collective-permute-start | bytes 884744 | tf_op jit(solution)/shard_map/ppermute | solution.py:317
  53.0 0.0 collective-permute-done.2.refs_1_
  53.0 4.6 %collective-permute-start.5 = (bf16[192,768]{1,0:T(8,128)(2,1)S(1)}, bf16[192,768]{1,0:T(8,128)(2,1)S(1)}, u32[]{:S(2)}, u32[]{:S(2)}) collective-permute-start(bf16[192,768]{1,0:T(8,128)(2,1)S(1)} %collective-permute-done.2.refs_1_), channel_id=1, source_target_pairs={{0,1},{1,0},{2,3},{3,2},{4,5},{5,4},{6,7},{7,6},{8,9},{9,8},{10,11... | collective-permute-start | bytes 884744 | tf_op jit(solution)/shard_map/ppermute | solution.py:317
  57.7 0.0 collective-permute-done.3.refs_2_
  57.7 0.2 collective-permute-start.6
  57.9 0.0 collective-permute-done.4.refs_3_
  57.9 1.3 %collective-permute-done.6.refs_5_ = bf16[128,768]{1,0:T(8,128)(2,1)S(1)} collective-permute-done((bf16[128,768]{1,0:T(8,128)(2,1)S(1)}, bf16[128,768]{1,0:T(8,128)(2,1)S(1)}, u32[]{:S(2)}, u32[]{:S(2)}) %collective-permute-start.6) | collective-permute-done | bytes 196640 | tf_op jit(solution)/shard_map/ppermute | solution.py:317
  59.1 0.0 collective-permute-done.5.refs_4_
  59.1 4.9 %couple.1 = bf16[2,64,2,768]{3,2,1,0:T(2,128)(2,1)} custom-call(bf16[192,768]{1,0:T(8,128)(2,1)S(1)} %get-tuple-element.11.refs_0_, bf16[192,768]{1,0:T(8,128)(2,1)S(1)} %collective-permute-done.2.refs_1_, bf16[128,768]{1,0:T(8,128)(2,1)S(1)} %collective-permute-done.3.refs_2_, bf16[192,768]{1,0:T(8,128)(2,1)S(1)} %collective-permute-done.4.refs_3_, ...), custom_call_target="tpu_custom_call" | custom-call | tf_op jit(solution)/shard_map/couple/pallas_call | solution.py:337
  (2 shorter events, 0.0 us)
Async XLA Ops:
  3.9 7.8 %copy-start.5 = (f32[64,3]{0,1:T(4,128)S(1)}, f32[64,3]{0,1:T(4,128)}, u32[]{:S(2)}) copy-start(f32[64,3]{0,1:T(4,128)} %param.18) | copy-start | bytes 2308
  4.0 8.0 %copy-start.1 = (bf16[2,64,16,16]{1,3,2,0:T(8,128)(2,1)S(1)}, bf16[2,64,16,16]{1,3,2,0:T(8,128)(2,1)}, u32[]{:S(2)}) copy-start(bf16[2,64,16,16]{1,3,2,0:T(8,128)(2,1)} %param.20) | copy-start | bytes 196612
  4.0 8.1 %copy-start = (bf16[2,2,64,16,16]{2,4,3,1,0:T(8,128)(2,1)S(1)}, bf16[2,2,64,16,16]{2,4,3,1,0:T(8,128)(2,1)}, u32[]{:S(2)}) copy-start(bf16[2,2,64,16,16]{2,4,3,1,0:T(8,128)(2,1)} %param.21) | copy-start | bytes 393220
  4.0 8.7 %copy-start.3 = (s32[64,16]{0,1:T(8,128)S(1)}, s32[64,16]{0,1:T(8,128)}, u32[]{:S(2)}) copy-start(s32[64,16]{0,1:T(8,128)} %param.22) | copy-start | bytes 12292
  4.0 8.7 %copy-start.2 = (s32[2,64,16]{1,2,0:T(8,128)S(1)}, s32[2,64,16]{1,2,0:T(8,128)}, u32[]{:S(2)}) copy-start(s32[2,64,16]{1,2,0:T(8,128)} %param.23) | copy-start | bytes 24580
  4.0 30.6 %all-to-all-start = ((bf16[16,64,768]{2,1,0:T(8,128)(2,1)}), bf16[16,64,768]{2,1,0:T(8,128)(2,1)S(1)}, u32[]{:S(2)}, u32[]{:S(2)}) async-start(bf16[16,64,768]{2,1,0:T(8,128)(2,1)} %rotate.1), calls=%async_computation | async-start | bytes 3145728 | tf_op jit(solution)/shard_map/all_to_all | solution.py:276
  11.7 1.1 %copy-start.4 = (s32[256,3]{0,1:T(4,128)S(1)}, s32[256,3]{0,1:T(4,128)}, u32[]{:S(2)}) copy-start(s32[256,3]{0,1:T(4,128)} %param.15) | copy-start | bytes 9220
  11.8 1.1 %copy-start.6 = (s32[256]{0:T(256)S(1)}, s32[256]{0:T(256)}, u32[]{:S(2)}) copy-start(s32[256]{0:T(256)} %param.16) | copy-start | bytes 3076
  34.8 8.8 %collective-permute-start = (bf16[64,768]{1,0:T(8,128)(2,1)S(1)}, bf16[64,768]{1,0:T(8,128)(2,1)S(1)}, u32[]{:S(2)}, u32[]{:S(2)}) collective-permute-start(bf16[64,768]{1,0:T(8,128)(2,1)S(1)} %add_up.1.own_ref), channel_id=1, source_target_pairs={{0,6},{1,7},{2,8},{3,9},{4,10},{5,11},{6,12},{7,13},{8,14},{9,15},... | collective-permute-start | bytes 294920 | tf_op jit(solution)/shard_map/ppermute | solution.py:314
  39.2 5.4 %collective-permute-start.1 = (bf16[64,768]{1,0:T(8,128)(2,1)S(1)}, bf16[64,768]{1,0:T(8,128)(2,1)S(1)}, u32[]{:S(2)}, u32[]{:S(2)}) collective-permute-start(bf16[64,768]{1,0:T(8,128)(2,1)S(1)} %add_up.1.own_ref), channel_id=1, source_target_pairs={{0,12},{1,13},{2,14},{3,15},{4,0},{5,1},{6,2},{7,3},{8,4},{9,5},{1... | collective-permute-start | bytes 294920 | tf_op jit(solution)/shard_map/ppermute | solution.py:314
  44.7 8.3 %collective-permute-start.2 = (bf16[192,768]{1,0:T(8,128)(2,1)S(1)}, bf16[192,768]{1,0:T(8,128)(2,1)S(1)}, u32[]{:S(2)}, u32[]{:S(2)}) collective-permute-start(bf16[192,768]{1,0:T(8,128)(2,1)S(1)} %get-tuple-element.11.refs_0_), channel_id=1, source_target_pairs={{0,2},{1,3},{2,4},{3,5},{4,6},{5,7},{6,8},{7,9},{8,10},{9,11},{10,... | collective-permute-start | bytes 884744 | tf_op jit(solution)/shard_map/ppermute | solution.py:314
  46.9 10.8 %collective-permute-start.3 = (bf16[128,768]{1,0:T(8,128)(2,1)S(1)}, bf16[128,768]{1,0:T(8,128)(2,1)S(1)}, u32[]{:S(2)}, u32[]{:S(2)}) collective-permute-start(bf16[128,768]{1,0:T(8,128)(2,1)S(1)} %get-tuple-element.12), channel_id=1, source_target_pairs={{0,14},{1,15},{2,0},{3,1},{4,2},{5,3},{6,4},{7,5},{8,6},{9,7},{10,... | collective-permute-start | bytes 589832 | tf_op jit(solution)/shard_map/ppermute | solution.py:314
  47.8 10.1 %collective-permute-start.4 = (bf16[192,768]{1,0:T(8,128)(2,1)S(1)}, bf16[192,768]{1,0:T(8,128)(2,1)S(1)}, u32[]{:S(2)}, u32[]{:S(2)}) collective-permute-start(bf16[192,768]{1,0:T(8,128)(2,1)S(1)} %get-tuple-element.11.refs_0_), channel_id=1, source_target_pairs={{0,1},{1,0},{2,3},{3,2},{4,5},{5,4},{6,7},{7,6},{8,9},{9,8},{10,11... | collective-permute-start | bytes 884744 | tf_op jit(solution)/shard_map/ppermute | solution.py:317
  53.0 6.1 %collective-permute-start.5 = (bf16[192,768]{1,0:T(8,128)(2,1)S(1)}, bf16[192,768]{1,0:T(8,128)(2,1)S(1)}, u32[]{:S(2)}, u32[]{:S(2)}) collective-permute-start(bf16[192,768]{1,0:T(8,128)(2,1)S(1)} %collective-permute-done.2.refs_1_), channel_id=1, source_target_pairs={{0,1},{1,0},{2,3},{3,2},{4,5},{5,4},{6,7},{7,6},{8,9},{9,8},{10,11... | collective-permute-start | bytes 884744 | tf_op jit(solution)/shard_map/ppermute | solution.py:317
  57.7 1.5 %collective-permute-start.6 = (bf16[128,768]{1,0:T(8,128)(2,1)S(1)}, bf16[128,768]{1,0:T(8,128)(2,1)S(1)}, u32[]{:S(2)}, u32[]{:S(2)}) collective-permute-start(bf16[128,768]{1,0:T(8,128)(2,1)S(1)} %collective-permute-done.3.refs_2_), channel_id=1, source_target_pairs={{0,1},{1,0},{2,3},{3,2},{4,5},{5,4},{6,7},{7,6},{8,9},{9,8},{10,11... | collective-permute-start | bytes 589832 | tf_op jit(solution)/shard_map/ppermute | solution.py:317

commit v10 on v9

--- a/solution.py
+++ b/solution.py
@@ -145,7 +145,7 @@
             lo_ref[i, b] = left[b * 16:(b + 1) * 16] * mq
 
 
-def pack_body(own_ref, back_ref, ahead_ref, order_ref, three_ref, two_ref):
+def pack_body(own_ref, back_ref, ahead_ref, three_ref, two_ref):
     for i, ref in enumerate((own_ref, back_ref, ahead_ref)):
         value = ref[...]
         three_ref[i * ROWS:(i + 1) * ROWS, :] = value
@@ -270,9 +270,15 @@
             pltpu.VMEM((2 * PER, LAT * STRIDE_O, 128), f32),
             pltpu.SemaphoreType.DMA((4 + 2 * CHUNKS,)),
         ],
-        compiler_params=pltpu.CompilerParams(vmem_limit_bytes=63 << 20),
+        compiler_params=pltpu.CompilerParams(vmem_limit_bytes=40 << 20),
         name="rotate",
-    )(q_points, rp_vectors, rp_weights[None, :], modes_rot, coarse)
+    )(
+        pltpu.with_memory_space_constraint(q_points, pltpu.HBM),
+        pltpu.with_memory_space_constraint(rp_vectors, pltpu.HBM),
+        rp_weights[None, :],
+        pltpu.with_memory_space_constraint(modes_rot, pltpu.HBM),
+        pltpu.with_memory_space_constraint(coarse, pltpu.HBM),
+    )
     parts = lax.all_to_all(rotated, "lat", 0, 0, tiled=True)
 
     index = lax.axis_index("kpt")
@@ -324,11 +330,11 @@
             jax.ShapeDtypeStruct((3 * ROWS, LANES), bf16),
             jax.ShapeDtypeStruct((2 * ROWS, LANES), bf16),
         ),
-        in_specs=[vmem()] * 3 + [pl.BlockSpec(memory_space=pl.ANY)],
+        in_specs=[vmem()] * 3,
         out_specs=(vmem(), vmem()),
         compiler_params=params(),
         name="pack",
-    )(own, back, ahead, phase)
+    )(own, back, ahead)
     plus = shift(packed, 1)
     minus = shift(pair, -1)
     near = [packed, plus, minus]

time: 64.2 us -> 61 us (0.950)
  blocking collectives: 0 us -> 29.1 us
  waiting for transfers between devices: 25.3 us -> 3.89 us
  starting transfers between devices: 27.1 us -> 17.4 us
  Pallas kernels: 9.69 us -> 8.52 us
    all_to_all x0 -> x1, blocking collectives: none -> 29.1 us  [per_device(): parts = lax.all_to_all(rotated, 'lat', 0, 0, tiled=True)]
    all_to_all x1 -> x0, waiting for transfers between devices: 21.7 us -> none  [per_device(): parts = lax.all_to_all(rotated, 'lat', 0, 0, tiled=True)]
    all_to_all x1 -> x0, starting transfers between devices: 7.73 us -> none  [per_device(): parts = lax.all_to_all(rotated, 'lat', 0, 0, tiled=True)]
    ppermute x3, starting transfers between devices: 10.1 us -> 8.19 us  [swap(): return lax.ppermute(x, 'kpt', [(i, i ^ 1) for i in range(16)])]
    ppermute x4, waiting for transfers between devices: 2.27 us -> 3.88 us  [shift(): return lax.ppermute(x, 'kpt', [(i, (i + 2 * step) % 16) for i in range(16)])]
    ppermute x3, waiting for transfers between devices: 1.28 us -> 0.01 us  [swap(): return lax.ppermute(x, 'kpt', [(i, i ^ 1) for i in range(16)])]
    pallas_call x1, Pallas kernels: 3.29 us -> 2.11 us  [per_device(): pl.pallas_call(rotate_body, out_shape=jax.ShapeDtypeStruct((LAT, ROWS, LA...]
  transfers between devices with their start and end apart: 8 -> 7, of which waited for: 4 -> 2; matrix products, arithmetic and copies ran while one was open for 2% -> 2% of each run, Pallas kernels for 2% -> 2%
where the time goes in v10:
time: 61 us; the launch traced here: 60.8 us
  blocking collectives  29.1 us (48%)
  starting transfers between devices  17.4 us (29%)
  Pallas kernels  8.52 us (14%)
  waiting for transfers between devices  3.89 us (6%)
  local copies, waits for them, and re-layouts  1 us (2%)
  between operations  0.79 us (1%)
    all_to_all x1, blocking collectives, per_device(): parts = lax.all_to_all(rotated, 'lat', 0, 0, tiled=True)  29.1 us
    ppermute x4, starting transfers between devices, shift(): return lax.ppermute(x, 'kpt', [(i, (i + 2 * step) % 16) for i in range(16)])  9.16 us
    ppermute x3, starting transfers between devices, swap(): return lax.ppermute(x, 'kpt', [(i, i ^ 1) for i in range(16)])  8.19 us
    pallas_call x1, Pallas kernels, per_device(): pl.pallas_call(couple_body, out_shape=jax.ShapeDtypeStruct((2, KPTS, NQ,...  4.89 us
    ppermute x4, waiting for transfers between devices, shift(): return lax.ppermute(x, 'kpt', [(i, (i + 2 * step) % 16) for i in range(16)])  3.88 us
    pallas_call x1, Pallas kernels, per_device(): pl.pallas_call(rotate_body, out_shape=jax.ShapeDtypeStruct((LAT, ROWS, LA...  2.11 us
    pallas_call x1, Pallas kernels, per_device(): pl.pallas_call(prep_body, out_shape=(jax.ShapeDtypeStruct((2 * KPTS, 512)...  1.28 us
  transfers between devices with their start and end apart: 7, of which 2 were waited for; matrix products, arithmetic and copies ran while one was open for 2% of the time, Pallas kernels for 2%

profile of v10, /device:TPU:1, one launch (start us, length us, event | category | flops | bytes accessed | tf_op | source)
XLA Modules:
  0.0 60.8 jit_solution(16203486309824441156)
XLA Ops:
  0.7 2.1 %rotate.1 = bf16[16,64,768]{2,1,0:T(8,128)(2,1)S(1)} custom-call(f32[2,3]{1,0:T(2,128)} %qp_hbm.1, s32[1,3]{1,0:T(1,128)} %rv_hbm.1, s32[1,1]{1,0:T(1,128)} %bitcast.9.rw_hbm, bf16[2,2,48,48]{3,2,1,0:T(8,128)(2,1)} %rot_hbm.1, bf16[2,1,16,12288]{3,2,1,0:T(8,128)(2,1)} %coarse_hbm.1), custom_call_target="tpu_custom_call" | custom-call | tf_op jit(solution)/shard_map/rotate/pallas_call | solution.py:257
  2.8 29.1 %all_to_all.5.x_ref = bf16[16,64,768]{2,1,0:T(8,128)(2,1)S(1)} all-to-all(bf16[16,64,768]{2,1,0:T(8,128)(2,1)S(1)} %rotate.1), channel_id=1, replica_groups=mesh['lat'=16,'kpt'=16] {'lat'}, dimensions={0} | all-to-all | bytes 3145728 | tf_op jit(solution)/shard_map/all_to_all | solution.py:282
  31.9 0.0 copy-start.5
  31.9 0.0 copy-start.1
  31.9 0.0 copy-start
  31.9 0.0 copy-start.3
  31.9 0.0 copy-start.2
  31.9 0.0 copy-start.4
  31.9 0.0 copy-start.6
  31.9 0.2 add_up.1.own_ref
  32.2 4.4 %collective-permute-start = (bf16[64,768]{1,0:T(8,128)(2,1)S(1)}, bf16[64,768]{1,0:T(8,128)(2,1)S(1)}, u32[]{:S(2)}, u32[]{:S(2)}) collective-permute-start(bf16[64,768]{1,0:T(8,128)(2,1)S(1)} %add_up.1.own_ref), channel_id=1, source_target_pairs={{0,6},{1,7},{2,8},{3,9},{4,10},{5,11},{6,12},{7,13},{8,14},{9,15},... | collective-permute-start | bytes 294920 | tf_op jit(solution)/shard_map/ppermute | solution.py:320
  36.6 1.8 %collective-permute-start.1 = (bf16[64,768]{1,0:T(8,128)(2,1)S(1)}, bf16[64,768]{1,0:T(8,128)(2,1)S(1)}, u32[]{:S(2)}, u32[]{:S(2)}) collective-permute-start(bf16[64,768]{1,0:T(8,128)(2,1)S(1)} %add_up.1.own_ref), channel_id=1, source_target_pairs={{0,12},{1,13},{2,14},{3,15},{4,0},{5,1},{6,2},{7,3},{8,4},{9,5},{1... | collective-permute-start | bytes 294920 | tf_op jit(solution)/shard_map/ppermute | solution.py:320
  38.3 2.6 %collective-permute-done.back_ref = bf16[64,768]{1,0:T(8,128)(2,1)S(1)} collective-permute-done((bf16[64,768]{1,0:T(8,128)(2,1)S(1)}, bf16[64,768]{1,0:T(8,128)(2,1)S(1)}, u32[]{:S(2)}, u32[]{:S(2)}) %collective-permute-start) | collective-permute-done | bytes 98336 | tf_op jit(solution)/shard_map/ppermute | solution.py:320
  40.9 1.3 %collective-permute-done.1.ahead_ref = bf16[64,768]{1,0:T(8,128)(2,1)S(1)} collective-permute-done((bf16[64,768]{1,0:T(8,128)(2,1)S(1)}, bf16[64,768]{1,0:T(8,128)(2,1)S(1)}, u32[]{:S(2)}, u32[]{:S(2)}) %collective-permute-start.1) | collective-permute-done | bytes 98336 | tf_op jit(solution)/shard_map/ppermute | solution.py:320
  42.3 2.0 %collective-permute-start.2 = (bf16[192,768]{1,0:T(8,128)(2,1)S(1)}, bf16[192,768]{1,0:T(8,128)(2,1)S(1)}, u32[]{:S(2)}, u32[]{:S(2)}) collective-permute-start(bf16[192,768]{1,0:T(8,128)(2,1)S(1)} %get-tuple-element.10.refs_0_), channel_id=1, source_target_pairs={{0,2},{1,3},{2,4},{3,5},{4,6},{5,7},{6,8},{7,9},{8,10},{9,11},{10,... | collective-permute-start | bytes 884744 | tf_op jit(solution)/shard_map/ppermute | solution.py:320
  44.2 1.0 %collective-permute-start.3 = (bf16[128,768]{1,0:T(8,128)(2,1)S(1)}, bf16[128,768]{1,0:T(8,128)(2,1)S(1)}, u32[]{:S(2)}, u32[]{:S(2)}) collective-permute-start(bf16[128,768]{1,0:T(8,128)(2,1)S(1)} %get-tuple-element.11), channel_id=1, source_target_pairs={{0,14},{1,15},{2,0},{3,1},{4,2},{5,3},{6,4},{7,5},{8,6},{9,7},{10,... | collective-permute-start | bytes 589832 | tf_op jit(solution)/shard_map/ppermute | solution.py:320
  45.2 0.0 copy-done.5
  45.2 0.1 copy.20.kp_ref
  45.3 0.1 pad.2.clone
  45.4 0.0 copy-done.1
  45.4 0.1 copy.21.u_ref
  45.5 0.0 copy-done
  45.5 0.3 copy.18
  45.8 0.1 reshape.10
  46.0 0.1 copy.22.uq_ref
  46.1 0.0 copy-done.3
  46.1 0.1 copy.23.mk_ref
  46.2 0.0 copy-done.2
  46.2 0.1 copy.19
  46.3 3.5 %collective-permute-start.4 = (bf16[192,768]{1,0:T(8,128)(2,1)S(1)}, bf16[192,768]{1,0:T(8,128)(2,1)S(1)}, u32[]{:S(2)}, u32[]{:S(2)}) collective-permute-start(bf16[192,768]{1,0:T(8,128)(2,1)S(1)} %get-tuple-element.10.refs_0_), channel_id=1, source_target_pairs={{0,1},{1,0},{2,3},{3,2},{4,5},{5,4},{6,7},{7,6},{8,9},{9,8},{10,11... | collective-permute-start | bytes 884744 | tf_op jit(solution)/shard_map/ppermute | solution.py:323
  49.8 0.0 collective-permute-done.2.refs_1_
  49.8 3.6 %collective-permute-start.5 = (bf16[192,768]{1,0:T(8,128)(2,1)S(1)}, bf16[192,768]{1,0:T(8,128)(2,1)S(1)}, u32[]{:S(2)}, u32[]{:S(2)}) collective-permute-start(bf16[192,768]{1,0:T(8,128)(2,1)S(1)} %collective-permute-done.2.refs_1_), channel_id=1, source_target_pairs={{0,1},{1,0},{2,3},{3,2},{4,5},{5,4},{6,7},{7,6},{8,9},{9,8},{10,11... | collective-permute-start | bytes 884744 | tf_op jit(solution)/shard_map/ppermute | solution.py:323
  53.4 0.1 pad_add_fusion.at_ref
  53.5 0.0 collective-permute-done.3.refs_2_
  53.5 1.0 %collective-permute-start.6 = (bf16[128,768]{1,0:T(8,128)(2,1)S(1)}, bf16[128,768]{1,0:T(8,128)(2,1)S(1)}, u32[]{:S(2)}, u32[]{:S(2)}) collective-permute-start(bf16[128,768]{1,0:T(8,128)(2,1)S(1)} %collective-permute-done.3.refs_2_), channel_id=1, source_target_pairs={{0,1},{1,0},{2,3},{3,2},{4,5},{5,4},{6,7},{7,6},{8,9},{9,8},{10,11... | collective-permute-start | bytes 589832 | tf_op jit(solution)/shard_map/ppermute | solution.py:323
  54.5 0.0 copy-done.4
  54.5 0.0 copy-done.6
  54.5 0.1 add_add_fusion.rv_ref
  54.6 1.3 %prep.1 = (bf16[128,512]{1,0:T(8,128)(2,1)S(1)}, f32[3,16,16,128]{3,2,1,0:T(8,128)S(1)}, f32[3,16,16,128]{3,2,1,0:T(8,128)S(1)}) custom-call(s32[2]{0:T(128)S(1)} %pad_add_fusion.at_ref, f32[64,3]{1,0:T(8,128)S(1)} %copy.20.kp_ref, s32[8,256]{1,0:T(8,128)S(1)} %add_add_fusion.rv_ref, bf16[2,64,256]{2,1,0:T(8,128)(2,1)S(1)} %copy.21.u_ref, ...), custom_call_target="tpu_custom_call" | custom-call | tf_op jit(solution)/shard_map/prep/pallas_call | solution.py:289
  55.9 0.0 collective-permute-done.4.refs_3_
  55.9 0.0 collective-permute-done.6.refs_5_
  55.9 0.0 collective-permute-done.5.refs_4_
  55.9 4.9 %couple.1 = bf16[2,64,2,768]{3,2,1,0:T(2,128)(2,1)} custom-call(bf16[192,768]{1,0:T(8,128)(2,1)S(1)} %get-tuple-element.10.refs_0_, bf16[192,768]{1,0:T(8,128)(2,1)S(1)} %collective-permute-done.2.refs_1_, bf16[128,768]{1,0:T(8,128)(2,1)S(1)} %collective-permute-done.3.refs_2_, bf16[192,768]{1,0:T(8,128)(2,1)S(1)} %collective-permute-done.4.refs_3_, ...), custom_call_target="tpu_custom_call" | custom-call | tf_op jit(solution)/shard_map/couple/pallas_call | solution.py:343
  (2 shorter events, 0.0 us)
Async XLA Ops:
  31.9 13.3 %copy-start.5 = (f32[64,3]{0,1:T(4,128)S(1)}, f32[64,3]{0,1:T(4,128)}, u32[]{:S(2)}) copy-start(f32[64,3]{0,1:T(4,128)} %param.18) | copy-start | bytes 2308
  31.9 13.5 %copy-start.1 = (bf16[2,64,16,16]{1,3,2,0:T(8,128)(2,1)S(1)}, bf16[2,64,16,16]{1,3,2,0:T(8,128)(2,1)}, u32[]{:S(2)}) copy-start(bf16[2,64,16,16]{1,3,2,0:T(8,128)(2,1)} %param.20) | copy-start | bytes 196612
  31.9 13.6 %copy-start = (bf16[2,2,64,16,16]{2,4,3,1,0:T(8,128)(2,1)S(1)}, bf16[2,2,64,16,16]{2,4,3,1,0:T(8,128)(2,1)}, u32[]{:S(2)}) copy-start(bf16[2,2,64,16,16]{2,4,3,1,0:T(8,128)(2,1)} %param.21) | copy-start | bytes 393220
  31.9 14.2 %copy-start.3 = (s32[64,16]{0,1:T(8,128)S(1)}, s32[64,16]{0,1:T(8,128)}, u32[]{:S(2)}) copy-start(s32[64,16]{0,1:T(8,128)} %param.22) | copy-start | bytes 12292
  31.9 14.3 %copy-start.2 = (s32[2,64,16]{1,2,0:T(8,128)S(1)}, s32[2,64,16]{1,2,0:T(8,128)}, u32[]{:S(2)}) copy-start(s32[2,64,16]{1,2,0:T(8,128)} %param.23) | copy-start | bytes 24580
  31.9 22.6 %copy-start.4 = (s32[256,3]{0,1:T(4,128)S(1)}, s32[256,3]{0,1:T(4,128)}, u32[]{:S(2)}) copy-start(s32[256,3]{0,1:T(4,128)} %param.15) | copy-start | bytes 9220
  31.9 22.6 %copy-start.6 = (s32[256]{0:T(256)S(1)}, s32[256]{0:T(256)}, u32[]{:S(2)}) copy-start(s32[256]{0:T(256)} %param.16) | copy-start | bytes 3076
  32.2 8.8 %collective-permute-start = (bf16[64,768]{1,0:T(8,128)(2,1)S(1)}, bf16[64,768]{1,0:T(8,128)(2,1)S(1)}, u32[]{:S(2)}, u32[]{:S(2)}) collective-permute-start(bf16[64,768]{1,0:T(8,128)(2,1)S(1)} %add_up.1.own_ref), channel_id=1, source_target_pairs={{0,6},{1,7},{2,8},{3,9},{4,10},{5,11},{6,12},{7,13},{8,14},{9,15},... | collective-permute-start | bytes 294920 | tf_op jit(solution)/shard_map/ppermute | solution.py:320
  36.6 5.6 %collective-permute-start.1 = (bf16[64,768]{1,0:T(8,128)(2,1)S(1)}, bf16[64,768]{1,0:T(8,128)(2,1)S(1)}, u32[]{:S(2)}, u32[]{:S(2)}) collective-permute-start(bf16[64,768]{1,0:T(8,128)(2,1)S(1)} %add_up.1.own_ref), channel_id=1, source_target_pairs={{0,12},{1,13},{2,14},{3,15},{4,0},{5,1},{6,2},{7,3},{8,4},{9,5},{1... | collective-permute-start | bytes 294920 | tf_op jit(solution)/shard_map/ppermute | solution.py:320
  42.3 7.5 %collective-permute-start.2 = (bf16[192,768]{1,0:T(8,128)(2,1)S(1)}, bf16[192,768]{1,0:T(8,128)(2,1)S(1)}, u32[]{:S(2)}, u32[]{:S(2)}) collective-permute-start(bf16[192,768]{1,0:T(8,128)(2,1)S(1)} %get-tuple-element.10.refs_0_), channel_id=1, source_target_pairs={{0,2},{1,3},{2,4},{3,5},{4,6},{5,7},{6,8},{7,9},{8,10},{9,11},{10,... | collective-permute-start | bytes 884744 | tf_op jit(solution)/shard_map/ppermute | solution.py:320
  44.2 9.3 %collective-permute-start.3 = (bf16[128,768]{1,0:T(8,128)(2,1)S(1)}, bf16[128,768]{1,0:T(8,128)(2,1)S(1)}, u32[]{:S(2)}, u32[]{:S(2)}) collective-permute-start(bf16[128,768]{1,0:T(8,128)(2,1)S(1)} %get-tuple-element.11), channel_id=1, source_target_pairs={{0,14},{1,15},{2,0},{3,1},{4,2},{5,3},{6,4},{7,5},{8,6},{9,7},{10,... | collective-permute-start | bytes 589832 | tf_op jit(solution)/shard_map/ppermute | solution.py:320
  46.3 9.6 %collective-permute-start.4 = (bf16[192,768]{1,0:T(8,128)(2,1)S(1)}, bf16[192,768]{1,0:T(8,128)(2,1)S(1)}, u32[]{:S(2)}, u32[]{:S(2)}) collective-permute-start(bf16[192,768]{1,0:T(8,128)(2,1)S(1)} %get-tuple-element.10.refs_0_), channel_id=1, source_target_pairs={{0,1},{1,0},{2,3},{3,2},{4,5},{5,4},{6,7},{7,6},{8,9},{9,8},{10,11... | collective-permute-start | bytes 884744 | tf_op jit(solution)/shard_map/ppermute | solution.py:323
  49.8 6.1 %collective-permute-start.5 = (bf16[192,768]{1,0:T(8,128)(2,1)S(1)}, bf16[192,768]{1,0:T(8,128)(2,1)S(1)}, u32[]{:S(2)}, u32[]{:S(2)}) collective-permute-start(bf16[192,768]{1,0:T(8,128)(2,1)S(1)} %collective-permute-done.2.refs_1_), channel_id=1, source_target_pairs={{0,1},{1,0},{2,3},{3,2},{4,5},{5,4},{6,7},{7,6},{8,9},{9,8},{10,11... | collective-permute-start | bytes 884744 | tf_op jit(solution)/shard_map/ppermute | solution.py:323
  53.5 2.4 %collective-permute-start.6 = (bf16[128,768]{1,0:T(8,128)(2,1)S(1)}, bf16[128,768]{1,0:T(8,128)(2,1)S(1)}, u32[]{:S(2)}, u32[]{:S(2)}) collective-permute-start(bf16[128,768]{1,0:T(8,128)(2,1)S(1)} %collective-permute-done.3.refs_2_), channel_id=1, source_target_pairs={{0,1},{1,0},{2,3},{3,2},{4,5},{5,4},{6,7},{7,6},{8,9},{9,8},{10,11... | collective-permute-start | bytes 589832 | tf_op jit(solution)/shard_map/ppermute | solution.py:323

commit v11 on v10

--- a/solution.py
+++ b/solution.py
@@ -145,15 +145,15 @@
             lo_ref[i, b] = left[b * 16:(b + 1) * 16] * mq
 
 
-def pack_body(own_ref, back_ref, ahead_ref, three_ref, two_ref):
-    for i, ref in enumerate((own_ref, back_ref, ahead_ref)):
+def pack_body(own_ref, back_ref, ahead_ref, prev_ref, next_ref, all_ref, two_ref):
+    for i, ref in enumerate((own_ref, back_ref, ahead_ref, prev_ref, next_ref)):
         value = ref[...]
-        three_ref[i * ROWS:(i + 1) * ROWS, :] = value
-        if i > 0:
+        all_ref[i * ROWS:(i + 1) * ROWS, :] = value
+        if i in (1, 2):
             two_ref[(i - 1) * ROWS:i * ROWS, :] = value
 
 
-PLACE = ((0, 0), (1, 0), (2, 0), (0, 1), (1, 1), (2, 1), (0, 2), (1, 2))
+PLACE = ((0, 0), (0, 3), (1, 0), (0, 1), (2, 0), (1, 1), (0, 2), (0, 4))
 
 
 def couple_body(*refs):
@@ -327,17 +327,15 @@
     packed, pair = pl.pallas_call(
         pack_body,
         out_shape=(
-            jax.ShapeDtypeStruct((3 * ROWS, LANES), bf16),
+            jax.ShapeDtypeStruct((5 * ROWS, LANES), bf16),
             jax.ShapeDtypeStruct((2 * ROWS, LANES), bf16),
         ),
-        in_specs=[vmem()] * 3,
+        in_specs=[vmem()] * 5,
         out_specs=(vmem(), vmem()),
         compiler_params=params(),
         name="pack",
-    )(own, back, ahead)
-    plus = shift(packed, 1)
-    minus = shift(pair, -1)
-    near = [packed, plus, minus]
+    )(own, back, ahead, shift(own, 1), shift(own, -1))
+    near = [packed, shift(pair, -1), shift(back, 1)]
     far = [swap(x) for x in near]
 
     result = pl.pallas_call(

time: 61 us -> 63.1 us (1.034)
  waiting for transfers between devices: 3.89 us -> 8.52 us
  starting transfers between devices: 17.4 us -> 14.9 us
    ppermute x4 -> x6, waiting for transfers between devices: 3.88 us -> 8.51 us  [shift(): return lax.ppermute(x, 'kpt', [(i, (i + 2 * step) % 16) for i in range(16)])]
    ppermute x3, starting transfers between devices: 8.19 us -> 4.44 us  [swap(): return lax.ppermute(x, 'kpt', [(i, i ^ 1) for i in range(16)])]
    ppermute x4 -> x6, starting transfers between devices: 9.16 us -> 10.4 us  [shift(): return lax.ppermute(x, 'kpt', [(i, (i + 2 * step) % 16) for i in range(16)])]
  transfers between devices with their start and end apart: 7 -> 9, of which waited for: 2 -> 4; matrix products, arithmetic and copies ran while one was open for 2% -> 2% of each run, Pallas kernels for 2% -> 2%
where the time goes in v11:
time: 63.1 us; the launch traced here: 63 us
  blocking collectives  29.1 us (46%)
  starting transfers between devices  14.9 us (24%)
  Pallas kernels  8.53 us (14%)
  waiting for transfers between devices  8.52 us (14%)
  local copies, waits for them, and re-layouts  1 us (2%)
  between operations  0.8 us (1%)
    all_to_all x1, blocking collectives, per_device(): parts = lax.all_to_all(rotated, 'lat', 0, 0, tiled=True)  29.1 us
    ppermute x6, starting transfers between devices, shift(): return lax.ppermute(x, 'kpt', [(i, (i + 2 * step) % 16) for i in range(16)])  10.4 us
    ppermute x6, waiting for transfers between devices, shift(): return lax.ppermute(x, 'kpt', [(i, (i + 2 * step) % 16) for i in range(16)])  8.51 us
    pallas_call x1, Pallas kernels, per_device(): pl.pallas_call(couple_body, out_shape=jax.ShapeDtypeStruct((2, KPTS, NQ,...  4.89 us
    ppermute x3, starting transfers between devices, swap(): return lax.ppermute(x, 'kpt', [(i, i ^ 1) for i in range(16)])  4.44 us
    pallas_call x1, Pallas kernels, per_device(): pl.pallas_call(rotate_body, out_shape=jax.ShapeDtypeStruct((LAT, ROWS, LA...  2.11 us
    pallas_call x1, Pallas kernels, per_device(): pl.pallas_call(prep_body, out_shape=(jax.ShapeDtypeStruct((2 * KPTS, 512)...  1.28 us
  transfers between devices with their start and end apart: 9, of which 4 were waited for; matrix products, arithmetic and copies ran while one was open for 2% of the time, Pallas kernels for 2%

profile of v11, /device:TPU:1, one launch (start us, length us, event | category | flops | bytes accessed | tf_op | source)
XLA Modules:
  0.0 63.0 jit_solution(5648807747597271525)
XLA Ops:
  0.7 2.1 %rotate.1 = bf16[16,64,768]{2,1,0:T(8,128)(2,1)S(1)} custom-call(f32[2,3]{1,0:T(2,128)} %qp_hbm.1, s32[1,3]{1,0:T(1,128)} %rv_hbm.1, s32[1,1]{1,0:T(1,128)} %bitcast.9.rw_hbm, bf16[2,2,48,48]{3,2,1,0:T(8,128)(2,1)} %rot_hbm.1, bf16[2,1,16,12288]{3,2,1,0:T(8,128)(2,1)} %coarse_hbm.1), custom_call_target="tpu_custom_call" | custom-call | tf_op jit(solution)/shard_map/rotate/pallas_call | solution.py:257
  2.8 29.1 %all_to_all.5.x_ref = bf16[16,64,768]{2,1,0:T(8,128)(2,1)S(1)} all-to-all(bf16[16,64,768]{2,1,0:T(8,128)(2,1)S(1)} %rotate.1), channel_id=1, replica_groups=mesh['lat'=16,'kpt'=16] {'lat'}, dimensions={0} | all-to-all | bytes 3145728 | tf_op jit(solution)/shard_map/all_to_all | solution.py:282
  31.9 0.0 copy-start.4
  31.9 0.0 copy-start.6
  31.9 0.0 copy-start.5
  31.9 0.0 copy-start.1
  31.9 0.0 copy-start
  31.9 0.0 copy-start.3
  31.9 0.0 copy-start.2
  31.9 0.2 add_up.1.own_ref
  32.2 4.4 %collective-permute-start = (bf16[64,768]{1,0:T(8,128)(2,1)S(1)}, bf16[64,768]{1,0:T(8,128)(2,1)S(1)}, u32[]{:S(2)}, u32[]{:S(2)}) collective-permute-start(bf16[64,768]{1,0:T(8,128)(2,1)S(1)} %add_up.1.own_ref), channel_id=1, source_target_pairs={{0,6},{1,7},{2,8},{3,9},{4,10},{5,11},{6,12},{7,13},{8,14},{9,15},... | collective-permute-start | bytes 294920 | tf_op jit(solution)/shard_map/ppermute | solution.py:320
  36.6 1.8 %collective-permute-start.1 = (bf16[64,768]{1,0:T(8,128)(2,1)S(1)}, bf16[64,768]{1,0:T(8,128)(2,1)S(1)}, u32[]{:S(2)}, u32[]{:S(2)}) collective-permute-start(bf16[64,768]{1,0:T(8,128)(2,1)S(1)} %add_up.1.own_ref), channel_id=1, source_target_pairs={{0,12},{1,13},{2,14},{3,15},{4,0},{5,1},{6,2},{7,3},{8,4},{9,5},{1... | collective-permute-start | bytes 294920 | tf_op jit(solution)/shard_map/ppermute | solution.py:320
  38.3 1.1 %collective-permute-start.2 = (bf16[64,768]{1,0:T(8,128)(2,1)S(1)}, bf16[64,768]{1,0:T(8,128)(2,1)S(1)}, u32[]{:S(2)}, u32[]{:S(2)}) collective-permute-start(bf16[64,768]{1,0:T(8,128)(2,1)S(1)} %add_up.1.own_ref), channel_id=1, source_target_pairs={{0,2},{1,3},{2,4},{3,5},{4,6},{5,7},{6,8},{7,9},{8,10},{9,11},{10,... | collective-permute-start | bytes 294920 | tf_op jit(solution)/shard_map/ppermute | solution.py:320
  39.4 1.6 %collective-permute-start.3 = (bf16[64,768]{1,0:T(8,128)(2,1)S(1)}, bf16[64,768]{1,0:T(8,128)(2,1)S(1)}, u32[]{:S(2)}, u32[]{:S(2)}) collective-permute-start(bf16[64,768]{1,0:T(8,128)(2,1)S(1)} %add_up.1.own_ref), channel_id=1, source_target_pairs={{0,14},{1,15},{2,0},{3,1},{4,2},{5,3},{6,4},{7,5},{8,6},{9,7},{10,... | collective-permute-start | bytes 294920 | tf_op jit(solution)/shard_map/ppermute | solution.py:320
  41.0 0.0 collective-permute-done.back_ref
  41.0 1.2 %collective-permute-done.1.ahead_ref = bf16[64,768]{1,0:T(8,128)(2,1)S(1)} collective-permute-done((bf16[64,768]{1,0:T(8,128)(2,1)S(1)}, bf16[64,768]{1,0:T(8,128)(2,1)S(1)}, u32[]{:S(2)}, u32[]{:S(2)}) %collective-permute-start.1) | collective-permute-done | bytes 98336 | tf_op jit(solution)/shard_map/ppermute | solution.py:320
  42.2 4.7 %collective-permute-done.2.prev_ref = bf16[64,768]{1,0:T(8,128)(2,1)S(1)} collective-permute-done((bf16[64,768]{1,0:T(8,128)(2,1)S(1)}, bf16[64,768]{1,0:T(8,128)(2,1)S(1)}, u32[]{:S(2)}, u32[]{:S(2)}) %collective-permute-start.2) | collective-permute-done | bytes 98336 | tf_op jit(solution)/shard_map/ppermute | solution.py:320
  46.9 0.0 collective-permute-done.3.next_ref
  46.9 1.5 %collective-permute-start.4 = (bf16[128,768]{1,0:T(8,128)(2,1)S(1)}, bf16[128,768]{1,0:T(8,128)(2,1)S(1)}, u32[]{:S(2)}, u32[]{:S(2)}) collective-permute-start(bf16[128,768]{1,0:T(8,128)(2,1)S(1)} %get-tuple-element.11), channel_id=1, source_target_pairs={{0,14},{1,15},{2,0},{3,1},{4,2},{5,3},{6,4},{7,5},{8,6},{9,7},{10,... | collective-permute-start | bytes 589832 | tf_op jit(solution)/shard_map/ppermute | solution.py:320
  48.5 1.7 %collective-permute-start.6 = (bf16[320,768]{1,0:T(8,128)(2,1)S(1)}, bf16[320,768]{1,0:T(8,128)(2,1)S(1)}, u32[]{:S(2)}, u32[]{:S(2)}) collective-permute-start(bf16[320,768]{1,0:T(8,128)(2,1)S(1)} %get-tuple-element.10.refs_0_), channel_id=1, source_target_pairs={{0,1},{1,0},{2,3},{3,2},{4,5},{5,4},{6,7},{7,6},{8,9},{9,8},{10,11... | collective-permute-start | bytes 1474568 | tf_op jit(solution)/shard_map/ppermute | solution.py:323
  50.2 0.1 pad.2.clone
  50.3 0.0 collective-permute-start.5
  50.3 2.1 %collective-permute-done.4.refs_1_ = bf16[128,768]{1,0:T(8,128)(2,1)S(1)} collective-permute-done((bf16[128,768]{1,0:T(8,128)(2,1)S(1)}, bf16[128,768]{1,0:T(8,128)(2,1)S(1)}, u32[]{:S(2)}, u32[]{:S(2)}) %collective-permute-start.4) | collective-permute-done | bytes 196640 | tf_op jit(solution)/shard_map/ppermute | solution.py:320
  52.4 1.9 %collective-permute-start.7 = (bf16[128,768]{1,0:T(8,128)(2,1)S(1)}, bf16[128,768]{1,0:T(8,128)(2,1)S(1)}, u32[]{:S(2)}, u32[]{:S(2)}) collective-permute-start(bf16[128,768]{1,0:T(8,128)(2,1)S(1)} %collective-permute-done.4.refs_1_), channel_id=1, source_target_pairs={{0,1},{1,0},{2,3},{3,2},{4,5},{5,4},{6,7},{7,6},{8,9},{9,8},{10,11... | collective-permute-start | bytes 589832 | tf_op jit(solution)/shard_map/ppermute | solution.py:323
  54.3 0.0 copy-done.4
  54.3 0.0 copy-done.6
  54.3 0.1 add_add_fusion.rv_ref
  54.4 0.0 copy-done.5
  54.4 0.1 copy.20.kp_ref
  54.5 0.0 copy-done.1
  54.5 0.1 copy.21.u_ref
  54.6 0.0 copy-done
  54.6 0.3 copy.18
  54.9 0.1 reshape.10
  55.0 0.1 copy.22.uq_ref
  55.2 0.0 copy-done.3
  55.2 0.1 copy.23.mk_ref
  55.3 0.0 copy-done.2
  55.3 0.1 copy.19
  55.3 0.6 collective-permute-done.5.refs_2_
  55.9 0.8 %collective-permute-start.8 = (bf16[64,768]{1,0:T(8,128)(2,1)S(1)}, bf16[64,768]{1,0:T(8,128)(2,1)S(1)}, u32[]{:S(2)}, u32[]{:S(2)}) collective-permute-start(bf16[64,768]{1,0:T(8,128)(2,1)S(1)} %collective-permute-done.5.refs_2_), channel_id=1, source_target_pairs={{0,1},{1,0},{2,3},{3,2},{4,5},{5,4},{6,7},{7,6},{8,9},{9,8},{10,11... | collective-permute-start | bytes 294920 | tf_op jit(solution)/shard_map/ppermute | solution.py:323
  56.7 0.1 pad_add_fusion.at_ref
  56.8 1.3 %prep.1 = (bf16[128,512]{1,0:T(8,128)(2,1)S(1)}, f32[3,16,16,128]{3,2,1,0:T(8,128)S(1)}, f32[3,16,16,128]{3,2,1,0:T(8,128)S(1)}) custom-call(s32[2]{0:T(128)S(1)} %pad_add_fusion.at_ref, f32[64,3]{1,0:T(8,128)S(1)} %copy.20.kp_ref, s32[8,256]{1,0:T(8,128)S(1)} %add_add_fusion.rv_ref, bf16[2,64,256]{2,1,0:T(8,128)(2,1)S(1)} %copy.21.u_ref, ...), custom_call_target="tpu_custom_call" | custom-call | tf_op jit(solution)/shard_map/prep/pallas_call | solution.py:289
  58.1 0.0 collective-permute-done.8.refs_5_
  58.1 0.0 collective-permute-done.7.refs_4_
  58.1 0.0 collective-permute-done.6.refs_3_
  58.1 4.9 %couple.1 = bf16[2,64,2,768]{3,2,1,0:T(2,128)(2,1)} custom-call(bf16[320,768]{1,0:T(8,128)(2,1)S(1)} %get-tuple-element.10.refs_0_, bf16[128,768]{1,0:T(8,128)(2,1)S(1)} %collective-permute-done.4.refs_1_, bf16[64,768]{1,0:T(8,128)(2,1)S(1)} %collective-permute-done.5.refs_2_, bf16[320,768]{1,0:T(8,128)(2,1)S(1)} %collective-permute-done.6.refs_3_, ...), custom_call_target="tpu_custom_call" | custom-call | tf_op jit(solution)/shard_map/couple/pallas_call | solution.py:341
  (2 shorter events, 0.0 us)
Async XLA Ops:
  31.9 22.4 %copy-start.4 = (s32[256,3]{0,1:T(4,128)S(1)}, s32[256,3]{0,1:T(4,128)}, u32[]{:S(2)}) copy-start(s32[256,3]{0,1:T(4,128)} %param.15) | copy-start | bytes 9220
  31.9 22.4 %copy-start.6 = (s32[256]{0:T(256)S(1)}, s32[256]{0:T(256)}, u32[]{:S(2)}) copy-start(s32[256]{0:T(256)} %param.16) | copy-start | bytes 3076
  31.9 22.5 %copy-start.5 = (f32[64,3]{0,1:T(4,128)S(1)}, f32[64,3]{0,1:T(4,128)}, u32[]{:S(2)}) copy-start(f32[64,3]{0,1:T(4,128)} %param.18) | copy-start | bytes 2308
  31.9 22.6 %copy-start.1 = (bf16[2,64,16,16]{1,3,2,0:T(8,128)(2,1)S(1)}, bf16[2,64,16,16]{1,3,2,0:T(8,128)(2,1)}, u32[]{:S(2)}) copy-start(bf16[2,64,16,16]{1,3,2,0:T(8,128)(2,1)} %param.20) | copy-start | bytes 196612
  31.9 22.7 %copy-start = (bf16[2,2,64,16,16]{2,4,3,1,0:T(8,128)(2,1)S(1)}, bf16[2,2,64,16,16]{2,4,3,1,0:T(8,128)(2,1)}, u32[]{:S(2)}) copy-start(bf16[2,2,64,16,16]{2,4,3,1,0:T(8,128)(2,1)} %param.21) | copy-start | bytes 393220
  31.9 23.3 %copy-start.3 = (s32[64,16]{0,1:T(8,128)S(1)}, s32[64,16]{0,1:T(8,128)}, u32[]{:S(2)}) copy-start(s32[64,16]{0,1:T(8,128)} %param.22) | copy-start | bytes 12292
  31.9 23.3 %copy-start.2 = (s32[2,64,16]{1,2,0:T(8,128)S(1)}, s32[2,64,16]{1,2,0:T(8,128)}, u32[]{:S(2)}) copy-start(s32[2,64,16]{1,2,0:T(8,128)} %param.23) | copy-start | bytes 24580
  32.2 8.9 %collective-permute-start = (bf16[64,768]{1,0:T(8,128)(2,1)S(1)}, bf16[64,768]{1,0:T(8,128)(2,1)S(1)}, u32[]{:S(2)}, u32[]{:S(2)}) collective-permute-start(bf16[64,768]{1,0:T(8,128)(2,1)S(1)} %add_up.1.own_ref), channel_id=1, source_target_pairs={{0,6},{1,7},{2,8},{3,9},{4,10},{5,11},{6,12},{7,13},{8,14},{9,15},... | collective-permute-start | bytes 294920 | tf_op jit(solution)/shard_map/ppermute | solution.py:320
  36.6 5.6 %collective-permute-start.1 = (bf16[64,768]{1,0:T(8,128)(2,1)S(1)}, bf16[64,768]{1,0:T(8,128)(2,1)S(1)}, u32[]{:S(2)}, u32[]{:S(2)}) collective-permute-start(bf16[64,768]{1,0:T(8,128)(2,1)S(1)} %add_up.1.own_ref), channel_id=1, source_target_pairs={{0,12},{1,13},{2,14},{3,15},{4,0},{5,1},{6,2},{7,3},{8,4},{9,5},{1... | collective-permute-start | bytes 294920 | tf_op jit(solution)/shard_map/ppermute | solution.py:320
  38.3 8.5 %collective-permute-start.2 = (bf16[64,768]{1,0:T(8,128)(2,1)S(1)}, bf16[64,768]{1,0:T(8,128)(2,1)S(1)}, u32[]{:S(2)}, u32[]{:S(2)}) collective-permute-start(bf16[64,768]{1,0:T(8,128)(2,1)S(1)} %add_up.1.own_ref), channel_id=1, source_target_pairs={{0,2},{1,3},{2,4},{3,5},{4,6},{5,7},{6,8},{7,9},{8,10},{9,11},{10,... | collective-permute-start | bytes 294920 | tf_op jit(solution)/shard_map/ppermute | solution.py:320
  39.4 7.4 %collective-permute-start.3 = (bf16[64,768]{1,0:T(8,128)(2,1)S(1)}, bf16[64,768]{1,0:T(8,128)(2,1)S(1)}, u32[]{:S(2)}, u32[]{:S(2)}) collective-permute-start(bf16[64,768]{1,0:T(8,128)(2,1)S(1)} %add_up.1.own_ref), channel_id=1, source_target_pairs={{0,14},{1,15},{2,0},{3,1},{4,2},{5,3},{6,4},{7,5},{8,6},{9,7},{10,... | collective-permute-start | bytes 294920 | tf_op jit(solution)/shard_map/ppermute | solution.py:320
  46.9 5.5 %collective-permute-start.4 = (bf16[128,768]{1,0:T(8,128)(2,1)S(1)}, bf16[128,768]{1,0:T(8,128)(2,1)S(1)}, u32[]{:S(2)}, u32[]{:S(2)}) collective-permute-start(bf16[128,768]{1,0:T(8,128)(2,1)S(1)} %get-tuple-element.11), channel_id=1, source_target_pairs={{0,14},{1,15},{2,0},{3,1},{4,2},{5,3},{6,4},{7,5},{8,6},{9,7},{10,... | collective-permute-start | bytes 589832 | tf_op jit(solution)/shard_map/ppermute | solution.py:320
  48.5 9.6 %collective-permute-start.6 = (bf16[320,768]{1,0:T(8,128)(2,1)S(1)}, bf16[320,768]{1,0:T(8,128)(2,1)S(1)}, u32[]{:S(2)}, u32[]{:S(2)}) collective-permute-start(bf16[320,768]{1,0:T(8,128)(2,1)S(1)} %get-tuple-element.10.refs_0_), channel_id=1, source_target_pairs={{0,1},{1,0},{2,3},{3,2},{4,5},{5,4},{6,7},{7,6},{8,9},{9,8},{10,11... | collective-permute-start | bytes 1474568 | tf_op jit(solution)/shard_map/ppermute | solution.py:323
  50.3 5.6 %collective-permute-start.5 = (bf16[64,768]{1,0:T(8,128)(2,1)S(1)}, bf16[64,768]{1,0:T(8,128)(2,1)S(1)}, u32[]{:S(2)}, u32[]{:S(2)}) collective-permute-start(bf16[64,768]{1,0:T(8,128)(2,1)S(1)} %collective-permute-done.back_ref), channel_id=1, source_target_pairs={{0,2},{1,3},{2,4},{3,5},{4,6},{5,7},{6,8},{7,9},{8,10},{9,11},{10,... | collective-permute-start | bytes 294920 | tf_op jit(solution)/shard_map/ppermute | solution.py:320
  52.4 5.7 %collective-permute-start.7 = (bf16[128,768]{1,0:T(8,128)(2,1)S(1)}, bf16[128,768]{1,0:T(8,128)(2,1)S(1)}, u32[]{:S(2)}, u32[]{:S(2)}) collective-permute-start(bf16[128,768]{1,0:T(8,128)(2,1)S(1)} %collective-permute-done.4.refs_1_), channel_id=1, source_target_pairs={{0,1},{1,0},{2,3},{3,2},{4,5},{5,4},{6,7},{7,6},{8,9},{9,8},{10,11... | collective-permute-start | bytes 589832 | tf_op jit(solution)/shard_map/ppermute | solution.py:323
  55.9 2.1 %collective-permute-start.8 = (bf16[64,768]{1,0:T(8,128)(2,1)S(1)}, bf16[64,768]{1,0:T(8,128)(2,1)S(1)}, u32[]{:S(2)}, u32[]{:S(2)}) collective-permute-start(bf16[64,768]{1,0:T(8,128)(2,1)S(1)} %collective-permute-done.5.refs_2_), channel_id=1, source_target_pairs={{0,1},{1,0},{2,3},{3,2},{4,5},{5,4},{6,7},{7,6},{8,9},{9,8},{10,11... | collective-permute-start | bytes 294920 | tf_op jit(solution)/shard_map/ppermute | solution.py:323

commit v12 on v11

--- a/solution.py
+++ b/solution.py
@@ -104,9 +104,21 @@
         out_ref[r:r + 16, :] = acc.astype(bf16)
 
 
-def prep_body(at_ref, kp_ref, rv_ref, u_ref, uq_ref, mk_ref, mq_ref, ph_ref, uo_ref, lo_ref):
-    z = at_ref[0]
-    c = at_ref[1]
+def prep_body(*refs):
+    ph_ref, uo_ref, lo_ref = refs[7:10]
+    kp_ref, rv_ref, rw_ref, u_ref, uq_ref, mk_ref, mq_ref = refs[10:17]
+    sems = refs[17]
+    loads = [
+        pltpu.make_async_copy(src, dst, sems.at[i])
+        for i, (src, dst) in enumerate(zip(refs[:7], refs[10:17]))
+    ]
+    for load in loads:
+        load.start()
+    for load in loads:
+        load.wait()
+    place_k = lax.axis_index("kpt")
+    z = place_k >> 1
+    c = place_k & 1
     lane = lax.broadcasted_iota(jnp.int32, (256, 512), 1)
     src = lax.broadcasted_iota(jnp.int32, (256, 512), 0)
     block = lane >> 5
@@ -114,11 +126,12 @@
     cell = (home << 4) + (lane & 15)
     pick = jnp.where(src == cell, 1.0, 0.0).astype(bf16)
     vec = jnp.dot(rv_ref[...].astype(f32).astype(bf16), pick, preferred_element_type=f32)
-    kp = kp_ref[...]
+    weight = jnp.dot(rw_ref[...].astype(f32).astype(bf16), pick, preferred_element_type=f32)
+    kp = kp_ref[...].T
     arg = two_pi * (
         kp[:, 0:1] * vec[0:1, :] + kp[:, 1:2] * vec[1:2, :] + kp[:, 2:3] * vec[2:3, :]
     )
-    inverse = 1.0 / vec[3:4, :]
+    inverse = 1.0 / weight
     co = jnp.cos(arg) * inverse
     si = jnp.sin(arg) * inverse
     first = (lax.broadcasted_iota(jnp.int32, (KPTS, 512), 1) & 16) == 0
@@ -127,42 +140,39 @@
     row = lax.broadcasted_iota(jnp.int32, (KPTS, 128), 0)
     col = lax.broadcasted_iota(jnp.int32, (KPTS, 128), 1)
     spread = jnp.where((col >> 1) == row, 1.0, 0.0).astype(bf16)
-    row2 = lax.broadcasted_iota(jnp.int32, (128, 128), 0)
-    col2 = lax.broadcasted_iota(jnp.int32, (128, 128), 1)
-    place = jnp.where((((col2 & 1) << 6) + (col2 >> 1)) == row2, 1.0, 0.0).astype(bf16)
-    dims = (((0,), (0,)), ((), ()))
-    mk = lax.dot_general(mk_ref[...].astype(f32).astype(bf16), spread, dims, preferred_element_type=f32)
-    mq = lax.dot_general(mq_ref[...].astype(f32).astype(bf16), place, dims, preferred_element_type=f32)
-    ur, ui = (
-        lax.dot_general(u_ref[part], spread, dims, preferred_element_type=f32) for part in range(2)
-    )
-    lr, li = (
-        lax.dot_general(uq_ref[part], place, dims, preferred_element_type=f32) for part in range(2)
-    )
+    place = [jnp.where(col == 2 * row + q, 1.0, 0.0).astype(bf16) for q in range(NQ)]
+
+    def by_q(values):
+        return sum(
+            jnp.dot(values[q], place[q], preferred_element_type=f32) for q in range(NQ)
+        )
+
+    mk = jnp.dot(mk_ref[...].astype(f32).astype(bf16), spread, preferred_element_type=f32)
+    mq = by_q([mq_ref[q].astype(f32).astype(bf16) for q in range(NQ)])
+    ur, ui = (jnp.dot(u_ref[part], spread, preferred_element_type=f32) for part in range(2))
+    lr, li = (by_q([uq_ref[part, q] for q in range(NQ)]) for part in range(2))
     for i, (u, left) in enumerate(((ur, lr), (ui - ur, -(li + lr)), (ur + ui, lr - li))):
         for b in range(BANDS):
             uo_ref[i, b] = u[b * 16:(b + 1) * 16] * mk
             lo_ref[i, b] = left[b * 16:(b + 1) * 16] * mq
 
 
-def pack_body(own_ref, back_ref, ahead_ref, prev_ref, next_ref, all_ref, two_ref):
-    for i, ref in enumerate((own_ref, back_ref, ahead_ref, prev_ref, next_ref)):
-        value = ref[...]
-        all_ref[i * ROWS:(i + 1) * ROWS, :] = value
-        if i in (1, 2):
-            two_ref[(i - 1) * ROWS:i * ROWS, :] = value
-
-
-PLACE = ((0, 0), (0, 3), (1, 0), (0, 1), (2, 0), (1, 1), (0, 2), (0, 4))
+def pack_body(own_ref, back_ref, ahead_ref, prev_ref, next_ref, order_ref, rest_ref, two_ref):
+    for out_ref, group in ((rest_ref, (own_ref, prev_ref, next_ref)), (two_ref, (back_ref, ahead_ref))):
+        for i, ref in enumerate(group):
+            out_ref[i * ROWS:(i + 1) * ROWS, :] = ref[...]
+
+
+PLACE = ((0, 0), (0, 1), (2, 0), (1, 0), (3, 0), (2, 1), (1, 1), (0, 2))
 
 
 def couple_body(*refs):
-    ph_ref, u_ref, l_ref, out_ref, y_ref, bl_ref, h_ref, r_ref = refs[6:]
+    ph_ref, u_ref, l_ref, out_ref, y_ref, bl_ref, h_ref, r_ref = refs[8:]
     ph = ph_ref[...]
     for q in range(NQ):
         x = jnp.concatenate(
             [
-                refs[side * 3 + i][j * ROWS + q * 32:j * ROWS + (q + 1) * 32, :]
+                refs[side * 4 + i][j * ROWS + q * 32:j * ROWS + (q + 1) * 32, :]
                 for side in range(2)
                 for i, j in PLACE
             ],
@@ -281,10 +291,14 @@
     )
     parts = lax.all_to_all(rotated, "lat", 0, 0, tiled=True)
 
-    index = lax.axis_index("kpt")
-    at = jnp.stack([index // 2, index % 2]).astype(jnp.int32)
-    lattice = jnp.concatenate(
-        [re_vectors.T, re_weights[None, :], jnp.zeros((4, re_weights.shape[0]), jnp.int32)], axis=0
+    given = (
+        k_points.T,
+        re_vectors.T,
+        re_weights[None, :],
+        jnp.transpose(u_k, (0, 2, 3, 1)).reshape(2, BANDS * BANDS, KPTS),
+        jnp.transpose(u_kq, (0, 1, 3, 4, 2)).reshape(2, NQ, BANDS * BANDS, KPTS),
+        mask_k.T,
+        jnp.transpose(mask_kq, (0, 2, 1)),
     )
     phase, right, left = pl.pallas_call(
         prep_body,
@@ -293,19 +307,13 @@
             jax.ShapeDtypeStruct((3, BANDS, BANDS, 128), f32),
             jax.ShapeDtypeStruct((3, BANDS, BANDS, 128), f32),
         ),
-        in_specs=[smem()] + [vmem()] * 6,
+        in_specs=[hbm()] * 7,
         out_specs=(vmem(),) * 3,
+        scratch_shapes=[pltpu.VMEM(x.shape, x.dtype) for x in given]
+        + [pltpu.SemaphoreType.DMA((len(given),))],
         compiler_params=params(),
         name="prep",
-    )(
-        at,
-        k_points,
-        lattice,
-        u_k.reshape(2, KPTS, BANDS * BANDS),
-        u_kq.reshape(2, NQ * KPTS, BANDS * BANDS),
-        mask_k,
-        mask_kq.reshape(NQ * KPTS, BANDS),
-    )
+    )(*(pltpu.with_memory_space_constraint(x, pltpu.HBM) for x in given))
 
     own = pl.pallas_call(
         sum_body,
@@ -324,24 +332,24 @@
 
     back = shift(own, 3)
     ahead = shift(own, -2)
-    packed, pair = pl.pallas_call(
+    rest, pair = pl.pallas_call(
         pack_body,
         out_shape=(
-            jax.ShapeDtypeStruct((5 * ROWS, LANES), bf16),
+            jax.ShapeDtypeStruct((3 * ROWS, LANES), bf16),
             jax.ShapeDtypeStruct((2 * ROWS, LANES), bf16),
         ),
-        in_specs=[vmem()] * 5,
+        in_specs=[vmem()] * 5 + [pl.BlockSpec(memory_space=pl.ANY)],
         out_specs=(vmem(), vmem()),
         compiler_params=params(),
         name="pack",
-    )(own, back, ahead, shift(own, 1), shift(own, -1))
-    near = [packed, shift(pair, -1), shift(back, 1)]
+    )(own, back, ahead, shift(own, 1), shift(own, -1), phase)
+    near = [rest, pair, shift(pair, -1), shift(back, 1)]
     far = [swap(x) for x in near]
 
     result = pl.pallas_call(
         couple_body,
         out_shape=jax.ShapeDtypeStruct((2, KPTS, NQ, LANES), bf16),
-        in_specs=[vmem()] * 9,
+        in_specs=[vmem()] * 11,
         out_specs=vmem(),
         scratch_shapes=[
             pltpu.VMEM((2, 2 * PER, 128, 128), f32),

time: 63.1 us -> 62.6 us (level)
  local copies, waits for them, and re-layouts: 1 us -> 0 us
  Pallas kernels: 8.53 us -> 9.17 us
    ppermute x6, waiting for transfers between devices: 8.51 us -> 7.02 us  [shift(): return lax.ppermute(x, 'kpt', [(i, (i + 2 * step) % 16) for i in range(16)])]
    ppermute x3 -> x4, waiting for transfers between devices: 0.01 us -> 0.95 us  [swap(): return lax.ppermute(x, 'kpt', [(i, i ^ 1) for i in range(16)])]
    pallas_call x1, Pallas kernels: 1.28 us -> 1.93 us  [per_device(): pl.pallas_call(prep_body, out_shape=(jax.ShapeDtypeStruct((2 * KPTS, 512)...]
    ppermute x3 -> x4, starting transfers between devices: 4.44 us -> 5.02 us  [swap(): return lax.ppermute(x, 'kpt', [(i, i ^ 1) for i in range(16)])]
  transfers between devices with their start and end apart: 9 -> 10, of which waited for: 4 -> 4; matrix products, arithmetic and copies ran while one was open for 2% -> 0% of each run, Pallas kernels for 2% -> 3%
where the time goes in v12:
time: 62.6 us; the launch traced here: 62.4 us
  blocking collectives  29.1 us (46%)
  starting transfers between devices  15.4 us (25%)
  Pallas kernels  9.17 us (15%)
  waiting for transfers between devices  7.97 us (13%)
  between operations  0.7 us (1%)
    all_to_all x1, blocking collectives, per_device(): parts = lax.all_to_all(rotated, 'lat', 0, 0, tiled=True)  29.1 us
    ppermute x6, starting transfers between devices, shift(): return lax.ppermute(x, 'kpt', [(i, (i + 2 * step) % 16) for i in range(16)])  10.4 us
    ppermute x6, waiting for transfers between devices, shift(): return lax.ppermute(x, 'kpt', [(i, (i + 2 * step) % 16) for i in range(16)])  7.02 us
    ppermute x4, starting transfers between devices, swap(): return lax.ppermute(x, 'kpt', [(i, i ^ 1) for i in range(16)])  5.02 us
    pallas_call x1, Pallas kernels, per_device(): pl.pallas_call(couple_body, out_shape=jax.ShapeDtypeStruct((2, KPTS, NQ,...  4.89 us
    pallas_call x1, Pallas kernels, per_device(): pl.pallas_call(rotate_body, out_shape=jax.ShapeDtypeStruct((LAT, ROWS, LA...  2.11 us
    pallas_call x1, Pallas kernels, per_device(): pl.pallas_call(prep_body, out_shape=(jax.ShapeDtypeStruct((2 * KPTS, 512)...  1.93 us
  transfers between devices with their start and end apart: 10, of which 4 were waited for; matrix products, arithmetic and copies ran while one was open for 0% of the time, Pallas kernels for 3%

profile of v12, /device:TPU:1, one launch (start us, length us, event | category | flops | bytes accessed | tf_op | source)
XLA Modules:
  0.0 62.4 jit_solution(13074057508133551708)
XLA Ops:
  0.7 2.1 %rotate.1 = bf16[16,64,768]{2,1,0:T(8,128)(2,1)S(1)} custom-call(f32[2,3]{1,0:T(2,128)} %qp_hbm.1, s32[1,3]{1,0:T(1,128)} %rv_hbm.1, s32[1,1]{1,0:T(1,128)} %bitcast.12.rw_hbm, bf16[2,2,48,48]{3,2,1,0:T(8,128)(2,1)} %rot_hbm.1, bf16[2,1,16,12288]{3,2,1,0:T(8,128)(2,1)} %coarse_hbm.1), custom_call_target="tpu_custom_call" | custom-call | tf_op jit(solution)/shard_map/rotate/pallas_call | solution.py:267
  2.8 29.1 %all_to_all.5.x_ref = bf16[16,64,768]{2,1,0:T(8,128)(2,1)S(1)} all-to-all(bf16[16,64,768]{2,1,0:T(8,128)(2,1)S(1)} %rotate.1), channel_id=1, replica_groups=mesh['lat'=16,'kpt'=16] {'lat'}, dimensions={0} | all-to-all | bytes 3145728 | tf_op jit(solution)/shard_map/all_to_all | solution.py:292
  31.9 0.2 add_up.1.own_ref
  32.1 4.4 %collective-permute-start = (bf16[64,768]{1,0:T(8,128)(2,1)S(1)}, bf16[64,768]{1,0:T(8,128)(2,1)S(1)}, u32[]{:S(2)}, u32[]{:S(2)}) collective-permute-start(bf16[64,768]{1,0:T(8,128)(2,1)S(1)} %add_up.1.own_ref), channel_id=1, source_target_pairs={{0,6},{1,7},{2,8},{3,9},{4,10},{5,11},{6,12},{7,13},{8,14},{9,15},... | collective-permute-start | bytes 294920 | tf_op jit(solution)/shard_map/ppermute | solution.py:328
  36.5 1.8 %collective-permute-start.1 = (bf16[64,768]{1,0:T(8,128)(2,1)S(1)}, bf16[64,768]{1,0:T(8,128)(2,1)S(1)}, u32[]{:S(2)}, u32[]{:S(2)}) collective-permute-start(bf16[64,768]{1,0:T(8,128)(2,1)S(1)} %add_up.1.own_ref), channel_id=1, source_target_pairs={{0,12},{1,13},{2,14},{3,15},{4,0},{5,1},{6,2},{7,3},{8,4},{9,5},{1... | collective-permute-start | bytes 294920 | tf_op jit(solution)/shard_map/ppermute | solution.py:328
  38.3 1.1 %collective-permute-start.2 = (bf16[64,768]{1,0:T(8,128)(2,1)S(1)}, bf16[64,768]{1,0:T(8,128)(2,1)S(1)}, u32[]{:S(2)}, u32[]{:S(2)}) collective-permute-start(bf16[64,768]{1,0:T(8,128)(2,1)S(1)} %add_up.1.own_ref), channel_id=1, source_target_pairs={{0,2},{1,3},{2,4},{3,5},{4,6},{5,7},{6,8},{7,9},{8,10},{9,11},{10,... | collective-permute-start | bytes 294920 | tf_op jit(solution)/shard_map/ppermute | solution.py:328
  39.4 1.6 %collective-permute-start.3 = (bf16[64,768]{1,0:T(8,128)(2,1)S(1)}, bf16[64,768]{1,0:T(8,128)(2,1)S(1)}, u32[]{:S(2)}, u32[]{:S(2)}) collective-permute-start(bf16[64,768]{1,0:T(8,128)(2,1)S(1)} %add_up.1.own_ref), channel_id=1, source_target_pairs={{0,14},{1,15},{2,0},{3,1},{4,2},{5,3},{6,4},{7,5},{8,6},{9,7},{10,... | collective-permute-start | bytes 294920 | tf_op jit(solution)/shard_map/ppermute | solution.py:328
  41.0 1.9 %prep.1 = (bf16[128,512]{1,0:T(8,128)(2,1)S(1)}, f32[3,16,16,128]{3,2,1,0:T(8,128)S(1)}, f32[3,16,16,128]{3,2,1,0:T(8,128)S(1)}) custom-call(f32[3,64]{1,0:T(4,128)} %bitcast.18, s32[3,256]{1,0:T(4,128)} %bitcast.17, s32[1,256]{1,0:T(1,128)} %bitcast.19, bf16[2,256,64]{2,1,0:T(8,128)(2,1)} %bitcast.14, bf16[2,2,256,64]{3,2,1,0:T(8,128)(2,1)} %bitcast.13, ...), custom_call_target="tpu_custom_call" | custom-call | tf_op jit(solution)/shard_map/prep/pallas_call | solution.py:303
  42.9 0.0 collective-permute-done.back_ref
  42.9 0.0 collective-permute-done.1.ahead_ref
  42.9 3.9 %collective-permute-done.2.prev_ref = bf16[64,768]{1,0:T(8,128)(2,1)S(1)} collective-permute-done((bf16[64,768]{1,0:T(8,128)(2,1)S(1)}, bf16[64,768]{1,0:T(8,128)(2,1)S(1)}, u32[]{:S(2)}, u32[]{:S(2)}) %collective-permute-start.2) | collective-permute-done | bytes 98336 | tf_op jit(solution)/shard_map/ppermute | solution.py:328
  46.8 0.0 collective-permute-done.3.next_ref
  46.9 1.5 %collective-permute-start.4 = (bf16[128,768]{1,0:T(8,128)(2,1)S(1)}, bf16[128,768]{1,0:T(8,128)(2,1)S(1)}, u32[]{:S(2)}, u32[]{:S(2)}) collective-permute-start(bf16[128,768]{1,0:T(8,128)(2,1)S(1)} %get-tuple-element.12.refs_1_), channel_id=1, source_target_pairs={{0,14},{1,15},{2,0},{3,1},{4,2},{5,3},{6,4},{7,5},{8,6},{9,7},{10,... | collective-permute-start | bytes 589832 | tf_op jit(solution)/shard_map/ppermute | solution.py:328
  48.4 1.7 %collective-permute-start.6 = (bf16[192,768]{1,0:T(8,128)(2,1)S(1)}, bf16[192,768]{1,0:T(8,128)(2,1)S(1)}, u32[]{:S(2)}, u32[]{:S(2)}) collective-permute-start(bf16[192,768]{1,0:T(8,128)(2,1)S(1)} %get-tuple-element.11.refs_0_), channel_id=1, source_target_pairs={{0,1},{1,0},{2,3},{3,2},{4,5},{5,4},{6,7},{7,6},{8,9},{9,8},{10,11... | collective-permute-start | bytes 884744 | tf_op jit(solution)/shard_map/ppermute | solution.py:331
  50.1 0.0 collective-permute-start.7
  50.1 0.0 collective-permute-start.5
  50.1 2.2 %collective-permute-done.4.refs_2_ = bf16[128,768]{1,0:T(8,128)(2,1)S(1)} collective-permute-done((bf16[128,768]{1,0:T(8,128)(2,1)S(1)}, bf16[128,768]{1,0:T(8,128)(2,1)S(1)}, u32[]{:S(2)}, u32[]{:S(2)}) %collective-permute-start.4) | collective-permute-done | bytes 196640 | tf_op jit(solution)/shard_map/ppermute | solution.py:328
  52.3 1.9 %collective-permute-start.8 = (bf16[128,768]{1,0:T(8,128)(2,1)S(1)}, bf16[128,768]{1,0:T(8,128)(2,1)S(1)}, u32[]{:S(2)}, u32[]{:S(2)}) collective-permute-start(bf16[128,768]{1,0:T(8,128)(2,1)S(1)} %collective-permute-done.4.refs_2_), channel_id=1, source_target_pairs={{0,1},{1,0},{2,3},{3,2},{4,5},{5,4},{6,7},{7,6},{8,9},{9,8},{10,11... | collective-permute-start | bytes 589832 | tf_op jit(solution)/shard_map/ppermute | solution.py:331
  54.3 0.9 %collective-permute-done.5.refs_3_ = bf16[64,768]{1,0:T(8,128)(2,1)S(1)} collective-permute-done((bf16[64,768]{1,0:T(8,128)(2,1)S(1)}, bf16[64,768]{1,0:T(8,128)(2,1)S(1)}, u32[]{:S(2)}, u32[]{:S(2)}) %collective-permute-start.5) | collective-permute-done | bytes 98336 | tf_op jit(solution)/shard_map/ppermute | solution.py:328
  55.2 1.4 %collective-permute-start.9 = (bf16[64,768]{1,0:T(8,128)(2,1)S(1)}, bf16[64,768]{1,0:T(8,128)(2,1)S(1)}, u32[]{:S(2)}, u32[]{:S(2)}) collective-permute-start(bf16[64,768]{1,0:T(8,128)(2,1)S(1)} %collective-permute-done.5.refs_3_), channel_id=1, source_target_pairs={{0,1},{1,0},{2,3},{3,2},{4,5},{5,4},{6,7},{7,6},{8,9},{9,8},{10,11... | collective-permute-start | bytes 294920 | tf_op jit(solution)/shard_map/ppermute | solution.py:331
  56.6 0.0 collective-permute-done.7.refs_5_
  56.6 0.9 %collective-permute-done.9.refs_7_ = bf16[64,768]{1,0:T(8,128)(2,1)S(1)} collective-permute-done((bf16[64,768]{1,0:T(8,128)(2,1)S(1)}, bf16[64,768]{1,0:T(8,128)(2,1)S(1)}, u32[]{:S(2)}, u32[]{:S(2)}) %collective-permute-start.9) | collective-permute-done | bytes 98336 | tf_op jit(solution)/shard_map/ppermute | solution.py:331
  57.5 0.0 collective-permute-done.6.refs_4_
  57.5 0.0 collective-permute-done.8.refs_6_
  57.5 4.9 %couple.1 = bf16[2,64,2,768]{3,2,1,0:T(2,128)(2,1)} custom-call(bf16[192,768]{1,0:T(8,128)(2,1)S(1)} %get-tuple-element.11.refs_0_, bf16[128,768]{1,0:T(8,128)(2,1)S(1)} %get-tuple-element.12.refs_1_, bf16[128,768]{1,0:T(8,128)(2,1)S(1)} %collective-permute-done.4.refs_2_, bf16[64,768]{1,0:T(8,128)(2,1)S(1)} %collective-permute-done.5.refs_3_, ...), custom_call_target="tpu_custom_call" | custom-call | tf_op jit(solution)/shard_map/couple/pallas_call | solution.py:349
  (1 shorter events, 0.0 us)
Async XLA Ops:
  32.1 10.8 %collective-permute-start = (bf16[64,768]{1,0:T(8,128)(2,1)S(1)}, bf16[64,768]{1,0:T(8,128)(2,1)S(1)}, u32[]{:S(2)}, u32[]{:S(2)}) collective-permute-start(bf16[64,768]{1,0:T(8,128)(2,1)S(1)} %add_up.1.own_ref), channel_id=1, source_target_pairs={{0,6},{1,7},{2,8},{3,9},{4,10},{5,11},{6,12},{7,13},{8,14},{9,15},... | collective-permute-start | bytes 294920 | tf_op jit(solution)/shard_map/ppermute | solution.py:328
  36.5 6.4 %collective-permute-start.1 = (bf16[64,768]{1,0:T(8,128)(2,1)S(1)}, bf16[64,768]{1,0:T(8,128)(2,1)S(1)}, u32[]{:S(2)}, u32[]{:S(2)}) collective-permute-start(bf16[64,768]{1,0:T(8,128)(2,1)S(1)} %add_up.1.own_ref), channel_id=1, source_target_pairs={{0,12},{1,13},{2,14},{3,15},{4,0},{5,1},{6,2},{7,3},{8,4},{9,5},{1... | collective-permute-start | bytes 294920 | tf_op jit(solution)/shard_map/ppermute | solution.py:328
  38.3 8.5 %collective-permute-start.2 = (bf16[64,768]{1,0:T(8,128)(2,1)S(1)}, bf16[64,768]{1,0:T(8,128)(2,1)S(1)}, u32[]{:S(2)}, u32[]{:S(2)}) collective-permute-start(bf16[64,768]{1,0:T(8,128)(2,1)S(1)} %add_up.1.own_ref), channel_id=1, source_target_pairs={{0,2},{1,3},{2,4},{3,5},{4,6},{5,7},{6,8},{7,9},{8,10},{9,11},{10,... | collective-permute-start | bytes 294920 | tf_op jit(solution)/shard_map/ppermute | solution.py:328
  39.4 7.4 %collective-permute-start.3 = (bf16[64,768]{1,0:T(8,128)(2,1)S(1)}, bf16[64,768]{1,0:T(8,128)(2,1)S(1)}, u32[]{:S(2)}, u32[]{:S(2)}) collective-permute-start(bf16[64,768]{1,0:T(8,128)(2,1)S(1)} %add_up.1.own_ref), channel_id=1, source_target_pairs={{0,14},{1,15},{2,0},{3,1},{4,2},{5,3},{6,4},{7,5},{8,6},{9,7},{10,... | collective-permute-start | bytes 294920 | tf_op jit(solution)/shard_map/ppermute | solution.py:328
  46.9 5.5 %collective-permute-start.4 = (bf16[128,768]{1,0:T(8,128)(2,1)S(1)}, bf16[128,768]{1,0:T(8,128)(2,1)S(1)}, u32[]{:S(2)}, u32[]{:S(2)}) collective-permute-start(bf16[128,768]{1,0:T(8,128)(2,1)S(1)} %get-tuple-element.12.refs_1_), channel_id=1, source_target_pairs={{0,14},{1,15},{2,0},{3,1},{4,2},{5,3},{6,4},{7,5},{8,6},{9,7},{10,... | collective-permute-start | bytes 589832 | tf_op jit(solution)/shard_map/ppermute | solution.py:328
  48.4 9.1 %collective-permute-start.6 = (bf16[192,768]{1,0:T(8,128)(2,1)S(1)}, bf16[192,768]{1,0:T(8,128)(2,1)S(1)}, u32[]{:S(2)}, u32[]{:S(2)}) collective-permute-start(bf16[192,768]{1,0:T(8,128)(2,1)S(1)} %get-tuple-element.11.refs_0_), channel_id=1, source_target_pairs={{0,1},{1,0},{2,3},{3,2},{4,5},{5,4},{6,7},{7,6},{8,9},{9,8},{10,11... | collective-permute-start | bytes 884744 | tf_op jit(solution)/shard_map/ppermute | solution.py:331
  50.1 6.4 %collective-permute-start.7 = (bf16[128,768]{1,0:T(8,128)(2,1)S(1)}, bf16[128,768]{1,0:T(8,128)(2,1)S(1)}, u32[]{:S(2)}, u32[]{:S(2)}) collective-permute-start(bf16[128,768]{1,0:T(8,128)(2,1)S(1)} %get-tuple-element.12.refs_1_), channel_id=1, source_target_pairs={{0,1},{1,0},{2,3},{3,2},{4,5},{5,4},{6,7},{7,6},{8,9},{9,8},{10,11... | collective-permute-start | bytes 589832 | tf_op jit(solution)/shard_map/ppermute | solution.py:331
  50.1 5.1 %collective-permute-start.5 = (bf16[64,768]{1,0:T(8,128)(2,1)S(1)}, bf16[64,768]{1,0:T(8,128)(2,1)S(1)}, u32[]{:S(2)}, u32[]{:S(2)}) collective-permute-start(bf16[64,768]{1,0:T(8,128)(2,1)S(1)} %collective-permute-done.back_ref), channel_id=1, source_target_pairs={{0,2},{1,3},{2,4},{3,5},{4,6},{5,7},{6,8},{7,9},{8,10},{9,11},{10,... | collective-permute-start | bytes 294920 | tf_op jit(solution)/shard_map/ppermute | solution.py:328
  52.3 5.2 %collective-permute-start.8 = (bf16[128,768]{1,0:T(8,128)(2,1)S(1)}, bf16[128,768]{1,0:T(8,128)(2,1)S(1)}, u32[]{:S(2)}, u32[]{:S(2)}) collective-permute-start(bf16[128,768]{1,0:T(8,128)(2,1)S(1)} %collective-permute-done.4.refs_2_), channel_id=1, source_target_pairs={{0,1},{1,0},{2,3},{3,2},{4,5},{5,4},{6,7},{7,6},{8,9},{9,8},{10,11... | collective-permute-start | bytes 589832 | tf_op jit(solution)/shard_map/ppermute | solution.py:331
  55.2 2.3 %collective-permute-start.9 = (bf16[64,768]{1,0:T(8,128)(2,1)S(1)}, bf16[64,768]{1,0:T(8,128)(2,1)S(1)}, u32[]{:S(2)}, u32[]{:S(2)}) collective-permute-start(bf16[64,768]{1,0:T(8,128)(2,1)S(1)} %collective-permute-done.5.refs_3_), channel_id=1, source_target_pairs={{0,1},{1,0},{2,3},{3,2},{4,5},{5,4},{6,7},{7,6},{8,9},{9,8},{10,11... | collective-permute-start | bytes 294920 | tf_op jit(solution)/shard_map/ppermute | solution.py:331

commit v13 on v12

--- a/solution.py
+++ b/solution.py
@@ -157,22 +157,24 @@
             lo_ref[i, b] = left[b * 16:(b + 1) * 16] * mq
 
 
-def pack_body(own_ref, back_ref, ahead_ref, prev_ref, next_ref, order_ref, rest_ref, two_ref):
-    for out_ref, group in ((rest_ref, (own_ref, prev_ref, next_ref)), (two_ref, (back_ref, ahead_ref))):
-        for i, ref in enumerate(group):
-            out_ref[i * ROWS:(i + 1) * ROWS, :] = ref[...]
-
-
-PLACE = ((0, 0), (0, 1), (2, 0), (1, 0), (3, 0), (2, 1), (1, 1), (0, 2))
+def pack_body(own_ref, back_ref, ahead_ref, order_ref, three_ref, two_ref):
+    for i, ref in enumerate((own_ref, back_ref, ahead_ref)):
+        value = ref[...]
+        three_ref[i * ROWS:(i + 1) * ROWS, :] = value
+        if i > 0:
+            two_ref[(i - 1) * ROWS:i * ROWS, :] = value
+
+
+PLACE = ((0, 0), (1, 0), (2, 0), (0, 1), (1, 1), (2, 1), (0, 2), (1, 2))
 
 
 def couple_body(*refs):
-    ph_ref, u_ref, l_ref, out_ref, y_ref, bl_ref, h_ref, r_ref = refs[8:]
+    ph_ref, u_ref, l_ref, out_ref, y_ref, bl_ref, h_ref, r_ref = refs[6:]
     ph = ph_ref[...]
     for q in range(NQ):
         x = jnp.concatenate(
             [
-                refs[side * 4 + i][j * ROWS + q * 32:j * ROWS + (q + 1) * 32, :]
+                refs[side * 3 + i][j * ROWS + q * 32:j * ROWS + (q + 1) * 32, :]
                 for side in range(2)
                 for i, j in PLACE
             ],
@@ -332,24 +334,26 @@
 
     back = shift(own, 3)
     ahead = shift(own, -2)
-    rest, pair = pl.pallas_call(
+    packed, pair = pl.pallas_call(
         pack_body,
         out_shape=(
             jax.ShapeDtypeStruct((3 * ROWS, LANES), bf16),
             jax.ShapeDtypeStruct((2 * ROWS, LANES), bf16),
         ),
-        in_specs=[vmem()] * 5 + [pl.BlockSpec(memory_space=pl.ANY)],
+        in_specs=[vmem()] * 3 + [pl.BlockSpec(memory_space=pl.ANY)],
         out_specs=(vmem(), vmem()),
         compiler_params=params(),
         name="pack",
-    )(own, back, ahead, shift(own, 1), shift(own, -1), phase)
-    near = [rest, pair, shift(pair, -1), shift(back, 1)]
+    )(own, back, ahead, phase)
+    plus = shift(packed, 1)
+    minus = shift(pair, -1)
+    near = [packed, plus, minus]
     far = [swap(x) for x in near]
 
     result = pl.pallas_call(
         couple_body,
         out_shape=jax.ShapeDtypeStruct((2, KPTS, NQ, LANES), bf16),
-        in_specs=[vmem()] * 11,
+        in_specs=[vmem()] * 9,
         out_specs=vmem(),
         scratch_shapes=[
             pltpu.VMEM((2, 2 * PER, 128, 128), f32),

time: 62.6 us -> 60.6 us (0.968)
  waiting for transfers between devices: 7.97 us -> 3.55 us
  starting transfers between devices: 15.4 us -> 17.9 us
    ppermute x6 -> x4, waiting for transfers between devices: 7.02 us -> 2.47 us  [shift(): return lax.ppermute(x, 'kpt', [(i, (i + 2 * step) % 16) for i in range(16)])]
    ppermute x4 -> x3, starting transfers between devices: 5.02 us -> 8.76 us  [swap(): return lax.ppermute(x, 'kpt', [(i, i ^ 1) for i in range(16)])]
    ppermute x6 -> x4, starting transfers between devices: 10.4 us -> 9.16 us  [shift(): return lax.ppermute(x, 'kpt', [(i, (i + 2 * step) % 16) for i in range(16)])]
  transfers between devices with their start and end apart: 10 -> 7, of which waited for: 4 -> 4; matrix products, arithmetic and copies ran while one was open for 0% -> 0% of each run, Pallas kernels for 3% -> 3%
where the time goes in v13:
time: 60.6 us; the launch traced here: 60.4 us
  blocking collectives  29.1 us (48%)
  starting transfers between devices  17.9 us (30%)
  Pallas kernels  9.16 us (15%)
  waiting for transfers between devices  3.55 us (6%)
  between operations  0.68 us (1%)
    all_to_all x1, blocking collectives, per_device(): parts = lax.all_to_all(rotated, 'lat', 0, 0, tiled=True)  29.1 us
    ppermute x4, starting transfers between devices, shift(): return lax.ppermute(x, 'kpt', [(i, (i + 2 * step) % 16) for i in range(16)])  9.16 us
    ppermute x3, starting transfers between devices, swap(): return lax.ppermute(x, 'kpt', [(i, i ^ 1) for i in range(16)])  8.76 us
    pallas_call x1, Pallas kernels, per_device(): pl.pallas_call(couple_body, out_shape=jax.ShapeDtypeStruct((2, KPTS, NQ,...  4.89 us
    ppermute x4, waiting for transfers between devices, shift(): return lax.ppermute(x, 'kpt', [(i, (i + 2 * step) % 16) for i in range(16)])  2.47 us
    pallas_call x1, Pallas kernels, per_device(): pl.pallas_call(rotate_body, out_shape=jax.ShapeDtypeStruct((LAT, ROWS, LA...  2.11 us
    pallas_call x1, Pallas kernels, per_device(): pl.pallas_call(prep_body, out_shape=(jax.ShapeDtypeStruct((2 * KPTS, 512)...  1.93 us
  transfers between devices with their start and end apart: 7, of which 4 were waited for; matrix products, arithmetic and copies ran while one was open for 0% of the time, Pallas kernels for 3%

profile of v13, /device:TPU:1, one launch (start us, length us, event | category | flops | bytes accessed | tf_op | source)
XLA Modules:
  0.0 60.4 jit_solution(14861372662517765056)
XLA Ops:
  0.7 2.1 %rotate.1 = bf16[16,64,768]{2,1,0:T(8,128)(2,1)S(1)} custom-call(f32[2,3]{1,0:T(2,128)} %qp_hbm.1, s32[1,3]{1,0:T(1,128)} %rv_hbm.1, s32[1,1]{1,0:T(1,128)} %bitcast.12.rw_hbm, bf16[2,2,48,48]{3,2,1,0:T(8,128)(2,1)} %rot_hbm.1, bf16[2,1,16,12288]{3,2,1,0:T(8,128)(2,1)} %coarse_hbm.1), custom_call_target="tpu_custom_call" | custom-call | tf_op jit(solution)/shard_map/rotate/pallas_call | solution.py:269
  2.8 29.1 %all_to_all.5.x_ref = bf16[16,64,768]{2,1,0:T(8,128)(2,1)S(1)} all-to-all(bf16[16,64,768]{2,1,0:T(8,128)(2,1)S(1)} %rotate.1), channel_id=1, replica_groups=mesh['lat'=16,'kpt'=16] {'lat'}, dimensions={0} | all-to-all | bytes 3145728 | tf_op jit(solution)/shard_map/all_to_all | solution.py:294
  31.9 0.2 add_up.1.own_ref
  32.1 4.4 %collective-permute-start = (bf16[64,768]{1,0:T(8,128)(2,1)S(1)}, bf16[64,768]{1,0:T(8,128)(2,1)S(1)}, u32[]{:S(2)}, u32[]{:S(2)}) collective-permute-start(bf16[64,768]{1,0:T(8,128)(2,1)S(1)} %add_up.1.own_ref), channel_id=1, source_target_pairs={{0,6},{1,7},{2,8},{3,9},{4,10},{5,11},{6,12},{7,13},{8,14},{9,15},... | collective-permute-start | bytes 294920 | tf_op jit(solution)/shard_map/ppermute | solution.py:330
  36.5 1.8 %collective-permute-start.1 = (bf16[64,768]{1,0:T(8,128)(2,1)S(1)}, bf16[64,768]{1,0:T(8,128)(2,1)S(1)}, u32[]{:S(2)}, u32[]{:S(2)}) collective-permute-start(bf16[64,768]{1,0:T(8,128)(2,1)S(1)} %add_up.1.own_ref), channel_id=1, source_target_pairs={{0,12},{1,13},{2,14},{3,15},{4,0},{5,1},{6,2},{7,3},{8,4},{9,5},{1... | collective-permute-start | bytes 294920 | tf_op jit(solution)/shard_map/ppermute | solution.py:330
  38.3 1.9 %prep.1 = (bf16[128,512]{1,0:T(8,128)(2,1)S(1)}, f32[3,16,16,128]{3,2,1,0:T(8,128)S(1)}, f32[3,16,16,128]{3,2,1,0:T(8,128)S(1)}) custom-call(f32[3,64]{1,0:T(4,128)} %bitcast.18, s32[3,256]{1,0:T(4,128)} %bitcast.17, s32[1,256]{1,0:T(1,128)} %bitcast.19, bf16[2,256,64]{2,1,0:T(8,128)(2,1)} %bitcast.14, bf16[2,2,256,64]{3,2,1,0:T(8,128)(2,1)} %bitcast.13, ...), custom_call_target="tpu_custom_call" | custom-call | tf_op jit(solution)/shard_map/prep/pallas_call | solution.py:305
  40.2 0.6 %collective-permute-done.back_ref = bf16[64,768]{1,0:T(8,128)(2,1)S(1)} collective-permute-done((bf16[64,768]{1,0:T(8,128)(2,1)S(1)}, bf16[64,768]{1,0:T(8,128)(2,1)S(1)}, u32[]{:S(2)}, u32[]{:S(2)}) %collective-permute-start) | collective-permute-done | bytes 98336 | tf_op jit(solution)/shard_map/ppermute | solution.py:330
  40.9 1.3 %collective-permute-done.1.ahead_ref = bf16[64,768]{1,0:T(8,128)(2,1)S(1)} collective-permute-done((bf16[64,768]{1,0:T(8,128)(2,1)S(1)}, bf16[64,768]{1,0:T(8,128)(2,1)S(1)}, u32[]{:S(2)}, u32[]{:S(2)}) %collective-permute-start.1) | collective-permute-done | bytes 98336 | tf_op jit(solution)/shard_map/ppermute | solution.py:330
  42.2 2.0 %collective-permute-start.2 = (bf16[192,768]{1,0:T(8,128)(2,1)S(1)}, bf16[192,768]{1,0:T(8,128)(2,1)S(1)}, u32[]{:S(2)}, u32[]{:S(2)}) collective-permute-start(bf16[192,768]{1,0:T(8,128)(2,1)S(1)} %get-tuple-element.11.refs_0_), channel_id=1, source_target_pairs={{0,2},{1,3},{2,4},{3,5},{4,6},{5,7},{6,8},{7,9},{8,10},{9,11},{10,... | collective-permute-start | bytes 884744 | tf_op jit(solution)/shard_map/ppermute | solution.py:330
  44.2 1.0 %collective-permute-start.3 = (bf16[128,768]{1,0:T(8,128)(2,1)S(1)}, bf16[128,768]{1,0:T(8,128)(2,1)S(1)}, u32[]{:S(2)}, u32[]{:S(2)}) collective-permute-start(bf16[128,768]{1,0:T(8,128)(2,1)S(1)} %get-tuple-element.12), channel_id=1, source_target_pairs={{0,14},{1,15},{2,0},{3,1},{4,2},{5,3},{6,4},{7,5},{8,6},{9,7},{10,... | collective-permute-start | bytes 589832 | tf_op jit(solution)/shard_map/ppermute | solution.py:330
  45.2 3.5 %collective-permute-start.4 = (bf16[192,768]{1,0:T(8,128)(2,1)S(1)}, bf16[192,768]{1,0:T(8,128)(2,1)S(1)}, u32[]{:S(2)}, u32[]{:S(2)}) collective-permute-start(bf16[192,768]{1,0:T(8,128)(2,1)S(1)} %get-tuple-element.11.refs_0_), channel_id=1, source_target_pairs={{0,1},{1,0},{2,3},{3,2},{4,5},{5,4},{6,7},{7,6},{8,9},{9,8},{10,11... | collective-permute-start | bytes 884744 | tf_op jit(solution)/shard_map/ppermute | solution.py:333
  48.7 0.5 collective-permute-done.2.refs_1_
  49.2 4.2 %collective-permute-start.5 = (bf16[192,768]{1,0:T(8,128)(2,1)S(1)}, bf16[192,768]{1,0:T(8,128)(2,1)S(1)}, u32[]{:S(2)}, u32[]{:S(2)}) collective-permute-start(bf16[192,768]{1,0:T(8,128)(2,1)S(1)} %collective-permute-done.2.refs_1_), channel_id=1, source_target_pairs={{0,1},{1,0},{2,3},{3,2},{4,5},{5,4},{6,7},{7,6},{8,9},{9,8},{10,11... | collective-permute-start | bytes 884744 | tf_op jit(solution)/shard_map/ppermute | solution.py:333
  53.4 0.0 collective-permute-done.3.refs_2_
  53.4 1.1 %collective-permute-start.6 = (bf16[128,768]{1,0:T(8,128)(2,1)S(1)}, bf16[128,768]{1,0:T(8,128)(2,1)S(1)}, u32[]{:S(2)}, u32[]{:S(2)}) collective-permute-start(bf16[128,768]{1,0:T(8,128)(2,1)S(1)} %collective-permute-done.3.refs_2_), channel_id=1, source_target_pairs={{0,1},{1,0},{2,3},{3,2},{4,5},{5,4},{6,7},{7,6},{8,9},{9,8},{10,11... | collective-permute-start | bytes 589832 | tf_op jit(solution)/shard_map/ppermute | solution.py:333
  54.5 0.0 collective-permute-done.4.refs_3_
  54.5 1.1 %collective-permute-done.6.refs_5_ = bf16[128,768]{1,0:T(8,128)(2,1)S(1)} collective-permute-done((bf16[128,768]{1,0:T(8,128)(2,1)S(1)}, bf16[128,768]{1,0:T(8,128)(2,1)S(1)}, u32[]{:S(2)}, u32[]{:S(2)}) %collective-permute-start.6) | collective-permute-done | bytes 196640 | tf_op jit(solution)/shard_map/ppermute | solution.py:333
  55.5 0.0 collective-permute-done.5.refs_4_
  55.5 4.9 %couple.1 = bf16[2,64,2,768]{3,2,1,0:T(2,128)(2,1)} custom-call(bf16[192,768]{1,0:T(8,128)(2,1)S(1)} %get-tuple-element.11.refs_0_, bf16[192,768]{1,0:T(8,128)(2,1)S(1)} %collective-permute-done.2.refs_1_, bf16[128,768]{1,0:T(8,128)(2,1)S(1)} %collective-permute-done.3.refs_2_, bf16[192,768]{1,0:T(8,128)(2,1)S(1)} %collective-permute-done.4.refs_3_, ...), custom_call_target="tpu_custom_call" | custom-call | tf_op jit(solution)/shard_map/couple/pallas_call | solution.py:353
  (1 shorter events, 0.0 us)
Async XLA Ops:
  32.1 8.8 %collective-permute-start = (bf16[64,768]{1,0:T(8,128)(2,1)S(1)}, bf16[64,768]{1,0:T(8,128)(2,1)S(1)}, u32[]{:S(2)}, u32[]{:S(2)}) collective-permute-start(bf16[64,768]{1,0:T(8,128)(2,1)S(1)} %add_up.1.own_ref), channel_id=1, source_target_pairs={{0,6},{1,7},{2,8},{3,9},{4,10},{5,11},{6,12},{7,13},{8,14},{9,15},... | collective-permute-start | bytes 294920 | tf_op jit(solution)/shard_map/ppermute | solution.py:330
  36.5 5.6 %collective-permute-start.1 = (bf16[64,768]{1,0:T(8,128)(2,1)S(1)}, bf16[64,768]{1,0:T(8,128)(2,1)S(1)}, u32[]{:S(2)}, u32[]{:S(2)}) collective-permute-start(bf16[64,768]{1,0:T(8,128)(2,1)S(1)} %add_up.1.own_ref), channel_id=1, source_target_pairs={{0,12},{1,13},{2,14},{3,15},{4,0},{5,1},{6,2},{7,3},{8,4},{9,5},{1... | collective-permute-start | bytes 294920 | tf_op jit(solution)/shard_map/ppermute | solution.py:330
  42.2 7.0 %collective-permute-start.2 = (bf16[192,768]{1,0:T(8,128)(2,1)S(1)}, bf16[192,768]{1,0:T(8,128)(2,1)S(1)}, u32[]{:S(2)}, u32[]{:S(2)}) collective-permute-start(bf16[192,768]{1,0:T(8,128)(2,1)S(1)} %get-tuple-element.11.refs_0_), channel_id=1, source_target_pairs={{0,2},{1,3},{2,4},{3,5},{4,6},{5,7},{6,8},{7,9},{8,10},{9,11},{10,... | collective-permute-start | bytes 884744 | tf_op jit(solution)/shard_map/ppermute | solution.py:330
  44.2 9.2 %collective-permute-start.3 = (bf16[128,768]{1,0:T(8,128)(2,1)S(1)}, bf16[128,768]{1,0:T(8,128)(2,1)S(1)}, u32[]{:S(2)}, u32[]{:S(2)}) collective-permute-start(bf16[128,768]{1,0:T(8,128)(2,1)S(1)} %get-tuple-element.12), channel_id=1, source_target_pairs={{0,14},{1,15},{2,0},{3,1},{4,2},{5,3},{6,4},{7,5},{8,6},{9,7},{10,... | collective-permute-start | bytes 589832 | tf_op jit(solution)/shard_map/ppermute | solution.py:330
  45.2 9.3 %collective-permute-start.4 = (bf16[192,768]{1,0:T(8,128)(2,1)S(1)}, bf16[192,768]{1,0:T(8,128)(2,1)S(1)}, u32[]{:S(2)}, u32[]{:S(2)}) collective-permute-start(bf16[192,768]{1,0:T(8,128)(2,1)S(1)} %get-tuple-element.11.refs_0_), channel_id=1, source_target_pairs={{0,1},{1,0},{2,3},{3,2},{4,5},{5,4},{6,7},{7,6},{8,9},{9,8},{10,11... | collective-permute-start | bytes 884744 | tf_op jit(solution)/shard_map/ppermute | solution.py:333
  49.2 6.4 %collective-permute-start.5 = (bf16[192,768]{1,0:T(8,128)(2,1)S(1)}, bf16[192,768]{1,0:T(8,128)(2,1)S(1)}, u32[]{:S(2)}, u32[]{:S(2)}) collective-permute-start(bf16[192,768]{1,0:T(8,128)(2,1)S(1)} %collective-permute-done.2.refs_1_), channel_id=1, source_target_pairs={{0,1},{1,0},{2,3},{3,2},{4,5},{5,4},{6,7},{7,6},{8,9},{9,8},{10,11... | collective-permute-start | bytes 884744 | tf_op jit(solution)/shard_map/ppermute | solution.py:333
  53.4 2.2 %collective-permute-start.6 = (bf16[128,768]{1,0:T(8,128)(2,1)S(1)}, bf16[128,768]{1,0:T(8,128)(2,1)S(1)}, u32[]{:S(2)}, u32[]{:S(2)}) collective-permute-start(bf16[128,768]{1,0:T(8,128)(2,1)S(1)} %collective-permute-done.3.refs_2_), channel_id=1, source_target_pairs={{0,1},{1,0},{2,3},{3,2},{4,5},{5,4},{6,7},{7,6},{8,9},{9,8},{10,11... | collective-permute-start | bytes 589832 | tf_op jit(solution)/shard_map/ppermute | solution.py:333

commit v14 on v13

--- a/solution.py
+++ b/solution.py
@@ -157,29 +157,35 @@
             lo_ref[i, b] = left[b * 16:(b + 1) * 16] * mq
 
 
-def pack_body(own_ref, back_ref, ahead_ref, order_ref, three_ref, two_ref):
-    for i, ref in enumerate((own_ref, back_ref, ahead_ref)):
-        value = ref[...]
-        three_ref[i * ROWS:(i + 1) * ROWS, :] = value
-        if i > 0:
-            two_ref[(i - 1) * ROWS:i * ROWS, :] = value
-
-
-PLACE = ((0, 0), (1, 0), (2, 0), (0, 1), (1, 1), (2, 1), (0, 2), (1, 2))
+def pack_body(own_ref, back_ref, ahead_ref, order_ref, all_ref, plus_ref, minus_ref):
+    half = ROWS // 2
+    own = own_ref[...]
+    back = back_ref[...]
+    ahead = ahead_ref[...]
+    for i, value in enumerate((own, back, ahead)):
+        all_ref[i * ROWS:(i + 1) * ROWS, :] = value
+    plus_ref[0:ROWS, :] = own
+    plus_ref[ROWS:2 * ROWS, :] = back
+    plus_ref[2 * ROWS:, :] = ahead[0:half]
+    minus_ref[0:ROWS, :] = back
+    minus_ref[ROWS:2 * ROWS, :] = ahead
+    minus_ref[2 * ROWS:, :] = own[half:]
+
+
+PLACE = ((0, 0), (1, 0), (2, 0), (0, 1), (1, 1), (2, 1), (0, 2))
 
 
 def couple_body(*refs):
     ph_ref, u_ref, l_ref, out_ref, y_ref, bl_ref, h_ref, r_ref = refs[6:]
     ph = ph_ref[...]
     for q in range(NQ):
-        x = jnp.concatenate(
-            [
-                refs[side * 3 + i][j * ROWS + q * 32:j * ROWS + (q + 1) * 32, :]
-                for side in range(2)
-                for i, j in PLACE
-            ],
-            axis=0,
-        )
+        pieces = []
+        for side in range(2):
+            for i, j in PLACE:
+                at = j * ROWS + q * 32
+                pieces.append(refs[side * 3 + i][at:at + 32, :])
+            pieces.append(refs[side * 3 + 1 + q][2 * ROWS:2 * ROWS + 32, :])
+        x = jnp.concatenate(pieces, axis=0)
         t = jnp.dot(ph, x, preferred_element_type=f32)
         for part in range(2):
             for v in range(2 * PER):
@@ -334,20 +340,19 @@
 
     back = shift(own, 3)
     ahead = shift(own, -2)
-    packed, pair = pl.pallas_call(
+    packed, forth, behind = pl.pallas_call(
         pack_body,
         out_shape=(
             jax.ShapeDtypeStruct((3 * ROWS, LANES), bf16),
-            jax.ShapeDtypeStruct((2 * ROWS, LANES), bf16),
+            jax.ShapeDtypeStruct((5 * ROWS // 2, LANES), bf16),
+            jax.ShapeDtypeStruct((5 * ROWS // 2, LANES), bf16),
         ),
         in_specs=[vmem()] * 3 + [pl.BlockSpec(memory_space=pl.ANY)],
-        out_specs=(vmem(), vmem()),
+        out_specs=(vmem(),) * 3,
         compiler_params=params(),
         name="pack",
     )(own, back, ahead, phase)
-    plus = shift(packed, 1)
-    minus = shift(pair, -1)
-    near = [packed, plus, minus]
+    near = [packed, shift(forth, 1), shift(behind, -1)]
     far = [swap(x) for x in near]
 
     result = pl.pallas_call(

time: 60.6 us -> 61.2 us (level)
  starting transfers between devices: 17.9 us -> 19 us
    ppermute x3, starting transfers between devices: 8.76 us -> 9.81 us  [swap(): return lax.ppermute(x, 'kpt', [(i, i ^ 1) for i in range(16)])]
  transfers between devices with their start and end apart: 7 -> 7, of which waited for: 4 -> 3; matrix products, arithmetic and copies ran while one was open for 0% -> 0% of each run, Pallas kernels for 3% -> 3%
where the time goes in v14:
time: 61.2 us; the launch traced here: 61 us
  blocking collectives  29.1 us (48%)
  starting transfers between devices  19 us (31%)
  Pallas kernels  9.18 us (15%)
  waiting for transfers between devices  3.08 us (5%)
  between operations  0.68 us (1%)
    all_to_all x1, blocking collectives, per_device(): parts = lax.all_to_all(rotated, 'lat', 0, 0, tiled=True)  29.1 us
    ppermute x3, starting transfers between devices, swap(): return lax.ppermute(x, 'kpt', [(i, i ^ 1) for i in range(16)])  9.81 us
    ppermute x4, starting transfers between devices, shift(): return lax.ppermute(x, 'kpt', [(i, (i + 2 * step) % 16) for i in range(16)])  9.16 us
    pallas_call x1, Pallas kernels, per_device(): pl.pallas_call(couple_body, out_shape=jax.ShapeDtypeStruct((2, KPTS, NQ,...  4.89 us
    pallas_call x1, Pallas kernels, per_device(): pl.pallas_call(rotate_body, out_shape=jax.ShapeDtypeStruct((LAT, ROWS, LA...  2.11 us
    ppermute x4, waiting for transfers between devices, shift(): return lax.ppermute(x, 'kpt', [(i, (i + 2 * step) % 16) for i in range(16)])  1.95 us
    pallas_call x1, Pallas kernels, per_device(): pl.pallas_call(prep_body, out_shape=(jax.ShapeDtypeStruct((2 * KPTS, 512)...  1.93 us
  transfers between devices with their start and end apart: 7, of which 3 were waited for; matrix products, arithmetic and copies ran while one was open for 0% of the time, Pallas kernels for 3%

profile of v14, /device:TPU:1, one launch (start us, length us, event | category | flops | bytes accessed | tf_op | source)
XLA Modules:
  0.0 61.0 jit_solution(6239007228825613316)
XLA Ops:
  0.7 2.1 %rotate.1 = bf16[16,64,768]{2,1,0:T(8,128)(2,1)S(1)} custom-call(f32[2,3]{1,0:T(2,128)} %qp_hbm.1, s32[1,3]{1,0:T(1,128)} %rv_hbm.1, s32[1,1]{1,0:T(1,128)} %bitcast.12.rw_hbm, bf16[2,2,48,48]{3,2,1,0:T(8,128)(2,1)} %rot_hbm.1, bf16[2,1,16,12288]{3,2,1,0:T(8,128)(2,1)} %coarse_hbm.1), custom_call_target="tpu_custom_call" | custom-call | tf_op jit(solution)/shard_map/rotate/pallas_call | solution.py:275
  2.8 29.1 %all_to_all.5.x_ref = bf16[16,64,768]{2,1,0:T(8,128)(2,1)S(1)} all-to-all(bf16[16,64,768]{2,1,0:T(8,128)(2,1)S(1)} %rotate.1), channel_id=1, replica_groups=mesh['lat'=16,'kpt'=16] {'lat'}, dimensions={0} | all-to-all | bytes 3145728 | tf_op jit(solution)/shard_map/all_to_all | solution.py:300
  31.9 0.2 add_up.1.own_ref
  32.1 4.4 %collective-permute-start = (bf16[64,768]{1,0:T(8,128)(2,1)S(1)}, bf16[64,768]{1,0:T(8,128)(2,1)S(1)}, u32[]{:S(2)}, u32[]{:S(2)}) collective-permute-start(bf16[64,768]{1,0:T(8,128)(2,1)S(1)} %add_up.1.own_ref), channel_id=1, source_target_pairs={{0,6},{1,7},{2,8},{3,9},{4,10},{5,11},{6,12},{7,13},{8,14},{9,15},... | collective-permute-start | bytes 294920 | tf_op jit(solution)/shard_map/ppermute | solution.py:336
  36.5 1.8 %collective-permute-start.1 = (bf16[64,768]{1,0:T(8,128)(2,1)S(1)}, bf16[64,768]{1,0:T(8,128)(2,1)S(1)}, u32[]{:S(2)}, u32[]{:S(2)}) collective-permute-start(bf16[64,768]{1,0:T(8,128)(2,1)S(1)} %add_up.1.own_ref), channel_id=1, source_target_pairs={{0,12},{1,13},{2,14},{3,15},{4,0},{5,1},{6,2},{7,3},{8,4},{9,5},{1... | collective-permute-start | bytes 294920 | tf_op jit(solution)/shard_map/ppermute | solution.py:336
  38.3 1.9 %prep.1 = (bf16[128,512]{1,0:T(8,128)(2,1)S(1)}, f32[3,16,16,128]{3,2,1,0:T(8,128)S(1)}, f32[3,16,16,128]{3,2,1,0:T(8,128)S(1)}) custom-call(f32[3,64]{1,0:T(4,128)} %bitcast.18, s32[3,256]{1,0:T(4,128)} %bitcast.17, s32[1,256]{1,0:T(1,128)} %bitcast.19, bf16[2,256,64]{2,1,0:T(8,128)(2,1)} %bitcast.14, bf16[2,2,256,64]{3,2,1,0:T(8,128)(2,1)} %bitcast.13, ...), custom_call_target="tpu_custom_call" | custom-call | tf_op jit(solution)/shard_map/prep/pallas_call | solution.py:311
  40.2 0.6 %collective-permute-done.back_ref = bf16[64,768]{1,0:T(8,128)(2,1)S(1)} collective-permute-done((bf16[64,768]{1,0:T(8,128)(2,1)S(1)}, bf16[64,768]{1,0:T(8,128)(2,1)S(1)}, u32[]{:S(2)}, u32[]{:S(2)}) %collective-permute-start) | collective-permute-done | bytes 98336 | tf_op jit(solution)/shard_map/ppermute | solution.py:336
  40.9 1.3 %collective-permute-done.1.ahead_ref = bf16[64,768]{1,0:T(8,128)(2,1)S(1)} collective-permute-done((bf16[64,768]{1,0:T(8,128)(2,1)S(1)}, bf16[64,768]{1,0:T(8,128)(2,1)S(1)}, u32[]{:S(2)}, u32[]{:S(2)}) %collective-permute-start.1) | collective-permute-done | bytes 98336 | tf_op jit(solution)/shard_map/ppermute | solution.py:336
  42.2 0.1 pack.1
  42.2 2.0 %collective-permute-start.2 = (bf16[160,768]{1,0:T(8,128)(2,1)S(1)}, bf16[160,768]{1,0:T(8,128)(2,1)S(1)}, u32[]{:S(2)}, u32[]{:S(2)}) collective-permute-start(bf16[160,768]{1,0:T(8,128)(2,1)S(1)} %get-tuple-element.13), channel_id=1, source_target_pairs={{0,2},{1,3},{2,4},{3,5},{4,6},{5,7},{6,8},{7,9},{8,10},{9,11},{10,... | collective-permute-start | bytes 737288 | tf_op jit(solution)/shard_map/ppermute | solution.py:336
  44.2 1.0 %collective-permute-start.3 = (bf16[160,768]{1,0:T(8,128)(2,1)S(1)}, bf16[160,768]{1,0:T(8,128)(2,1)S(1)}, u32[]{:S(2)}, u32[]{:S(2)}) collective-permute-start(bf16[160,768]{1,0:T(8,128)(2,1)S(1)} %get-tuple-element.14), channel_id=1, source_target_pairs={{0,14},{1,15},{2,0},{3,1},{4,2},{5,3},{6,4},{7,5},{8,6},{9,7},{10,... | collective-permute-start | bytes 737288 | tf_op jit(solution)/shard_map/ppermute | solution.py:336
  45.2 3.5 %collective-permute-start.4 = (bf16[192,768]{1,0:T(8,128)(2,1)S(1)}, bf16[192,768]{1,0:T(8,128)(2,1)S(1)}, u32[]{:S(2)}, u32[]{:S(2)}) collective-permute-start(bf16[192,768]{1,0:T(8,128)(2,1)S(1)} %get-tuple-element.12.refs_0_), channel_id=1, source_target_pairs={{0,1},{1,0},{2,3},{3,2},{4,5},{5,4},{6,7},{7,6},{8,9},{9,8},{10,11... | collective-permute-start | bytes 884744 | tf_op jit(solution)/shard_map/ppermute | solution.py:339
  48.7 0.0 collective-permute-done.2.refs_1_
  48.7 4.2 %collective-permute-start.5 = (bf16[160,768]{1,0:T(8,128)(2,1)S(1)}, bf16[160,768]{1,0:T(8,128)(2,1)S(1)}, u32[]{:S(2)}, u32[]{:S(2)}) collective-permute-start(bf16[160,768]{1,0:T(8,128)(2,1)S(1)} %collective-permute-done.2.refs_1_), channel_id=1, source_target_pairs={{0,1},{1,0},{2,3},{3,2},{4,5},{5,4},{6,7},{7,6},{8,9},{9,8},{10,11... | collective-permute-start | bytes 737288 | tf_op jit(solution)/shard_map/ppermute | solution.py:339
  52.8 0.0 collective-permute-done.3.refs_2_
  52.9 2.2 %collective-permute-start.6 = (bf16[160,768]{1,0:T(8,128)(2,1)S(1)}, bf16[160,768]{1,0:T(8,128)(2,1)S(1)}, u32[]{:S(2)}, u32[]{:S(2)}) collective-permute-start(bf16[160,768]{1,0:T(8,128)(2,1)S(1)} %collective-permute-done.3.refs_2_), channel_id=1, source_target_pairs={{0,1},{1,0},{2,3},{3,2},{4,5},{5,4},{6,7},{7,6},{8,9},{9,8},{10,11... | collective-permute-start | bytes 737288 | tf_op jit(solution)/shard_map/ppermute | solution.py:339
  55.0 0.0 collective-permute-done.4.refs_3_
  55.0 0.0 collective-permute-done.5.refs_4_
  55.0 1.1 %collective-permute-done.6.refs_5_ = bf16[160,768]{1,0:T(8,128)(2,1)S(1)} collective-permute-done((bf16[160,768]{1,0:T(8,128)(2,1)S(1)}, bf16[160,768]{1,0:T(8,128)(2,1)S(1)}, u32[]{:S(2)}, u32[]{:S(2)}) %collective-permute-start.6) | collective-permute-done | bytes 245792 | tf_op jit(solution)/shard_map/ppermute | solution.py:339
  56.2 4.9 %couple.1 = bf16[2,64,2,768]{3,2,1,0:T(2,128)(2,1)} custom-call(bf16[192,768]{1,0:T(8,128)(2,1)S(1)} %get-tuple-element.12.refs_0_, bf16[160,768]{1,0:T(8,128)(2,1)S(1)} %collective-permute-done.2.refs_1_, bf16[160,768]{1,0:T(8,128)(2,1)S(1)} %collective-permute-done.3.refs_2_, bf16[192,768]{1,0:T(8,128)(2,1)S(1)} %collective-permute-done.4.refs_3_, ...), custom_call_target="tpu_custom_call" | custom-call | tf_op jit(solution)/shard_map/couple/pallas_call | solution.py:358
Async XLA Ops:
  32.1 8.8 %collective-permute-start = (bf16[64,768]{1,0:T(8,128)(2,1)S(1)}, bf16[64,768]{1,0:T(8,128)(2,1)S(1)}, u32[]{:S(2)}, u32[]{:S(2)}) collective-permute-start(bf16[64,768]{1,0:T(8,128)(2,1)S(1)} %add_up.1.own_ref), channel_id=1, source_target_pairs={{0,6},{1,7},{2,8},{3,9},{4,10},{5,11},{6,12},{7,13},{8,14},{9,15},... | collective-permute-start | bytes 294920 | tf_op jit(solution)/shard_map/ppermute | solution.py:336
  36.5 5.6 %collective-permute-start.1 = (bf16[64,768]{1,0:T(8,128)(2,1)S(1)}, bf16[64,768]{1,0:T(8,128)(2,1)S(1)}, u32[]{:S(2)}, u32[]{:S(2)}) collective-permute-start(bf16[64,768]{1,0:T(8,128)(2,1)S(1)} %add_up.1.own_ref), channel_id=1, source_target_pairs={{0,12},{1,13},{2,14},{3,15},{4,0},{5,1},{6,2},{7,3},{8,4},{9,5},{1... | collective-permute-start | bytes 294920 | tf_op jit(solution)/shard_map/ppermute | solution.py:336
  42.2 6.5 %collective-permute-start.2 = (bf16[160,768]{1,0:T(8,128)(2,1)S(1)}, bf16[160,768]{1,0:T(8,128)(2,1)S(1)}, u32[]{:S(2)}, u32[]{:S(2)}) collective-permute-start(bf16[160,768]{1,0:T(8,128)(2,1)S(1)} %get-tuple-element.13), channel_id=1, source_target_pairs={{0,2},{1,3},{2,4},{3,5},{4,6},{5,7},{6,8},{7,9},{8,10},{9,11},{10,... | collective-permute-start | bytes 737288 | tf_op jit(solution)/shard_map/ppermute | solution.py:336
  44.2 8.7 %collective-permute-start.3 = (bf16[160,768]{1,0:T(8,128)(2,1)S(1)}, bf16[160,768]{1,0:T(8,128)(2,1)S(1)}, u32[]{:S(2)}, u32[]{:S(2)}) collective-permute-start(bf16[160,768]{1,0:T(8,128)(2,1)S(1)} %get-tuple-element.14), channel_id=1, source_target_pairs={{0,14},{1,15},{2,0},{3,1},{4,2},{5,3},{6,4},{7,5},{8,6},{9,7},{10,... | collective-permute-start | bytes 737288 | tf_op jit(solution)/shard_map/ppermute | solution.py:336
  45.2 9.8 %collective-permute-start.4 = (bf16[192,768]{1,0:T(8,128)(2,1)S(1)}, bf16[192,768]{1,0:T(8,128)(2,1)S(1)}, u32[]{:S(2)}, u32[]{:S(2)}) collective-permute-start(bf16[192,768]{1,0:T(8,128)(2,1)S(1)} %get-tuple-element.12.refs_0_), channel_id=1, source_target_pairs={{0,1},{1,0},{2,3},{3,2},{4,5},{5,4},{6,7},{7,6},{8,9},{9,8},{10,11... | collective-permute-start | bytes 884744 | tf_op jit(solution)/shard_map/ppermute | solution.py:339
  48.7 6.3 %collective-permute-start.5 = (bf16[160,768]{1,0:T(8,128)(2,1)S(1)}, bf16[160,768]{1,0:T(8,128)(2,1)S(1)}, u32[]{:S(2)}, u32[]{:S(2)}) collective-permute-start(bf16[160,768]{1,0:T(8,128)(2,1)S(1)} %collective-permute-done.2.refs_1_), channel_id=1, source_target_pairs={{0,1},{1,0},{2,3},{3,2},{4,5},{5,4},{6,7},{7,6},{8,9},{9,8},{10,11... | collective-permute-start | bytes 737288 | tf_op jit(solution)/shard_map/ppermute | solution.py:339
  52.9 3.3 %collective-permute-start.6 = (bf16[160,768]{1,0:T(8,128)(2,1)S(1)}, bf16[160,768]{1,0:T(8,128)(2,1)S(1)}, u32[]{:S(2)}, u32[]{:S(2)}) collective-permute-start(bf16[160,768]{1,0:T(8,128)(2,1)S(1)} %collective-permute-done.3.refs_2_), channel_id=1, source_target_pairs={{0,1},{1,0},{2,3},{3,2},{4,5},{5,4},{6,7},{7,6},{8,9},{9,8},{10,11... | collective-permute-start | bytes 737288 | tf_op jit(solution)/shard_map/ppermute | solution.py:339

commit v15 on v13

--- a/solution.py
+++ b/solution.py
@@ -193,7 +193,7 @@
         bl_ref[1, rows, :] = xr
         bl_ref[2, rows, :] = xi
 
-    group = 4
+    group = 8
 
     def first(i, _):
         base = i * group * BANDS

time: 60.6 us -> 60.5 us (level)
  no operation moved by 1% of the time
where the time goes in v15:
time: 60.5 us; the launch traced here: 60.3 us
  blocking collectives  29.1 us (48%)
  starting transfers between devices  17.9 us (30%)
  Pallas kernels  9.04 us (15%)
  waiting for transfers between devices  3.55 us (6%)
  between operations  0.68 us (1%)
    all_to_all x1, blocking collectives, per_device(): parts = lax.all_to_all(rotated, 'lat', 0, 0, tiled=True)  29.1 us
    ppermute x4, starting transfers between devices, shift(): return lax.ppermute(x, 'kpt', [(i, (i + 2 * step) % 16) for i in range(16)])  9.16 us
    ppermute x3, starting transfers between devices, swap(): return lax.ppermute(x, 'kpt', [(i, i ^ 1) for i in range(16)])  8.76 us
    pallas_call x1, Pallas kernels, per_device(): pl.pallas_call(couple_body, out_shape=jax.ShapeDtypeStruct((2, KPTS, NQ,...  4.76 us
    ppermute x4, waiting for transfers between devices, shift(): return lax.ppermute(x, 'kpt', [(i, (i + 2 * step) % 16) for i in range(16)])  2.47 us
    pallas_call x1, Pallas kernels, per_device(): pl.pallas_call(rotate_body, out_shape=jax.ShapeDtypeStruct((LAT, ROWS, LA...  2.11 us
    pallas_call x1, Pallas kernels, per_device(): pl.pallas_call(prep_body, out_shape=(jax.ShapeDtypeStruct((2 * KPTS, 512)...  1.93 us
  transfers between devices with their start and end apart: 7, of which 4 were waited for; matrix products, arithmetic and copies ran while one was open for 0% of the time, Pallas kernels for 3%

profile of v15, /device:TPU:1, one launch (start us, length us, event | category | flops | bytes accessed | tf_op | source)
XLA Modules:
  0.0 60.3 jit_solution(3576700436684376048)
XLA Ops:
  0.7 2.1 %rotate.1 = bf16[16,64,768]{2,1,0:T(8,128)(2,1)S(1)} custom-call(f32[2,3]{1,0:T(2,128)} %qp_hbm.1, s32[1,3]{1,0:T(1,128)} %rv_hbm.1, s32[1,1]{1,0:T(1,128)} %bitcast.12.rw_hbm, bf16[2,2,48,48]{3,2,1,0:T(8,128)(2,1)} %rot_hbm.1, bf16[2,1,16,12288]{3,2,1,0:T(8,128)(2,1)} %coarse_hbm.1), custom_call_target="tpu_custom_call" | custom-call | tf_op jit(solution)/shard_map/rotate/pallas_call | solution.py:269
  2.8 29.1 %all_to_all.5.x_ref = bf16[16,64,768]{2,1,0:T(8,128)(2,1)S(1)} all-to-all(bf16[16,64,768]{2,1,0:T(8,128)(2,1)S(1)} %rotate.1), channel_id=1, replica_groups=mesh['lat'=16,'kpt'=16] {'lat'}, dimensions={0} | all-to-all | bytes 3145728 | tf_op jit(solution)/shard_map/all_to_all | solution.py:294
  31.9 0.2 add_up.1.own_ref
  32.1 4.4 %collective-permute-start = (bf16[64,768]{1,0:T(8,128)(2,1)S(1)}, bf16[64,768]{1,0:T(8,128)(2,1)S(1)}, u32[]{:S(2)}, u32[]{:S(2)}) collective-permute-start(bf16[64,768]{1,0:T(8,128)(2,1)S(1)} %add_up.1.own_ref), channel_id=1, source_target_pairs={{0,6},{1,7},{2,8},{3,9},{4,10},{5,11},{6,12},{7,13},{8,14},{9,15},... | collective-permute-start | bytes 294920 | tf_op jit(solution)/shard_map/ppermute | solution.py:330
  36.5 1.8 %collective-permute-start.1 = (bf16[64,768]{1,0:T(8,128)(2,1)S(1)}, bf16[64,768]{1,0:T(8,128)(2,1)S(1)}, u32[]{:S(2)}, u32[]{:S(2)}) collective-permute-start(bf16[64,768]{1,0:T(8,128)(2,1)S(1)} %add_up.1.own_ref), channel_id=1, source_target_pairs={{0,12},{1,13},{2,14},{3,15},{4,0},{5,1},{6,2},{7,3},{8,4},{9,5},{1... | collective-permute-start | bytes 294920 | tf_op jit(solution)/shard_map/ppermute | solution.py:330
  38.3 1.9 %prep.1 = (bf16[128,512]{1,0:T(8,128)(2,1)S(1)}, f32[3,16,16,128]{3,2,1,0:T(8,128)S(1)}, f32[3,16,16,128]{3,2,1,0:T(8,128)S(1)}) custom-call(f32[3,64]{1,0:T(4,128)} %bitcast.18, s32[3,256]{1,0:T(4,128)} %bitcast.17, s32[1,256]{1,0:T(1,128)} %bitcast.19, bf16[2,256,64]{2,1,0:T(8,128)(2,1)} %bitcast.14, bf16[2,2,256,64]{3,2,1,0:T(8,128)(2,1)} %bitcast.13, ...), custom_call_target="tpu_custom_call" | custom-call | tf_op jit(solution)/shard_map/prep/pallas_call | solution.py:305
  40.2 0.6 %collective-permute-done.back_ref = bf16[64,768]{1,0:T(8,128)(2,1)S(1)} collective-permute-done((bf16[64,768]{1,0:T(8,128)(2,1)S(1)}, bf16[64,768]{1,0:T(8,128)(2,1)S(1)}, u32[]{:S(2)}, u32[]{:S(2)}) %collective-permute-start) | collective-permute-done | bytes 98336 | tf_op jit(solution)/shard_map/ppermute | solution.py:330
  40.9 1.3 %collective-permute-done.1.ahead_ref = bf16[64,768]{1,0:T(8,128)(2,1)S(1)} collective-permute-done((bf16[64,768]{1,0:T(8,128)(2,1)S(1)}, bf16[64,768]{1,0:T(8,128)(2,1)S(1)}, u32[]{:S(2)}, u32[]{:S(2)}) %collective-permute-start.1) | collective-permute-done | bytes 98336 | tf_op jit(solution)/shard_map/ppermute | solution.py:330
  42.2 2.0 %collective-permute-start.2 = (bf16[192,768]{1,0:T(8,128)(2,1)S(1)}, bf16[192,768]{1,0:T(8,128)(2,1)S(1)}, u32[]{:S(2)}, u32[]{:S(2)}) collective-permute-start(bf16[192,768]{1,0:T(8,128)(2,1)S(1)} %get-tuple-element.11.refs_0_), channel_id=1, source_target_pairs={{0,2},{1,3},{2,4},{3,5},{4,6},{5,7},{6,8},{7,9},{8,10},{9,11},{10,... | collective-permute-start | bytes 884744 | tf_op jit(solution)/shard_map/ppermute | solution.py:330
  44.2 1.0 %collective-permute-start.3 = (bf16[128,768]{1,0:T(8,128)(2,1)S(1)}, bf16[128,768]{1,0:T(8,128)(2,1)S(1)}, u32[]{:S(2)}, u32[]{:S(2)}) collective-permute-start(bf16[128,768]{1,0:T(8,128)(2,1)S(1)} %get-tuple-element.12), channel_id=1, source_target_pairs={{0,14},{1,15},{2,0},{3,1},{4,2},{5,3},{6,4},{7,5},{8,6},{9,7},{10,... | collective-permute-start | bytes 589832 | tf_op jit(solution)/shard_map/ppermute | solution.py:330
  45.2 3.5 %collective-permute-start.4 = (bf16[192,768]{1,0:T(8,128)(2,1)S(1)}, bf16[192,768]{1,0:T(8,128)(2,1)S(1)}, u32[]{:S(2)}, u32[]{:S(2)}) collective-permute-start(bf16[192,768]{1,0:T(8,128)(2,1)S(1)} %get-tuple-element.11.refs_0_), channel_id=1, source_target_pairs={{0,1},{1,0},{2,3},{3,2},{4,5},{5,4},{6,7},{7,6},{8,9},{9,8},{10,11... | collective-permute-start | bytes 884744 | tf_op jit(solution)/shard_map/ppermute | solution.py:333
  48.7 0.5 collective-permute-done.2.refs_1_
  49.2 4.2 %collective-permute-start.5 = (bf16[192,768]{1,0:T(8,128)(2,1)S(1)}, bf16[192,768]{1,0:T(8,128)(2,1)S(1)}, u32[]{:S(2)}, u32[]{:S(2)}) collective-permute-start(bf16[192,768]{1,0:T(8,128)(2,1)S(1)} %collective-permute-done.2.refs_1_), channel_id=1, source_target_pairs={{0,1},{1,0},{2,3},{3,2},{4,5},{5,4},{6,7},{7,6},{8,9},{9,8},{10,11... | collective-permute-start | bytes 884744 | tf_op jit(solution)/shard_map/ppermute | solution.py:333
  53.4 0.0 collective-permute-done.3.refs_2_
  53.4 1.1 %collective-permute-start.6 = (bf16[128,768]{1,0:T(8,128)(2,1)S(1)}, bf16[128,768]{1,0:T(8,128)(2,1)S(1)}, u32[]{:S(2)}, u32[]{:S(2)}) collective-permute-start(bf16[128,768]{1,0:T(8,128)(2,1)S(1)} %collective-permute-done.3.refs_2_), channel_id=1, source_target_pairs={{0,1},{1,0},{2,3},{3,2},{4,5},{5,4},{6,7},{7,6},{8,9},{9,8},{10,11... | collective-permute-start | bytes 589832 | tf_op jit(solution)/shard_map/ppermute | solution.py:333
  54.5 0.0 collective-permute-done.4.refs_3_
  54.5 1.1 %collective-permute-done.6.refs_5_ = bf16[128,768]{1,0:T(8,128)(2,1)S(1)} collective-permute-done((bf16[128,768]{1,0:T(8,128)(2,1)S(1)}, bf16[128,768]{1,0:T(8,128)(2,1)S(1)}, u32[]{:S(2)}, u32[]{:S(2)}) %collective-permute-start.6) | collective-permute-done | bytes 196640 | tf_op jit(solution)/shard_map/ppermute | solution.py:333
  55.5 0.0 collective-permute-done.5.refs_4_
  55.5 4.8 %couple.1 = bf16[2,64,2,768]{3,2,1,0:T(2,128)(2,1)} custom-call(bf16[192,768]{1,0:T(8,128)(2,1)S(1)} %get-tuple-element.11.refs_0_, bf16[192,768]{1,0:T(8,128)(2,1)S(1)} %collective-permute-done.2.refs_1_, bf16[128,768]{1,0:T(8,128)(2,1)S(1)} %collective-permute-done.3.refs_2_, bf16[192,768]{1,0:T(8,128)(2,1)S(1)} %collective-permute-done.4.refs_3_, ...), custom_call_target="tpu_custom_call" | custom-call | tf_op jit(solution)/shard_map/couple/pallas_call | solution.py:353
  (1 shorter events, 0.0 us)
Async XLA Ops:
  32.1 8.8 %collective-permute-start = (bf16[64,768]{1,0:T(8,128)(2,1)S(1)}, bf16[64,768]{1,0:T(8,128)(2,1)S(1)}, u32[]{:S(2)}, u32[]{:S(2)}) collective-permute-start(bf16[64,768]{1,0:T(8,128)(2,1)S(1)} %add_up.1.own_ref), channel_id=1, source_target_pairs={{0,6},{1,7},{2,8},{3,9},{4,10},{5,11},{6,12},{7,13},{8,14},{9,15},... | collective-permute-start | bytes 294920 | tf_op jit(solution)/shard_map/ppermute | solution.py:330
  36.5 5.6 %collective-permute-start.1 = (bf16[64,768]{1,0:T(8,128)(2,1)S(1)}, bf16[64,768]{1,0:T(8,128)(2,1)S(1)}, u32[]{:S(2)}, u32[]{:S(2)}) collective-permute-start(bf16[64,768]{1,0:T(8,128)(2,1)S(1)} %add_up.1.own_ref), channel_id=1, source_target_pairs={{0,12},{1,13},{2,14},{3,15},{4,0},{5,1},{6,2},{7,3},{8,4},{9,5},{1... | collective-permute-start | bytes 294920 | tf_op jit(solution)/shard_map/ppermute | solution.py:330
  42.2 7.0 %collective-permute-start.2 = (bf16[192,768]{1,0:T(8,128)(2,1)S(1)}, bf16[192,768]{1,0:T(8,128)(2,1)S(1)}, u32[]{:S(2)}, u32[]{:S(2)}) collective-permute-start(bf16[192,768]{1,0:T(8,128)(2,1)S(1)} %get-tuple-element.11.refs_0_), channel_id=1, source_target_pairs={{0,2},{1,3},{2,4},{3,5},{4,6},{5,7},{6,8},{7,9},{8,10},{9,11},{10,... | collective-permute-start | bytes 884744 | tf_op jit(solution)/shard_map/ppermute | solution.py:330
  44.2 9.2 %collective-permute-start.3 = (bf16[128,768]{1,0:T(8,128)(2,1)S(1)}, bf16[128,768]{1,0:T(8,128)(2,1)S(1)}, u32[]{:S(2)}, u32[]{:S(2)}) collective-permute-start(bf16[128,768]{1,0:T(8,128)(2,1)S(1)} %get-tuple-element.12), channel_id=1, source_target_pairs={{0,14},{1,15},{2,0},{3,1},{4,2},{5,3},{6,4},{7,5},{8,6},{9,7},{10,... | collective-permute-start | bytes 589832 | tf_op jit(solution)/shard_map/ppermute | solution.py:330
  45.2 9.3 %collective-permute-start.4 = (bf16[192,768]{1,0:T(8,128)(2,1)S(1)}, bf16[192,768]{1,0:T(8,128)(2,1)S(1)}, u32[]{:S(2)}, u32[]{:S(2)}) collective-permute-start(bf16[192,768]{1,0:T(8,128)(2,1)S(1)} %get-tuple-element.11.refs_0_), channel_id=1, source_target_pairs={{0,1},{1,0},{2,3},{3,2},{4,5},{5,4},{6,7},{7,6},{8,9},{9,8},{10,11... | collective-permute-start | bytes 884744 | tf_op jit(solution)/shard_map/ppermute | solution.py:333
  49.2 6.4 %collective-permute-start.5 = (bf16[192,768]{1,0:T(8,128)(2,1)S(1)}, bf16[192,768]{1,0:T(8,128)(2,1)S(1)}, u32[]{:S(2)}, u32[]{:S(2)}) collective-permute-start(bf16[192,768]{1,0:T(8,128)(2,1)S(1)} %collective-permute-done.2.refs_1_), channel_id=1, source_target_pairs={{0,1},{1,0},{2,3},{3,2},{4,5},{5,4},{6,7},{7,6},{8,9},{9,8},{10,11... | collective-permute-start | bytes 884744 | tf_op jit(solution)/shard_map/ppermute | solution.py:333
  53.4 2.2 %collective-permute-start.6 = (bf16[128,768]{1,0:T(8,128)(2,1)S(1)}, bf16[128,768]{1,0:T(8,128)(2,1)S(1)}, u32[]{:S(2)}, u32[]{:S(2)}) collective-permute-start(bf16[128,768]{1,0:T(8,128)(2,1)S(1)} %collective-permute-done.3.refs_2_), channel_id=1, source_target_pairs={{0,1},{1,0},{2,3},{3,2},{4,5},{5,4},{6,7},{7,6},{8,9},{9,8},{10,11... | collective-permute-start | bytes 589832 | tf_op jit(solution)/shard_map/ppermute | solution.py:333
